TPU v7x, 32 devices: a whole 2x2x4 slice. The times are simulated.
32 devices in a mesh: dp: 8 (over y, x, core), frame: 4 (over z).
Axes of the slice: x: 2, y: 2, z: 4, core: 2. Of those that a mesh axis runs over, the one named last changes fastest.
Arguments:
- frames_in: bfloat16 [128, 256, 768], P(('dp', 'frame')), may hold values from -6 to 6
- condition: bfloat16 [128, 768], P(('dp', 'frame')), may hold values from -6 to 6
- segments: int32 [8, 16], P('dp'), may hold values from 0 to 1, as said below
- spatial_in: bfloat16 [768, 2304], P('frame'), may hold values from -0.21875 to 0.21875
- spatial_in_bias: bfloat16 [2304], P('frame'), may hold values from -3 to 3
- spatial_out: bfloat16 [768, 768], P('frame'), may hold values from -0.875 to 0.875
- spatial_out_bias: bfloat16 [768], P('frame'), may hold values from -3 to 3
- temporal_in: bfloat16 [768, 2304], P('frame'), may hold values from -0.21875 to 0.21875
- temporal_in_bias: bfloat16 [2304], P('frame'), may hold values from -3 to 3
- temporal_out: bfloat16 [768, 768], P('frame'), may hold values from -0.3125 to 0.3125
- temporal_out_bias: bfloat16 [768], P('frame'), may hold values from -3 to 3
- expand_weight: bfloat16 [768, 3072], P('frame'), may hold values from -0.21875 to 0.21875
- expand_bias: bfloat16 [3072], P('frame'), may hold values from -3 to 3
- shrink_weight: bfloat16 [3072, 768], P('frame'), may hold values from -0.109375 to 0.109375
- shrink_bias: bfloat16 [768], P('frame'), may hold values from -3 to 3
- modulate_weight: bfloat16 [768, 6912], P('frame'), may hold values from -0.21875 to 0.21875
- modulate_bias: bfloat16 [6912], P('frame'), may hold values from -3 to 3
- cotangent: bfloat16 [128, 256, 768], P(('dp', 'frame')), may hold values from -6 to 6
Outputs:
- frames_out: bfloat16 [128, 256, 768], P(('dp', 'frame'))
- grad_frames: float32 [128, 256, 768], P(('dp', 'frame'))
- grad_condition: float32 [128, 768], P(('dp', 'frame'))
- grad_spatial_in: float32 [768, 2304], P('frame')
- grad_spatial_in_bias: float32 [2304], P('frame')
- grad_spatial_out: float32 [768, 768], P('frame')
- grad_spatial_out_bias: float32 [768], P('frame')
- grad_temporal_in: float32 [768, 2304], P('frame')
- grad_temporal_in_bias: float32 [2304], P('frame')
- grad_temporal_out: float32 [768, 768], P('frame')
- grad_temporal_out_bias: float32 [768], P('frame')
- grad_expand_weight: float32 [768, 3072], P('frame')
- grad_expand_bias: float32 [3072], P('frame')
- grad_shrink_weight: float32 [3072, 768], P('frame')
- grad_shrink_bias: float32 [768], P('frame')
- grad_modulate_weight: float32 [768, 6912], P('frame')
- grad_modulate_bias: float32 [6912], P('frame')
Inputs may be any that keep to these rules, and one draw needn't show every extreme that they name: `segments`: each row holds two clips numbered 0 and 1 in order, never falling: one of exactly 12 frames and one of 4 frames, in either order.
All inputs are finite; a program needn't handle non-finite values.
Results may differ from a plain program's by a relative error of at most 0.03.
Values may be sent and summed in bfloat16 or wider, within the bound.
No kernel may reach another device: no remote copies, remote signals or barrier semaphores. Data moves between devices by JAX's collectives and lax.ppermute only.
A program may use at most 320 MiB of HBM per device.

v0:
```python
import jax
import jax.numpy as jnp
from jax import lax
from jax.sharding import PartitionSpec as P

HEADS = 12
HEAD_DIM = 64
WINDOW = 2


def extended(block, sides, width):
    for axis, dim in sides:
        count = lax.axis_size(axis)
        forward = [(i, i + 1) for i in range(count - 1)]
        backward = [(target, source) for source, target in forward]
        low = lax.ppermute(
            lax.slice_in_dim(block, block.shape[dim] - width, None, axis=dim), axis, forward
        )
        high = lax.ppermute(lax.slice_in_dim(block, 0, width, axis=dim), axis, backward)
        block = jnp.concatenate([low, block, high], axis=dim)
    return block


def passed_along(x, axis, by):
    peers = lax.axis_size(axis)
    pairs = [(i, i + by) for i in range(peers) if 0 <= i + by < peers]
    return lax.ppermute(x, axis, pairs)


def norm_mod(values, shifts, scaling):
    average = jnp.mean(values, axis=-1, keepdims=True)
    centred = values - average
    spread = jnp.mean(centred * centred, axis=-1, keepdims=True)
    return centred * lax.rsqrt(spread + 1e-06) * (1.0 + scaling[:, None, :]) + shifts[:, None, :]


def gelu_exact(values):
    return jax.nn.gelu(values, approximate=False)


def mat_dot(values, matrix):
    return lax.dot_general(
        values, matrix, (((values.ndim - 1,), (0,)), ((), ())), preferred_element_type=jnp.float32
    )


def back_dot(values, matrix):
    return lax.dot_general(
        values, matrix, (((values.ndim - 1,), (1,)), ((), ())), preferred_element_type=jnp.float32
    )


def outer_sum(left_rows, right_rows):
    left_flat = left_rows.reshape(-1, left_rows.shape[-1])
    right_flat = right_rows.reshape(-1, right_rows.shape[-1])
    return lax.dot_general(
        left_flat, right_flat, (((0,), (0,)), ((), ())), preferred_element_type=jnp.float32
    )


def column_sum(values):
    return jnp.sum(values.astype(jnp.float32).reshape(-1, values.shape[-1]), axis=0)


def arrange_rows(grad_part, parts, groups):
    shape_all = grad_part.shape
    block_rows = shape_all[0] // (parts * groups)
    moved = grad_part.reshape((parts, groups, block_rows) + shape_all[1:])
    return jnp.swapaxes(moved, 0, 1).reshape(shape_all)


def per_device(
    frames_in,
    condition,
    segments,
    spatial_in,
    spatial_in_bias,
    spatial_out,
    spatial_out_bias,
    temporal_in,
    temporal_in_bias,
    temporal_out,
    temporal_out_bias,
    expand_weight,
    expand_bias,
    shrink_weight,
    shrink_bias,
    modulate_weight,
    modulate_bias,
    cotangent,
):
    (
        full_spatial_in,
        full_spatial_inb,
        full_spatial_out,
        full_spatial_outb,
        full_temporal_in,
        full_temporal_inb,
        full_temporal_out,
        full_temporal_outb,
        full_expand,
        full_expand_bias,
        full_shrink,
        full_shrink_bias,
        full_modulate,
        full_modulate_bias,
    ) = (
        lax.all_gather(spatial_in, "frame", axis=0, tiled=True),
        lax.all_gather(spatial_in_bias, "frame", axis=0, tiled=True),
        lax.all_gather(spatial_out, "frame", axis=0, tiled=True),
        lax.all_gather(spatial_out_bias, "frame", axis=0, tiled=True),
        lax.all_gather(temporal_in, "frame", axis=0, tiled=True),
        lax.all_gather(temporal_in_bias, "frame", axis=0, tiled=True),
        lax.all_gather(temporal_out, "frame", axis=0, tiled=True),
        lax.all_gather(temporal_out_bias, "frame", axis=0, tiled=True),
        lax.all_gather(expand_weight, "frame", axis=0, tiled=True),
        lax.all_gather(expand_bias, "frame", axis=0, tiled=True),
        lax.all_gather(shrink_weight, "frame", axis=0, tiled=True),
        lax.all_gather(shrink_bias, "frame", axis=0, tiled=True),
        lax.all_gather(modulate_weight, "frame", axis=0, tiled=True),
        lax.all_gather(modulate_bias, "frame", axis=0, tiled=True),
    )
    frames, patches, model_width = frames_in.shape
    heads_shape = (frames, patches, HEADS, HEAD_DIM)
    scaling = HEAD_DIM ** (-0.5)
    span_count = 2 * WINDOW + 1
    bfloat = jnp.bfloat16
    cond_float = condition.astype(jnp.float32)
    cond_act = jax.nn.silu(cond_float).astype(bfloat)
    modvec = mat_dot(cond_act, full_modulate) + full_modulate_bias
    pieces = jnp.split(modvec, 9, axis=1)
    hidden_in = frames_in.astype(jnp.float32)
    normed_one = norm_mod(hidden_in, pieces[0], pieces[1]).astype(bfloat)
    qkv_one = (mat_dot(normed_one, full_spatial_in) + full_spatial_inb).astype(bfloat)
    queries = qkv_one[..., :model_width].reshape(heads_shape)
    keyset = qkv_one[..., model_width : 2 * model_width].reshape(heads_shape)
    valset = qkv_one[..., 2 * model_width :].reshape(heads_shape)
    raw_one = (
        jnp.einsum("fphd,fqhd->fhpq", queries, keyset, preferred_element_type=jnp.float32) * scaling
    )
    top_one = jnp.max(raw_one, axis=-1, keepdims=True)
    expo_one = jnp.exp(raw_one - top_one)
    total_one = jnp.sum(expo_one, axis=-1, keepdims=True)
    probs_one = (expo_one / total_one).astype(bfloat)
    lse_one = top_one + jnp.log(total_one)
    attn_one = jnp.einsum("fhpq,fqhd->fphd", probs_one, valset, preferred_element_type=jnp.float32)
    attn_one = attn_one.astype(bfloat).reshape(frames, patches, model_width)
    branch_one = mat_dot(attn_one, full_spatial_out) + full_spatial_outb
    after_one = hidden_in + pieces[2][:, None, :] * branch_one
    normed_two = norm_mod(after_one, pieces[3], pieces[4]).astype(bfloat)
    qkv_two = (mat_dot(normed_two, full_temporal_in) + full_temporal_inb).astype(bfloat)
    query_two = qkv_two[..., :model_width].reshape(heads_shape)
    kv_ext = extended(qkv_two[..., model_width:], (("frame", 0),), WINDOW)
    seg_row = segments[0]
    seg_pad = jnp.pad(seg_row, (WINDOW, WINDOW), constant_values=-1)
    begin = lax.axis_index("frame") * frames
    nearby = lax.dynamic_slice_in_dim(seg_pad, begin, frames + 2 * WINDOW)
    own_seg = nearby[WINDOW : WINDOW + frames]
    allowed = jnp.stack(
        [nearby[offset : offset + frames] == own_seg for offset in range(span_count)]
    )
    key_stack = jnp.stack(
        [kv_ext[offset : offset + frames, :, :model_width] for offset in range(span_count)]
    )
    key_stack = key_stack.reshape((span_count,) + heads_shape)
    val_stack = jnp.stack(
        [kv_ext[offset : offset + frames, :, model_width:] for offset in range(span_count)]
    )
    val_stack = val_stack.reshape((span_count,) + heads_shape)
    raw_two = (
        jnp.einsum("fphd,jfphd->jfhp", query_two, key_stack, preferred_element_type=jnp.float32)
        * scaling
    )
    masked = jnp.where(allowed[:, :, None, None], raw_two, -1e30)
    top_two = jnp.max(masked, axis=0, keepdims=True)
    expo_two = jnp.exp(masked - top_two)
    probs_two = expo_two / jnp.sum(expo_two, axis=0, keepdims=True)
    probs_low = probs_two.astype(bfloat)
    attn_two = jnp.einsum(
        "jfhp,jfphd->fphd", probs_low, val_stack, preferred_element_type=jnp.float32
    )
    attn_two = attn_two.astype(bfloat).reshape(frames, patches, model_width)
    branch_two = mat_dot(attn_two, full_temporal_out) + full_temporal_outb
    after_two = after_one + pieces[5][:, None, :] * branch_two
    normed_three = norm_mod(after_two, pieces[6], pieces[7]).astype(bfloat)
    pre_act = mat_dot(normed_three, full_expand) + full_expand_bias
    activ, gelu_pull = jax.vjp(gelu_exact, pre_act)
    activ_low = activ.astype(bfloat)
    branch_three = mat_dot(activ_low, full_shrink) + full_shrink_bias
    result = after_two + pieces[8][:, None, :] * branch_three
    frames_out = result.astype(bfloat)
    grad_three = cotangent.astype(jnp.float32)
    dgate_three = jnp.sum(grad_three * branch_three, axis=1)
    dbranch_three = (pieces[8][:, None, :] * grad_three).astype(bfloat)
    grad_shrink_weight = outer_sum(activ_low, dbranch_three)
    grad_shrink_bias = column_sum(dbranch_three)
    dactiv = back_dot(dbranch_three, full_shrink)
    dpre = gelu_pull(dactiv)[0].astype(bfloat)
    grad_expand_weight = outer_sum(normed_three, dpre)
    grad_expand_bias = column_sum(dpre)
    dnormed_three = back_dot(dpre, full_expand)
    dafter_two, dshift_three, dscale_three = jax.vjp(norm_mod, after_two, pieces[6], pieces[7])[1](
        dnormed_three
    )
    grad_two = grad_three + dafter_two
    dgate_two = jnp.sum(grad_two * branch_two, axis=1)
    dbranch_two = (pieces[5][:, None, :] * grad_two).astype(bfloat)
    grad_temporal_out = outer_sum(attn_two, dbranch_two)
    grad_temporal_out_bias = column_sum(dbranch_two)
    dattn_two = back_dot(dbranch_two, full_temporal_out).astype(bfloat).reshape(heads_shape)
    dprob_two = jnp.einsum(
        "fphd,jfphd->jfhp", dattn_two, val_stack, preferred_element_type=jnp.float32
    )
    rowdot_two = jnp.sum(probs_two * dprob_two, axis=0, keepdims=True)
    dscore_two = (probs_two * (dprob_two - rowdot_two)).astype(bfloat)
    dquery_two = (
        jnp.einsum("jfhp,jfphd->fphd", dscore_two, key_stack, preferred_element_type=jnp.float32)
        * scaling
    )
    dkey_stack = (
        jnp.einsum("jfhp,fphd->jfphd", dscore_two, query_two, preferred_element_type=jnp.float32)
        * scaling
    )
    dval_stack = jnp.einsum(
        "jfhp,fphd->jfphd", probs_low, dattn_two, preferred_element_type=jnp.float32
    )
    stack_shape = (span_count, frames, patches, model_width)
    dkv_stack = jnp.concatenate(
        [dkey_stack.reshape(stack_shape), dval_stack.reshape(stack_shape)], axis=-1
    )
    ext_grad = jnp.zeros((frames + 2 * WINDOW, patches, 2 * model_width), jnp.float32)
    for offset in range(span_count):
        ext_grad = ext_grad.at[offset : offset + frames].add(dkv_stack[offset])
    from_right = passed_along(ext_grad[:WINDOW].astype(jnp.bfloat16), "frame", -1).astype(
        jnp.float32
    )
    from_left = passed_along(ext_grad[frames + WINDOW :].astype(jnp.bfloat16), "frame", 1).astype(
        jnp.float32
    )
    inner_grad = ext_grad[WINDOW : WINDOW + frames]
    inner_grad = inner_grad.at[:WINDOW].add(from_left).at[frames - WINDOW :].add(from_right)
    dqkv_two = jnp.concatenate(
        [dquery_two.reshape(frames, patches, model_width), inner_grad], axis=-1
    ).astype(bfloat)
    grad_temporal_in = outer_sum(normed_two, dqkv_two)
    grad_temporal_in_bias = column_sum(dqkv_two)
    dnormed_two = back_dot(dqkv_two, full_temporal_in)
    dafter_one, dshift_two, dscale_two = jax.vjp(norm_mod, after_one, pieces[3], pieces[4])[1](
        dnormed_two
    )
    grad_one = grad_two + dafter_one
    dgate_one = jnp.sum(grad_one * branch_one, axis=1)
    dbranch_one = (pieces[2][:, None, :] * grad_one).astype(bfloat)
    grad_spatial_out = outer_sum(attn_one, dbranch_one)
    grad_spatial_out_bias = column_sum(dbranch_one)
    dattn_one = back_dot(dbranch_one, full_spatial_out).astype(bfloat).reshape(heads_shape)
    raw_again = (
        jnp.einsum("fphd,fqhd->fhpq", queries, keyset, preferred_element_type=jnp.float32) * scaling
    )
    probs_again = jnp.exp(raw_again - lse_one)
    dprob_one = jnp.einsum("fphd,fqhd->fhpq", dattn_one, valset, preferred_element_type=jnp.float32)
    rowdot_one = jnp.sum(probs_again * dprob_one, axis=-1, keepdims=True)
    dscore_one = (probs_again * (dprob_one - rowdot_one)).astype(bfloat)
    dquery_one = (
        jnp.einsum("fhpq,fqhd->fphd", dscore_one, keyset, preferred_element_type=jnp.float32)
        * scaling
    )
    dkeys_one = (
        jnp.einsum("fhpq,fphd->fqhd", dscore_one, queries, preferred_element_type=jnp.float32)
        * scaling
    )
    dvals_one = jnp.einsum(
        "fhpq,fphd->fqhd", probs_again.astype(bfloat), dattn_one, preferred_element_type=jnp.float32
    )
    row_shape = (frames, patches, model_width)
    dqkv_one = jnp.concatenate(
        [dquery_one.reshape(row_shape), dkeys_one.reshape(row_shape), dvals_one.reshape(row_shape)],
        axis=-1,
    ).astype(bfloat)
    grad_spatial_in = outer_sum(normed_one, dqkv_one)
    grad_spatial_in_bias = column_sum(dqkv_one)
    dnormed_one = back_dot(dqkv_one, full_spatial_in)
    dinput, dshift_one, dscale_one = jax.vjp(norm_mod, hidden_in, pieces[0], pieces[1])[1](
        dnormed_one
    )
    grad_frames = grad_one + dinput
    dmod = jnp.concatenate(
        [
            dshift_one,
            dscale_one,
            dgate_one,
            dshift_two,
            dscale_two,
            dgate_two,
            dshift_three,
            dscale_three,
            dgate_three,
        ],
        axis=1,
    ).astype(bfloat)
    grad_modulate_weight = outer_sum(cond_act, dmod)
    grad_modulate_bias = column_sum(dmod)
    dcond_act = back_dot(dmod, full_modulate)
    grad_condition = jax.vjp(jax.nn.silu, cond_float)[1](dcond_act)[0]
    groups = lax.axis_size("dp")
    parts = lax.axis_size("frame")
    share_list = (
        lax.psum_scatter(
            arrange_rows(grad_spatial_in, parts, groups),
            ("dp", "frame"),
            scatter_dimension=0,
            tiled=True,
        ),
        lax.psum_scatter(
            arrange_rows(grad_spatial_in_bias, parts, groups),
            ("dp", "frame"),
            scatter_dimension=0,
            tiled=True,
        ),
        lax.psum_scatter(
            arrange_rows(grad_spatial_out, parts, groups),
            ("dp", "frame"),
            scatter_dimension=0,
            tiled=True,
        ),
        lax.psum_scatter(
            arrange_rows(grad_spatial_out_bias, parts, groups),
            ("dp", "frame"),
            scatter_dimension=0,
            tiled=True,
        ),
        lax.psum_scatter(
            arrange_rows(grad_temporal_in, parts, groups),
            ("dp", "frame"),
            scatter_dimension=0,
            tiled=True,
        ),
        lax.psum_scatter(
            arrange_rows(grad_temporal_in_bias, parts, groups),
            ("dp", "frame"),
            scatter_dimension=0,
            tiled=True,
        ),
        lax.psum_scatter(
            arrange_rows(grad_temporal_out, parts, groups),
            ("dp", "frame"),
            scatter_dimension=0,
            tiled=True,
        ),
        lax.psum_scatter(
            arrange_rows(grad_temporal_out_bias, parts, groups),
            ("dp", "frame"),
            scatter_dimension=0,
            tiled=True,
        ),
        lax.psum_scatter(
            arrange_rows(grad_expand_weight, parts, groups),
            ("dp", "frame"),
            scatter_dimension=0,
            tiled=True,
        ),
        lax.psum_scatter(
            arrange_rows(grad_expand_bias, parts, groups),
            ("dp", "frame"),
            scatter_dimension=0,
            tiled=True,
        ),
        lax.psum_scatter(
            arrange_rows(grad_shrink_weight, parts, groups),
            ("dp", "frame"),
            scatter_dimension=0,
            tiled=True,
        ),
        lax.psum_scatter(
            arrange_rows(grad_shrink_bias, parts, groups),
            ("dp", "frame"),
            scatter_dimension=0,
            tiled=True,
        ),
        lax.psum_scatter(
            arrange_rows(grad_modulate_weight, parts, groups),
            ("dp", "frame"),
            scatter_dimension=0,
            tiled=True,
        ),
        lax.psum_scatter(
            arrange_rows(grad_modulate_bias, parts, groups),
            ("dp", "frame"),
            scatter_dimension=0,
            tiled=True,
        ),
    )
    summed = (
        lax.all_gather(share_list[0].astype(jnp.bfloat16), "dp", axis=0, tiled=True).astype(
            jnp.float32
        ),
        lax.all_gather(share_list[1].astype(jnp.bfloat16), "dp", axis=0, tiled=True).astype(
            jnp.float32
        ),
        lax.all_gather(share_list[2].astype(jnp.bfloat16), "dp", axis=0, tiled=True).astype(
            jnp.float32
        ),
        lax.all_gather(share_list[3].astype(jnp.bfloat16), "dp", axis=0, tiled=True).astype(
            jnp.float32
        ),
        lax.all_gather(share_list[4].astype(jnp.bfloat16), "dp", axis=0, tiled=True).astype(
            jnp.float32
        ),
        lax.all_gather(share_list[5].astype(jnp.bfloat16), "dp", axis=0, tiled=True).astype(
            jnp.float32
        ),
        lax.all_gather(share_list[6].astype(jnp.bfloat16), "dp", axis=0, tiled=True).astype(
            jnp.float32
        ),
        lax.all_gather(share_list[7].astype(jnp.bfloat16), "dp", axis=0, tiled=True).astype(
            jnp.float32
        ),
        lax.all_gather(share_list[8].astype(jnp.bfloat16), "dp", axis=0, tiled=True).astype(
            jnp.float32
        ),
        lax.all_gather(share_list[9].astype(jnp.bfloat16), "dp", axis=0, tiled=True).astype(
            jnp.float32
        ),
        lax.all_gather(share_list[10].astype(jnp.bfloat16), "dp", axis=0, tiled=True).astype(
            jnp.float32
        ),
        lax.all_gather(share_list[11].astype(jnp.bfloat16), "dp", axis=0, tiled=True).astype(
            jnp.float32
        ),
        lax.all_gather(share_list[12].astype(jnp.bfloat16), "dp", axis=0, tiled=True).astype(
            jnp.float32
        ),
        lax.all_gather(share_list[13].astype(jnp.bfloat16), "dp", axis=0, tiled=True).astype(
            jnp.float32
        ),
    )
    return (
        frames_out,
        grad_frames,
        grad_condition,
        summed[0],
        summed[1],
        summed[2],
        summed[3],
        summed[4],
        summed[5],
        summed[6],
        summed[7],
        summed[8],
        summed[9],
        summed[10],
        summed[11],
        summed[12],
        summed[13],
    )


def solution(mesh):
    in_specs = (
        P(("dp", "frame"), None, None),
        P(("dp", "frame"), None),
        P("dp", None),
        P("frame", None),
        P("frame"),
        P("frame", None),
        P("frame"),
        P("frame", None),
        P("frame"),
        P("frame", None),
        P("frame"),
        P("frame", None),
        P("frame"),
        P("frame", None),
        P("frame"),
        P("frame", None),
        P("frame"),
        P(("dp", "frame"), None, None),
    )
    out_specs = (
        P(("dp", "frame"), None, None),
        P(("dp", "frame"), None, None),
        P(("dp", "frame"), None),
        P("frame", None),
        P("frame"),
        P("frame", None),
        P("frame"),
        P("frame", None),
        P("frame"),
        P("frame", None),
        P("frame"),
        P("frame", None),
        P("frame"),
        P("frame", None),
        P("frame"),
        P("frame", None),
        P("frame"),
    )
    return jax.shard_map(
        per_device, mesh=mesh, in_specs=in_specs, out_specs=out_specs, check_vma=False
    )
```

profile of v0, /device:TPU:0, one launch (start us, length us, event | category | flops | bytes accessed | tf_op | source)
XLA Modules:
  0.0 1718.6 jit_solution(596738419373905486)
XLA Ops:
  16.3 28.5 %all-reduce.24 = (bf16[6912]{0:T(1024)(128)(2,1)S(1)}, bf16[2304]{0:T(1024)(128)(2,1)S(1)}, bf16[768]{0:T(1024)(128)(2,1)S(1)}, bf16[2304]{0:T(1024)(128)(2,1)S(...) all-reduce(bf16[6912]{0:T(1024)(128)(2,1)S(1)} %dynamic-update-slic, ...), channel_id=1, replica_groups=mesh['dp'=8,'frame'=4] {'frame'}, use_global_device_ids=true, to_apply=%add.2 | all-reduce | flops 13824 | bytes 55296
  44.9 154.2 %all-gather.12.cloned.1.call-done = bf16[768,6912]{1,0:T(8,128)(2,1)} async-done(((bf16[192,6912]{1,0:T(8,128)(2,1)}), bf16[768,6912]{1,0:T(8,128)(2,1)}) %all-gather.12.cloned.1.call-update) | async-done | bytes 10616848 | tf_op jit(solution)/shard_map/all_gather | solution.py:120
  207.1 62.0 %all-gather.14.cloned.1.call-done = bf16[768,2304]{1,0:T(8,128)(2,1)} async-done(((bf16[192,2304]{1,0:T(8,128)(2,1)}), bf16[768,2304]{1,0:T(8,128)(2,1)}) %all-gather.14.cloned.1.call-update) | async-done | bytes 3538960 | tf_op jit(solution)/shard_map/all_gather | solution.py:108
  307.9 62.2 %all-gather.18.cloned.1.call-done = bf16[768,2304]{1,0:T(8,128)(2,1)} async-done(((bf16[192,2304]{1,0:T(8,128)(2,1)}), bf16[768,2304]{1,0:T(8,128)(2,1)}) %all-gather.18.cloned.1.call-update) | async-done | bytes 3538960 | tf_op jit(solution)/shard_map/all_gather | solution.py:112
  386.7 63.4 %all-gather = bf16[4,1,768]{2,1,0:T(2,128)(2,1)S(1)} all-gather(bf16[1,1,768]{2,1,0:T(2,128)(2,1)S(1)} %reshape.654), channel_id=1, replica_groups=mesh['dp'=8,'frame'=4] {'frame'}, dimensions={0}, use_global_device_ids=true | all-gather | bytes 7680 | tf_op jit(solution)/shard_map/all_gather | solution.py:117
  504.3 7.5 multiply_reduce_fusion.3
  531.0 10.9 fusion.68
  546.5 30.3 %multiply_convert_fusion.1 = (bf16[4,256,3072]{2,1,0:T(8,128)(2,1)}, f32[4,256,3072]{2,1,0:T(8,128)}) fusion(f32[4,256,3072]{2,1,0:T(8,128)S(1)} %get-tuple-element.196, f32[3072]{0:T(1024)S(1)} %bitcast.401, u8[256,3072]{1,0:T(8,128)(4,1)S(1)} %get-tuple-element.102, u8[256,3072]{1,0:T(8,128)(4,1)S(1)} %get-tuple-element.101), kind=kLoop, calls=%fused_computation.25 | loop fusion | flops 223346688 | bytes 33042432 | tf_op jit(solution)/shard_map/convert_element_type | solution.py:188
  576.7 24.1 %all-gather.24.cloned.1.call-done = bf16[3072,768]{1,0:T(8,128)(2,1)} async-done(((bf16[768,768]{1,0:T(8,128)(2,1)}), bf16[3072,768]{1,0:T(8,128)(2,1)}) %all-gather.24.cloned.1.call-update) | async-done | bytes 4718608 | tf_op jit(solution)/shard_map/all_gather | solution.py:118
  600.9 17.1 convert_reduce_fusion
  617.9 7.2 convolution_bitcast_fusion
  631.3 10.5 multiply_reduce_fusion.6
  648.8 6.7 multiply_reduce_fusion.1
  656.3 8.5 broadcast_multiply_fusion
  664.8 16.3 copy.236
  683.0 7.8 multiply_multiply_fusion
  690.8 15.7 copy.235
  706.6 7.1 fusion.15
  713.7 9.6 scatter-add.24
  723.4 6.7 fusion.19
  730.1 6.9 fusion.23
  744.9 9.3 fusion.25
  763.7 10.3 multiply_reduce_fusion
  782.6 8.8 copy.268
  792.7 7.5 convolution_bitcast_fusion.3
  809.5 19.9 %collective-permute-done.3 = bf16[2,256,1536]{2,1,0:T(8,128)(2,1)} collective-permute-done((bf16[2,256,1536]{2,1,0:T(8,128)(2,1)S(1)}, bf16[2,256,1536]{2,1,0:T(8,128)(2,1)}, u32[]{:S(2)}, u32[]{:S(2)}) %collective-permute-start.3) | collective-permute-done | bytes 1572896 | tf_op jit(solution)/shard_map/ppermute | solution.py:27
  847.5 11.2 fusion.64
  862.7 6.9 fusion.70
  871.4 7.2 multiply_reduce_fusion.4
  878.6 7.4 multiply_convert_fusion
  897.3 7.2 fusion.62
  912.2 7.5 copy.271
  936.8 6.8 convolution_bitcast_fusion.1
  976.1 191.4 %reduce-scatter.20.cloned.1.call-done = f32[24,6912]{1,0:T(8,128)} async-done(((f32[768,6912]{1,0:T(8,128)}), f32[24,6912]{1,0:T(8,128)}) %reduce-scatter.20.cloned.1.call-update) | async-done | bytes 663568 | tf_op jit(solution)/shard_map/reduce_scatter | solution.py:380
  1178.9 41.4 %all-reduce.22 = (bf16[2304]{0:T(1024)(128)(2,1)S(1)}, bf16[768]{0:T(1024)(128)(2,1)S(1)}, bf16[2304]{0:T(1024)(128)(2,1)S(1)}, bf16[768]{0:T(1024)(128)(2,1)S(1...) all-reduce(f32[2304]{0:T(1024)S(1)} %reshape.588, ...), channel_id=3, replica_groups=mesh['dp'=8,'frame'=4] {'dp','frame'}, use_global_device_ids=true, to_apply=%region_29.30.clone | all-reduce | flops 16896 | bytes 101376
  1222.3 23.6 %all-reduce.23 = (bf16[576]{0:T(1024)(128)(2,1)S(1)}, bf16[192]{0:T(256)(128)(2,1)S(1)}, bf16[576]{0:T(1024)(128)(2,1)S(1)}, bf16[192]{0:T(256)(128)(2,1)S(1)}, ...) all-reduce(bf16[576]{0:T(1024)(128)(2,1)S(1)} %dynamic-update-slice, ...), channel_id=1, replica_groups=mesh['dp'=8,'frame'=4] {'dp'}, use_global_device_ids=true, to_apply=%add.8 | all-reduce | flops 4224 | bytes 16896
  1250.0 7.6 fusion.98
  1257.6 15.0 reduce-scatter.14.cloned.1.call-done
  1273.5 9.3 all_gather.104
  1283.6 93.3 %reduce-scatter.10.cloned.1.call-done = f32[24,768]{1,0:T(8,128)} async-done(((f32[768,768]{1,0:T(8,128)}), f32[24,768]{1,0:T(8,128)}) %reduce-scatter.10.cloned.1.call-update) | async-done | bytes 73744 | tf_op jit(solution)/shard_map/reduce_scatter | solution.py:320
  1377.8 9.3 all_gather.100
  1388.0 113.2 %reduce-scatter.12.cloned.1.call-done = f32[24,2304]{1,0:T(8,128)} async-done(((f32[768,2304]{1,0:T(8,128)}), f32[24,2304]{1,0:T(8,128)}) %reduce-scatter.12.cloned.1.call-update) | async-done | bytes 221200 | tf_op jit(solution)/shard_map/reduce_scatter | solution.py:332
  1502.2 10.6 all_gather.102
  1514.1 111.1 %reduce-scatter.8.cloned.1.call-done = f32[24,2304]{1,0:T(8,128)} async-done(((f32[768,2304]{1,0:T(8,128)}), f32[24,2304]{1,0:T(8,128)}) %reduce-scatter.8.cloned.1.call-update) | async-done | bytes 221200 | tf_op jit(solution)/shard_map/reduce_scatter | solution.py:308
  1626.2 10.7 all_gather.98
  1638.2 11.6 all-gather.26.cloned.1.call-done
  1652.8 22.8 %all-gather.28.cloned.1.call-done = bf16[768,768]{1,0:T(8,128)(2,1)} async-done(((bf16[96,768]{1,0:T(8,128)(2,1)}), bf16[768,768]{1,0:T(8,128)(2,1)}) %all-gather.28.cloned.1.call-update) | async-done | bytes 1179664 | tf_op jit(solution)/shard_map/all_gather | solution.py:424
  1678.4 29.0 %all-gather.30.cloned.1.call-done = bf16[192,6912]{1,0:T(8,128)(2,1)} async-done(((bf16[24,6912]{1,0:T(8,128)(2,1)}), bf16[192,6912]{1,0:T(8,128)(2,1)}) %all-gather.30.cloned.1.call-update) | async-done | bytes 2654224 | tf_op jit(solution)/shard_map/all_gather | solution.py:430
  (533 shorter events, 324.9 us)
Async XLA Ops:
  7.2 191.8 %all-gather.12.cloned.1.call-start = ((), (), s32[]{:S(2)}) async-start(), calls=%async_computation.7 | async-start | bytes 13271040 | tf_op jit(solution)/shard_map/all_gather | solution.py:120
  8.0 261.1 %all-gather.14.cloned.1.call-start = ((), (), s32[]{:S(2)}) async-start(), calls=%async_computation.8 | async-start | bytes 4423680 | tf_op jit(solution)/shard_map/all_gather | solution.py:108
  8.8 190.3 %copy-start.71 = (bf16[4,768]{1,0:T(4,128)(2,1)S(1)}, bf16[4,768]{1,0:T(4,128)(2,1)}, u32[]{:S(2)}) copy-start(bf16[4,768]{1,0:T(4,128)(2,1)} %param.33) | copy-start | bytes 18436
  8.8 290.7 %all-gather.16.cloned.1.call-start = ((), (), s32[]{:S(2)}) async-start(), calls=%async_computation.9 | async-start | bytes 1474560 | tf_op jit(solution)/shard_map/all_gather | solution.py:110
  9.5 360.6 %all-gather.18.cloned.1.call-start = ((), (), s32[]{:S(2)}) async-start(), calls=%async_computation.10 | async-start | bytes 4423680 | tf_op jit(solution)/shard_map/all_gather | solution.py:112
  10.1 513.0 %all-gather.20.cloned.1.call-start = ((), (), s32[]{:S(2)}) async-start(), calls=%async_computation.11 | async-start | bytes 1474560 | tf_op jit(solution)/shard_map/all_gather | solution.py:114
  10.7 520.3 %all-gather.22.cloned.1.call-start = ((), (), s32[]{:S(2)}) async-start(), calls=%async_computation.12 | async-start | bytes 5898240 | tf_op jit(solution)/shard_map/all_gather | solution.py:116
  11.2 589.6 %all-gather.24.cloned.1.call-start = ((), (), s32[]{:S(2)}) async-start(), calls=%async_computation.13 | async-start | bytes 5898240 | tf_op jit(solution)/shard_map/all_gather | solution.py:118
  14.1 191.1 %copy-start.69 = (f32[4,256]{1,0:T(4,128)}, f32[4,256]{1,0:T(4,128)S(1)}, u32[]{:S(2)}) copy-start(f32[4,256]{1,0:T(4,128)S(1)} %broadcast_multiply_fusion.3) | copy-start | bytes 12292
  14.8 190.5 %copy-start.73 = (f32[4,256]{1,0:T(4,128)}, f32[4,256]{1,0:T(4,128)S(1)}, u32[]{:S(2)}) copy-start(f32[4,256]{1,0:T(4,128)S(1)} %fusion.99) | copy-start | bytes 12292
  44.8 254.7 %copy-start.83 = (f32[768]{0:T(1024)}, f32[768]{0:T(1024)S(1)}, u32[]{:S(2)}) copy-start(f32[768]{0:T(1024)S(1)} %convert_element_type.228) | copy-start | bytes 9220
  205.2 94.3 %copy-start.80 = (f32[4,768]{1,0:T(4,128)}, f32[4,768]{1,0:T(4,128)S(1)}, u32[]{:S(2)}) copy-start(f32[4,768]{1,0:T(4,128)S(1)} %get-tuple-element.187) | copy-start | bytes 36868
  205.2 100.4 %copy-start.66 = (f32[4,768]{1,0:T(4,128)}, f32[4,768]{1,0:T(4,128)S(1)}, u32[]{:S(2)}) copy-start(f32[4,768]{1,0:T(4,128)S(1)} %get-tuple-element.183) | copy-start | bytes 36868
  205.2 265.6 %copy-start.78 = (f32[4,768]{1,0:T(4,128)}, f32[4,768]{1,0:T(4,128)S(1)}, u32[]{:S(2)}) copy-start(f32[4,768]{1,0:T(4,128)S(1)} %get-tuple-element.179) | copy-start | bytes 36868
  207.0 68.0 %copy-start.33 = (bf16[4,256,768]{2,1,0:T(8,128)(2,1)}, bf16[4,256,768]{2,1,0:T(8,128)(2,1)S(1)}, u32[]{:S(2)}) copy-start(bf16[4,256,768]{2,1,0:T(8,128)(2,1)S(1)} %fusion.59) | copy-start | bytes 4718596
  305.0 218.1 %copy-start.3 = (f32[4,256,768]{2,1,0:T(8,128)}, f32[4,256,768]{2,1,0:T(8,128)S(1)}, u32[]{:S(2)}) copy-start(f32[4,256,768]{2,1,0:T(8,128)S(1)} %get-tuple-element.150) | copy-start | bytes 9437188
  305.5 70.9 %copy-start.91 = (f32[4,256]{1,0:T(4,128)}, f32[4,256]{1,0:T(4,128)S(1)}, u32[]{:S(2)}) copy-start(f32[4,256]{1,0:T(4,128)S(1)} %multiply_reduce_fusion.13) | copy-start | bytes 12292
  305.5 70.9 %copy-start.87 = (f32[4,256]{1,0:T(4,128)}, f32[4,256]{1,0:T(4,128)S(1)}, u32[]{:S(2)}) copy-start(f32[4,256]{1,0:T(4,128)S(1)} %fusion.100) | copy-start | bytes 12292
  376.5 75.4 %copy-start.115 = (s32[1,16]{1,0:T(1,128)S(1)}, s32[1,16]{1,0:T(1,128)}, u32[]{:S(2)}) copy-start(s32[1,16]{1,0:T(1,128)} %param.34) | copy-start | bytes 196
  379.6 93.4 %collective-permute-start.1 = (bf16[2,256,1536]{2,1,0:T(8,128)(2,1)}, bf16[2,256,1536]{2,1,0:T(8,128)(2,1)}, u32[]{:S(2)}, u32[]{:S(2)}) collective-permute-start(bf16[2,256,1536]{2,1,0:T(8,128)(2,1)} %get-tuple-element.165), channel_id=1, source_target_pairs={{1,0},{2,1},{3,2},{5,4},{6,5},{7,6},{9,8},{10,9},{11,10},{13,12},{... | collective-permute-start | bytes 4718600 | tf_op jit(solution)/shard_map/ppermute | solution.py:19
  380.9 92.1 %collective-permute-start = (bf16[2,256,1536]{2,1,0:T(8,128)(2,1)}, bf16[2,256,1536]{2,1,0:T(8,128)(2,1)}, u32[]{:S(2)}, u32[]{:S(2)}) collective-permute-start(bf16[2,256,1536]{2,1,0:T(8,128)(2,1)} %get-tuple-element.166), channel_id=1, source_target_pairs={{0,1},{1,2},{2,3},{4,5},{5,6},{6,7},{8,9},{9,10},{10,11},{12,13},{... | collective-permute-start | bytes 4718600 | tf_op jit(solution)/shard_map/ppermute | solution.py:16
  386.6 585.8 %reduce-scatter.16.cloned.1.call-start = ((), (), s32[]{:S(2)}) async-start(), calls=%async_computation.18 | async-start | bytes 9732096 | tf_op jit(solution)/shard_map/reduce_scatter | solution.py:356
  452.1 60.0 %copy-start.95 = (pred[5,4]{1,0:T(8,128)(4,1)}, pred[5,4]{1,0:T(8,128)(4,1)S(1)}, u32[]{:S(2)}) copy-start(pred[5,4]{1,0:T(8,128)(4,1)S(1)} %stack.59) | copy-start | bytes 64
  531.0 15.5 copy-start.77
  546.5 54.4 %copy-start.52 = (bf16[4,256,768]{2,1,0:T(8,128)(2,1)S(1)}, bf16[4,256,768]{2,1,0:T(8,128)(2,1)}, u32[]{:S(2)}) copy-start(bf16[4,256,768]{2,1,0:T(8,128)(2,1)} %get-tuple-element.135) | copy-start | bytes 4718596
  629.5 344.9 %reduce-scatter.18.cloned.1.call-start = ((), (), s32[]{:S(2)}) async-start(), calls=%async_computation.20 | async-start | bytes 9732096 | tf_op jit(solution)/shard_map/reduce_scatter | solution.py:368
  664.8 18.2 %copy-start.27 = (f32[4,256,12,64]{1,3,2,0:T(8,128)S(1)}, f32[4,256,12,64]{1,3,2,0:T(8,128)}, u32[]{:S(2)}) copy-start(f32[4,256,12,64]{1,3,2,0:T(8,128)} %convert.79) | copy-start | bytes 9437188
  706.6 16.7 slice-start
  706.6 16.7 slice-start.1
  706.6 16.7 slice-start.2
  723.3 13.7 slice-start.4
  723.3 15.4 slice-start.6
  744.9 15.5 copy-start.1
  757.9 47.1 %collective-permute-start.2 = (bf16[2,256,1536]{2,1,0:T(8,128)(2,1)}, bf16[2,256,1536]{2,1,0:T(8,128)(2,1)}, u32[]{:S(2)}, u32[]{:S(2)}) collective-permute-start(bf16[2,256,1536]{2,1,0:T(8,128)(2,1)} %slice.446), channel_id=1, source_target_pairs={{0,1},{1,2},{2,3},{4,5},{5,6},{6,7},{8,9},{9,10},{10,11},{12,13},{... | collective-permute-start | bytes 4718600 | tf_op jit(solution)/shard_map/ppermute | solution.py:27
  791.4 38.0 %collective-permute-start.3 = (bf16[2,256,1536]{2,1,0:T(8,128)(2,1)S(1)}, bf16[2,256,1536]{2,1,0:T(8,128)(2,1)}, u32[]{:S(2)}, u32[]{:S(2)}) collective-permute-start(bf16[2,256,1536]{2,1,0:T(8,128)(2,1)S(1)} %copy-done.55), channel_id=1, source_target_pairs={{1,0},{2,1},{3,2},{5,4},{6,5},{7,6},{9,8},{10,9},{11,10},{13,12},{... | collective-permute-start | bytes 4718600 | tf_op jit(solution)/shard_map/ppermute | solution.py:27
  804.9 362.5 %reduce-scatter.20.cloned.1.call-start = ((), (), s32[]{:S(2)}) async-start(), calls=%async_computation.22 | async-start | bytes 21897216 | tf_op jit(solution)/shard_map/reduce_scatter | solution.py:380
  919.8 352.8 %reduce-scatter.14.cloned.1.call-start = ((), (), s32[]{:S(2)}) async-start(), calls=%async_computation.17 | async-start | bytes 2433024 | tf_op jit(solution)/shard_map/reduce_scatter | solution.py:344
  925.9 451.1 %reduce-scatter.10.cloned.1.call-start = ((), (), s32[]{:S(2)}) async-start(), calls=%async_computation.15 | async-start | bytes 2433024 | tf_op jit(solution)/shard_map/reduce_scatter | solution.py:320
  930.9 570.3 %reduce-scatter.12.cloned.1.call-start = ((), (), s32[]{:S(2)}) async-start(), calls=%async_computation.16 | async-start | bytes 7299072 | tf_op jit(solution)/shard_map/reduce_scatter | solution.py:332
  947.2 678.0 %reduce-scatter.8.cloned.1.call-start = ((), (), s32[]{:S(2)}) async-start(), calls=%async_computation.14 | async-start | bytes 7299072 | tf_op jit(solution)/shard_map/reduce_scatter | solution.py:308
  972.3 197.0 %copy-start.117 = (u32[32]{0:T(128)S(1)}, u32[32]{0:T(128)}, u32[]{:S(2)}) copy-start(u32[32]{0:T(128)} %constant.332) | copy-start | bytes 388
  972.3 200.2 %copy-start.97 = (f32[768]{0:T(1024)S(1)}, f32[768]{0:T(1024)}, u32[]{:S(2)}) copy-start(f32[768]{0:T(1024)} %get-tuple-element.134) | copy-start | bytes 9220
  972.3 200.4 %copy-start.103 = (f32[3072]{0:T(1024)S(1)}, f32[3072]{0:T(1024)}, u32[]{:S(2)}) copy-start(f32[3072]{0:T(1024)} %get-tuple-element.204) | copy-start | bytes 36868
  972.3 200.6 %copy-start.100 = (f32[768]{0:T(1024)S(1)}, f32[768]{0:T(1024)}, u32[]{:S(2)}) copy-start(f32[768]{0:T(1024)} %get-tuple-element.136) | copy-start | bytes 9220
  972.3 200.8 %copy-start.32 = (bf16[4,256,1536]{2,1,0:T(8,128)(2,1)S(1)}, bf16[4,256,1536]{2,1,0:T(8,128)(2,1)}, u32[]{:S(2)}) copy-start(bf16[4,256,1536]{2,1,0:T(8,128)(2,1)} %copy-done.31) | copy-start | bytes 9437188
  972.4 677.5 %all-gather.26.cloned.1.call-start = ((), (), s32[]{:S(2)}) async-start(), calls=%async_computation.19 | async-start | bytes 1327104 | tf_op jit(solution)/shard_map/all_gather | solution.py:418
  974.3 701.2 %all-gather.28.cloned.1.call-start = ((), (), s32[]{:S(2)}) async-start(), calls=%async_computation.21 | async-start | bytes 1327104 | tf_op jit(solution)/shard_map/all_gather | solution.py:424
  976.0 731.4 %all-gather.30.cloned.1.call-start = ((), (), s32[]{:S(2)}) async-start(), calls=%async_computation.23 | async-start | bytes 2985984 | tf_op jit(solution)/shard_map/all_gather | solution.py:430
  (103 other events, 459.6 us)
Sparse Core Ops, SparseCore 0:
  9.6 189.4 all-gather.11
  200.6 68.3 all-gather.13
  270.6 28.8 all-gather.15
  300.9 69.1 all-gather.17
  371.5 38.2 all-gather.19
  411.2 99.6 all-gather.21
  512.5 88.3 all-gather.23
  629.6 134.5 reduce-scatter.15
  805.1 136.6 reduce-scatter.17
  948.0 219.3 reduce-scatter.19
  1173.3 99.2 reduce-scatter.13
  1278.3 98.6 reduce-scatter.9
  1382.6 118.5 reduce-scatter.11
  1506.7 118.4 reduce-scatter.7
  1627.0 22.8 all-gather.25
  1651.6 23.9 all-gather.27
  1677.2 30.1 all-gather.29
where the time goes:
time: 1720 us
  waiting for transfers between devices  918 us (53%)
  local copies, waits for them, and re-layouts  205 us (12%)
  other arithmetic  205 us (12%)
  blocking collectives  197 us (11%)
  matrix products  162 us (9%)
  between operations  20.7 us (1%)
    reduce_scatter x1, waiting for transfers between devices, per_device(): lax.psum_scatter(arrange_rows(grad_modulate_weight, parts, groups), ('dp'...  191 us
    all_gather x1, waiting for transfers between devices, per_device(): lax.all_gather(modulate_weight, 'frame', axis=0, tiled=True)  154 us
    reduce_scatter x1, waiting for transfers between devices, per_device(): lax.psum_scatter(arrange_rows(grad_temporal_in, parts, groups), ('dp', 'f...  113 us
    reduce_scatter x1, waiting for transfers between devices, per_device(): lax.psum_scatter(arrange_rows(grad_spatial_in, parts, groups), ('dp', 'fr...  111 us
    unnamed x3, blocking collectives  93.5 us
    reduce_scatter x1, waiting for transfers between devices, per_device(): lax.psum_scatter(arrange_rows(grad_spatial_out, parts, groups), ('dp', 'f...  93.3 us
    all_gather x1, blocking collectives, per_device(): lax.all_gather(expand_bias, 'frame', axis=0, tiled=True)  63.4 us
    all_gather x1, waiting for transfers between devices, per_device(): lax.all_gather(temporal_in, 'frame', axis=0, tiled=True)  62.2 us
  transfers between devices with their start and end apart: 21, of which 14 were waited for; matrix products, arithmetic and copies ran while one was open for 29% of the time, Pallas kernels for 0%

commit v1 on v0

--- a/solution.py
+++ b/solution.py
@@ -62,11 +62,83 @@
     return jnp.sum(values.astype(jnp.float32).reshape(-1, values.shape[-1]), axis=0)
 
 
-def arrange_rows(grad_part, parts, groups):
-    shape_all = grad_part.shape
-    block_rows = shape_all[0] // (parts * groups)
-    moved = grad_part.reshape((parts, groups, block_rows) + shape_all[1:])
-    return jnp.swapaxes(moved, 0, 1).reshape(shape_all)
+def own_part(vector):
+    size = vector.shape[0] // lax.axis_size("frame")
+    return lax.dynamic_slice_in_dim(vector, lax.axis_index("frame") * size, size)
+
+
+def stacked(block, width):
+    count = block.shape[-1] // width
+    return jnp.concatenate(
+        [block[..., k * width : (k + 1) * width] for k in range(count)], axis=-2
+    )
+
+
+def unstacked(block, count):
+    rows = block.shape[-2] // count
+    return jnp.concatenate(
+        [block[..., k * rows : (k + 1) * rows, :] for k in range(count)], axis=-1
+    )
+
+
+def gathered(shards):
+    groups, parts = lax.axis_size("dp"), lax.axis_size("frame")
+    width = min(shard.shape[1] for shard in shards)
+    pieces = []
+    for shard in shards:
+        rows = shard.shape[0] // groups
+        piece = lax.dynamic_slice_in_dim(shard, lax.axis_index("dp") * rows, rows)
+        pieces.append(stacked(piece, width))
+    mine = jnp.concatenate(pieces, axis=0)
+    column = lax.all_gather(mine, "frame", axis=0)
+    whole = lax.all_gather(column, "dp", axis=0)
+    results, at = [], 0
+    for shard, piece in zip(shards, pieces):
+        part = unstacked(whole[:, :, at : at + piece.shape[0]], shard.shape[1] // width)
+        results.append(jnp.swapaxes(part, 0, 1).reshape(parts * shard.shape[0], shard.shape[1]))
+        at += piece.shape[0]
+    return results
+
+
+def gathered_small(biases, condition):
+    parts = lax.axis_size("frame")
+    flat = jnp.concatenate(biases + [condition.reshape(-1)])
+    rows = lax.all_gather(flat, "frame", axis=0)
+    results, at = [], 0
+    for bias in biases:
+        results.append(rows[:, at : at + bias.shape[0]].reshape(-1))
+        at += bias.shape[0]
+    results.append(rows[:, at:].reshape(parts * condition.shape[0], condition.shape[1]))
+    return results
+
+
+def modulated(act_group, matrix, frames):
+    parts = lax.axis_size("frame")
+    rows, width = matrix.shape
+    columns = lax.dynamic_slice_in_dim(act_group, lax.axis_index("frame") * rows, rows, axis=1)
+    partial = mat_dot(columns, matrix).reshape(parts, frames, width)
+    return jnp.sum(lax.all_to_all(partial, "frame", split_axis=0, concat_axis=0), axis=0)
+
+
+def reduced(grads):
+    groups, parts = lax.axis_size("dp"), lax.axis_size("frame")
+    width = min(grad.shape[1] for grad in grads)
+    blocks = []
+    for grad in grads:
+        rows = grad.shape[0] // (groups * parts)
+        part = grad.astype(jnp.bfloat16).reshape(parts, groups, rows, grad.shape[1])
+        blocks.append(stacked(jnp.swapaxes(part, 0, 1), width))
+    stack = jnp.concatenate(blocks, axis=2)
+    size = stack.shape[2]
+    column = lax.psum_scatter(stack.reshape(-1, width), "dp", scatter_dimension=0, tiled=True)
+    mine = lax.psum_scatter(column, "frame", scatter_dimension=0, tiled=True)
+    whole = lax.all_gather(mine, "dp", axis=0, tiled=True).reshape(groups, size, width)
+    results, at = [], 0
+    for grad, block in zip(grads, blocks):
+        part = unstacked(whole[:, at : at + block.shape[2]], grad.shape[1] // width)
+        results.append(part.reshape(-1, grad.shape[1]).astype(jnp.float32))
+        at += block.shape[2]
+    return results
 
 
 def per_device(
@@ -89,45 +161,38 @@
     modulate_bias,
     cotangent,
 ):
+    bfloat = jnp.bfloat16
+    full_spatial_in = gathered([spatial_in])[0]
+    full_spatial_out, full_temporal_in, full_temporal_out = gathered(
+        [spatial_out, temporal_in, temporal_out]
+    )
+    full_expand, full_shrink = gathered([expand_weight, shrink_weight])
+    biases = [
+        spatial_in_bias,
+        spatial_out_bias,
+        temporal_in_bias,
+        temporal_out_bias,
+        expand_bias,
+        shrink_bias,
+        modulate_bias,
+    ]
     (
-        full_spatial_in,
         full_spatial_inb,
-        full_spatial_out,
         full_spatial_outb,
-        full_temporal_in,
         full_temporal_inb,
-        full_temporal_out,
         full_temporal_outb,
-        full_expand,
         full_expand_bias,
-        full_shrink,
         full_shrink_bias,
-        full_modulate,
         full_modulate_bias,
-    ) = (
-        lax.all_gather(spatial_in, "frame", axis=0, tiled=True),
-        lax.all_gather(spatial_in_bias, "frame", axis=0, tiled=True),
-        lax.all_gather(spatial_out, "frame", axis=0, tiled=True),
-        lax.all_gather(spatial_out_bias, "frame", axis=0, tiled=True),
-        lax.all_gather(temporal_in, "frame", axis=0, tiled=True),
-        lax.all_gather(temporal_in_bias, "frame", axis=0, tiled=True),
-        lax.all_gather(temporal_out, "frame", axis=0, tiled=True),
-        lax.all_gather(temporal_out_bias, "frame", axis=0, tiled=True),
-        lax.all_gather(expand_weight, "frame", axis=0, tiled=True),
-        lax.all_gather(expand_bias, "frame", axis=0, tiled=True),
-        lax.all_gather(shrink_weight, "frame", axis=0, tiled=True),
-        lax.all_gather(shrink_bias, "frame", axis=0, tiled=True),
-        lax.all_gather(modulate_weight, "frame", axis=0, tiled=True),
-        lax.all_gather(modulate_bias, "frame", axis=0, tiled=True),
-    )
+        cond_group,
+    ) = gathered_small(biases, condition)
     frames, patches, model_width = frames_in.shape
     heads_shape = (frames, patches, HEADS, HEAD_DIM)
     scaling = HEAD_DIM ** (-0.5)
     span_count = 2 * WINDOW + 1
-    bfloat = jnp.bfloat16
     cond_float = condition.astype(jnp.float32)
-    cond_act = jax.nn.silu(cond_float).astype(bfloat)
-    modvec = mat_dot(cond_act, full_modulate) + full_modulate_bias
+    act_group = jax.nn.silu(cond_group.astype(jnp.float32)).astype(bfloat)
+    modvec = modulated(act_group, modulate_weight, frames) + full_modulate_bias
     pieces = jnp.split(modvec, 9, axis=1)
     hidden_in = frames_in.astype(jnp.float32)
     normed_one = norm_mod(hidden_in, pieces[0], pieces[1]).astype(bfloat)
@@ -298,160 +363,60 @@
         ],
         axis=1,
     ).astype(bfloat)
-    grad_modulate_weight = outer_sum(cond_act, dmod)
-    grad_modulate_bias = column_sum(dmod)
-    dcond_act = back_dot(dmod, full_modulate)
+    own_act = jax.nn.silu(cond_float).astype(bfloat)
+    every = lax.all_gather(jnp.concatenate([own_act, dmod], axis=1), "frame", axis=0, tiled=True)
+    dmod_group = every[:, model_width:]
+    every = lax.all_gather(every, "dp", axis=0, tiled=True)
+    rows = modulate_weight.shape[0]
+    place = lax.axis_index("frame")
+    parts = lax.axis_size("frame")
+    own_columns = lax.dynamic_slice_in_dim(every[:, :model_width], place * rows, rows, axis=1)
+    grad_modulate_weight = outer_sum(own_columns, every[:, model_width:])
+    grad_modulate_bias = own_part(column_sum(every[:, model_width:]))
+    dact_group = back_dot(dmod_group, modulate_weight)
+    pieces_act = lax.all_to_all(
+        dact_group.reshape(parts, frames, rows), "frame", split_axis=0, concat_axis=0
+    )
+    dcond_act = jnp.swapaxes(pieces_act, 0, 1).reshape(frames, parts * rows)
     grad_condition = jax.vjp(jax.nn.silu, cond_float)[1](dcond_act)[0]
-    groups = lax.axis_size("dp")
-    parts = lax.axis_size("frame")
-    share_list = (
-        lax.psum_scatter(
-            arrange_rows(grad_spatial_in, parts, groups),
-            ("dp", "frame"),
-            scatter_dimension=0,
-            tiled=True,
-        ),
-        lax.psum_scatter(
-            arrange_rows(grad_spatial_in_bias, parts, groups),
-            ("dp", "frame"),
-            scatter_dimension=0,
-            tiled=True,
-        ),
-        lax.psum_scatter(
-            arrange_rows(grad_spatial_out, parts, groups),
-            ("dp", "frame"),
-            scatter_dimension=0,
-            tiled=True,
-        ),
-        lax.psum_scatter(
-            arrange_rows(grad_spatial_out_bias, parts, groups),
-            ("dp", "frame"),
-            scatter_dimension=0,
-            tiled=True,
-        ),
-        lax.psum_scatter(
-            arrange_rows(grad_temporal_in, parts, groups),
-            ("dp", "frame"),
-            scatter_dimension=0,
-            tiled=True,
-        ),
-        lax.psum_scatter(
-            arrange_rows(grad_temporal_in_bias, parts, groups),
-            ("dp", "frame"),
-            scatter_dimension=0,
-            tiled=True,
-        ),
-        lax.psum_scatter(
-            arrange_rows(grad_temporal_out, parts, groups),
-            ("dp", "frame"),
-            scatter_dimension=0,
-            tiled=True,
-        ),
-        lax.psum_scatter(
-            arrange_rows(grad_temporal_out_bias, parts, groups),
-            ("dp", "frame"),
-            scatter_dimension=0,
-            tiled=True,
-        ),
-        lax.psum_scatter(
-            arrange_rows(grad_expand_weight, parts, groups),
-            ("dp", "frame"),
-            scatter_dimension=0,
-            tiled=True,
-        ),
-        lax.psum_scatter(
-            arrange_rows(grad_expand_bias, parts, groups),
-            ("dp", "frame"),
-            scatter_dimension=0,
-            tiled=True,
-        ),
-        lax.psum_scatter(
-            arrange_rows(grad_shrink_weight, parts, groups),
-            ("dp", "frame"),
-            scatter_dimension=0,
-            tiled=True,
-        ),
-        lax.psum_scatter(
-            arrange_rows(grad_shrink_bias, parts, groups),
-            ("dp", "frame"),
-            scatter_dimension=0,
-            tiled=True,
-        ),
-        lax.psum_scatter(
-            arrange_rows(grad_modulate_weight, parts, groups),
-            ("dp", "frame"),
-            scatter_dimension=0,
-            tiled=True,
-        ),
-        lax.psum_scatter(
-            arrange_rows(grad_modulate_bias, parts, groups),
-            ("dp", "frame"),
-            scatter_dimension=0,
-            tiled=True,
-        ),
-    )
-    summed = (
-        lax.all_gather(share_list[0].astype(jnp.bfloat16), "dp", axis=0, tiled=True).astype(
-            jnp.float32
-        ),
-        lax.all_gather(share_list[1].astype(jnp.bfloat16), "dp", axis=0, tiled=True).astype(
-            jnp.float32
-        ),
-        lax.all_gather(share_list[2].astype(jnp.bfloat16), "dp", axis=0, tiled=True).astype(
-            jnp.float32
-        ),
-        lax.all_gather(share_list[3].astype(jnp.bfloat16), "dp", axis=0, tiled=True).astype(
-            jnp.float32
-        ),
-        lax.all_gather(share_list[4].astype(jnp.bfloat16), "dp", axis=0, tiled=True).astype(
-            jnp.float32
-        ),
-        lax.all_gather(share_list[5].astype(jnp.bfloat16), "dp", axis=0, tiled=True).astype(
-            jnp.float32
-        ),
-        lax.all_gather(share_list[6].astype(jnp.bfloat16), "dp", axis=0, tiled=True).astype(
-            jnp.float32
-        ),
-        lax.all_gather(share_list[7].astype(jnp.bfloat16), "dp", axis=0, tiled=True).astype(
-            jnp.float32
-        ),
-        lax.all_gather(share_list[8].astype(jnp.bfloat16), "dp", axis=0, tiled=True).astype(
-            jnp.float32
-        ),
-        lax.all_gather(share_list[9].astype(jnp.bfloat16), "dp", axis=0, tiled=True).astype(
-            jnp.float32
-        ),
-        lax.all_gather(share_list[10].astype(jnp.bfloat16), "dp", axis=0, tiled=True).astype(
-            jnp.float32
-        ),
-        lax.all_gather(share_list[11].astype(jnp.bfloat16), "dp", axis=0, tiled=True).astype(
-            jnp.float32
-        ),
-        lax.all_gather(share_list[12].astype(jnp.bfloat16), "dp", axis=0, tiled=True).astype(
-            jnp.float32
-        ),
-        lax.all_gather(share_list[13].astype(jnp.bfloat16), "dp", axis=0, tiled=True).astype(
-            jnp.float32
-        ),
-    )
+    grad_expand_sum, grad_shrink_sum = reduced([grad_expand_weight, grad_shrink_weight])
+    (
+        grad_spatial_in_sum,
+        grad_spatial_out_sum,
+        grad_temporal_in_sum,
+        grad_temporal_out_sum,
+    ) = reduced([grad_spatial_in, grad_spatial_out, grad_temporal_in, grad_temporal_out])
+    bias_grads = [
+        grad_spatial_in_bias,
+        grad_spatial_out_bias,
+        grad_temporal_in_bias,
+        grad_temporal_out_bias,
+        grad_expand_bias,
+        grad_shrink_bias,
+    ]
+    together = lax.psum(jnp.concatenate(bias_grads), ("dp", "frame"))
+    bias_sums, at = [], 0
+    for grad in bias_grads:
+        bias_sums.append(own_part(together[at : at + grad.shape[0]]))
+        at += grad.shape[0]
     return (
         frames_out,
         grad_frames,
         grad_condition,
-        summed[0],
-        summed[1],
-        summed[2],
-        summed[3],
-        summed[4],
-        summed[5],
-        summed[6],
-        summed[7],
-        summed[8],
-        summed[9],
-        summed[10],
-        summed[11],
-        summed[12],
-        summed[13],
+        grad_spatial_in_sum,
+        bias_sums[0],
+        grad_spatial_out_sum,
+        bias_sums[1],
+        grad_temporal_in_sum,
+        bias_sums[2],
+        grad_temporal_out_sum,
+        bias_sums[3],
+        grad_expand_sum,
+        bias_sums[4],
+        grad_shrink_sum,
+        bias_sums[5],
+        grad_modulate_weight,
+        grad_modulate_bias,
     )
 
 

time: 1720 us -> 882 us (0.51)
  waiting for transfers between devices: 918 us -> 155 us
  blocking collectives: 197 us -> 113 us
  local copies, waits for them, and re-layouts: 205 us -> 232 us
  other arithmetic: 205 us -> 185 us
    reduce_scatter x7 -> x4, waiting for transfers between devices: 524 us -> 83 us  [the longest x2 65.6 us: reduced(): lax.psum_scatter(stack.reshape(-1, width), 'dp', scatter_dimension=0, til...]
    all_gather x10 -> x7, waiting for transfers between devices: 370 us -> 45.9 us  [the longest x2 28.7 us: reduced(): lax.all_gather(mine, 'dp', axis=0, tiled=True).reshape(groups, size, width)]
    unnamed x3 -> x0, blocking collectives: 93.5 us -> none
    psum x0 -> x1, blocking collectives: none -> 39.8 us  [per_device(): together = lax.psum(jnp.concatenate(bias_grads), ('dp', 'frame'))]
    all_gather x5 -> x4, blocking collectives: 103 us -> 73 us  [the longest x2 43.6 us: gathered(): column = lax.all_gather(mine, 'frame', axis=0)]
    convert_element_type x28 -> x7, other arithmetic: 33.1 us -> 7.37 us  [the longest x5 7.28 us: reduced(): results.append(part.reshape(-1, grad.shape[1]).astype(jnp.float32))]
    unnamed x318 -> x301, local copies, waits for them, and re-layouts: 45.4 us -> 69.7 us
  transfers between devices with their start and end apart: 21 -> 17, of which waited for: 14 -> 12; matrix products, arithmetic and copies ran while one was open for 29% -> 45% of each run, Pallas kernels for 0% -> 0%
where the time goes in v1:
time: 882 us; the launch traced here: 877 us
  local copies, waits for them, and re-layouts  232 us (26%)
  other arithmetic  185 us (21%)
  waiting for transfers between devices  155 us (18%)
  matrix products  154 us (17%)
  blocking collectives  113 us (13%)
  starting transfers between devices  22.8 us (3%)
  between operations  15.9 us (2%)
    unnamed x301, local copies, waits for them, and re-layouts  69.7 us
    reduce_scatter x2, waiting for transfers between devices, reduced(): lax.psum_scatter(stack.reshape(-1, width), 'dp', scatter_dimension=0, til...  65.6 us
    dot_general x7, matrix products, back_dot(): lax.dot_general(values, matrix, (((values.ndim - 1,), (1,)), ((), ())), p...  49.5 us
    all_gather x2, blocking collectives, gathered(): column = lax.all_gather(mine, 'frame', axis=0)  43.6 us
    psum x1, blocking collectives, per_device(): together = lax.psum(jnp.concatenate(bias_grads), ('dp', 'frame'))  39.8 us
    dot_general x7, matrix products, mat_dot(): lax.dot_general(values, matrix, (((values.ndim - 1,), (0,)), ((), ())), p...  36.6 us
    dot_general x7, matrix products, outer_sum(): lax.dot_general(left_flat, right_flat, (((0,), (0,)), ((), ())), preferre...  34 us
    convert_element_type x1, other arithmetic, per_device(): activ_low = activ.astype(bfloat)  30.3 us
  transfers between devices with their start and end apart: 17, of which 12 were waited for; matrix products, arithmetic and copies ran while one was open for 45% of the time, Pallas kernels for 0%

profile of v1, /device:TPU:0, one launch (start us, length us, event | category | flops | bytes accessed | tf_op | source)
XLA Modules:
  0.0 877.2 jit_solution(3949753211304222967)
XLA Ops:
  13.2 20.4 %all-gather.1 = bf16[96,2304]{1,0:T(8,128)(2,1)} all-gather(bf16[24,2304]{1,0:T(8,128)(2,1)S(1)} %constant_dynamic-slice_fusion), channel_id=3, replica_groups=mesh['dp'=8,'frame'=4] {'frame'}, dimensions={0}, use_global_device_ids=true | all-gather | bytes 552960 | tf_op jit(solution)/shard_map/all_gather | solution.py:93
  37.5 23.2 %all-gather.3 = bf16[480,768]{1,0:T(8,128)(2,1)} all-gather(bf16[120,768]{1,0:T(8,128)(2,1)S(1)} %constant_dynamic-update-slice_fusion), channel_id=5, replica_groups=mesh['dp'=8,'frame'=4] {'frame'}, dimensions={0}, use_global_device_ids=true | all-gather | bytes 921600 | tf_op jit(solution)/shard_map/all_gather | solution.py:93
  61.0 13.3 %all-gather.7 = bf16[4,1,7296]{2,1,0:T(2,128)(2,1)S(1)} all-gather(bf16[1,1,7296]{2,1,0:T(2,128)(2,1)S(1)} %reshape.659), channel_id=2, replica_groups=mesh['dp'=8,'frame'=4] {'frame'}, dimensions={0}, use_global_device_ids=true | all-gather | bytes 72960 | tf_op jit(solution)/shard_map/all_gather | solution.py:106
  75.8 4.9 all-to-all-start
  85.5 4.6 all-to-all-done
  94.1 4.6 add_convert_fusion.2
  121.3 16.0 %all-gather.25.cloned.1.call-done = bf16[32,120,768]{2,1,0:T(8,128)(2,1)} async-done(((bf16[4,120,768]{2,1,0:T(8,128)(2,1)}), bf16[32,120,768]{2,1,0:T(8,128)(2,1)}) %all-gather.25.cloned.1.call-update) | async-done | bytes 5898256 | tf_op jit(solution)/shard_map/all_gather | solution.py:94
  149.2 4.6 add_convert_fusion.1
  158.3 5.7 collective-permute-start
  188.8 7.0 collective-permute-done.1
  196.9 6.6 pad_maximum_fusion.7
  228.5 7.5 multiply_reduce_fusion.3
  263.6 10.8 %fusion.45 = (u8[256,3072]{1,0:T(8,128)(4,1)S(1)}, u8[256,3072]{1,0:T(8,128)(4,1)S(1)}, f32[4,256,3072]{2,1,0:T(8,128)S(1)}) fusion(f32[3072]{0:T(1024)S(1)} %reshape.644, bf16[768,3072,1]{1,0,2:T(8,128)(2,1)} %bitcast.354, f32[4,256,768]{2,1,0:T(8,128)S(1)} %copy-done.13, f32[4,768]{1,0:T(4,128)S(1)} %get-tuple-element.179, ...), kind=kOutput, calls=%fused_computation.146 | convolution fusion | flops 4878237696 | bytes 22065152 | tf_op jit(solution)/shard_map/dot_general | solution.py:42
  274.4 30.3 %multiply_convert_fusion.1 = (bf16[4,256,3072]{2,1,0:T(8,128)(2,1)}, f32[4,256,3072]{2,1,0:T(8,128)}) fusion(f32[4,256,3072]{2,1,0:T(8,128)S(1)} %get-tuple-element.205, f32[3072]{0:T(1024)S(1)} %reshape.644, u8[256,3072]{1,0:T(8,128)(4,1)S(1)} %get-tuple-element.102, u8[256,3072]{1,0:T(8,128)(4,1)S(1)} %get-tuple-element.101), kind=kLoop, calls=%fused_computation.25 | loop fusion | flops 223346688 | bytes 33042432 | tf_op jit(solution)/shard_map/convert_element_type | solution.py:253
  304.8 19.0 %convert_reduce_fusion = (f32[3072]{0:T(1024)}, bf16[4,256,3072]{2,1,0:T(8,128)(2,1)}) fusion(f32[4,256,3072]{2,1,0:T(8,128)} %get-tuple-element.125, bf16[3072,768,1]{1,0,2:T(8,128)(2,1)} %bitcast.347, bf16[4,256,768]{2,1,0:T(8,128)(2,1)} %param.49, f32[4,768]{1,0:T(4,128)S(1)} %get-tuple-element.178, f32[4,256,3072]{2,1,0:T(8,128)} %copy-done.20, ...), kind=kOutput, calls=%fused_computation.20 | convolution fusion | flops 4887671808 | bytes 37785600 | tf_op jit(solution)/shard_map/dot_general | solution.py:48
  323.8 11.0 %multiply_reduce_fusion.6 = (bf16[4,768]{1,0:T(4,128)(2,1)}, f32[4,256]{1,0:T(4,128)S(1)}, bf16[4,768]{1,0:T(4,128)(2,1)}, f32[4,256,768]{2,1,0:T(8,128)}) fusion(f32[4,256,768]{2,1,0:T(8,128)S(1)} %copy-done.13, f32[4,256]{1,0:T(4,128)S(1)} %fusion.88, f32[4,256]{1,0:T(4,128)S(1)} %broadcast_multiply_fusion.1, f32[4,768]{1,0:T(4,128)S(1)} %get-tuple-element.180, ...), kind=kOutput, calls=%fused_computation.126 | convolution fusion | flops 4838122496 | bytes 17338368 | tf_op jit(solution)/shard_map/dot_general | solution.py:48
  334.8 6.4 bitcast_convert_fusion.1
  345.1 7.3 bitcast_convert_fusion
  355.1 9.4 %convert_reduce_fusion.5 = (f32[768]{0:T(1024)}, bf16[4,768]{1,0:T(4,128)(2,1)}, bf16[4,768]{1,0:T(4,128)(2,1)}, f32[768]{0:T(1024)}, bf16[4,256,768]{2,1,0:T(8,128)(2,1)S(1)}, /*index=5*/bf16[4,256,768]{2,1,0:T(8,128)(2,1)}) fusion(bf16[4,256,768]{2,1,0:T(8,128)(2,1)S(1)} %copy-done.53, f32[4,768]{1,0:T(4,128)S(1)} %get-tuple-element.178, ...), kind=kOutput, calls=%fused_computation.123 | convolution fusion | flops 4847558656 | bytes 25219072 | tf_op jit(solution)/shard_map/dot_general | solution.py:42
  372.8 6.4 multiply_reduce_fusion.1
  391.3 11.9 %broadcast_multiply_fusion = f32[4,256,12,64,5]{1,3,2,0,4:T(8,128)} fusion(f32[4,256,12,5]{1,2,0,3:T(8,128)S(1)} %copy-done.59, f32[4,256,12,64]{1,3,2,0:T(8,128)} %convert.95), kind=kLoop, calls=%fused_computation.49 | loop fusion | flops 3932160 | bytes 19120128 | tf_op jit(solution)/shard_map/jfhp,fphd->jfphd/dot_general | solution.py:289
  403.1 16.6 %copy.133 = f32[5,4,256,768]{3,2,1,0:T(8,128)} copy(f32[5,4,256,768]{2,3,1,0:T(8,128)} %bitcast.283) | data formatting | bytes 31457280 | tf_op jit(solution)/shard_map/reshape | solution.py:294
  419.8 10.2 %multiply_multiply_fusion = f32[4,256,12,64,5]{1,3,2,0,4:T(8,128)} fusion(f32[4,256,12,5]{1,2,0,3:T(8,128)S(1)} %copy-done.60, f32[4,256,12,64]{1,3,2,0:T(8,128)} %convert.93), kind=kLoop, calls=%fused_computation.13 | loop fusion | flops 7864320 | bytes 19120128 | tf_op jit(solution)/shard_map/mul | solution.py:286
  430.0 15.7 %copy.132 = f32[5,4,256,768]{3,2,1,0:T(8,128)} copy(f32[5,4,256,768]{2,3,1,0:T(8,128)} %bitcast.284) | data formatting | bytes 31457280 | tf_op jit(solution)/shard_map/reshape | solution.py:294
  445.8 7.0 fusion.15
  452.8 9.9 %scatter-add.24 = f32[8,256,1536]{2,1,0:T(8,128)} pad(f32[4,256,1536]{2,1,0:T(8,128)} %fusion.15, f32[]{:T(128)} %constant.265.clone.1), padding=0_4x0_0x0_0 | pad | bytes 18874372 | tf_op jit(solution)/shard_map/scatter-add | solution.py:298
  462.7 6.2 fusion.19
  469.0 6.9 fusion.23
  478.7 5.0 fusion.13
  483.7 5.9 fusion.25
  490.9 5.3 collective-permute-start.2
  504.2 7.5 multiply_reduce_fusion
  523.5 4.8 collective-permute-done.2
  532.9 7.5 collective-permute-done.3
  540.4 4.5 fusion.42
  572.7 8.5 fusion.49
  583.8 8.9 %multiply_reduce_fusion.4 = (f32[4,12,256]{2,1,0:T(8,128)S(1)}, f32[4,12,256,256]{2,3,1,0:T(8,128)S(1)}) fusion(f32[4,12,256,256]{2,3,1,0:T(8,128)} %copy-done.1, f32[4,12,256]{2,1,0:T(8,128)S(1)} %copy-done.62, bf16[4,256,12,64]{1,3,2,0:T(8,128)(2,1)} %bitcast.316, bf16[4,256,12,64]{1,3,2,0:T(8,128)(2,1)} %bitcast.320), kind=kOutput, calls=%fused_computation.22 | convolution fusion | flops 415223808 | bytes 28409856 | tf_op jit(solution)/shard_map/fphd,fqhd->fhpq/dot_general | solution.py:326
  592.7 7.2 multiply_convert_fusion
  605.8 5.6 multiply_convert_fusion.3
  614.2 7.0 bitcast_convert_fusion.3
  633.0 9.6 %fusion.39 = (f32[4,256]{1,0:T(4,128)S(1)}, f32[4,256,768]{2,1,0:T(8,128)}) fusion(bf16[4,256,768]{2,1,0:T(8,128)(2,1)} %param.32, f32[4,768]{1,0:T(4,128)S(1)} %copy-done.65, f32[4,256]{1,0:T(4,128)S(1)} %copy-done.71, bf16[768,2304,1]{1,0,2:T(8,128)(2,1)} %bitcast.360, bf16[4,256,768]{2,1,0:T(8,128)(2,1)} %copy.141, bf16[4,256,768]{2,1,0:T(8,128)(2,1)} %copy.140, ...), kind=kOutput, calls=%fused_computation.114 | convolution fusion | flops 3641965568 | bytes 12996608 | tf_op jit(solution)/shard_map/dot_general | solution.py:48
  642.6 65.6 %reduce-scatter.5.cloned.1.call-done = bf16[768,768]{1,0:T(8,128)(2,1)} async-done(((bf16[6144,768]{1,0:T(8,128)(2,1)}), bf16[768,768]{1,0:T(8,128)(2,1)}) %reduce-scatter.5.cloned.1.call-update) | async-done | bytes 1179664 | tf_op jit(solution)/shard_map/reduce_scatter | solution.py:133
  712.2 4.8 multiply_reduce_fusion.9
  717.1 16.1 %all-gather.8 = bf16[4,4,7680]{2,1,0:T(4,128)(2,1)S(1)} all-gather(bf16[1,4,7680]{2,1,0:T(4,128)(2,1)S(1)} %bitcast.382), channel_id=1, replica_groups=mesh['dp'=8,'frame'=4] {'frame'}, dimensions={0}, use_global_device_ids=true | all-gather | bytes 307200 | tf_op jit(solution)/shard_map/all_gather | solution.py:367
  734.3 9.6 %reduce-scatter.11.cloned.1.call-done = bf16[192,768]{1,0:T(8,128)(2,1)} async-done(((bf16[768,768]{1,0:T(8,128)(2,1)}), bf16[192,768]{1,0:T(8,128)(2,1)}) %reduce-scatter.11.cloned.1.call-update) | async-done | bytes 294928 | tf_op jit(solution)/shard_map/reduce_scatter | solution.py:134
  766.5 7.8 reduce-scatter.7.cloned.1.call-done
  778.9 39.8 %psum.7 = f32[9984]{0:T(1024)S(1)} all-reduce(f32[9984]{0:T(1024)S(1)} %constant_dynamic-update-slice_fusion.33), channel_id=1, replica_groups=mesh['dp'=8,'frame'=4] {'dp','frame'}, use_global_device_ids=true, to_apply=%region_36.37 | all-reduce | flops 9984 | bytes 79872 | tf_op jit(solution)/shard_map/psum | solution.py:397
  839.5 25.2 %all-gather.17.cloned.1.call-done = bf16[1536,768]{1,0:T(8,128)(2,1)} async-done(((bf16[192,768]{1,0:T(8,128)(2,1)}), bf16[1536,768]{1,0:T(8,128)(2,1)}) %all-gather.17.cloned.1.call-update) | async-done | bytes 2359312 | tf_op jit(solution)/shard_map/all_gather | solution.py:135
  (500 shorter events, 301.6 us)
Async XLA Ops:
  7.2 67.2 %copy-start = (bf16[192,6912]{1,0:T(8,128)(2,1)S(1)}, bf16[192,6912]{1,0:T(8,128)(2,1)}, u32[]{:S(2)}) copy-start(bf16[192,6912]{1,0:T(8,128)(2,1)} %param.47) | copy-start | bytes 7962628
  7.2 53.5 %copy-start.74 = (bf16[4,768]{1,0:T(4,128)(2,1)S(1)}, bf16[4,768]{1,0:T(4,128)(2,1)}, u32[]{:S(2)}) copy-start(bf16[4,768]{1,0:T(4,128)(2,1)} %param.33) | copy-start | bytes 18436
  7.2 53.5 %copy-start.97 = (bf16[1728]{0:T(1024)(128)(2,1)S(1)}, bf16[1728]{0:T(1024)(128)(2,1)}, u32[]{:S(2)}) copy-start(bf16[1728]{0:T(1024)(128)(2,1)} %param.48) | copy-start | bytes 10372
  7.2 53.5 %copy-start.105 = (bf16[192]{0:T(256)(128)(2,1)S(1)}, bf16[192]{0:T(256)(128)(2,1)}, u32[]{:S(2)}) copy-start(bf16[192]{0:T(256)(128)(2,1)} %param.46) | copy-start | bytes 1156
  7.2 53.5 %copy-start.102 = (bf16[768]{0:T(1024)(128)(2,1)S(1)}, bf16[768]{0:T(1024)(128)(2,1)}, u32[]{:S(2)}) copy-start(bf16[768]{0:T(1024)(128)(2,1)} %param.44) | copy-start | bytes 4612
  7.2 53.5 %copy-start.104 = (bf16[192]{0:T(256)(128)(2,1)S(1)}, bf16[192]{0:T(256)(128)(2,1)}, u32[]{:S(2)}) copy-start(bf16[192]{0:T(256)(128)(2,1)} %param.42) | copy-start | bytes 1156
  7.3 53.5 %copy-start.101 = (bf16[576]{0:T(1024)(128)(2,1)S(1)}, bf16[576]{0:T(1024)(128)(2,1)}, u32[]{:S(2)}) copy-start(bf16[576]{0:T(1024)(128)(2,1)} %param.40) | copy-start | bytes 3460
  7.3 53.5 %copy-start.103 = (bf16[192]{0:T(256)(128)(2,1)S(1)}, bf16[192]{0:T(256)(128)(2,1)}, u32[]{:S(2)}) copy-start(bf16[192]{0:T(256)(128)(2,1)} %param.38) | copy-start | bytes 1156
  7.3 53.5 %copy-start.100 = (bf16[576]{0:T(1024)(128)(2,1)S(1)}, bf16[576]{0:T(1024)(128)(2,1)}, u32[]{:S(2)}) copy-start(bf16[576]{0:T(1024)(128)(2,1)} %param.36) | copy-start | bytes 3460
  7.3 82.9 %all-gather.27.cloned.1.call-start = ((), (), s32[]{:S(2)}) async-start(), calls=%async_computation.15 | async-start | bytes 1474560 | tf_op jit(solution)/shard_map/all_gather | solution.py:93
  12.2 79.4 %all-gather.23.cloned.1.call-start = ((), (), s32[]{:S(2)}) async-start(), calls=%async_computation.13 | async-start | bytes 3981312 | tf_op jit(solution)/shard_map/all_gather | solution.py:94
  33.6 103.7 %all-gather.25.cloned.1.call-start = ((), (), s32[]{:S(2)}) async-start(), calls=%async_computation.14 | async-start | bytes 6635520 | tf_op jit(solution)/shard_map/all_gather | solution.py:94
  75.8 14.3 %all-to-all-start = ((f32[4,4,6912]{2,1,0:T(4,128)}), f32[4,4,6912]{2,1,0:T(4,128)S(1)}, u32[]{:S(2)}, u32[]{:S(2)}) async-start(f32[4,4,6912]{2,1,0:T(4,128)} %reshape.599), calls=%async_computation | async-start | bytes 884736 | tf_op jit(solution)/shard_map/all_to_all | solution.py:120
  80.7 170.5 %all-gather.29.cloned.1.call-start = ((), (), s32[]{:S(2)}) async-start(), calls=%async_computation.16 | async-start | bytes 10616832 | tf_op jit(solution)/shard_map/all_gather | solution.py:94
  80.9 61.4 %copy-start.76 = (f32[768]{0:T(1024)}, f32[768]{0:T(1024)S(1)}, u32[]{:S(2)}) copy-start(f32[768]{0:T(1024)S(1)} %reshape.641) | copy-start | bytes 9220
  82.9 11.1 %copy-start.70 = (f32[4,256]{1,0:T(4,128)}, f32[4,256]{1,0:T(4,128)S(1)}, u32[]{:S(2)}) copy-start(f32[4,256]{1,0:T(4,128)S(1)} %broadcast_multiply_fusion.3) | copy-start | bytes 12292
  90.3 541.9 %reduce-scatter.9.cloned.1.call-start = ((), (), s32[]{:S(2)}) async-start(), calls=%async_computation.9 | async-start | bytes 10616832 | tf_op jit(solution)/shard_map/reduce_scatter | solution.py:133
  90.4 51.9 %copy-start.68 = (f32[4,768]{1,0:T(4,128)}, f32[4,768]{1,0:T(4,128)S(1)}, u32[]{:S(2)}) copy-start(f32[4,768]{1,0:T(4,128)S(1)} %get-tuple-element.186) | copy-start | bytes 36868
  90.4 58.8 %copy-start.66 = (f32[4,768]{1,0:T(4,128)}, f32[4,768]{1,0:T(4,128)S(1)}, u32[]{:S(2)}) copy-start(f32[4,768]{1,0:T(4,128)S(1)} %get-tuple-element.182) | copy-start | bytes 36868
  90.4 58.8 %copy-start.90 = (f32[4,768]{1,0:T(4,128)}, f32[4,768]{1,0:T(4,128)S(1)}, u32[]{:S(2)}) copy-start(f32[4,768]{1,0:T(4,128)S(1)} %get-tuple-element.181) | copy-start | bytes 36868
  153.9 10.3 %copy-start.106 = (s32[1,16]{1,0:T(1,128)S(1)}, s32[1,16]{1,0:T(1,128)}, u32[]{:S(2)}) copy-start(s32[1,16]{1,0:T(1,128)} %param.34) | copy-start | bytes 196
  157.0 38.7 %collective-permute-start.1 = (bf16[2,256,1536]{2,1,0:T(8,128)(2,1)}, bf16[2,256,1536]{2,1,0:T(8,128)(2,1)}, u32[]{:S(2)}, u32[]{:S(2)}) collective-permute-start(bf16[2,256,1536]{2,1,0:T(8,128)(2,1)} %get-tuple-element.152), channel_id=1, source_target_pairs={{1,0},{2,1},{3,2},{5,4},{6,5},{7,6},{9,8},{10,9},{11,10},{13,12},{... | collective-permute-start | bytes 4718600 | tf_op jit(solution)/shard_map/ppermute | solution.py:19
  158.3 38.6 %collective-permute-start = (bf16[2,256,1536]{2,1,0:T(8,128)(2,1)}, bf16[2,256,1536]{2,1,0:T(8,128)(2,1)}, u32[]{:S(2)}, u32[]{:S(2)}) collective-permute-start(bf16[2,256,1536]{2,1,0:T(8,128)(2,1)} %get-tuple-element.153), channel_id=1, source_target_pairs={{0,1},{1,2},{2,3},{4,5},{5,6},{6,7},{8,9},{9,10},{10,11},{12,13},{... | collective-permute-start | bytes 4718600 | tf_op jit(solution)/shard_map/ppermute | solution.py:16
  186.5 10.4 %slice-start.10 = ((bf16[4,256,2304]{2,1,0:T(8,128)(2,1)}), bf16[4,256,1536]{2,1,0:T(8,128)(2,1)S(1)}, s32[]{:S(2)}) async-start(bf16[4,256,2304]{2,1,0:T(8,128)(2,1)} %copy-done.14), calls=%async_computation.27 | async-start | bytes 6291456 | tf_op jit(solution)/shard_map/slice | solution.py:218
  274.4 30.3 %copy-start.20 = (f32[4,256,3072]{2,1,0:T(8,128)}, f32[4,256,3072]{2,1,0:T(8,128)S(1)}, u32[]{:S(2)}) copy-start(f32[4,256,3072]{2,1,0:T(8,128)S(1)} %get-tuple-element.205) | copy-start | bytes 37748740
  323.8 11.0 %copy-start.108 = (bf16[4,256,3072]{2,1,0:T(8,128)(2,1)S(1)}, bf16[4,256,3072]{2,1,0:T(8,128)(2,1)}, u32[]{:S(2)}) copy-start(bf16[4,256,3072]{2,1,0:T(8,128)(2,1)} %get-tuple-element.214) | copy-start | bytes 18874372
  341.2 13.9 %slice-start.13 = ((s8[4718592]{0:T(1024)(128)(4,1)}), s8[4194304]{0:T(1024)(128)(4,1)S(1)}, s32[]{:S(2)}) async-start(s8[4718592]{0:T(1024)(128)(4,1)} %bitcast.348), calls=%async_computation.30 | async-start | bytes 8388608
  342.5 12.5 %copy-start.21 = (f32[4,256,768]{2,1,0:T(8,128)}, f32[4,256,768]{2,1,0:T(8,128)S(1)}, u32[]{:S(2)}) copy-start(f32[4,256,768]{2,1,0:T(8,128)S(1)} %get-tuple-element.123) | copy-start | bytes 9437188
  342.5 12.5 %copy-start.86 = (f32[4,256]{1,0:T(4,128)}, f32[4,256]{1,0:T(4,128)S(1)}, u32[]{:S(2)}) copy-start(f32[4,256]{1,0:T(4,128)S(1)} %negate_multiply_fusion.3) | copy-start | bytes 12292
  355.1 10.6 %copy-start.46 = (bf16[4,8,24,768]{3,2,1,0:T(8,128)(2,1)S(1)}, bf16[4,8,24,768]{3,2,1,0:T(8,128)(2,1)}, u32[]{:S(2)}) copy-start(bf16[4,8,24,768]{3,2,1,0:T(8,128)(2,1)} %copy.127) | copy-start | bytes 3538948
  370.8 12.2 %slice-start.11 = ((s8[4718592]{0:T(1024)(128)(4,1)}), s8[4194304]{0:T(1024)(128)(4,1)S(1)}, s32[]{:S(2)}) async-start(s8[4718592]{0:T(1024)(128)(4,1)} %bitcast.291), calls=%async_computation.28 | async-start | bytes 8388608
  390.3 317.9 %reduce-scatter.5.cloned.1.call-start = ((), (), s32[]{:S(2)}) async-start(), calls=%async_computation.6 | async-start | bytes 10616832 | tf_op jit(solution)/shard_map/reduce_scatter | solution.py:133
  403.1 16.6 %copy-start.60 = (f32[4,256,12,5]{1,2,0,3:T(8,128)S(1)}, f32[4,256,12,5]{1,2,0,3:T(8,128)}, u32[]{:S(2)}) copy-start(f32[4,256,12,5]{1,2,0,3:T(8,128)} %convert_bitcast_fusion.1) | copy-start | bytes 737284
  445.7 16.9 %slice-start = ((s8[15728640]{0:T(1024)(128)(4,1)}), s8[4194304]{0:T(1024)(128)(4,1)S(1)}, s32[]{:S(2)}) async-start(s8[15728640]{0:T(1024)(128)(4,1)} %bitcast.279), calls=%async_computation.17 | async-start | bytes 8388608
  445.7 16.9 %slice-start.1 = ((s8[15728640]{0:T(1024)(128)(4,1)}), s8[4194304]{0:T(1024)(128)(4,1)S(1)}, s32[]{:S(2)}) async-start(s8[15728640]{0:T(1024)(128)(4,1)} %bitcast.279), calls=%async_computation.18 | async-start | bytes 8388608
  445.8 16.9 %slice-start.2 = ((s8[15728640]{0:T(1024)(128)(4,1)}), s8[4194304]{0:T(1024)(128)(4,1)S(1)}, s32[]{:S(2)}) async-start(s8[15728640]{0:T(1024)(128)(4,1)} %bitcast.279), calls=%async_computation.19 | async-start | bytes 8388608
  462.7 13.2 %slice-start.4 = ((s8[15728640]{0:T(1024)(128)(4,1)}), s8[4194304]{0:T(1024)(128)(4,1)S(1)}, s32[]{:S(2)}) async-start(s8[15728640]{0:T(1024)(128)(4,1)} %bitcast.281), calls=%async_computation.21 | async-start | bytes 8388608
  462.7 13.1 %slice-start.5 = ((s8[15728640]{0:T(1024)(128)(4,1)}), s8[4194304]{0:T(1024)(128)(4,1)S(1)}, s32[]{:S(2)}) async-start(s8[15728640]{0:T(1024)(128)(4,1)} %bitcast.281), calls=%async_computation.22 | async-start | bytes 8388608
  490.9 37.5 %collective-permute-start.2 = (bf16[2,256,1536]{2,1,0:T(8,128)(2,1)}, bf16[2,256,1536]{2,1,0:T(8,128)(2,1)}, u32[]{:S(2)}, u32[]{:S(2)}) collective-permute-start(bf16[2,256,1536]{2,1,0:T(8,128)(2,1)} %slice.773), channel_id=1, source_target_pairs={{0,1},{1,2},{2,3},{4,5},{5,6},{6,7},{8,9},{9,10},{10,11},{12,13},{... | collective-permute-start | bytes 4718600 | tf_op jit(solution)/shard_map/ppermute | solution.py:27
  499.2 12.5 %copy-start.2 = (f32[8,256,1536]{2,1,0:T(8,128)S(1)}, f32[8,256,1536]{2,1,0:T(8,128)}, u32[]{:S(2)}) copy-start(f32[8,256,1536]{2,1,0:T(8,128)} %constant_dynamic-update-slice_fusion.35) | copy-start | bytes 37748740
  502.7 37.7 %collective-permute-start.3 = (bf16[2,256,1536]{2,1,0:T(8,128)(2,1)}, bf16[2,256,1536]{2,1,0:T(8,128)(2,1)}, u32[]{:S(2)}, u32[]{:S(2)}) collective-permute-start(bf16[2,256,1536]{2,1,0:T(8,128)(2,1)} %slice.772), channel_id=1, source_target_pairs={{1,0},{2,1},{3,2},{5,4},{6,5},{7,6},{9,8},{10,9},{11,10},{13,12},{... | collective-permute-start | bytes 4718600 | tf_op jit(solution)/shard_map/ppermute | solution.py:27
  632.1 111.7 %reduce-scatter.11.cloned.1.call-start = ((), (), s32[]{:S(2)}) async-start(), calls=%async_computation.10 | async-start | bytes 1474560 | tf_op jit(solution)/shard_map/reduce_scatter | solution.py:134
  632.9 141.5 %reduce-scatter.7.cloned.1.call-start = ((), (), s32[]{:S(2)}) async-start(), calls=%async_computation.7 | async-start | bytes 1474560 | tf_op jit(solution)/shard_map/reduce_scatter | solution.py:134
  642.6 69.5 %copy-start.77 = (f32[768]{0:T(1024)S(1)}, f32[768]{0:T(1024)}, u32[]{:S(2)}) copy-start(f32[768]{0:T(1024)} %copy-done.76) | copy-start | bytes 9220
  708.2 115.2 %all-gather.21.cloned.1.call-start = ((), (), s32[]{:S(2)}) async-start(), calls=%async_computation.12 | async-start | bytes 2211840 | tf_op jit(solution)/shard_map/all_gather | solution.py:369
  734.0 99.8 %all-gather.19.cloned.1.call-start = ((), (), s32[]{:S(2)}) async-start(), calls=%async_computation.11 | async-start | bytes 2654208 | tf_op jit(solution)/shard_map/all_gather | solution.py:135
  756.2 66.4 %all-to-all-start.1 = ((f32[4,4,192]{2,1,0:T(4,128)}), f32[4,4,192]{2,1,0:T(4,128)S(1)}, u32[]{:S(2)}, u32[]{:S(2)}) async-start(f32[4,4,192]{2,1,0:T(4,128)} %reshape.624), calls=%async_computation.1 | async-start | bytes 32768 | tf_op jit(solution)/shard_map/all_to_all | solution.py:377
  759.5 105.1 %all-gather.17.cloned.1.call-start = ((), (), s32[]{:S(2)}) async-start(), calls=%async_computation.8 | async-start | bytes 2654208 | tf_op jit(solution)/shard_map/all_gather | solution.py:135
  (95 other events, 371.4 us)
Sparse Core Ops, SparseCore 0:
  12.4 43.2 all-gather.26
  57.6 34.0 all-gather.22
  93.5 43.7 all-gather.24
  139.0 58.6 all-gather.28
  390.4 78.9 reduce-scatter.8
  632.3 75.8 reduce-scatter.4
  710.5 33.2 reduce-scatter.10
  746.2 28.1 reduce-scatter.6
  776.8 25.9 all-gather.20
  804.6 29.2 all-gather.18
  835.7 28.8 all-gather.16

commit v2 on v1

v2 whole, which is shorter than its diff:
```python
import functools

import jax
import jax.numpy as jnp
from jax import lax
from jax.experimental import pallas as pl
from jax.experimental.pallas import tpu as pltpu
from jax.sharding import PartitionSpec as P

HEADS = 12
HEAD_DIM = 64
WINDOW = 2

F32 = jnp.float32
BF16 = jnp.bfloat16
SCALE = HEAD_DIM ** (-0.5)
SPAN = 2 * WINDOW + 1


def mm(a, b):
    return lax.dot_general(a, b, (((1,), (0,)), ((), ())), preferred_element_type=F32)


def mm_nt(a, b):
    return lax.dot_general(a, b, (((1,), (1,)), ((), ())), preferred_element_type=F32)


def mm_tn(a, b):
    return lax.dot_general(a, b, (((0,), (0,)), ((), ())), preferred_element_type=F32)


def unit(x):
    centred = x - jnp.mean(x, axis=-1, keepdims=True)
    inv = lax.rsqrt(jnp.mean(centred * centred, axis=-1, keepdims=True) + 1e-06)
    return centred * inv, inv


def unit_back(dn, xhat, inv, scale):
    e = dn * (1.0 + scale)
    first = jnp.mean(e, axis=-1, keepdims=True)
    second = jnp.mean(e * xhat, axis=-1, keepdims=True)
    return inv * (e - first - xhat * second)


def down(x):
    return jnp.sum(x, axis=0, keepdims=True)


def low_half(rows):
    return lax.broadcasted_iota(jnp.int32, (rows, 2 * HEAD_DIM), 1) < HEAD_DIM


def soft(scores):
    e = jnp.exp(scores - jnp.max(scores, axis=-1, keepdims=True))
    return e / jnp.sum(e, axis=-1, keepdims=True)


def params(flops, nbytes, trans=0):
    return dict(
        compiler_params=pltpu.CompilerParams(vmem_limit_bytes=60 * 2**20),
        cost_estimate=pl.CostEstimate(
            flops=int(flops), bytes_accessed=int(nbytes), transcendentals=int(trans)
        ),
    )


def fixed(shape):
    return pl.BlockSpec(shape, lambda *_: (0,) * len(shape), pipeline_mode=pl.Buffered(1))


def per_first(shape):
    return pl.BlockSpec((1,) + shape, lambda i: (i,) + (0,) * len(shape))


def per_second(lead, tile, width):
    return pl.BlockSpec((lead, tile, width), lambda i: (0, i, 0))


def spatial_kernel(
    x_ref, mod_ref, wsi, bsi, wso, bso, wti, bti,
    n1_ref, qkv1_ref, attn_ref, branch_ref, after_ref, n2_ref, qkv2_ref,
):
    x = x_ref[0].astype(F32)
    width = x.shape[1]
    xhat, _ = unit(x)
    n1 = (xhat * (1.0 + mod_ref[0, 1:2]) + mod_ref[0, 0:1]).astype(BF16)
    n1_ref[0] = n1
    qkv1_ref[0] = (mm(n1, wsi[...]) + bsi[...]).astype(BF16)
    half = low_half(x.shape[0])
    for pair in range(width // (2 * HEAD_DIM)):
        at = pair * 2 * HEAD_DIM
        q = qkv1_ref[0, :, at : at + 2 * HEAD_DIM]
        k = qkv1_ref[0, :, width + at : width + at + 2 * HEAD_DIM]
        v = qkv1_ref[0, :, 2 * width + at : 2 * width + at + 2 * HEAD_DIM]
        zero = jnp.zeros_like(q)
        first = soft(mm_nt(jnp.where(half, q, zero), k) * SCALE).astype(BF16)
        second = soft(mm_nt(jnp.where(half, zero, q), k) * SCALE).astype(BF16)
        out = jnp.where(half, mm(first, v), mm(second, v))
        attn_ref[0, :, at : at + 2 * HEAD_DIM] = out.astype(BF16)
    branch = mm(attn_ref[0], wso[...]) + bso[...]
    branch_ref[0] = branch
    after = x + mod_ref[0, 2:3] * branch
    after_ref[0] = after
    xhat2, _ = unit(after)
    n2 = (xhat2 * (1.0 + mod_ref[0, 4:5]) + mod_ref[0, 3:4]).astype(BF16)
    n2_ref[0] = n2
    qkv2_ref[0] = (mm(n2, wti[...]) + bti[...]).astype(BF16)


def spatial_forward(x, mod, wsi, bsi, wso, bso, wti, bti):
    frames, patches, width = x.shape
    shape = lambda n, t: jax.ShapeDtypeStruct((frames, patches, n), t)
    block = lambda n: per_first((patches, n))
    outs = [(width, BF16), (3 * width, BF16), (width, BF16), (width, F32), (width, F32),
            (width, BF16), (3 * width, BF16)]
    tokens = frames * patches
    return pl.pallas_call(
        spatial_kernel,
        grid=(frames,),
        in_specs=[block(width), per_first(mod.shape[1:])]
        + [fixed(w.shape) for w in (wsi, bsi, wso, bso, wti, bti)],
        out_specs=[block(n) for n, _ in outs],
        out_shape=[shape(n, t) for n, t in outs],
        name="spatial_forward",
        **params(2 * tokens * width * (7 * width + 2 * patches), 24e6, tokens * patches * HEADS),
    )(x, mod, wsi, bsi, wso, bso, wti, bti)


def split_store(hi_ref, lo_ref, row, prod):
    hi = prod.astype(BF16)
    hi_ref[row] = hi
    lo_ref[row] = (prod - hi.astype(F32)).astype(BF16)


def ext_rows(e, frames, left, own, right, base, width):
    if e < WINDOW:
        return left[e, :, base - width : base]
    if e < WINDOW + frames:
        return own[e - WINDOW, :, base : base + width]
    return right[e - WINDOW - frames, :, base - width : base]


def head_sums(hi_ref, lo_ref, first, count, ones):
    tile, width = hi_ref.shape[1:]
    hi = hi_ref[first : first + count].reshape(count * tile, width)
    lo = lo_ref[first : first + count].reshape(count * tile, width)
    return mm(hi, ones) + mm(lo, ones)


def temporal_kernel(
    allowed, qkv_ref, left_ref, right_ref, after_ref, mod_ref, wto, bto, ones, ones_t,
    probs_ref, attn_ref, branch_ref, out_ref, hi_ref, lo_ref,
):
    frames, tile, width = after_ref.shape
    for t in range(frames):
        q = qkv_ref[t, :, :width].astype(F32)
        for o in range(SPAN):
            k = ext_rows(t + o, frames, left_ref, qkv_ref, right_ref, width, width)
            split_store(hi_ref, lo_ref, t * SPAN + o, q * k.astype(F32))
    for t in range(frames):
        raw = head_sums(hi_ref, lo_ref, t * SPAN, SPAN, ones[...]) * SCALE
        raw = [
            jnp.where(allowed[o, t] > 0, raw[o * tile : (o + 1) * tile], -1e30)
            for o in range(SPAN)
        ]
        top = raw[0]
        for o in range(1, SPAN):
            top = jnp.maximum(top, raw[o])
        expo = [jnp.exp(r - top) for r in raw]
        total = expo[0]
        for o in range(1, SPAN):
            total = total + expo[o]
        inv = 1.0 / total
        probs = [e * inv for e in expo]
        for o in range(SPAN):
            probs_ref[t, o] = probs[o]
        wide = mm(jnp.concatenate(probs, axis=0).astype(BF16), ones_t[...])
        total = None
        for o in range(SPAN):
            v = ext_rows(t + o, frames, left_ref, qkv_ref, right_ref, 2 * width, width)
            term = wide[o * tile : (o + 1) * tile] * v.astype(F32)
            total = term if total is None else total + term
        attn_ref[t] = total.astype(BF16)
    branch = mm(attn_ref[...].reshape(frames * tile, width), wto[...]) + bto[...]
    for t in range(frames):
        part = branch[t * tile : (t + 1) * tile]
        branch_ref[t] = part
        out_ref[t] = after_ref[t] + mod_ref[t, 5:6] * part


def head_ones(width):
    head = jnp.arange(width, dtype=jnp.int32)[:, None] // HEAD_DIM
    return (head == jnp.arange(128, dtype=jnp.int32)[None, :]).astype(BF16)


def temporal_forward(allowed, qkv, left, right, after, mod, wto, bto):
    frames, patches, width = after.shape
    tile = 64
    ones = head_ones(width)
    spec = lambda n: per_second(frames, tile, n)
    halo = per_second(WINDOW, tile, 2 * width)
    shape = lambda t: jax.ShapeDtypeStruct((frames, patches, width), t)
    tokens = frames * patches
    return pl.pallas_call(
        temporal_kernel,
        grid=(patches // tile,),
        in_specs=[
            pl.BlockSpec(memory_space=pltpu.SMEM),
            spec(3 * width), halo, halo, spec(width),
            fixed(mod.shape), fixed(wto.shape), fixed(bto.shape),
            fixed(ones.shape), fixed(ones.shape[::-1]),
        ],
        out_specs=[
            pl.BlockSpec((frames, SPAN, tile, 128), lambda i: (0, 0, i, 0)),
            spec(width), spec(width), spec(width),
        ],
        out_shape=[
            jax.ShapeDtypeStruct((frames, SPAN, patches, 128), F32),
            shape(BF16), shape(F32), shape(F32),
        ],
        scratch_shapes=[pltpu.VMEM((frames * SPAN, tile, width), BF16)] * 2,
        name="temporal_forward",
        **params(2 * tokens * width * (width + SPAN * 400), 22e6, tokens * SPAN * 128),
    )(allowed, qkv, left, right, after, mod, wto, bto, ones, ones.T)


def feed_kernel(
    after_ref, cot_ref, mod_ref, w1, b1, w2, b2,
    out_ref, g_ref, n_ref, act_ref, dpre_ref, db_ref, dmod_ref, sum1_ref, sum2_ref,
):
    after = after_ref[0]
    width = after.shape[1]
    hidden = w1.shape[1]
    xhat, inv = unit(after)
    scale = mod_ref[0, 7:8]
    gate = mod_ref[0, 8:9]
    n = (xhat * (1.0 + scale) + mod_ref[0, 6:7]).astype(BF16)
    n_ref[0] = n
    g3 = cot_ref[0].astype(F32)
    db = (gate * g3).astype(BF16)
    db_ref[0] = db

    @pl.when(pl.program_id(0) == 0)
    def _():
        sum1_ref[...] = jnp.zeros_like(sum1_ref)
        sum2_ref[...] = jnp.zeros_like(sum2_ref)

    sum2_ref[...] += down(db.astype(F32))
    branch = jnp.zeros_like(after)
    dn = jnp.zeros_like(after)
    chunk = width
    for c in range(hidden // chunk):
        cols = slice(c * chunk, (c + 1) * chunk)
        pre = mm(n, w1[:, cols]) + b1[:, cols]
        dact = mm_nt(db, w2[cols, :])
        phi = 0.5 * (1.0 + lax.erf(pre * 0.7071067811865476))
        act = (pre * phi).astype(BF16)
        slope = phi + pre * (jnp.exp(-0.5 * pre * pre) * 0.3989422804014327)
        dpre = (dact * slope).astype(BF16)
        act_ref[0, :, cols] = act
        dpre_ref[0, :, cols] = dpre
        sum1_ref[:, cols] += down(dpre.astype(F32))
        branch += mm(act, w2[cols, :])
        dn += mm_nt(dpre, w1[:, cols])
    branch = branch + b2[...]
    out_ref[0] = (after + gate * branch).astype(BF16)
    dmod_ref[0, 0:1] = down(dn)
    dmod_ref[0, 1:2] = down(dn * xhat)
    dmod_ref[0, 2:3] = down(g3 * branch)
    g_ref[0] = g3 + unit_back(dn, xhat, inv, scale)


def feed_forward(after, cot, mod, w1, b1, w2, b2):
    frames, patches, width = after.shape
    hidden = w1.shape[1]
    shape = lambda n, t: jax.ShapeDtypeStruct((frames, patches, n), t)
    block = lambda n: per_first((patches, n))
    outs = [(width, BF16), (width, F32), (width, BF16), (hidden, BF16), (hidden, BF16), (width, BF16)]
    tokens = frames * patches
    return pl.pallas_call(
        feed_kernel,
        grid=(frames,),
        in_specs=[block(width), block(width), per_first(mod.shape[1:])]
        + [fixed(w.shape) for w in (w1, b1, w2, b2)],
        out_specs=[block(n) for n, _ in outs]
        + [per_first((3, width)), pl.BlockSpec((1, hidden), lambda i: (0, 0)),
           pl.BlockSpec((1, width), lambda i: (0, 0))],
        out_shape=[shape(n, t) for n, t in outs]
        + [jax.ShapeDtypeStruct((frames, 3, width), F32),
           jax.ShapeDtypeStruct((1, hidden), F32), jax.ShapeDtypeStruct((1, width), F32)],
        name="feed_forward",
        **params(8 * tokens * width * hidden, 32e6, 2 * tokens * hidden),
    )(after, cot, mod, w1, b1, w2, b2)


def temporal_back_kernel(
    g_ref, branch_ref, mod_ref, wto, qkv_ref, left_ref, right_ref, probs_ref, ones, ones_t,
    db_ref, dq_ref, dkv_ref, dleft_ref, dright_ref, dgate_ref, sum_ref,
    hi_ref, lo_ref, da_ref, ds_ref, pw_ref,
):
    frames, tile, width = g_ref.shape

    @pl.when(pl.program_id(0) == 0)
    def _():
        dgate_ref[...] = jnp.zeros_like(dgate_ref)
        sum_ref[...] = jnp.zeros_like(sum_ref)

    for t in range(frames):
        g = g_ref[t]
        dgate_ref[t : t + 1] += down(g * branch_ref[t])
        db = (mod_ref[t, 5:6] * g).astype(BF16)
        db_ref[t] = db
        sum_ref[...] += down(db.astype(F32))
    da_all = mm_nt(db_ref[...].reshape(frames * tile, width), wto[...]).astype(BF16)
    da_ref[...] = da_all.reshape(frames, tile, width)
    for t in range(frames):
        da = da_ref[t].astype(F32)
        for o in range(SPAN):
            v = ext_rows(t + o, frames, left_ref, qkv_ref, right_ref, 2 * width, width)
            split_store(hi_ref, lo_ref, t * SPAN + o, da * v.astype(F32))
    for t in range(frames):
        dp = head_sums(hi_ref, lo_ref, t * SPAN, SPAN, ones[...])
        probs = probs_ref[t].reshape(SPAN * tile, 128)
        both = probs * dp
        dot = both[:tile]
        for o in range(1, SPAN):
            dot = dot + both[o * tile : (o + 1) * tile]
        ds = both - probs * jnp.concatenate([dot] * SPAN, axis=0)
        wide = mm(ds.astype(BF16), ones_t[...]).astype(BF16)
        ds_ref[t * SPAN : (t + 1) * SPAN] = wide.reshape(SPAN, tile, width)
        wide = mm(probs.astype(BF16), ones_t[...]).astype(BF16)
        pw_ref[t * SPAN : (t + 1) * SPAN] = wide.reshape(SPAN, tile, width)
    for t in range(frames):
        total = None
        for o in range(SPAN):
            k = ext_rows(t + o, frames, left_ref, qkv_ref, right_ref, width, width)
            term = ds_ref[t * SPAN + o].astype(F32) * k.astype(F32)
            total = term if total is None else total + term
        dq_ref[t] = (total * SCALE).astype(BF16)
    for e in range(frames + 2 * WINDOW):
        dk = dv = None
        for t in range(max(0, e - SPAN + 1), min(frames, e + 1)):
            row = t * SPAN + e - t
            q = qkv_ref[t, :, :width].astype(F32)
            term = ds_ref[row].astype(F32) * q
            dk = term if dk is None else dk + term
            term = pw_ref[row].astype(F32) * da_ref[t].astype(F32)
            dv = term if dv is None else dv + term
        dk = dk * SCALE
        if e < WINDOW:
            dleft_ref[e, :, :width] = dk.astype(BF16)
            dleft_ref[e, :, width:] = dv.astype(BF16)
        elif e < WINDOW + frames:
            dkv_ref[e - WINDOW, :, :width] = dk
            dkv_ref[e - WINDOW, :, width:] = dv
        else:
            dright_ref[e - WINDOW - frames, :, :width] = dk.astype(BF16)
            dright_ref[e - WINDOW - frames, :, width:] = dv.astype(BF16)


def temporal_backward(g, branch, mod, wto, qkv, left, right, probs):
    frames, patches, width = g.shape
    tile = 64
    ones = head_ones(width)
    spec = lambda n: per_second(frames, tile, n)
    halo = per_second(WINDOW, tile, 2 * width)
    shape = lambda f, n, t: jax.ShapeDtypeStruct((f, patches, n), t)
    tokens = frames * patches
    return pl.pallas_call(
        temporal_back_kernel,
        grid=(patches // tile,),
        in_specs=[
            spec(width), spec(width), fixed(mod.shape), fixed(wto.shape), spec(3 * width), halo, halo,
            pl.BlockSpec((frames, SPAN, tile, 128), lambda i: (0, 0, i, 0)),
            fixed(ones.shape), fixed(ones.shape[::-1]),
        ],
        out_specs=[
            spec(width), spec(width), spec(2 * width), halo, halo,
            pl.BlockSpec((frames, width), lambda i: (0, 0)),
            pl.BlockSpec((1, width), lambda i: (0, 0)),
        ],
        out_shape=[
            shape(frames, width, BF16), shape(frames, width, BF16), shape(frames, 2 * width, F32),
            shape(WINDOW, 2 * width, BF16), shape(WINDOW, 2 * width, BF16),
            jax.ShapeDtypeStruct((frames, width), F32), jax.ShapeDtypeStruct((1, width), F32),
        ],
        scratch_shapes=[pltpu.VMEM((frames * SPAN, tile, width), BF16)] * 2
        + [pltpu.VMEM((frames, tile, width), BF16)]
        + [pltpu.VMEM((frames * SPAN, tile, width), BF16)] * 2,
        name="temporal_backward",
        **params(2 * tokens * width * (width + SPAN * 500), 36e6),
    )(g, branch, mod, wto, qkv, left, right, probs, ones, ones.T)


def spatial_back_kernel(
    dq2_ref, dkv2_ref, fl_ref, fr_ref, after_ref, g2_ref, branch_ref, x_ref, qkv_ref, mod_ref,
    wti, wso, wsi,
    dqkv2_ref, db_ref, dqkv1_ref, grad_ref, dmod_ref, sum2_ref, sumb_ref, sum1_ref, da_ref,
):
    tokens, width = after_ref.shape[1:]
    at = pl.program_id(0)

    @pl.when(at == 0)
    def _():
        sum2_ref[...] = jnp.zeros_like(sum2_ref)
        sumb_ref[...] = jnp.zeros_like(sumb_ref)
        sum1_ref[...] = jnp.zeros_like(sum1_ref)

    dqkv2_ref[0, :, :width] = dq2_ref[0]
    extra = jnp.where(at < WINDOW, fl_ref[0].astype(F32), fr_ref[0].astype(F32))
    dqkv2_ref[0, :, width:] = (dkv2_ref[0] + extra).astype(BF16)
    sum2_ref[...] += down(dqkv2_ref[0].astype(F32))
    dn = mm_nt(dqkv2_ref[0], wti[...])
    xhat, inv = unit(after_ref[0])
    dmod_ref[0, 3:4] = down(dn)
    dmod_ref[0, 4:5] = down(dn * xhat)
    g1 = g2_ref[0] + unit_back(dn, xhat, inv, mod_ref[0, 4:5])
    dmod_ref[0, 2:3] = down(g1 * branch_ref[0])
    db = (mod_ref[0, 2:3] * g1).astype(BF16)
    db_ref[0] = db
    sumb_ref[...] += down(db.astype(F32))
    grad_ref[0] = g1
    da_ref[...] = mm_nt(db, wso[...]).astype(BF16)
    half = low_half(tokens)
    for pair in range(width // (2 * HEAD_DIM)):
        cols = slice(pair * 2 * HEAD_DIM, (pair + 1) * 2 * HEAD_DIM)
        kcols = slice(width + cols.start, width + cols.stop)
        vcols = slice(2 * width + cols.start, 2 * width + cols.stop)
        q = qkv_ref[0, :, cols]
        k = qkv_ref[0, :, kcols]
        v = qkv_ref[0, :, vcols]
        da = da_ref[:, cols]
        zero = jnp.zeros_like(q)
        parts = []
        for side in range(2):
            pick = (lambda u: jnp.where(half, u, zero)) if side == 0 else (
                lambda u: jnp.where(half, zero, u))
            probs = soft(mm_nt(pick(q), k) * SCALE)
            dp = mm_nt(pick(da), v)
            both = probs * dp
            ds = (both - probs * jnp.sum(both, axis=-1, keepdims=True)).astype(BF16)
            parts.append((mm(ds, k), mm_tn(ds, q), mm_tn(probs.astype(BF16), da)))
        dq, dk, dv = (jnp.where(half, a, b) for a, b in zip(*parts))
        dqkv1_ref[0, :, cols] = (dq * SCALE).astype(BF16)
        dqkv1_ref[0, :, kcols] = (dk * SCALE).astype(BF16)
        dqkv1_ref[0, :, vcols] = dv.astype(BF16)
    sum1_ref[...] += down(dqkv1_ref[0].astype(F32))
    dn = mm_nt(dqkv1_ref[0], wsi[...])
    xhat, inv = unit(x_ref[0].astype(F32))
    dmod_ref[0, 0:1] = down(dn)
    dmod_ref[0, 1:2] = down(dn * xhat)
    grad_ref[0] += unit_back(dn, xhat, inv, mod_ref[0, 1:2])


def spatial_backward(dq2, dkv2, from_left, from_right, after, g2, branch, x, qkv1, mod, wti, wso, wsi):
    frames, patches, width = x.shape
    shape = lambda n, t: jax.ShapeDtypeStruct((frames, patches, n), t)
    block = lambda n: per_first((patches, n))
    vector = lambda n: pl.BlockSpec((1, n), lambda i: (0, 0))
    tokens = frames * patches
    return pl.pallas_call(
        spatial_back_kernel,
        grid=(frames,),
        in_specs=[
            block(width), block(2 * width),
            pl.BlockSpec((1, patches, 2 * width), lambda i: (jnp.minimum(i, WINDOW - 1), 0, 0)),
            pl.BlockSpec((1, patches, 2 * width), lambda i: (jnp.maximum(i - WINDOW, 0), 0, 0)),
            block(width), block(width), block(width), block(width), block(3 * width),
            per_first(mod.shape[1:]), fixed(wti.shape), fixed(wso.shape), fixed(wsi.shape),
        ],
        out_specs=[
            block(3 * width), block(width), block(3 * width), block(width), per_first((5, width)),
            vector(3 * width), vector(width), vector(3 * width),
        ],
        out_shape=[
            shape(3 * width, BF16), shape(width, BF16), shape(3 * width, BF16), shape(width, F32),
            jax.ShapeDtypeStruct((frames, 5, width), F32),
            jax.ShapeDtypeStruct((1, 3 * width), F32), jax.ShapeDtypeStruct((1, width), F32),
            jax.ShapeDtypeStruct((1, 3 * width), F32),
        ],
        scratch_shapes=[pltpu.VMEM((patches, width), BF16)],
        name="spatial_backward",
        **params(2 * tokens * width * (7 * width + 5 * patches), 45e6, tokens * patches * HEADS),
    )(dq2, dkv2, from_left, from_right, after, g2, branch, x, qkv1, mod, wti, wso, wsi)


def outer_kernel(left_ref, right_ref, out_ref, *, groups):
    total = mm_tn(left_ref[...], right_ref[...])
    parts = out_ref.shape[1]
    rows = out_ref.shape[2]
    for f in range(parts):
        for d in range(groups):
            at = (f * groups + d) * rows
            out_ref[d, f] = total[at : at + rows].astype(BF16)


def outer_pieces(left, right, width, groups, parts):
    left = left.reshape(-1, left.shape[-1])
    right = right.reshape(-1, right.shape[-1])
    tokens, depth = left.shape
    rows = depth // (groups * parts)
    stacks = right.shape[1] // width
    if rows % 8:
        total = mm_tn(left, right).astype(BF16).reshape(parts, groups, rows, stacks, width)
        return total.transpose(1, 0, 3, 2, 4).reshape(groups, parts, stacks * rows, width)
    step = 1
    while (step * depth // parts) % 128:
        step *= 2
    return pl.pallas_call(
        functools.partial(outer_kernel, groups=groups),
        grid=(parts // step, stacks),
        in_specs=[
            pl.BlockSpec((tokens, step * depth // parts), lambda i, j: (0, i)),
            pl.BlockSpec((tokens, width), lambda i, j: (0, j)),
        ],
        out_specs=pl.BlockSpec((groups, step, rows, width), lambda i, j: (0, i, j, 0)),
        out_shape=jax.ShapeDtypeStruct((groups, parts, stacks * rows, width), BF16),
        name="outer_pieces",
        **params(2 * tokens * depth * right.shape[1], 2 * (left.size + right.size * 2)),
    )(left, right)


def own_part(vector):
    size = vector.shape[0] // lax.axis_size("frame")
    return lax.dynamic_slice_in_dim(vector, lax.axis_index("frame") * size, size)


def stacked(block, width):
    count = block.shape[-1] // width
    return jnp.concatenate(
        [block[..., k * width : (k + 1) * width] for k in range(count)], axis=-2
    )


def unstacked(block, count):
    rows = block.shape[-2] // count
    return jnp.concatenate(
        [block[..., k * rows : (k + 1) * rows, :] for k in range(count)], axis=-1
    )


def gathered(shards):
    groups, parts = lax.axis_size("dp"), lax.axis_size("frame")
    width = min(shard.shape[1] for shard in shards)
    pieces = []
    for shard in shards:
        rows = shard.shape[0] // groups
        piece = lax.dynamic_slice_in_dim(shard, lax.axis_index("dp") * rows, rows)
        pieces.append(stacked(piece, width))
    mine = jnp.concatenate(pieces, axis=0)
    column = lax.all_gather(mine, "frame", axis=0)
    whole = lax.all_gather(column, "dp", axis=0)
    results, at = [], 0
    for shard, piece in zip(shards, pieces):
        part = unstacked(whole[:, :, at : at + piece.shape[0]], shard.shape[1] // width)
        results.append(jnp.swapaxes(part, 0, 1).reshape(parts * shard.shape[0], shard.shape[1]))
        at += piece.shape[0]
    return results


def gathered_small(biases, condition):
    parts = lax.axis_size("frame")
    flat = jnp.concatenate(biases + [condition.reshape(-1)])
    rows = lax.all_gather(flat, "frame", axis=0)
    results, at = [], 0
    for bias in biases:
        results.append(rows[:, at : at + bias.shape[0]].reshape(-1))
        at += bias.shape[0]
    results.append(rows[:, at:].reshape(parts * condition.shape[0], condition.shape[1]))
    return results


def modulated(act_group, matrix, frames):
    parts = lax.axis_size("frame")
    rows, width = matrix.shape
    columns = lax.dynamic_slice_in_dim(act_group, lax.axis_index("frame") * rows, rows, axis=1)
    partial = mm(columns, matrix).reshape(parts, frames, width)
    return jnp.sum(lax.all_to_all(partial, "frame", split_axis=0, concat_axis=0), axis=0)


def passed_along(x, axis, by):
    peers = lax.axis_size(axis)
    pairs = [(i, i + by) for i in range(peers) if 0 <= i + by < peers]
    return lax.ppermute(x, axis, pairs)


def reduced(blocks, width_of):
    groups, parts = lax.axis_size("dp"), lax.axis_size("frame")
    stack = jnp.concatenate(blocks, axis=2)
    size, width = stack.shape[2:]
    column = lax.psum_scatter(stack.reshape(-1, width), "dp", scatter_dimension=0, tiled=True)
    mine = lax.psum_scatter(column, "frame", scatter_dimension=0, tiled=True)
    whole = lax.all_gather(mine, "dp", axis=0, tiled=True).reshape(groups, size, width)
    results, at = [], 0
    for block, full in zip(blocks, width_of):
        part = unstacked(whole[:, at : at + block.shape[2]], full // width)
        results.append(part.reshape(-1, full).astype(F32))
        at += block.shape[2]
    return results


def per_device(
    frames_in,
    condition,
    segments,
    spatial_in,
    spatial_in_bias,
    spatial_out,
    spatial_out_bias,
    temporal_in,
    temporal_in_bias,
    temporal_out,
    temporal_out_bias,
    expand_weight,
    expand_bias,
    shrink_weight,
    shrink_bias,
    modulate_weight,
    modulate_bias,
    cotangent,
):
    groups, parts = lax.axis_size("dp"), lax.axis_size("frame")
    place = lax.axis_index("frame")
    frames, patches, width = frames_in.shape
    full_spatial_in = gathered([spatial_in])[0]
    full_spatial_out, full_temporal_in, full_temporal_out = gathered(
        [spatial_out, temporal_in, temporal_out]
    )
    full_expand, full_shrink = gathered([expand_weight, shrink_weight])
    biases = [
        spatial_in_bias,
        spatial_out_bias,
        temporal_in_bias,
        temporal_out_bias,
        expand_bias,
        shrink_bias,
        modulate_bias,
    ]
    *full_biases, cond_group = gathered_small(biases, condition)
    sinb, soutb, tinb, toutb, expb, shrb, modb = [b.astype(F32)[None, :] for b in full_biases]
    act_group = jax.nn.silu(cond_group.astype(F32)).astype(BF16)
    modvec = modulated(act_group, modulate_weight, frames) + modb
    mod = modvec.reshape(frames, 9, width)
    n1, qkv1, attn1, branch1, after1, n2, qkv2 = spatial_forward(
        frames_in, mod, full_spatial_in, sinb, full_spatial_out, soutb, full_temporal_in, tinb
    )
    left = passed_along(qkv2[frames - WINDOW :, :, width:], "frame", 1)
    right = passed_along(qkv2[:WINDOW, :, width:], "frame", -1)
    seg_row = segments[0]
    seg_pad = jnp.pad(seg_row, (WINDOW, WINDOW), constant_values=-1)
    nearby = lax.dynamic_slice_in_dim(seg_pad, place * frames, frames + 2 * WINDOW)
    own_seg = nearby[WINDOW : WINDOW + frames]
    allowed = jnp.stack([nearby[o : o + frames] == own_seg for o in range(SPAN)]).astype(jnp.int32)
    probs, attn2, branch2, after2 = temporal_forward(
        allowed, qkv2, left, right, after1, mod, full_temporal_out, toutb
    )
    frames_out, g2, n3, act, dpre, db3, dmod3, sum_exp, sum_shr = feed_forward(
        after2, cotangent, mod, full_expand, expb, full_shrink, shrb
    )
    sums = reduced(
        [
            outer_pieces(n3, dpre, width, groups, parts),
            outer_pieces(act, db3, width, groups, parts),
        ],
        [dpre.shape[-1], width],
    )
    grad_expand_sum, grad_shrink_sum = sums
    db2, dq2, dkv2, dleft, dright, dgate2, sum_tout = temporal_backward(
        g2, branch2, mod, full_temporal_out, qkv2, left, right, probs
    )
    from_right = passed_along(dleft, "frame", -1)
    from_left = passed_along(dright, "frame", 1)
    dqkv2, db1, dqkv1, grad_frames, dmod12, sum_tin, sum_sout, sum_sin = spatial_backward(
        dq2, dkv2, from_left, from_right, after1, g2, branch1, frames_in, qkv1, mod,
        full_temporal_in, full_spatial_out, full_spatial_in,
    )
    (
        grad_temporal_out_sum,
        grad_temporal_in_sum,
        grad_spatial_out_sum,
        grad_spatial_in_sum,
    ) = reduced(
        [
            outer_pieces(attn2, db2, width, groups, parts),
            outer_pieces(n2, dqkv2, width, groups, parts),
            outer_pieces(attn1, db1, width, groups, parts),
            outer_pieces(n1, dqkv1, width, groups, parts),
        ],
        [width, 3 * width, width, 3 * width],
    )
    dmod = jnp.concatenate([dmod12, dgate2[:, None], dmod3], axis=1)
    dmod = dmod.reshape(frames, 9 * width).astype(BF16)
    cond_float = condition.astype(F32)
    own_act = jax.nn.silu(cond_float).astype(BF16)
    every = lax.all_gather(jnp.concatenate([own_act, dmod], axis=1), "frame", axis=0, tiled=True)
    dmod_group = every[:, width:]
    every = lax.all_gather(every, "dp", axis=0, tiled=True)
    rows = modulate_weight.shape[0]
    own_columns = lax.dynamic_slice_in_dim(every[:, :width], place * rows, rows, axis=1)
    grad_modulate_weight = mm_tn(own_columns, every[:, width:])
    grad_modulate_bias = own_part(jnp.sum(every[:, width:].astype(F32), axis=0))
    dact_group = mm_nt(dmod_group, modulate_weight)
    pieces_act = lax.all_to_all(
        dact_group.reshape(parts, frames, rows), "frame", split_axis=0, concat_axis=0
    )
    dcond_act = jnp.swapaxes(pieces_act, 0, 1).reshape(frames, parts * rows)
    grad_condition = jax.vjp(jax.nn.silu, cond_float)[1](dcond_act)[0]
    bias_grads = [s[0] for s in (sum_sin, sum_sout, sum_tin, sum_tout, sum_exp, sum_shr)]
    together = lax.psum(jnp.concatenate(bias_grads), ("dp", "frame"))
    bias_sums, at = [], 0
    for grad in bias_grads:
        bias_sums.append(own_part(together[at : at + grad.shape[0]]))
        at += grad.shape[0]
    return (
        frames_out,
        grad_frames,
        grad_condition,
        grad_spatial_in_sum,
        bias_sums[0],
        grad_spatial_out_sum,
        bias_sums[1],
        grad_temporal_in_sum,
        bias_sums[2],
        grad_temporal_out_sum,
        bias_sums[3],
        grad_expand_sum,
        bias_sums[4],
        grad_shrink_sum,
        bias_sums[5],
        grad_modulate_weight,
        grad_modulate_bias,
    )


def solution(mesh):
    in_specs = (
        P(("dp", "frame"), None, None),
        P(("dp", "frame"), None),
        P("dp", None),
        P("frame", None),
        P("frame"),
        P("frame", None),
        P("frame"),
        P("frame", None),
        P("frame"),
        P("frame", None),
        P("frame"),
        P("frame", None),
        P("frame"),
        P("frame", None),
        P("frame"),
        P("frame", None),
        P("frame"),
        P(("dp", "frame"), None, None),
    )
    out_specs = (
        P(("dp", "frame"), None, None),
        P(("dp", "frame"), None, None),
        P(("dp", "frame"), None),
        P("frame", None),
        P("frame"),
        P("frame", None),
        P("frame"),
        P("frame", None),
        P("frame"),
        P("frame", None),
        P("frame"),
        P("frame", None),
        P("frame"),
        P("frame", None),
        P("frame"),
        P("frame", None),
        P("frame"),
    )
    return jax.shard_map(
        per_device, mesh=mesh, in_specs=in_specs, out_specs=out_specs, check_vma=False
    )
```

time: 882 us -> 698 us (0.79)
  Pallas kernels: 0 us -> 203 us
  local copies, waits for them, and re-layouts: 232 us -> 54.3 us
  other arithmetic: 185 us -> 30.5 us
  matrix products: 154 us -> 5.57 us
  waiting for transfers between devices: 155 us -> 250 us
    pallas_call x0 -> x11, Pallas kernels: none -> 203 us  [the longest x6 57.5 us: outer_pieces(): pl.pallas_call(functools.partial(outer_kernel, groups=groups), grid=(part...]
    dot_general x27 -> x3, matrix products: 154 us -> 5.57 us  [the longest x1 3.34 us: mm_tn(): lax.dot_general(a, b, (((0,), (0,)), ((), ())), preferred_element_type=F32)]
    unnamed x301 -> x66, local copies, waits for them, and re-layouts: 69.7 us -> 11.3 us
    reshape x10 -> x1, local copies, waits for them, and re-layouts: 49 us -> 0.89 us  [modulated(): partial = mm(columns, matrix).reshape(parts, frames, width)]
    slice x24 -> x4, local copies, waits for them, and re-layouts: 52.7 us -> 7.93 us  [the longest x1 3.75 us: per_device(): right = passed_along(qkv2[:WINDOW, :, width:], 'frame', -1)]
    ppermute x2 -> x4, waiting for transfers between devices: 12.4 us -> 53.5 us  [passed_along(): return lax.ppermute(x, axis, pairs)]
    dot_general x5 -> x0, other arithmetic: 35.7 us -> none  [the longest x1 11.9 us: per_device(): jnp.einsum('jfhp,fphd->jfphd', probs_low, dattn_two, preferred_element_ty...]
    convert_element_type x12 -> x13, other arithmetic: 45 us -> 9.64 us  [the longest x5 7.28 us: reduced(): results.append(part.reshape(-1, full).astype(F32))]
  transfers between devices with their start and end apart: 17 -> 17, of which waited for: 12 -> 12; matrix products, arithmetic and copies ran while one was open for 45% -> 9% of each run, Pallas kernels for 0% -> 22%
where the time goes in v2:
time: 698 us; the launch traced here: 691 us
  waiting for transfers between devices  250 us (36%)
  Pallas kernels  203 us (29%)
  blocking collectives  113 us (16%)
  local copies, waits for them, and re-layouts  54.3 us (8%)
  other arithmetic  30.5 us (4%)
  starting transfers between devices  19.5 us (3%)
  between operations  14.9 us (2%)
    reduce_scatter x2, waiting for transfers between devices, reduced(): lax.psum_scatter(stack.reshape(-1, width), 'dp', scatter_dimension=0, til...  73.6 us
    pallas_call x6, Pallas kernels, outer_pieces(): pl.pallas_call(functools.partial(outer_kernel, groups=groups), grid=(part...  57.5 us
    ppermute x4, waiting for transfers between devices, passed_along(): return lax.ppermute(x, axis, pairs)  53.5 us
    pallas_call x1, Pallas kernels, spatial_backward(): pl.pallas_call(spatial_back_kernel, grid=(frames,), in_specs=[block(width...  48.5 us
    reduce_scatter x2, waiting for transfers between devices, reduced(): mine = lax.psum_scatter(column, 'frame', scatter_dimension=0, tiled=True)  47 us
    all_gather x2, blocking collectives, gathered(): column = lax.all_gather(mine, 'frame', axis=0)  43.6 us
    all_gather x3, waiting for transfers between devices, gathered(): whole = lax.all_gather(column, 'dp', axis=0)  41.7 us
    psum x1, blocking collectives, per_device(): together = lax.psum(jnp.concatenate(bias_grads), ('dp', 'frame'))  41.3 us
  transfers between devices with their start and end apart: 17, of which 12 were waited for; matrix products, arithmetic and copies ran while one was open for 9% of the time, Pallas kernels for 22%

profile of v2, /device:TPU:0, one launch (start us, length us, event | category | flops | bytes accessed | tf_op | source)
XLA Modules:
  0.0 690.5 jit_solution(7707401491588568394)
XLA Ops:
  13.1 20.4 %all-gather.1 = bf16[96,2304]{1,0:T(8,128)(2,1)} all-gather(bf16[24,2304]{1,0:T(8,128)(2,1)S(1)} %constant_dynamic-slice_fusion), channel_id=3, replica_groups=mesh['dp'=8,'frame'=4] {'frame'}, dimensions={0}, use_global_device_ids=true | all-gather | bytes 552960 | tf_op jit(solution)/shard_map/all_gather | solution.py:551
  37.4 23.2 %all-gather.3 = bf16[480,768]{1,0:T(8,128)(2,1)} all-gather(bf16[120,768]{1,0:T(8,128)(2,1)S(1)} %dynamic-slice_dynamic-update-slice_fusion.8), channel_id=5, replica_groups=mesh['dp'=8,'frame'=4] {'frame'}, dimensions={0}, use_global_device_ids=true | all-gather | bytes 921600 | tf_op jit(solution)/shard_map/all_gather | solution.py:551
  61.4 13.3 %all-gather.7 = bf16[4,1,7296]{2,1,0:T(2,128)(2,1)S(1)} all-gather(bf16[1,1,7296]{2,1,0:T(2,128)(2,1)S(1)} %reshape.312), channel_id=2, replica_groups=mesh['dp'=8,'frame'=4] {'frame'}, dimensions={0}, use_global_device_ids=true | all-gather | bytes 72960 | tf_op jit(solution)/shard_map/all_gather | solution.py:564
  76.3 4.9 all-to-all-start
  83.5 7.1 %all-to-all-done = f32[4,4,6912]{2,1,0:T(4,128)S(1)} async-done(((f32[4,4,6912]{2,1,0:T(4,128)}), f32[4,4,6912]{2,1,0:T(4,128)S(1)}, u32[]{:S(2)}, u32[]{:S(2)}) %all-to-all-start) | async-done | bytes 442400 | tf_op jit(solution)/shard_map/all_to_all | solution.py:578
  91.6 4.0 copy.52
  95.6 41.6 %all-gather.25.cloned.1.call-done = bf16[32,120,768]{2,1,0:T(8,128)(2,1)} async-done(((bf16[4,120,768]{2,1,0:T(8,128)(2,1)}), bf16[32,120,768]{2,1,0:T(8,128)(2,1)}) %all-gather.25.cloned.1.call-update) | async-done | bytes 5898256 | tf_op jit(solution)/shard_map/all_gather | solution.py:552
  137.2 4.3 slice_bitcast_fusion.1
  141.8 2.1 copy.54
  144.9 27.7 %spatial_forward.1 = (bf16[4,256,768]{2,1,0:T(8,128)(2,1)}, bf16[4,256,2304]{2,1,0:T(8,128)(2,1)}, bf16[4,256,768]{2,1,0:T(8,128)(2,1)}, f32[4,256,768]{2,1,0:T(...) custom-call(bf16[4,256,768]{2,1,0:T(8,128)(2,1)} %x_ref.3, ...), custom_call_target="tpu_custom_call" | custom-call | flops 9261023232 | bytes 24000000 | tf_op jit(solution)/shard_map/spatial_forward/pallas_call | solution.py:117
  172.6 3.8 fusion.22
  176.4 4.5 collective-permute-start
  180.9 1.5 collective-permute-start.1
  186.8 2.4 copy.55
  189.2 25.0 %collective-permute-done.left_ref = bf16[2,256,1536]{2,1,0:T(8,128)(2,1)} collective-permute-done((bf16[2,256,1536]{2,1,0:T(8,128)(2,1)}, bf16[2,256,1536]{2,1,0:T(8,128)(2,1)}, u32[]{:S(2)}, u32[]{:S(2)}) %collective-permute-start) | collective-permute-done | bytes 1572896 | tf_op jit(solution)/shard_map/ppermute | solution.py:584
  214.2 5.3 collective-permute-done.1.right_ref
  219.5 18.8 %temporal_forward.1 = (f32[4,5,256,128]{3,2,1,0:T(8,128)}, bf16[4,256,768]{2,1,0:T(8,128)(2,1)}, f32[4,256,768]{2,1,0:T(8,128)}, f32[4,256,768]{2,1,0:T(8,128)}) custom-call(s32[5,4]{1,0:T(8,128)} %convert_element_type.159.allowed, bf16[4,256,2304]{2,1,0:T(8,128)(2,1)} %get-tuple-element.52.qkv_ref, bf16[2,256,1536]{2,1,0:T(8,128)(2,1)} %collective-permute-done.left_ref, ...), custom_call_target="tpu_custom_call" | custom-call | flops 4353687552 | bytes 22000000 | tf_op jit(solution)/shard_map/temporal_forward/pallas_call | solution.py:204
  238.3 2.8 fusion.21
  241.2 2.3 copy-done.1
  244.5 2.6 copy.56
  247.0 2.6 copy.57
  249.7 30.9 %feed_forward.1 = (bf16[4,256,768]{2,1,0:T(8,128)(2,1)}, f32[4,256,768]{2,1,0:T(8,128)}, bf16[4,256,768]{2,1,0:T(8,128)(2,1)}, bf16[4,256,3072]{2,1,0:T(8,128)(2...) custom-call(f32[4,256,768]{2,1,0:T(8,128)} %get-tuple-element.54.aft, ...), custom_call_target="tpu_custom_call" | custom-call | flops 19327352832 | bytes 32000000 | tf_op jit(solution)/shard_map/feed_forward/pallas_call | solution.py:280
  280.5 12.0 %outer_pieces.10 = bf16[8,4,96,768]{3,2,1,0:T(8,128)(2,1)} custom-call(bf16[1024,768]{1,0:T(8,128)(2,1)} %bitcast.128, bf16[1024,3072]{1,0:T(8,128)(2,1)} %bitcast.118), custom_call_target="tpu_custom_call" | custom-call | flops 4831838208 | bytes 14155776 | tf_op jit(solution)/shard_map/outer_pieces/pallas_call | solution.py:509
  292.6 9.2 %outer_pieces.11 = bf16[8,4,96,768]{3,2,1,0:T(8,128)(2,1)} custom-call(bf16[1024,3072]{1,0:T(8,128)(2,1)} %bitcast.117, bf16[1024,768]{1,0:T(8,128)(2,1)} %bitcast.127), custom_call_target="tpu_custom_call" | custom-call | flops 4831838208 | bytes 9437184 | tf_op jit(solution)/shard_map/outer_pieces/pallas_call | solution.py:509
  301.7 7.6 %pad_maximum_fusion.1 = bf16[8,4,192,768]{3,2,1,0:T(8,128)(2,1)} fusion(bf16[8,4,96,768]{3,2,1,0:T(8,128)(2,1)} %outer_pieces.11, bf16[8,4,96,768]{3,2,1,0:T(8,128)(2,1)} %outer_pieces.10), kind=kLoop, calls=%fused_computation.1 | loop fusion | flops 18874368 | bytes 18874368 | tf_op jit(solution)/shard_map/concatenate | solution.py:589
  309.4 19.3 %temporal_backward.1 = (bf16[4,256,768]{2,1,0:T(8,128)(2,1)}, bf16[4,256,768]{2,1,0:T(8,128)(2,1)}, f32[4,256,1536]{2,1,0:T(8,128)}, bf16[2,256,1536]{2,1,0:T(8,...) custom-call(f32[4,256,768]{2,1,0:T(8,128)} %get-tuple-element.56.g_ref.g2_ref, ...), custom_call_target="tpu_custom_call" | custom-call | flops 5140119552 | bytes 36000000 | tf_op jit(solution)/shard_map/temporal_backward/pallas_call | solution.py:369
  328.7 3.4 collective-permute-start.2
  333.4 12.9 %outer_pieces.6 = bf16[8,4,24,768]{3,2,1,0:T(8,128)(2,1)} custom-call(bf16[1024,768]{1,0:T(8,128)(2,1)} %bitcast.124, bf16[1024,768]{1,0:T(8,128)(2,1)} %bitcast.125), custom_call_target="tpu_custom_call" | custom-call | flops 1207959552 | bytes 4718592 | tf_op jit(solution)/shard_map/outer_pieces/pallas_call | solution.py:509
  346.3 18.0 %collective-permute-done.2.fl_ref = bf16[2,256,1536]{2,1,0:T(8,128)(2,1)} collective-permute-done((bf16[2,256,1536]{2,1,0:T(8,128)(2,1)}, bf16[2,256,1536]{2,1,0:T(8,128)(2,1)}, u32[]{:S(2)}, u32[]{:S(2)}) %collective-permute-start.2) | collective-permute-done | bytes 1572896 | tf_op jit(solution)/shard_map/ppermute | solution.py:584
  364.3 5.3 collective-permute-done.3.fr_ref
  369.5 48.5 %spatial_backward.1 = (bf16[4,256,2304]{2,1,0:T(8,128)(2,1)}, bf16[4,256,768]{2,1,0:T(8,128)(2,1)}, bf16[4,256,2304]{2,1,0:T(8,128)(2,1)}, f32[4,256,768]{2,1,0:...) custom-call(bf16[4,256,768]{2,1,0:T(8,128)(2,1)} %get-tuple-element.59.dq2_ref, ...), custom_call_target="tpu_custom_call" | custom-call | flops 10468982784 | bytes 45000000 | tf_op jit(solution)/shard_map/spatial_backward/pallas_call | solution.py:461
  418.0 4.2 outer_pieces.8
  422.2 9.6 %outer_pieces.7 = bf16[8,4,72,768]{3,2,1,0:T(8,128)(2,1)} custom-call(bf16[1024,768]{1,0:T(8,128)(2,1)} %bitcast.122, bf16[1024,2304]{1,0:T(8,128)(2,1)} %bitcast.120), custom_call_target="tpu_custom_call" | custom-call | flops 3623878656 | bytes 11010048 | tf_op jit(solution)/shard_map/outer_pieces/pallas_call | solution.py:509
  431.8 9.6 %outer_pieces.9 = bf16[8,4,72,768]{3,2,1,0:T(8,128)(2,1)} custom-call(bf16[1024,768]{1,0:T(8,128)(2,1)} %bitcast.121, bf16[1024,2304]{1,0:T(8,128)(2,1)} %bitcast.119), custom_call_target="tpu_custom_call" | custom-call | flops 3623878656 | bytes 11010048 | tf_op jit(solution)/shard_map/outer_pieces/pallas_call | solution.py:509
  441.4 8.5 %pad_maximum_fusion = bf16[8,4,192,768]{3,2,1,0:T(8,128)(2,1)} fusion(bf16[8,4,72,768]{3,2,1,0:T(8,128)(2,1)} %outer_pieces.9, bf16[8,4,24,768]{3,2,1,0:T(8,128)(2,1)} %outer_pieces.8, bf16[8,4,72,768]{3,2,1,0:T(8,128)(2,1)} %outer_pieces.7, bf16[8,4,24,768]{3,2,1,0:T(8,128)(2,1)S(1)} %copy-done.4), kind=kLoop, calls=%fused_computation | loop fusion | flops 37748736 | bytes 18874368 | tf_op jit(solution)/shard_map/concatenate | solution.py:589
  450.8 73.5 %reduce-scatter.5.cloned.1.call-done = bf16[768,768]{1,0:T(8,128)(2,1)} async-done(((bf16[6144,768]{1,0:T(8,128)(2,1)}), bf16[768,768]{1,0:T(8,128)(2,1)}) %reduce-scatter.5.cloned.1.call-update) | async-done | bytes 1179664 | tf_op jit(solution)/shard_map/reduce_scatter | solution.py:591
  524.7 14.9 %all-gather.8 = bf16[4,4,7680]{2,1,0:T(4,128)(2,1)S(1)} all-gather(bf16[1,4,7680]{2,1,0:T(4,128)(2,1)S(1)} %maximum_bitcast_fusion.3), channel_id=1, replica_groups=mesh['dp'=8,'frame'=4] {'frame'}, dimensions={0}, use_global_device_ids=true | all-gather | bytes 307200 | tf_op jit(solution)/shard_map/all_gather | solution.py:695
  540.4 16.4 %reduce-scatter.11.cloned.1.call-done = bf16[192,768]{1,0:T(8,128)(2,1)} async-done(((bf16[768,768]{1,0:T(8,128)(2,1)}), bf16[192,768]{1,0:T(8,128)(2,1)}) %reduce-scatter.11.cloned.1.call-update) | async-done | bytes 294928 | tf_op jit(solution)/shard_map/reduce_scatter | solution.py:592
  556.9 30.6 %reduce-scatter.7.cloned.1.call-done = bf16[192,768]{1,0:T(8,128)(2,1)} async-done(((bf16[768,768]{1,0:T(8,128)(2,1)}), bf16[192,768]{1,0:T(8,128)(2,1)}) %reduce-scatter.7.cloned.1.call-update) | async-done | bytes 294928 | tf_op jit(solution)/shard_map/reduce_scatter | solution.py:592
  587.7 1.7 fusion.4
  590.1 3.3 all-to-all-start.1
  593.5 41.3 %psum.7 = f32[9984]{0:T(1024)S(1)} all-reduce(f32[9984]{0:T(1024)S(1)} %constant_dynamic-update-slice_fusion.1), channel_id=1, replica_groups=mesh['dp'=8,'frame'=4] {'dp','frame'}, use_global_device_ids=true, to_apply=%region_3.4 | all-reduce | flops 9984 | bytes 79872 | tf_op jit(solution)/shard_map/psum | solution.py:709
  639.4 1.9 convert_reduce_fusion
  643.0 3.3 fusion
  649.3 1.7 bitcast_convert_fusion
  651.1 1.7 bitcast_convert_fusion.1
  652.8 25.1 %all-gather.17.cloned.1.call-done = bf16[1536,768]{1,0:T(8,128)(2,1)} async-done(((bf16[192,768]{1,0:T(8,128)(2,1)}), bf16[1536,768]{1,0:T(8,128)(2,1)}) %all-gather.17.cloned.1.call-update) | async-done | bytes 2359312 | tf_op jit(solution)/shard_map/all_gather | solution.py:593
  678.0 1.7 fusion.24
  (165 shorter events, 39.3 us)
Async XLA Ops:
  7.2 67.7 %copy-start = (bf16[192,6912]{1,0:T(8,128)(2,1)S(1)}, bf16[192,6912]{1,0:T(8,128)(2,1)}, u32[]{:S(2)}) copy-start(bf16[192,6912]{1,0:T(8,128)(2,1)} %param.33) | copy-start | bytes 7962628
  7.2 53.5 %all-gather.27.cloned.1.call-start = ((), (), s32[]{:S(2)}) async-start(), calls=%async_computation.15 | async-start | bytes 1474560 | tf_op jit(solution)/shard_map/all_gather | solution.py:551
  11.4 0.7 copy-start.5
  11.4 49.8 %copy-start.7 = (bf16[4,768]{1,0:T(4,128)(2,1)S(1)}, bf16[4,768]{1,0:T(4,128)(2,1)}, u32[]{:S(2)}) copy-start(bf16[4,768]{1,0:T(4,128)(2,1)} %param.19) | copy-start | bytes 18436
  11.4 49.8 %copy-start.13 = (bf16[1728]{0:T(1024)(128)(2,1)S(1)}, bf16[1728]{0:T(1024)(128)(2,1)}, u32[]{:S(2)}) copy-start(bf16[1728]{0:T(1024)(128)(2,1)} %param.34) | copy-start | bytes 10372
  11.5 49.8 %copy-start.17 = (bf16[576]{0:T(1024)(128)(2,1)S(1)}, bf16[576]{0:T(1024)(128)(2,1)}, u32[]{:S(2)}) copy-start(bf16[576]{0:T(1024)(128)(2,1)} %param.22) | copy-start | bytes 3460
  11.5 49.8 %copy-start.18 = (bf16[576]{0:T(1024)(128)(2,1)S(1)}, bf16[576]{0:T(1024)(128)(2,1)}, u32[]{:S(2)}) copy-start(bf16[576]{0:T(1024)(128)(2,1)} %param.26) | copy-start | bytes 3460
  11.5 49.8 %copy-start.19 = (bf16[768]{0:T(1024)(128)(2,1)S(1)}, bf16[768]{0:T(1024)(128)(2,1)}, u32[]{:S(2)}) copy-start(bf16[768]{0:T(1024)(128)(2,1)} %param.30) | copy-start | bytes 4612
  11.5 49.8 %copy-start.20 = (bf16[192]{0:T(256)(128)(2,1)S(1)}, bf16[192]{0:T(256)(128)(2,1)}, u32[]{:S(2)}) copy-start(bf16[192]{0:T(256)(128)(2,1)} %param.24) | copy-start | bytes 1156
  11.5 49.8 %copy-start.21 = (bf16[192]{0:T(256)(128)(2,1)S(1)}, bf16[192]{0:T(256)(128)(2,1)}, u32[]{:S(2)}) copy-start(bf16[192]{0:T(256)(128)(2,1)} %param.28) | copy-start | bytes 1156
  11.5 49.8 %copy-start.22 = (bf16[192]{0:T(256)(128)(2,1)S(1)}, bf16[192]{0:T(256)(128)(2,1)}, u32[]{:S(2)}) copy-start(bf16[192]{0:T(256)(128)(2,1)} %param.32) | copy-start | bytes 1156
  12.2 79.4 %all-gather.23.cloned.1.call-start = ((), (), s32[]{:S(2)}) async-start(), calls=%async_computation.13 | async-start | bytes 3981312 | tf_op jit(solution)/shard_map/all_gather | solution.py:552
  33.5 103.7 %all-gather.25.cloned.1.call-start = ((), (), s32[]{:S(2)}) async-start(), calls=%async_computation.14 | async-start | bytes 6635520 | tf_op jit(solution)/shard_map/all_gather | solution.py:552
  60.6 177.7 %all-gather.29.cloned.1.call-start = ((), (), s32[]{:S(2)}) async-start(), calls=%async_computation.16 | async-start | bytes 10616832 | tf_op jit(solution)/shard_map/all_gather | solution.py:552
  76.3 14.3 %all-to-all-start = ((f32[4,4,6912]{2,1,0:T(4,128)}), f32[4,4,6912]{2,1,0:T(4,128)S(1)}, u32[]{:S(2)}, u32[]{:S(2)}) async-start(f32[4,4,6912]{2,1,0:T(4,128)} %reshape.266), calls=%async_computation | async-start | bytes 884736 | tf_op jit(solution)/shard_map/all_to_all | solution.py:578
  81.2 369.1 %reduce-scatter.9.cloned.1.call-start = ((), (), s32[]{:S(2)}) async-start(), calls=%async_computation.9 | async-start | bytes 10616832 | tf_op jit(solution)/shard_map/reduce_scatter | solution.py:591
  172.6 9.8 %copy-start.23 = (s32[1,16]{1,0:T(1,128)S(1)}, s32[1,16]{1,0:T(1,128)}, u32[]{:S(2)}) copy-start(s32[1,16]{1,0:T(1,128)} %param.20) | copy-start | bytes 196
  176.4 37.8 %collective-permute-start = (bf16[2,256,1536]{2,1,0:T(8,128)(2,1)}, bf16[2,256,1536]{2,1,0:T(8,128)(2,1)}, u32[]{:S(2)}, u32[]{:S(2)}) collective-permute-start(bf16[2,256,1536]{2,1,0:T(8,128)(2,1)} %get-tuple-element.97), channel_id=1, source_target_pairs={{0,1},{1,2},{2,3},{4,5},{5,6},{6,7},{8,9},{9,10},{10,11},{12,13},{... | collective-permute-start | bytes 4718600 | tf_op jit(solution)/shard_map/ppermute | solution.py:584
  180.9 38.5 %collective-permute-start.1 = (bf16[2,256,1536]{2,1,0:T(8,128)(2,1)}, bf16[2,256,1536]{2,1,0:T(8,128)(2,1)}, u32[]{:S(2)}, u32[]{:S(2)}) collective-permute-start(bf16[2,256,1536]{2,1,0:T(8,128)(2,1)} %get-tuple-element.96), channel_id=1, source_target_pairs={{1,0},{2,1},{3,2},{5,4},{6,5},{7,6},{9,8},{10,9},{11,10},{13,12},{... | collective-permute-start | bytes 4718600 | tf_op jit(solution)/shard_map/ppermute | solution.py:584
  238.3 5.1 copy-start.1
  309.3 215.0 %reduce-scatter.5.cloned.1.call-start = ((), (), s32[]{:S(2)}) async-start(), calls=%async_computation.6 | async-start | bytes 10616832 | tf_op jit(solution)/shard_map/reduce_scatter | solution.py:591
  328.7 35.5 %collective-permute-start.2 = (bf16[2,256,1536]{2,1,0:T(8,128)(2,1)}, bf16[2,256,1536]{2,1,0:T(8,128)(2,1)}, u32[]{:S(2)}, u32[]{:S(2)}) collective-permute-start(bf16[2,256,1536]{2,1,0:T(8,128)(2,1)} %get-tuple-element.61), channel_id=1, source_target_pairs={{0,1},{1,2},{2,3},{4,5},{5,6},{6,7},{8,9},{9,10},{10,11},{12,13},{... | collective-permute-start | bytes 4718600 | tf_op jit(solution)/shard_map/ppermute | solution.py:584
  332.1 37.4 %collective-permute-start.3 = (bf16[2,256,1536]{2,1,0:T(8,128)(2,1)}, bf16[2,256,1536]{2,1,0:T(8,128)(2,1)}, u32[]{:S(2)}, u32[]{:S(2)}) collective-permute-start(bf16[2,256,1536]{2,1,0:T(8,128)(2,1)} %get-tuple-element.62), channel_id=1, source_target_pairs={{1,0},{2,1},{3,2},{5,4},{6,5},{7,6},{9,8},{10,9},{11,10},{13,12},{... | collective-permute-start | bytes 4718600 | tf_op jit(solution)/shard_map/ppermute | solution.py:584
  431.8 9.7 %copy-start.4 = (bf16[8,4,24,768]{3,2,1,0:T(8,128)(2,1)S(1)}, bf16[8,4,24,768]{3,2,1,0:T(8,128)(2,1)}, u32[]{:S(2)}) copy-start(bf16[8,4,24,768]{3,2,1,0:T(8,128)(2,1)} %outer_pieces.6) | copy-start | bytes 3538948
  450.0 74.5 %copy-start.10 = (f32[4,768]{1,0:T(4,128)S(1)}, f32[4,768]{1,0:T(4,128)}, u32[]{:S(2)}) copy-start(f32[4,768]{1,0:T(4,128)} %get-tuple-element.67) | copy-start | bytes 36868
  450.0 74.5 %copy-start.8 = (f32[4,3,768]{2,1,0:T(4,128)S(1)}, f32[4,3,768]{2,1,0:T(4,128)}, u32[]{:S(2)}) copy-start(f32[4,3,768]{2,1,0:T(4,128)} %get-tuple-element.68) | copy-start | bytes 110596
  450.0 74.5 %copy-start.6 = (f32[4,5,768]{2,1,0:T(8,128)S(1)}, f32[4,5,768]{2,1,0:T(8,128)}, u32[]{:S(2)}) copy-start(f32[4,5,768]{2,1,0:T(8,128)} %get-tuple-element.66) | copy-start | bytes 184324
  450.0 106.8 %reduce-scatter.11.cloned.1.call-start = ((), (), s32[]{:S(2)}) async-start(), calls=%async_computation.10 | async-start | bytes 1474560 | tf_op jit(solution)/shard_map/reduce_scatter | solution.py:592
  450.3 137.3 %copy-start.15 = (f32[1,768]{1,0:T(1,128)S(1)}, f32[1,768]{1,0:T(1,128)}, u32[]{:S(2)}) copy-start(f32[1,768]{1,0:T(1,128)} %get-tuple-element.80) | copy-start | bytes 9220
  450.3 137.3 %copy-start.14 = (f32[1,768]{1,0:T(1,128)S(1)}, f32[1,768]{1,0:T(1,128)}, u32[]{:S(2)}) copy-start(f32[1,768]{1,0:T(1,128)} %get-tuple-element.82) | copy-start | bytes 9220
  450.3 137.3 %copy-start.12 = (f32[1,2304]{1,0:T(1,128)S(1)}, f32[1,2304]{1,0:T(1,128)}, u32[]{:S(2)}) copy-start(f32[1,2304]{1,0:T(1,128)} %get-tuple-element.77) | copy-start | bytes 27652
  450.3 137.3 %copy-start.16 = (f32[1,768]{1,0:T(1,128)S(1)}, f32[1,768]{1,0:T(1,128)}, u32[]{:S(2)}) copy-start(f32[1,768]{1,0:T(1,128)} %get-tuple-element.78) | copy-start | bytes 9220
  450.3 137.3 %copy-start.11 = (f32[1,2304]{1,0:T(1,128)S(1)}, f32[1,2304]{1,0:T(1,128)}, u32[]{:S(2)}) copy-start(f32[1,2304]{1,0:T(1,128)} %get-tuple-element.79) | copy-start | bytes 27652
  450.8 136.8 %reduce-scatter.7.cloned.1.call-start = ((), (), s32[]{:S(2)}) async-start(), calls=%async_computation.7 | async-start | bytes 1474560 | tf_op jit(solution)/shard_map/reduce_scatter | solution.py:592
  524.4 115.0 %all-gather.21.cloned.1.call-start = ((), (), s32[]{:S(2)}) async-start(), calls=%async_computation.12 | async-start | bytes 2211840 | tf_op jit(solution)/shard_map/all_gather | solution.py:697
  524.7 68.7 %copy-start.9 = (f32[1,3072]{1,0:T(1,128)S(1)}, f32[1,3072]{1,0:T(1,128)}, u32[]{:S(2)}) copy-start(f32[1,3072]{1,0:T(1,128)} %get-tuple-element.81) | copy-start | bytes 36868
  540.4 106.8 %all-gather.19.cloned.1.call-start = ((), (), s32[]{:S(2)}) async-start(), calls=%async_computation.11 | async-start | bytes 2654208 | tf_op jit(solution)/shard_map/all_gather | solution.py:593
  556.9 121.1 %all-gather.17.cloned.1.call-start = ((), (), s32[]{:S(2)}) async-start(), calls=%async_computation.8 | async-start | bytes 2654208 | tf_op jit(solution)/shard_map/all_gather | solution.py:593
  590.1 48.6 %all-to-all-start.1 = ((f32[4,4,192]{2,1,0:T(4,128)}), f32[4,4,192]{2,1,0:T(4,128)S(1)}, u32[]{:S(2)}, u32[]{:S(2)}) async-start(f32[4,4,192]{2,1,0:T(4,128)} %reshape.273), calls=%async_computation.1 | async-start | bytes 32768 | tf_op jit(solution)/shard_map/all_to_all | solution.py:703
  639.4 3.5 copy-start.2
  647.2 2.0 copy-start.3
Sparse Core Ops, SparseCore 0:
  12.3 43.2 all-gather.26
  57.5 34.0 all-gather.22
  93.4 43.7 all-gather.24
  138.9 58.6 all-gather.28
  309.4 74.7 reduce-scatter.8
  450.1 74.1 reduce-scatter.4
  526.7 30.1 reduce-scatter.10
  559.2 28.3 reduce-scatter.6
  590.0 26.2 all-gather.20
  618.0 29.1 all-gather.18
  649.1 28.8 all-gather.16

commit v3 on v2

v3 whole, which is shorter than its diff:
```python
import functools

import jax
import jax.numpy as jnp
from jax import lax
from jax.experimental import pallas as pl
from jax.experimental.pallas import tpu as pltpu
from jax.sharding import PartitionSpec as P


HEADS = 12
HEAD_DIM = 64
WINDOW = 2

F32 = jnp.float32
BF16 = jnp.bfloat16
SCALE = HEAD_DIM ** (-0.5)
SPAN = 2 * WINDOW + 1


def mm(a, b):
    return lax.dot_general(a, b, (((1,), (0,)), ((), ())), preferred_element_type=F32)


def mm_nt(a, b):
    return lax.dot_general(a, b, (((1,), (1,)), ((), ())), preferred_element_type=F32)


def mm_tn(a, b):
    return lax.dot_general(a, b, (((0,), (0,)), ((), ())), preferred_element_type=F32)


def unit(x):
    centred = x - jnp.mean(x, axis=-1, keepdims=True)
    inv = lax.rsqrt(jnp.mean(centred * centred, axis=-1, keepdims=True) + 1e-06)
    return centred * inv, inv


def unit_back(dn, xhat, inv, scale):
    e = dn * (1.0 + scale)
    first = jnp.mean(e, axis=-1, keepdims=True)
    second = jnp.mean(e * xhat, axis=-1, keepdims=True)
    return inv * (e - first - xhat * second)


def down(x):
    return jnp.sum(x, axis=0, keepdims=True)


def low_half(rows):
    return lax.broadcasted_iota(jnp.int32, (rows, 2 * HEAD_DIM), 1) < HEAD_DIM


def soft(scores):
    e = jnp.exp(scores - jnp.max(scores, axis=-1, keepdims=True))
    return e / jnp.sum(e, axis=-1, keepdims=True)


def params(flops, nbytes, trans=0):
    return dict(
        compiler_params=pltpu.CompilerParams(vmem_limit_bytes=60 * 2**20),
        cost_estimate=pl.CostEstimate(
            flops=int(flops), bytes_accessed=int(nbytes), transcendentals=int(trans)
        ),
    )


def fixed(shape):
    return pl.BlockSpec(shape, lambda *_: (0,) * len(shape), pipeline_mode=pl.Buffered(1))


def per_first(shape):
    return pl.BlockSpec((1,) + shape, lambda i: (i,) + (0,) * len(shape))


def per_second(lead, tile, width):
    return pl.BlockSpec((lead, tile, width), lambda i: (0, i, 0))


def spatial_kernel(x_ref, mod_ref, wsi, bsi, n1_ref, qkv1_ref, attn_ref):
    x = x_ref[0].astype(F32)
    width = x.shape[1]
    xhat, _ = unit(x)
    n1 = (xhat * (1.0 + mod_ref[0, 1:2]) + mod_ref[0, 0:1]).astype(BF16)
    n1_ref[0] = n1
    qkv1_ref[0] = (mm(n1, wsi[...]) + bsi[...]).astype(BF16)
    half = low_half(x.shape[0])
    for pair in range(width // (2 * HEAD_DIM)):
        at = pair * 2 * HEAD_DIM
        q = qkv1_ref[0, :, at : at + 2 * HEAD_DIM]
        k = qkv1_ref[0, :, width + at : width + at + 2 * HEAD_DIM]
        v = qkv1_ref[0, :, 2 * width + at : 2 * width + at + 2 * HEAD_DIM]
        zero = jnp.zeros_like(q)
        first = soft(mm_nt(jnp.where(half, q, zero), k) * SCALE).astype(BF16)
        second = soft(mm_nt(jnp.where(half, zero, q), k) * SCALE).astype(BF16)
        out = jnp.where(half, mm(first, v), mm(second, v))
        attn_ref[0, :, at : at + 2 * HEAD_DIM] = out.astype(BF16)


def spatial_forward(x, mod, wsi, bsi):
    frames, patches, width = x.shape
    block = lambda n: per_first((patches, n))
    outs = [width, 3 * width, width]
    tokens = frames * patches
    return pl.pallas_call(
        spatial_kernel,
        grid=(frames,),
        in_specs=[block(width), per_first(mod.shape[1:]), fixed(wsi.shape), fixed(bsi.shape)],
        out_specs=[block(n) for n in outs],
        out_shape=[jax.ShapeDtypeStruct((frames, patches, n), BF16) for n in outs],
        name="spatial_forward",
        **params(2 * tokens * width * (3 * width + 4 * patches), 12e6, tokens * patches * HEADS),
    )(x, mod, wsi, bsi)


def project_kernel(x_ref, attn_ref, mod_ref, wso, bso, branch_ref, after_ref, n2_ref):
    branch = mm(attn_ref[0], wso[...]) + bso[...]
    branch_ref[0] = branch
    after = x_ref[0].astype(F32) + mod_ref[0, 2:3] * branch
    after_ref[0] = after
    xhat, _ = unit(after)
    n2_ref[0] = (xhat * (1.0 + mod_ref[0, 4:5]) + mod_ref[0, 3:4]).astype(BF16)


def project_forward(x, attn, mod, wso, bso):
    frames, patches, width = x.shape
    block = per_first((patches, width))
    tokens = frames * patches
    return pl.pallas_call(
        project_kernel,
        grid=(frames,),
        in_specs=[block, block, per_first(mod.shape[1:]), fixed(wso.shape), fixed(bso.shape)],
        out_specs=[block] * 3,
        out_shape=[jax.ShapeDtypeStruct(x.shape, t) for t in (F32, F32, BF16)],
        name="project_forward",
        **params(2 * tokens * width * width, 13e6),
    )(x, attn, mod, wso, bso)


def split_store(hi_ref, lo_ref, row, prod):
    hi = prod.astype(BF16)
    hi_ref[row] = hi
    lo_ref[row] = (prod - hi.astype(F32)).astype(BF16)


def ext_rows(e, frames, left, own, right, base, width):
    if e < WINDOW:
        return left[e, :, base - width : base]
    if e < WINDOW + frames:
        return own[e - WINDOW, :, base : base + width]
    return right[e - WINDOW - frames, :, base - width : base]


def head_sums(hi_ref, lo_ref, first, count, ones):
    tile, width = hi_ref.shape[1:]
    hi = hi_ref[first : first + count].reshape(count * tile, width)
    lo = lo_ref[first : first + count].reshape(count * tile, width)
    return mm(hi, ones) + mm(lo, ones)


def temporal_kernel(
    allowed, qkv_ref, nl_ref, nr_ref, after_ref, mod_ref, wti, bti, wto, bto, ones, ones_t,
    probs_ref, attn_ref, branch_ref, out_ref, left_ref, right_ref, hi_ref, lo_ref,
):
    frames, tile, width = after_ref.shape
    for near, kv_ref in ((nl_ref, left_ref), (nr_ref, right_ref)):
        kv = mm(near[...].reshape(WINDOW * tile, width), wti[:, width:]) + bti[:, width:]
        kv_ref[...] = kv.astype(BF16).reshape(WINDOW, tile, 2 * width)
    for t in range(frames):
        q = qkv_ref[t, :, :width].astype(F32)
        for o in range(SPAN):
            k = ext_rows(t + o, frames, left_ref, qkv_ref, right_ref, width, width)
            split_store(hi_ref, lo_ref, t * SPAN + o, q * k.astype(F32))
    for t in range(frames):
        raw = head_sums(hi_ref, lo_ref, t * SPAN, SPAN, ones[...]) * SCALE
        raw = [
            jnp.where(allowed[o, t] > 0, raw[o * tile : (o + 1) * tile], -1e30)
            for o in range(SPAN)
        ]
        top = raw[0]
        for o in range(1, SPAN):
            top = jnp.maximum(top, raw[o])
        expo = [jnp.exp(r - top) for r in raw]
        total = expo[0]
        for o in range(1, SPAN):
            total = total + expo[o]
        inv = 1.0 / total
        probs = [e * inv for e in expo]
        for o in range(SPAN):
            probs_ref[t, o] = probs[o]
        wide = mm(jnp.concatenate(probs, axis=0).astype(BF16), ones_t[...])
        total = None
        for o in range(SPAN):
            v = ext_rows(t + o, frames, left_ref, qkv_ref, right_ref, 2 * width, width)
            term = wide[o * tile : (o + 1) * tile] * v.astype(F32)
            total = term if total is None else total + term
        attn_ref[t] = total.astype(BF16)
    branch = mm(attn_ref[...].reshape(frames * tile, width), wto[...]) + bto[...]
    for t in range(frames):
        part = branch[t * tile : (t + 1) * tile]
        branch_ref[t] = part
        out_ref[t] = after_ref[t] + mod_ref[t, 5:6] * part


def head_ones(width):
    head = jnp.arange(width, dtype=jnp.int32)[:, None] // HEAD_DIM
    return (head == jnp.arange(128, dtype=jnp.int32)[None, :]).astype(BF16)


def temporal_forward(allowed, qkv, near_left, near_right, after, mod, wti, bti, wto, bto):
    frames, patches, width = after.shape
    tile = 64
    ones = head_ones(width)
    spec = lambda n: per_second(frames, tile, n)
    halo = per_second(WINDOW, tile, 2 * width)
    near = per_second(WINDOW, tile, width)
    shape = lambda t: jax.ShapeDtypeStruct((frames, patches, width), t)
    tokens = frames * patches
    return pl.pallas_call(
        temporal_kernel,
        grid=(patches // tile,),
        in_specs=[
            pl.BlockSpec(memory_space=pltpu.SMEM),
            spec(3 * width), near, near, spec(width), fixed(mod.shape),
            fixed(wti.shape), fixed(bti.shape), fixed(wto.shape), fixed(bto.shape),
            fixed(ones.shape), fixed(ones.shape[::-1]),
        ],
        out_specs=[
            pl.BlockSpec((frames, SPAN, tile, 128), lambda i: (0, 0, i, 0)),
            spec(width), spec(width), spec(width), halo, halo,
        ],
        out_shape=[
            jax.ShapeDtypeStruct((frames, SPAN, patches, 128), F32),
            shape(BF16), shape(F32), shape(F32),
            jax.ShapeDtypeStruct((WINDOW, patches, 2 * width), BF16),
            jax.ShapeDtypeStruct((WINDOW, patches, 2 * width), BF16),
        ],
        scratch_shapes=[pltpu.VMEM((frames * SPAN, tile, width), BF16)] * 2,
        name="temporal_forward",
        **params(2 * tokens * width * (width + SPAN * 400), 22e6, tokens * SPAN * 128),
    )(allowed, qkv, near_left, near_right, after, mod, wti, bti, wto, bto, ones, ones.T)


def feed_kernel(
    after_ref, cot_ref, mod_ref, w1, b1, w2, b2,
    out_ref, g_ref, n_ref, act_ref, dpre_ref, db_ref, dmod_ref, sum1_ref, sum2_ref,
):
    after = after_ref[0]
    width = after.shape[1]
    hidden = w1.shape[1]
    xhat, inv = unit(after)
    scale = mod_ref[0, 7:8]
    gate = mod_ref[0, 8:9]
    n = (xhat * (1.0 + scale) + mod_ref[0, 6:7]).astype(BF16)
    n_ref[0] = n
    g3 = cot_ref[0].astype(F32)
    db = (gate * g3).astype(BF16)
    db_ref[0] = db

    @pl.when(pl.program_id(0) == 0)
    def _():
        sum1_ref[...] = jnp.zeros_like(sum1_ref)
        sum2_ref[...] = jnp.zeros_like(sum2_ref)

    sum2_ref[...] += down(db.astype(F32))
    branch = jnp.zeros_like(after)
    dn = jnp.zeros_like(after)
    chunk = width
    for c in range(hidden // chunk):
        cols = slice(c * chunk, (c + 1) * chunk)
        pre = mm(n, w1[:, cols]) + b1[:, cols]
        dact = mm_nt(db, w2[cols, :])
        phi = 0.5 * (1.0 + lax.erf(pre * 0.7071067811865476))
        act = (pre * phi).astype(BF16)
        slope = phi + pre * (jnp.exp(-0.5 * pre * pre) * 0.3989422804014327)
        dpre = (dact * slope).astype(BF16)
        act_ref[0, :, cols] = act
        dpre_ref[0, :, cols] = dpre
        sum1_ref[:, cols] += down(dpre.astype(F32))
        branch += mm(act, w2[cols, :])
        dn += mm_nt(dpre, w1[:, cols])
    branch = branch + b2[...]
    out_ref[0] = (after + gate * branch).astype(BF16)
    dmod_ref[0, 0:1] = down(dn)
    dmod_ref[0, 1:2] = down(dn * xhat)
    dmod_ref[0, 2:3] = down(g3 * branch)
    g_ref[0] = g3 + unit_back(dn, xhat, inv, scale)


def feed_forward(after, cot, mod, w1, b1, w2, b2):
    frames, patches, width = after.shape
    hidden = w1.shape[1]
    shape = lambda n, t: jax.ShapeDtypeStruct((frames, patches, n), t)
    block = lambda n: per_first((patches, n))
    outs = [(width, BF16), (width, F32), (width, BF16), (hidden, BF16), (hidden, BF16), (width, BF16)]
    tokens = frames * patches
    return pl.pallas_call(
        feed_kernel,
        grid=(frames,),
        in_specs=[block(width), block(width), per_first(mod.shape[1:])]
        + [fixed(w.shape) for w in (w1, b1, w2, b2)],
        out_specs=[block(n) for n, _ in outs]
        + [per_first((3, width)), pl.BlockSpec((1, hidden), lambda i: (0, 0)),
           pl.BlockSpec((1, width), lambda i: (0, 0))],
        out_shape=[shape(n, t) for n, t in outs]
        + [jax.ShapeDtypeStruct((frames, 3, width), F32),
           jax.ShapeDtypeStruct((1, hidden), F32), jax.ShapeDtypeStruct((1, width), F32)],
        name="feed_forward",
        **params(8 * tokens * width * hidden, 32e6, 2 * tokens * hidden),
    )(after, cot, mod, w1, b1, w2, b2)


def temporal_back_kernel(
    g_ref, branch_ref, mod_ref, wto, wti, qkv_ref, left_ref, right_ref, probs_ref, ones, ones_t,
    db_ref, dqkv_ref, dleft_ref, dright_ref, nleft_ref, nright_ref, dgate_ref, sum_ref, sumq_ref,
    hi_ref, lo_ref, da_ref, ds_ref, pw_ref,
):
    frames, tile, width = g_ref.shape

    @pl.when(pl.program_id(0) == 0)
    def _():
        dgate_ref[...] = jnp.zeros_like(dgate_ref)
        sum_ref[...] = jnp.zeros_like(sum_ref)
        sumq_ref[...] = jnp.zeros_like(sumq_ref)

    for t in range(frames):
        g = g_ref[t]
        dgate_ref[t : t + 1] += down(g * branch_ref[t])
        db = (mod_ref[t, 5:6] * g).astype(BF16)
        db_ref[t] = db
        sum_ref[...] += down(db.astype(F32))
    da_all = mm_nt(db_ref[...].reshape(frames * tile, width), wto[...]).astype(BF16)
    da_ref[...] = da_all.reshape(frames, tile, width)
    for t in range(frames):
        da = da_ref[t].astype(F32)
        for o in range(SPAN):
            v = ext_rows(t + o, frames, left_ref, qkv_ref, right_ref, 2 * width, width)
            split_store(hi_ref, lo_ref, t * SPAN + o, da * v.astype(F32))
    for t in range(frames):
        dp = head_sums(hi_ref, lo_ref, t * SPAN, SPAN, ones[...])
        probs = probs_ref[t].reshape(SPAN * tile, 128)
        both = probs * dp
        dot = both[:tile]
        for o in range(1, SPAN):
            dot = dot + both[o * tile : (o + 1) * tile]
        ds = both - probs * jnp.concatenate([dot] * SPAN, axis=0)
        wide = mm(ds.astype(BF16), ones_t[...]).astype(BF16)
        ds_ref[t * SPAN : (t + 1) * SPAN] = wide.reshape(SPAN, tile, width)
        wide = mm(probs.astype(BF16), ones_t[...]).astype(BF16)
        pw_ref[t * SPAN : (t + 1) * SPAN] = wide.reshape(SPAN, tile, width)
    for t in range(frames):
        total = None
        for o in range(SPAN):
            k = ext_rows(t + o, frames, left_ref, qkv_ref, right_ref, width, width)
            term = ds_ref[t * SPAN + o].astype(F32) * k.astype(F32)
            total = term if total is None else total + term
        dqkv_ref[t, :, :width] = (total * SCALE).astype(BF16)
    for e in range(frames + 2 * WINDOW):
        dk = dv = None
        for t in range(max(0, e - SPAN + 1), min(frames, e + 1)):
            row = t * SPAN + e - t
            q = qkv_ref[t, :, :width].astype(F32)
            term = ds_ref[row].astype(F32) * q
            dk = term if dk is None else dk + term
            term = pw_ref[row].astype(F32) * da_ref[t].astype(F32)
            dv = term if dv is None else dv + term
        dk = (dk * SCALE).astype(BF16)
        dv = dv.astype(BF16)
        if e < WINDOW:
            dleft_ref[e, :, :width] = dk
            dleft_ref[e, :, width:] = dv
        elif e < WINDOW + frames:
            dqkv_ref[e - WINDOW, :, width : 2 * width] = dk
            dqkv_ref[e - WINDOW, :, 2 * width :] = dv
        else:
            dright_ref[e - WINDOW - frames, :, :width] = dk
            dright_ref[e - WINDOW - frames, :, width:] = dv
    for dkv_ref, near_ref in ((dleft_ref, nleft_ref), (dright_ref, nright_ref)):
        flat = dkv_ref[...].reshape(WINDOW * tile, 2 * width)
        sumq_ref[:, width:] += down(flat.astype(F32))
        near_ref[...] = mm_nt(flat, wti[:, width:]).astype(BF16).reshape(WINDOW, tile, width)
    sumq_ref[...] += down(dqkv_ref[...].reshape(frames * tile, 3 * width).astype(F32))


def temporal_backward(g, branch, mod, wto, wti, qkv, left, right, probs):
    frames, patches, width = g.shape
    tile = 64
    ones = head_ones(width)
    spec = lambda n: per_second(frames, tile, n)
    halo = per_second(WINDOW, tile, 2 * width)
    near = per_second(WINDOW, tile, width)
    shape = lambda f, n, t: jax.ShapeDtypeStruct((f, patches, n), t)
    tokens = frames * patches
    return pl.pallas_call(
        temporal_back_kernel,
        grid=(patches // tile,),
        in_specs=[
            spec(width), spec(width), fixed(mod.shape), fixed(wto.shape), fixed(wti.shape),
            spec(3 * width), halo, halo,
            pl.BlockSpec((frames, SPAN, tile, 128), lambda i: (0, 0, i, 0)),
            fixed(ones.shape), fixed(ones.shape[::-1]),
        ],
        out_specs=[
            spec(width), spec(3 * width), halo, halo, near, near,
            pl.BlockSpec((frames, width), lambda i: (0, 0)),
            pl.BlockSpec((1, width), lambda i: (0, 0)),
            pl.BlockSpec((1, 3 * width), lambda i: (0, 0)),
        ],
        out_shape=[
            shape(frames, width, BF16), shape(frames, 3 * width, BF16),
            shape(WINDOW, 2 * width, BF16), shape(WINDOW, 2 * width, BF16),
            shape(WINDOW, width, BF16), shape(WINDOW, width, BF16),
            jax.ShapeDtypeStruct((frames, width), F32), jax.ShapeDtypeStruct((1, width), F32),
            jax.ShapeDtypeStruct((1, 3 * width), F32),
        ],
        scratch_shapes=[pltpu.VMEM((frames * SPAN, tile, width), BF16)] * 2
        + [pltpu.VMEM((frames, tile, width), BF16)]
        + [pltpu.VMEM((frames * SPAN, tile, width), BF16)] * 2,
        name="temporal_backward",
        **params(2 * tokens * width * (width + SPAN * 500), 36e6),
    )(g, branch, mod, wto, wti, qkv, left, right, probs, ones, ones.T)


def project_back_kernel(
    dn_ref, fl_ref, fr_ref, after_ref, g2_ref, branch_ref, mod_ref, wso,
    g_ref, db_ref, da_ref, dmod_ref, sum_ref,
):
    at = pl.program_id(0)

    @pl.when(at == 0)
    def _():
        sum_ref[...] = jnp.zeros_like(sum_ref)

    dn = dn_ref[0] + jnp.where(at < WINDOW, fl_ref[0].astype(F32), fr_ref[0].astype(F32))
    xhat, inv = unit(after_ref[0])
    dmod_ref[0, 1:2] = down(dn)
    dmod_ref[0, 2:3] = down(dn * xhat)
    g1 = g2_ref[0] + unit_back(dn, xhat, inv, mod_ref[0, 4:5])
    dmod_ref[0, 0:1] = down(g1 * branch_ref[0])
    g_ref[0] = g1
    db = (mod_ref[0, 2:3] * g1).astype(BF16)
    db_ref[0] = db
    sum_ref[...] += down(db.astype(F32))
    da_ref[0] = mm_nt(db, wso[...]).astype(BF16)


def project_backward(dn2, from_left, from_right, after, g2, branch, mod, wso):
    frames, patches, width = after.shape
    block = per_first((patches, width))
    tokens = frames * patches
    return pl.pallas_call(
        project_back_kernel,
        grid=(frames,),
        in_specs=[
            block,
            pl.BlockSpec((1, patches, width), lambda i: (jnp.minimum(i, WINDOW - 1), 0, 0)),
            pl.BlockSpec((1, patches, width), lambda i: (jnp.maximum(i - WINDOW, 0), 0, 0)),
            block, block, block, per_first(mod.shape[1:]), fixed(wso.shape),
        ],
        out_specs=[block, block, block, per_first((3, width)),
                   pl.BlockSpec((1, width), lambda i: (0, 0))],
        out_shape=[jax.ShapeDtypeStruct(after.shape, t) for t in (F32, BF16, BF16)]
        + [jax.ShapeDtypeStruct((frames, 3, width), F32), jax.ShapeDtypeStruct((1, width), F32)],
        name="project_backward",
        **params(2 * tokens * width * width, 22e6),
    )(dn2, from_left, from_right, after, g2, branch, mod, wso)


def heads_back(q_ref, k_ref, v_ref, da_ref, out_ref, sum_ref):
    tokens, width = q_ref.shape[1:]

    @pl.when(pl.program_id(0) == 0)
    def _():
        sum_ref[...] = jnp.zeros_like(sum_ref)

    half = low_half(tokens)
    for pair in range(width // (2 * HEAD_DIM)):
        cols = slice(pair * 2 * HEAD_DIM, (pair + 1) * 2 * HEAD_DIM)
        q, k, v, da = (ref[0, :, cols] for ref in (q_ref, k_ref, v_ref, da_ref))
        zero = jnp.zeros_like(q)
        parts = []
        for side in range(2):
            pick = (lambda u: jnp.where(half, u, zero)) if side == 0 else (
                lambda u: jnp.where(half, zero, u))
            probs = soft(mm_nt(pick(q), k) * SCALE)
            dp = mm_nt(pick(da), v)
            both = probs * dp
            ds = (both - probs * jnp.sum(both, axis=-1, keepdims=True)).astype(BF16)
            parts.append((mm(ds, k), mm_tn(ds, q), mm_tn(probs.astype(BF16), da)))
        grads = [jnp.where(half, a, b) for a, b in zip(*parts)]
        for at, grad in enumerate((grads[0] * SCALE, grads[1] * SCALE, grads[2])):
            out_ref[0, :, at * width + cols.start : at * width + cols.stop] = grad.astype(BF16)
    sum_ref[...] += down(out_ref[0].astype(F32))


def first_heads_kernel(q_ref, k_ref, v_ref, da_ref, out_ref, sum_ref):
    heads_back(q_ref, k_ref, v_ref, da_ref, out_ref, sum_ref)


def last_heads_kernel(
    q_ref, k_ref, v_ref, da_ref, first_ref, g_ref, x_ref, mod_ref, wsi,
    out_ref, sum_ref, grad_ref, dmod_ref,
):
    heads_back(q_ref, k_ref, v_ref, da_ref, out_ref, sum_ref)
    width = q_ref.shape[2]
    dn = None
    for at in range(3):
        for side, ref in enumerate((first_ref, out_ref)):
            cols = slice((2 * at + side) * width, (2 * at + side + 1) * width)
            term = mm_nt(ref[0, :, at * width : (at + 1) * width], wsi[:, cols])
            dn = term if dn is None else dn + term
    xhat, inv = unit(x_ref[0].astype(F32))
    dmod_ref[0, 0:1] = down(dn)
    dmod_ref[0, 1:2] = down(dn * xhat)
    grad_ref[0] = g_ref[0] + unit_back(dn, xhat, inv, mod_ref[0, 1:2])


def heads_backward(qkv1, da1, side, rest=None):
    frames, patches, width = da1.shape
    part = width // 2
    column = lambda at: pl.BlockSpec((1, patches, part), lambda i: (i, 0, at))
    block = lambda n: per_first((patches, n))
    tokens = frames * patches
    in_specs = [column(side), column(2 + side), column(4 + side), column(side)]
    operands = [qkv1, qkv1, qkv1, da1]
    out_specs = [block(3 * part), pl.BlockSpec((1, 3 * part), lambda i: (0, 0))]
    out_shape = [
        jax.ShapeDtypeStruct((frames, patches, 3 * part), BF16),
        jax.ShapeDtypeStruct((1, 3 * part), F32),
    ]
    if rest is not None:
        first, g1, x, mod, wsi = rest
        in_specs += [block(3 * part), block(width), block(width), per_first(mod.shape[1:]),
                     fixed(wsi.shape)]
        operands += [first, g1, x, mod, wsi]
        out_specs += [block(width), per_first((2, width))]
        out_shape += [
            jax.ShapeDtypeStruct((frames, patches, width), F32),
            jax.ShapeDtypeStruct((frames, 2, width), F32),
        ]
    return pl.pallas_call(
        first_heads_kernel if rest is None else last_heads_kernel,
        grid=(frames,),
        in_specs=in_specs,
        out_specs=out_specs,
        out_shape=out_shape,
        name="first_heads_backward" if rest is None else "last_heads_backward",
        **params(2 * tokens * width * (5 * patches + (0 if rest is None else 3 * width)),
                 16e6, tokens * patches * HEADS // 2),
    )(*operands)


def outer_kernel(*refs, jobs, order):
    out_ref = refs[-1]
    parts = out_ref.shape[1]
    groups = len(order)
    top = 0
    turned = {}
    for terms in jobs:
        total = None
        for left, right in terms:
            if left not in turned:
                turned[left] = refs[left][...].T
            term = mm(turned[left], refs[right][...])
            total = term if total is None else total + term
        rows = total.shape[0] // (groups * parts)
        width = out_ref.shape[3]
        for tile in range(total.shape[1] // width):
            for f in range(parts):
                for d in range(groups):
                    row = (f * groups + d) * rows
                    out_ref[order[d], f, top : top + rows] = total[
                        row : row + rows, tile * width : (tile + 1) * width
                    ].astype(BF16)
            top += rows


def outer_pieces(jobs, width, groups, parts, order, total_rows=None, into=None):
    shaped = {}

    def flat(a):
        return shaped.setdefault(id(a), a.reshape(-1, a.shape[-1]))

    jobs = [[(flat(left), flat(right), *tiles) for left, right, *tiles in job] for job in jobs]
    depth = jobs[0][0][0].shape[1]
    rows = depth // (groups * parts)
    height = sum(job[0][3] for job in jobs) * rows
    total_rows = total_rows or height
    if rows % 8:
        pieces = [] if into is None else [into[:, :, : total_rows - height]]
        for job in jobs:
            for tile in range(job[0][3]):
                cut = lambda r, t: r[:, (t + tile) * width : (t + tile + 1) * width]
                total = sum(mm_tn(l, cut(r, t)) for l, r, t, _ in job)
                total = total.astype(BF16).reshape(parts, groups, rows, width).swapaxes(0, 1)
                pieces.append(jnp.stack([total[order.index(d)] for d in range(groups)]))
        whole = jnp.concatenate(pieces, axis=2)
        return jnp.pad(whole, ((0, 0), (0, 0), (0, total_rows - whole.shape[2]), (0, 0)))
    step = 1
    while (step * depth // parts) % 128:
        step *= 2
    specs, operands, flops, known, terms = [], [], 0, {}, []

    def operand(array, spec, key):
        if key not in known:
            known[key] = len(operands)
            operands.append(array)
            specs.append(spec)
        return known[key]

    for job in jobs:
        pairs = []
        for left, right, tile, tiles in job:
            tokens = left.shape[0]
            spec = pl.BlockSpec((tokens, step * depth // parts), lambda i: (0, i))
            first = operand(left, spec, (id(left), None))
            spec = pl.BlockSpec(
                (tokens, tiles * width),
                lambda i, at=tile // tiles: (0, at),
                pipeline_mode=pl.Buffered(1),
            )
            pairs.append((first, operand(right, spec, (id(right), tile, tiles))))
            flops += 2 * tokens * depth * width * tiles
        terms.append(tuple(pairs))
    place = 0
    aliases = {}
    if into is not None:
        place = total_rows // height - 1
        aliases = {len(operands): 0}
        specs.append(pl.BlockSpec(memory_space=pl.ANY))
        operands.append(into)
    return pl.pallas_call(
        functools.partial(outer_kernel, jobs=tuple(terms), order=tuple(order)),
        grid=(parts // step,),
        in_specs=specs,
        out_specs=pl.BlockSpec((groups, step, height, width), lambda i: (0, i, place, 0)),
        out_shape=jax.ShapeDtypeStruct((groups, parts, total_rows, width), BF16),
        input_output_aliases=aliases,
        name="outer_pieces",
        **params(flops, 12e6),
    )(*operands)


def own_part(vector):
    size = vector.shape[0] // lax.axis_size("frame")
    return lax.dynamic_slice_in_dim(vector, lax.axis_index("frame") * size, size)


def stacked(block, width):
    count = block.shape[-1] // width
    return jnp.concatenate(
        [block[..., k * width : (k + 1) * width] for k in range(count)], axis=-2
    )


def unstacked(block, count):
    rows = block.shape[-2] // count
    return jnp.concatenate(
        [block[..., k * rows : (k + 1) * rows, :] for k in range(count)], axis=-1
    )


def line_gathered(mine):
    parts = lax.axis_size("frame")
    copies = jnp.broadcast_to(mine[None], (parts,) + mine.shape)
    return lax.all_to_all(copies, "frame", split_axis=0, concat_axis=0)


def line_swapped(pieces):
    parts = lax.axis_size("frame")
    place = lax.axis_index("frame")
    pick = lambda at: lax.dynamic_index_in_dim(pieces, (place + at) % parts, keepdims=False)
    seen = [pick(0)]
    for far in range(1, parts):
        pairs = [(i, (i + far) % parts) for i in range(parts)]
        seen.append(lax.ppermute(pick(far), "frame", pairs))
    seen = jnp.stack(seen)
    return jnp.stack(
        [
            lax.dynamic_index_in_dim(seen, (place - source) % parts, keepdims=False)
            for source in range(parts)
        ]
    )


def line_rotated(mine):
    parts = lax.axis_size("frame")
    place = lax.axis_index("frame")
    seen = [mine]
    for far in range(1, parts):
        seen.append(lax.ppermute(mine, "frame", [(i, (i + far) % parts) for i in range(parts)]))
    seen = jnp.stack(seen)
    return jnp.stack(
        [
            lax.dynamic_index_in_dim(seen, (place - source) % parts, keepdims=False)
            for source in range(parts)
        ]
    )


def packed(shards):
    groups = lax.axis_size("dp")
    width = min(shard.shape[1] for shard in shards)
    pieces = []
    for shard in shards:
        rows = shard.shape[0] // groups
        piece = lax.dynamic_slice_in_dim(shard, lax.axis_index("dp") * rows, rows)
        pieces.append(stacked(piece, width))
    return jnp.concatenate(pieces, axis=0)


def unpacked(whole, shards):
    groups, parts = lax.axis_size("dp"), lax.axis_size("frame")
    width = whole.shape[-1]
    results, at = [], 0
    for shard in shards:
        stacks = shard.shape[1] // width
        height = stacks * shard.shape[0] // groups
        part = unstacked(whole[:, :, at : at + height], stacks)
        results.append(jnp.swapaxes(part, 0, 1).reshape(parts * shard.shape[0], shard.shape[1]))
        at += height
    return results


def gathered_small(biases, condition):
    parts = lax.axis_size("frame")
    flat = jnp.concatenate(biases + [condition.reshape(-1)])
    rows = line_gathered(flat)
    results, at = [], 0
    for bias in biases:
        results.append(rows[:, at : at + bias.shape[0]].reshape(-1))
        at += bias.shape[0]
    results.append(rows[:, at:].reshape(parts * condition.shape[0], condition.shape[1]))
    return results


def modulated(act_group, matrix, frames):
    parts = lax.axis_size("frame")
    rows, width = matrix.shape
    columns = lax.dynamic_slice_in_dim(act_group, lax.axis_index("frame") * rows, rows, axis=1)
    return mm(columns, matrix).reshape(parts, frames, width)


def passed_along(x, axis, by):
    peers = lax.axis_size(axis)
    pairs = [(i, i + by) for i in range(peers) if 0 <= i + by < peers]
    return lax.ppermute(x, axis, pairs)


def own_bit(bit):
    return (lax.axis_index("dp") >> bit) & 1


def swapped(x, bit):
    return lax.ppermute(x, "dp", [(i, i ^ (1 << bit)) for i in range(lax.axis_size("dp"))])


def added(a, b):
    return (a.astype(F32) + b.astype(F32)).astype(BF16)


def halved(blocks, bit):
    half = blocks.shape[0] // 2
    mine = own_bit(bit)
    sent = lax.dynamic_slice_in_dim(blocks, (1 - mine) * half, half)
    kept = lax.dynamic_slice_in_dim(blocks, mine * half, half)
    return added(kept, swapped(sent, bit))


def summed(pieces):
    return jnp.sum(pieces.astype(F32), axis=0).astype(BF16)


def core_order():
    groups = lax.axis_size("dp")
    return [(d & 1) * (groups // 2) + (d >> 1) for d in range(groups)]


def plane_summed(blocks):
    groups = lax.axis_size("dp")
    same = [list(range(core, groups, 2)) for core in range(2)]
    return summed(
        lax.all_to_all(blocks, "dp", split_axis=0, concat_axis=0, axis_index_groups=same)
    )


def dp_summed_start(blocks):
    return lax.all_to_all(blocks, "dp", split_axis=0, concat_axis=0)


def line_summed(blocks):
    return summed(lax.all_to_all(blocks, "frame", split_axis=0, concat_axis=0))


def plane_gathered(piece):
    groups = lax.axis_size("dp")
    copies = jnp.broadcast_to(piece[None], (groups,) + piece.shape)
    return lax.all_to_all(copies, "dp", split_axis=0, concat_axis=0)


def per_device(
    frames_in,
    condition,
    segments,
    spatial_in,
    spatial_in_bias,
    spatial_out,
    spatial_out_bias,
    temporal_in,
    temporal_in_bias,
    temporal_out,
    temporal_out_bias,
    expand_weight,
    expand_bias,
    shrink_weight,
    shrink_bias,
    modulate_weight,
    modulate_bias,
    cotangent,
):
    groups, parts = lax.axis_size("dp"), lax.axis_size("frame")
    place = lax.axis_index("frame")
    frames, patches, width = frames_in.shape
    space, time = [spatial_in, spatial_out], [temporal_in, temporal_out]
    dense = [expand_weight, shrink_weight]
    biases = [
        spatial_in_bias,
        spatial_out_bias,
        temporal_in_bias,
        temporal_out_bias,
        expand_bias,
        shrink_bias,
        modulate_bias,
    ]
    space_column = line_gathered(packed(space))
    condition_held, space_column = lax.optimization_barrier((condition, space_column))
    *full_biases, cond_group = gathered_small(biases, condition_held)
    full_spatial_in, full_spatial_out = unpacked(lax.all_gather(space_column, "dp", axis=0), space)
    sinb, soutb, tinb, toutb, expb, shrb, modb = [b.astype(F32)[None, :] for b in full_biases]
    act_group = jax.nn.silu(cond_group.astype(F32)).astype(BF16)
    partial = modulated(act_group, modulate_weight, frames)
    partial = lax.all_to_all(partial, "frame", split_axis=0, concat_axis=0)
    time_piece, partial = lax.optimization_barrier((packed(time), partial))
    mod = (jnp.sum(partial, axis=0) + modb).reshape(frames, 9, width)
    time_column = line_gathered(time_piece)
    full_temporal_in, full_temporal_out = unpacked(lax.all_gather(time_column, "dp", axis=0), time)
    dense_piece, time_column, mod = lax.optimization_barrier((packed(dense), time_column, mod))
    dense_column = line_rotated(dense_piece)
    full_expand, full_shrink = unpacked(lax.all_gather(dense_column, "dp", axis=0), dense)
    n1, qkv1, attn1 = spatial_forward(frames_in, mod, full_spatial_in, sinb)
    branch1, after1, n2 = project_forward(frames_in, attn1, mod, full_spatial_out, soutb)
    near_left = passed_along(n2[frames - WINDOW :], "frame", 1)
    near_right = passed_along(n2[:WINDOW], "frame", -1)
    qkv2 = (mm(n2.reshape(-1, width), full_temporal_in) + tinb).astype(BF16)
    qkv2 = qkv2.reshape(frames, patches, 3 * width)
    seg_row = segments[0]
    seg_pad = jnp.pad(seg_row, (WINDOW, WINDOW), constant_values=-1)
    nearby = lax.dynamic_slice_in_dim(seg_pad, place * frames, frames + 2 * WINDOW)
    own_seg = nearby[WINDOW : WINDOW + frames]
    allowed = jnp.stack([nearby[o : o + frames] == own_seg for o in range(SPAN)]).astype(jnp.int32)
    probs, attn2, branch2, after2, left, right = temporal_forward(
        allowed, qkv2, near_left, near_right, after1, mod, full_temporal_in, tinb,
        full_temporal_out, toutb,
    )
    frames_out, g2, n3, act, dpre, db3, dmod3, sum_exp, sum_shr = feed_forward(
        after2, cotangent, mod, full_expand, expb, full_shrink, shrb
    )
    plain = list(range(groups))
    hidden = dpre.shape[-1]
    high = 2 * (hidden // width) * modulate_weight.shape[0] // groups
    feed = outer_pieces(
        [[(n3, dpre, 0, hidden // width)]], width, groups, parts, plain, total_rows=high
    )
    feed = outer_pieces(
        [[(act, db3, 0, 1)]], width, groups, parts, plain, total_rows=high, into=feed
    )
    feed = lax.psum_scatter(feed.reshape(-1, width), "dp", scatter_dimension=0, tiled=True)
    db2, dqkv2, dleft, dright, nleft, nright, dgate2, sum_tout, sum_tin = temporal_backward(
        g2, branch2, mod, full_temporal_out, full_temporal_in, qkv2, left, right, probs
    )
    from_right = passed_along(nleft, "frame", -1)
    from_left = passed_along(nright, "frame", 1)
    order = core_order()
    halo = lambda t: [(near_left, dleft, t, 1), (near_right, dright, t, 1)]
    temporal = outer_pieces(
        [
            [(n2, dqkv2, 0, 1)],
            [(n2, dqkv2, 1, 1)] + halo(0),
            [(n2, dqkv2, 2, 1)] + halo(1),
            [(attn2, db2, 0, 1)],
        ],
        width, groups, parts, order,
    )
    temporal = halved(temporal, 0)
    dn2 = mm_nt(dqkv2.reshape(-1, 3 * width), full_temporal_in).reshape(frames, patches, width)
    dn2, temporal = lax.optimization_barrier((dn2, temporal))
    temporal = plane_summed(temporal)
    g1, db1, da1, dmod1, sum_sout = project_backward(
        dn2, from_left, from_right, after1, g2, branch1, mod, full_spatial_out
    )
    cond_float = condition.astype(F32)
    own_act = jax.nn.silu(cond_float).astype(BF16)
    early_mod = jnp.concatenate([dmod1, dgate2[:, None], dmod3], axis=1)
    early_mod = early_mod.reshape(frames, 7 * width).astype(BF16)
    early_sums = [s[0] for s in (sum_sout, sum_tin, sum_tout, sum_exp, sum_shr)]
    early_rows = jnp.concatenate(early_sums).astype(BF16).reshape(frames, -1)
    early = line_rotated(jnp.concatenate([own_act, early_mod, early_rows], axis=1))
    dheads, sum_first = heads_backward(qkv1, da1, 0)
    early_rows = jnp.sum(early[:, :, 8 * width :].astype(F32), axis=0).astype(BF16)
    early = early[:, :, : 8 * width].reshape(parts * frames, 8 * width)
    early_group = early[:, width:]
    early = jnp.concatenate([early, early_rows.reshape(parts * frames, -1)], axis=1)
    dheads, temporal, feed, early = lax.optimization_barrier((dheads, temporal, feed, early))
    early = lax.all_gather(early, "dp", axis=0, tiled=True)
    feed = jnp.concatenate([feed.reshape(parts, high, width), temporal], axis=1)
    total_high = feed.shape[1]
    feed = lax.psum_scatter(
        feed.reshape(-1, width), "frame", scatter_dimension=0, tiled=True
    )
    part = width // 2
    first = outer_pieces(
        [[(n1, dheads, 0, 3)], [(attn1, db1, 0, 2)]], part, groups, parts, plain
    )
    dheads, first = lax.optimization_barrier((dheads, first))
    first = dp_summed_start(first)
    dtail, sum_last, grad_frames, dmod0 = heads_backward(
        qkv1, da1, 1, (dheads, g1, frames_in, mod, full_spatial_in)
    )
    dtail, dmod0, sum_first, sum_last, feed = lax.optimization_barrier(
        (dtail, dmod0, sum_first, sum_last, feed)
    )
    feed = lax.all_gather(feed, "dp", axis=0, tiled=True).reshape(groups, total_high, width)
    sums = [s[0].reshape(3, part) for s in (sum_first, sum_last)]
    sum_sin = jnp.stack(sums, axis=1).reshape(1, 3 * width)
    late_mod = dmod0.reshape(frames, 2 * width).astype(BF16)
    late_rows = sum_sin.astype(BF16).reshape(frames, -1)
    late = line_rotated(jnp.concatenate([late_mod, late_rows], axis=1))
    last = outer_pieces([[(n1, dtail, 0, 3)]], part, groups, parts, order)
    last = halved(last, 0)
    first = summed(first)
    last, first, late = lax.optimization_barrier((last, first, late))
    last = plane_summed(last)
    late_rows = jnp.sum(late[:, :, 2 * width :].astype(F32), axis=0).astype(BF16)
    late_group = late[:, :, : 2 * width].reshape(parts * frames, 2 * width)
    both = line_summed(jnp.concatenate([first, last], axis=1))
    sizes = [first.shape[1], last.shape[1], 4 * parts * frames, 3 * width // part]
    both = plane_gathered(
        jnp.concatenate(
            [both, late_group.reshape(-1, part), late_rows.reshape(-1, part)], axis=0
        )
    )
    cuts = [sum(sizes[: at + 1]) for at in range(3)]
    first, last, late, late_rows = jnp.split(both, cuts, axis=1)
    blocks = lambda whole, count: jnp.split(whole, count, axis=1)
    flat = lambda pieces: jnp.concatenate(
        [p.reshape(-1, p.shape[-1]) for p in pieces], axis=1
    ).astype(F32)
    feed, temporal = feed[:, :high], feed[:, high:]
    *wide, narrow = blocks(temporal, 4)
    grad_temporal_in_sum, grad_temporal_out_sum = flat(wide), flat([narrow])
    starts, ends = blocks(first, 5), blocks(last, 3)
    grad_spatial_in_sum = flat([p for pair in zip(starts[:3], ends) for p in pair])
    grad_spatial_out_sum = flat(starts[3:])
    wide = unstacked(feed[:, : high // 2], hidden // width)
    grad_expand_sum = wide.reshape(-1, hidden).astype(F32)
    grad_shrink_sum = feed[:, high // 2 :].reshape(-1, width).astype(F32)
    rows = modulate_weight.shape[0]
    own_columns = lax.dynamic_slice_in_dim(early[:, :width], place * rows, rows, axis=1)
    late_all = late.reshape(groups * parts * frames, 2 * width)
    dmod_all = jnp.concatenate([late_all, early[:, width : 8 * width]], axis=1)
    grad_modulate_weight = mm_tn(own_columns, dmod_all)
    grad_modulate_bias = own_part(jnp.sum(dmod_all.astype(F32), axis=0))
    dact_group = mm_nt(late_group, modulate_weight[:, : 2 * width])
    dact_group = dact_group + mm_nt(early_group, modulate_weight[:, 2 * width :])
    pieces_act = line_swapped(dact_group.reshape(parts, frames, rows))
    dcond_act = jnp.swapaxes(pieces_act, 0, 1).reshape(frames, parts * rows)
    grad_condition = jax.vjp(jax.nn.silu, cond_float)[1](dcond_act)[0]
    early_rows = early[:, 8 * width :].astype(F32).reshape(groups, parts * frames, -1)
    early_rows = jnp.sum(early_rows, axis=0).reshape(-1)
    late_rows = jnp.sum(late_rows.astype(F32), axis=0).reshape(-1)
    bias_sums, at = [own_part(late_rows)], 0
    for grad in early_sums:
        bias_sums.append(own_part(early_rows[at : at + grad.shape[0]]))
        at += grad.shape[0]
    return (
        frames_out,
        grad_frames,
        grad_condition,
        grad_spatial_in_sum,
        bias_sums[0],
        grad_spatial_out_sum,
        bias_sums[1],
        grad_temporal_in_sum,
        bias_sums[2],
        grad_temporal_out_sum,
        bias_sums[3],
        grad_expand_sum,
        bias_sums[4],
        grad_shrink_sum,
        bias_sums[5],
        grad_modulate_weight,
        grad_modulate_bias,
    )


def solution(mesh):
    in_specs = (
        P(("dp", "frame"), None, None),
        P(("dp", "frame"), None),
        P("dp", None),
        P("frame", None),
        P("frame"),
        P("frame", None),
        P("frame"),
        P("frame", None),
        P("frame"),
        P("frame", None),
        P("frame"),
        P("frame", None),
        P("frame"),
        P("frame", None),
        P("frame"),
        P("frame", None),
        P("frame"),
        P(("dp", "frame"), None, None),
    )
    out_specs = (
        P(("dp", "frame"), None, None),
        P(("dp", "frame"), None, None),
        P(("dp", "frame"), None),
        P("frame", None),
        P("frame"),
        P("frame", None),
        P("frame"),
        P("frame", None),
        P("frame"),
        P("frame", None),
        P("frame"),
        P("frame", None),
        P("frame"),
        P("frame", None),
        P("frame"),
        P("frame", None),
        P("frame"),
    )

    return jax.shard_map(
        per_device, mesh=mesh, in_specs=in_specs, out_specs=out_specs, check_vma=False
    )
```

time: 698 us -> 543 us (0.78)
  waiting for transfers between devices: 250 us -> 92.9 us
  blocking collectives: 113 us -> 56.5 us
  starting transfers between devices: 19.5 us -> 52.2 us
  matrix products: 5.57 us -> 22.8 us
    reduce_scatter x4 -> x2, waiting for transfers between devices: 121 us -> 0.02 us  [the longest x1 0.02 us: per_device(): lax.psum_scatter(feed.reshape(-1, width), 'dp', scatter_dimension=0, tile...]
    all_gather x4 -> x0, blocking collectives: 71.8 us -> none  [the longest x2 43.6 us: gathered(): column = lax.all_gather(mine, 'frame', axis=0)]
    all_gather x7 -> x5, waiting for transfers between devices: 67.8 us -> 0.07 us  [the longest x1 0.02 us: per_device(): lax.all_gather(time_column, 'dp', axis=0)]
    all_to_all x0 -> x3, blocking collectives: none -> 56.5 us  [the longest x2 39.6 us: line_gathered(): return lax.all_to_all(copies, 'frame', split_axis=0, concat_axis=0)]
    all_to_all x2 -> x6, waiting for transfers between devices: 7.11 us -> 55.3 us  [the longest x1 12.7 us: line_summed(): return summed(lax.all_to_all(blocks, 'frame', split_axis=0, concat_axis=0))]
    psum x1 -> x0, blocking collectives: 41.3 us -> none  [per_device(): together = lax.psum(jnp.concatenate(bias_grads), ('dp', 'frame'))]
    ppermute x4, waiting for transfers between devices: 53.5 us -> 16.6 us  [passed_along(): return lax.ppermute(x, axis, pairs)]
    ppermute x0 -> x14, waiting for transfers between devices: none -> 20.3 us  [the longest x9 17.9 us: line_rotated(): lax.ppermute(mine, 'frame', [(i, (i + far) % parts) for i in range(parts)])]
  transfers between devices with their start and end apart: 17 -> 31, of which waited for: 12 -> 13; matrix products, arithmetic and copies ran while one was open for 9% -> 16% of each run, Pallas kernels for 22% -> 29%
where the time goes in v3:
time: 543 us; the launch traced here: 535 us
  Pallas kernels  205 us (38%)
  waiting for transfers between devices  92.9 us (17%)
  local copies, waits for them, and re-layouts  59.8 us (11%)
  blocking collectives  56.5 us (10%)
  starting transfers between devices  52.2 us (10%)
  other arithmetic  29.5 us (5%)
  matrix products  22.8 us (4%)
  between operations  15.6 us (3%)
    pallas_call x5, Pallas kernels, outer_pieces(): pl.pallas_call(functools.partial(outer_kernel, jobs=tuple(terms), order=t...  45.5 us
    pallas_call x2, Pallas kernels, heads_backward(): pl.pallas_call(first_heads_kernel if rest is None else last_heads_kernel,...  42 us
    all_to_all x2, blocking collectives, line_gathered(): return lax.all_to_all(copies, 'frame', split_axis=0, concat_axis=0)  39.6 us
    pallas_call x1, Pallas kernels, feed_forward(): pl.pallas_call(feed_kernel, grid=(frames,), in_specs=[block(width), block...  31 us
    pallas_call x1, Pallas kernels, temporal_backward(): pl.pallas_call(temporal_back_kernel, grid=(patches // tile,), in_specs=[s...  26.1 us
    pallas_call x1, Pallas kernels, temporal_forward(): pl.pallas_call(temporal_kernel, grid=(patches // tile,), in_specs=[pl.Blo...  24.1 us
    pallas_call x1, Pallas kernels, spatial_forward(): pl.pallas_call(spatial_kernel, grid=(frames,), in_specs=[block(width), pe...  18.9 us
    ppermute x9, waiting for transfers between devices, line_rotated(): lax.ppermute(mine, 'frame', [(i, (i + far) % parts) for i in range(parts)])  17.9 us
  transfers between devices with their start and end apart: 31, of which 13 were waited for; matrix products, arithmetic and copies ran while one was open for 16% of the time, Pallas kernels for 29%

profile of v3, /device:TPU:0, one launch (start us, length us, event | category | flops | bytes accessed | tf_op | source)
XLA Modules:
  0.0 534.6 jit_solution(563157909652714651)
XLA Ops:
  10.3 22.3 %all_to_all.49 = bf16[4,96,768]{2,1,0:T(8,128)(2,1)} all-to-all(bf16[4,96,768]{2,1,0:T(8,128)(2,1)S(1)} %broadcast_in_dim.11), channel_id=1, replica_groups=mesh['dp'=8,'frame'=4] {'frame'}, dimensions={0} | all-to-all | bytes 1179648 | tf_op jit(solution)/shard_map/all_to_all | solution.py:666
  35.2 3.3 all-to-all-start.1
  38.5 5.7 %all-to-all-done.1 = bf16[4,2,3648]{2,1,0:T(2,128)(2,1)S(1)} async-done(((bf16[4,2,3648]{2,1,0:T(2,128)(2,1)}), bf16[4,2,3648]{2,1,0:T(2,128)(2,1)S(1)}, u32[]{:S(2)}, u32[]{:S(2)}) %all-to-all-start.1) | async-done | bytes 58400 | tf_op jit(solution)/shard_map/all_to_all | solution.py:666
  47.1 3.6 all-to-all-start.2
  51.6 10.2 %all-to-all-done.2 = f32[4,4,6912]{2,1,0:T(4,128)S(1)} async-done(((f32[4,4,6912]{2,1,0:T(4,128)}), f32[4,4,6912]{2,1,0:T(4,128)S(1)}, u32[]{:S(2)}, u32[]{:S(2)}) %all-to-all-start.2) | async-done | bytes 442400 | tf_op jit(solution)/shard_map/all_to_all | solution.py:842
  61.8 17.4 %all_to_all.50 = bf16[4,96,768]{2,1,0:T(8,128)(2,1)} all-to-all(bf16[4,96,768]{2,1,0:T(8,128)(2,1)S(1)} %broadcast_in_dim.13), channel_id=1, replica_groups=mesh['dp'=8,'frame'=4] {'frame'}, dimensions={0} | all-to-all | bytes 1179648 | tf_op jit(solution)/shard_map/all_to_all | solution.py:666
  87.4 7.9 %collective-permute-done.2 = bf16[192,768]{1,0:T(8,128)(2,1)S(1)} collective-permute-done((bf16[192,768]{1,0:T(8,128)(2,1)S(1)}, bf16[192,768]{1,0:T(8,128)(2,1)S(1)}, u32[]{:S(2)}, u32[]{:S(2)}) %collective-permute-start.2) | collective-permute-done | bytes 294944 | tf_op jit(solution)/shard_map/ppermute | solution.py:691
  95.4 9.9 %collective-permute-done.3 = bf16[192,768]{1,0:T(8,128)(2,1)S(1)} collective-permute-done((bf16[192,768]{1,0:T(8,128)(2,1)S(1)}, bf16[192,768]{1,0:T(8,128)(2,1)S(1)}, u32[]{:S(2)}, u32[]{:S(2)}) %collective-permute-start.3) | collective-permute-done | bytes 294944 | tf_op jit(solution)/shard_map/ppermute | solution.py:691
  113.3 2.7 slice_bitcast_fusion.1
  119.5 18.9 %spatial_forward.1 = (bf16[4,256,768]{2,1,0:T(8,128)(2,1)}, bf16[4,256,2304]{2,1,0:T(8,128)(2,1)}, bf16[4,256,768]{2,1,0:T(8,128)(2,1)}) custom-call(bf16[4,256,768]{2,1,0:T(8,128)(2,1)} %x_ref.5, f32[4,9,768]{2,1,0:T(8,128)} %broadcast_add_fusion.mod_ref, bf16[768,2304]{1,0:T(8,128)(2,1)} %bitcast.127, f32[1,2304]{1,0:T(1,128)} %reshape.418.bsi), custom_call_target="tpu_custom_call" | custom-call | flops 5234491392 | bytes 12000000 | tf_op jit(solution)/shard_map/spatial_forward/pallas_call | solution.py:105
  138.5 6.8 %project_forward.1 = (f32[4,256,768]{2,1,0:T(8,128)}, f32[4,256,768]{2,1,0:T(8,128)}, bf16[4,256,768]{2,1,0:T(8,128)(2,1)}) custom-call(bf16[4,256,768]{2,1,0:T(8,128)(2,1)} %x_ref.5, bf16[4,256,768]{2,1,0:T(8,128)(2,1)} %get-tuple-element.85.attn_ref, f32[4,9,768]{2,1,0:T(8,128)} %broadcast_add_fusion.mod_ref, bf16[768,768]{1,0:T(8,128)(2,1)} %bitcast.133, ...), custom_call_target="tpu_custom_call" | custom-call | flops 1207959552 | bytes 13000000 | tf_op jit(solution)/shard_map/project_forward/pallas_call | solution.py:129
  146.7 9.2 %collective-permute-start = (bf16[2,256,768]{2,1,0:T(8,128)(2,1)S(1)}, bf16[2,256,768]{2,1,0:T(8,128)(2,1)}, u32[]{:S(2)}, u32[]{:S(2)}) collective-permute-start(bf16[2,256,768]{2,1,0:T(8,128)(2,1)S(1)} %get-tuple-element.172), channel_id=1, source_target_pairs={{0,1},{1,2},{2,3},{4,5},{5,6},{6,7},{8,9},{9,10},{10,11},{12,13},{... | collective-permute-start | bytes 2359304 | tf_op jit(solution)/shard_map/ppermute | solution.py:747
  157.4 2.8 slice_bitcast_fusion
  163.3 5.5 %add_convert_fusion = bf16[1024,2304]{1,0:T(8,128)(2,1)} fusion(bf16[1024,768]{1,0:T(8,128)(2,1)S(1)} %bitcast.140, bf16[768,2304]{1,0:T(8,128)(2,1)S(1)} %bitcast.129, f32[2304]{0:T(1024)S(1)} %reshape.420), kind=kOutput, calls=%fused_computation | convolution fusion | flops 3628597248 | bytes 9839616 | tf_op jit(solution)/shard_map/dot_general | solution.py:22
  171.1 5.1 collective-permute-done.1.nr_ref
  176.3 24.1 %temporal_forward.1 = (f32[4,5,256,128]{3,2,1,0:T(8,128)}, bf16[4,256,768]{2,1,0:T(8,128)(2,1)}, f32[4,256,768]{2,1,0:T(8,128)}, f32[4,256,768]{2,1,0:T(8,128)},...) custom-call(s32[5,4]{1,0:T(8,128)} %convert_element_type.211.allowed, bf16[4,256,2304]{2,1,0:T(8,128)(2,1)} %bitcast.149, ...), custom_call_target="tpu_custom_call" | custom-call | flops 4353687552 | bytes 22000000 | tf_op jit(solution)/shard_map/temporal_forward/pallas_call | solution.py:219
  200.4 2.8 fusion.30
  203.2 2.3 copy-done.3
  206.6 2.5 copy.97
  209.1 2.5 copy.96
  211.6 31.0 %feed_forward.1 = (bf16[4,256,768]{2,1,0:T(8,128)(2,1)}, f32[4,256,768]{2,1,0:T(8,128)}, bf16[4,256,768]{2,1,0:T(8,128)(2,1)}, bf16[4,256,3072]{2,1,0:T(8,128)(2...) custom-call(f32[4,256,768]{2,1,0:T(8,128)} %get-tuple-element.88.aft, ...), custom_call_target="tpu_custom_call" | custom-call | flops 19327352832 | bytes 32000000 | tf_op jit(solution)/shard_map/feed_forward/pallas_call | solution.py:297
  242.7 9.8 %outer_pieces.6.refs_2_ = bf16[8,4,192,768]{3,2,1,0:T(8,128)(2,1)} custom-call(bf16[1024,768]{1,0:T(8,128)(2,1)} %bitcast.202, bf16[1024,3072]{1,0:T(8,128)(2,1)} %bitcast.199), custom_call_target="tpu_custom_call" | custom-call | flops 4831838208 | bytes 12000000 | tf_op jit(solution)/shard_map/outer_pieces/pallas_call | solution.py:632
  252.5 9.2 %outer_pieces.7 = bf16[8,4,192,768]{3,2,1,0:T(8,128)(2,1)} custom-call(bf16[1024,3072]{1,0:T(8,128)(2,1)} %bitcast.138, bf16[1024,768]{1,0:T(8,128)(2,1)} %bitcast.156, bf16[8,4,192,768]{3,2,1,0:T(8,128)(2,1)} %outer_pieces.6.refs_2_), custom_call_target="tpu_custom_call", output_to_operand_aliasing={{}: (2, {})} | custom-call | flops 4831838208 | bytes 12000000 | tf_op jit(solution)/shard_map/outer_pieces/pallas_call | solution.py:632
  261.7 26.1 %temporal_backward.1 = (bf16[4,256,768]{2,1,0:T(8,128)(2,1)}, bf16[4,256,2304]{2,1,0:T(8,128)(2,1)}, bf16[2,256,1536]{2,1,0:T(8,128)(2,1)}, bf16[2,256,1536]{2,1...) custom-call(f32[4,256,768]{2,1,0:T(8,128)} %get-tuple-element.92.g_r, ...), custom_call_target="tpu_custom_call" | custom-call | flops 5140119552 | bytes 36000000 | tf_op jit(solution)/shard_map/temporal_backward/pallas_call | solution.py:394
  287.8 13.7 %outer_pieces.5 = bf16[8,4,96,768]{3,2,1,0:T(8,128)(2,1)} custom-call(bf16[1024,768]{1,0:T(8,128)(2,1)} %bitcast.139, bf16[1024,2304]{1,0:T(8,128)(2,1)} %bitcast.121, bf16[1024,2304]{1,0:T(8,128)(2,1)} %bitcast.122, bf16[512,768]{1,0:T(8,128)(2,1)} %bitcast.28.refs_3_, bf16[512,1536]{1,0:T(8,128)(2,1)} %bitcast.141, bf16[512,768]{1,0:T(8,128)(2,1)} %bitcast.30.refs_5_, ...), custom_call_target="tpu_custom_call" | custom-call | flops 7247757312 | bytes 12000000 | tf_op jit(solution)/shard_map/outer_pieces/pallas_call | solution.py:632
  301.5 3.5 constant_dynamic-slice_fusion.17
  308.7 9.1 %fusion.35.dn_ref = f32[4,256,768]{2,1,0:T(8,128)} fusion(bf16[4,256,2304]{2,1,0:T(8,128)(2,1)} %get-tuple-element.97, bf16[768,2304,1]{1,0,2:T(8,128)(2,1)} %bitcast.132), kind=kOutput, calls=%fused_computation.144 | convolution fusion | flops 3623878656 | bytes 11403264 | tf_op jit(solution)/shard_map/dot_general | solution.py:26
  320.2 4.2 collective-permute-done.6.fl_ref
  324.4 5.0 collective-permute-done.7.fr_ref
  329.4 11.0 %project_backward.1 = (f32[4,256,768]{2,1,0:T(8,128)}, bf16[4,256,768]{2,1,0:T(8,128)(2,1)}, bf16[4,256,768]{2,1,0:T(8,128)(2,1)}, f32[4,3,768]{2,1,0:T(4,128)}, f32[1,768]{1,0:T(1,128)}) custom-call(f32[4,256,768]{2,1,0:T(8,128)} %fusion.35.dn_ref, bf16[2,256,768]{2,1,0:T(8,128)(2,1)} %collective-permute-done.6.fl_ref, ...), custom_call_target="tpu_custom_call" | custom-call | flops 1207959552 | bytes 22000000 | tf_op jit(solution)/shard_map/project_backward/pallas_call | solution.py:451
  343.4 3.7 collective-permute-start.10
  347.1 3.6 all-to-all-start.4
  350.8 16.1 %first_heads_backward.1 = (bf16[4,256,1152]{2,1,0:T(8,128)(2,1)}, f32[1,1152]{1,0:T(1,128)}) custom-call(bf16[4,256,2304]{2,1,0:T(8,128)(2,1)} %get-tuple-element.91.q_ref.k_ref.v_ref, bf16[4,256,2304]{2,1,0:T(8,128)(2,1)} %get-tuple-element.91.q_ref.k_ref.v_ref, bf16[4,256,2304]{2,1,0:T(8,128)(2,1)} %get-tuple-element.91.q_ref.k_ref.v_ref, ...), custom_call_target="tpu_custom_call" | custom-call | flops 2013265920 | bytes 16000000 | tf_op jit(solution)/shard_map/first_heads_backward/pallas_call | solution.py:541
  368.5 9.3 %all-to-all-done.4 = bf16[4,4,96,768]{3,2,1,0:T(8,128)(2,1)S(1)} async-done(((bf16[4,4,96,768]{3,2,1,0:T(8,128)(2,1)}), bf16[4,4,96,768]{3,2,1,0:T(8,128)(2,1)S(1)}, u32[]{:S(2)}, u32[]{:S(2)}) %all-to-all-start.4) | async-done | bytes 2359328 | tf_op jit(solution)/shard_map/all_to_all | solution.py:783
  378.5 2.6 pad_maximum_fusion.1
  381.1 7.5 %outer_pieces.8 = bf16[8,4,120,384]{3,2,1,0:T(8,128)(2,1)} custom-call(bf16[1024,768]{1,0:T(8,128)(2,1)} %bitcast.200, bf16[1024,1152]{1,0:T(8,128)(2,1)} %bitcast.155, bf16[1024,768]{1,0:T(8,128)(2,1)} %bitcast.157, bf16[1024,768]{1,0:T(8,128)(2,1)} %bitcast.197), custom_call_target="tpu_custom_call" | custom-call | flops 3019898880 | bytes 12000000 | tf_op jit(solution)/shard_map/outer_pieces/pallas_call | solution.py:632
  388.6 3.6 all-to-all-start.5
  392.9 25.9 %last_heads_backward.1 = (bf16[4,256,1152]{2,1,0:T(8,128)(2,1)}, f32[1,1152]{1,0:T(1,128)}, f32[4,256,768]{2,1,0:T(8,128)}, f32[4,2,768]{2,1,0:T(2,128)}) custom-call(bf16[4,256,2304]{2,1,0:T(8,128)(2,1)} %get-tuple-element.91.q_ref.k_ref.v_ref, bf16[4,256,2304]{2,1,0:T(8,128)(2,1)} %get-tuple-element.91.q_ref.k_ref.v_ref, ...), custom_call_target="tpu_custom_call" | custom-call | flops 5637144576 | bytes 16000000 | tf_op jit(solution)/shard_map/last_heads_backward/pallas_call | solution.py:541
  418.8 9.1 %all-to-all-done.5 = bf16[8,4,120,384]{3,2,1,0:T(8,128)(2,1)S(1)} async-done(((bf16[8,4,120,384]{3,2,1,0:T(8,128)(2,1)}), bf16[8,4,120,384]{3,2,1,0:T(8,128)(2,1)S(1)}, u32[]{:S(2)}, u32[]{:S(2)}) %all-to-all-start.5) | async-done | bytes 2949152 | tf_op jit(solution)/shard_map/all_to_all | solution.py:788
  431.3 2.8 collective-permute-start.14
  434.2 5.3 outer_pieces.9
  441.2 2.3 collective-permute-done.11
  443.8 16.9 %all_to_all.51 = bf16[4,4,72,384]{3,2,1,0:T(8,128)(2,1)S(1)} all-to-all(bf16[4,4,72,384]{3,2,1,0:T(8,128)(2,1)S(1)} %add_convert_fusion.2), channel_id=1, replica_groups={{0,8,16,24},{4,12,20,28},{1,9,17,25},{5,13,21,29},{2,10,18,26},{6,14,22..., dimensions={0} | all-to-all | bytes 1769472 | tf_op jit(solution)/shard_map/all_to_all | solution.py:783
  461.8 3.5 all-to-all-start.7
  466.6 12.7 %all-to-all-done.7 = bf16[4,192,384]{2,1,0:T(8,128)(2,1)S(1)} async-done(((bf16[4,192,384]{2,1,0:T(8,128)(2,1)}), bf16[4,192,384]{2,1,0:T(8,128)(2,1)S(1)}, u32[]{:S(2)}, u32[]{:S(2)}) %all-to-all-start.7) | async-done | bytes 589856 | tf_op jit(solution)/shard_map/all_to_all | solution.py:792
  480.7 3.6 all-to-all-start.8
  497.5 8.3 %all-to-all-done.8 = bf16[8,262,384]{2,1,0:T(8,128)(2,1)S(1)} async-done(((bf16[8,262,384]{2,1,0:T(8,128)(2,1)}), bf16[8,262,384]{2,1,0:T(8,128)(2,1)S(1)}, u32[]{:S(2)}, u32[]{:S(2)}) %all-to-all-start.8) | async-done | bytes 1609760 | tf_op jit(solution)/shard_map/all_to_all | solution.py:798
  515.3 3.3 fusion.2
  (271 shorter events, 90.5 us)
Async XLA Ops:
  7.2 43.6 %copy-start = (bf16[192,768]{1,0:T(8,128)(2,1)S(1)}, bf16[192,768]{1,0:T(8,128)(2,1)}, u32[]{:S(2)}) copy-start(bf16[192,768]{1,0:T(8,128)(2,1)} %param.27) | copy-start | bytes 884740
  7.2 25.4 %copy-start.10 = (bf16[4,768]{1,0:T(4,128)(2,1)S(1)}, bf16[4,768]{1,0:T(4,128)(2,1)}, u32[]{:S(2)}) copy-start(bf16[4,768]{1,0:T(4,128)(2,1)} %param.19) | copy-start | bytes 18436
  7.2 25.5 %copy-start.21 = (bf16[576]{0:T(1024)(128)(2,1)S(1)}, bf16[576]{0:T(1024)(128)(2,1)}, u32[]{:S(2)}) copy-start(bf16[576]{0:T(1024)(128)(2,1)} %param.22) | copy-start | bytes 3460
  7.2 25.5 %copy-start.24 = (bf16[192]{0:T(256)(128)(2,1)S(1)}, bf16[192]{0:T(256)(128)(2,1)}, u32[]{:S(2)}) copy-start(bf16[192]{0:T(256)(128)(2,1)} %param.24) | copy-start | bytes 1156
  7.2 25.5 %copy-start.22 = (bf16[576]{0:T(1024)(128)(2,1)S(1)}, bf16[576]{0:T(1024)(128)(2,1)}, u32[]{:S(2)}) copy-start(bf16[576]{0:T(1024)(128)(2,1)} %param.26) | copy-start | bytes 3460
  7.2 25.5 %copy-start.25 = (bf16[192]{0:T(256)(128)(2,1)S(1)}, bf16[192]{0:T(256)(128)(2,1)}, u32[]{:S(2)}) copy-start(bf16[192]{0:T(256)(128)(2,1)} %param.28) | copy-start | bytes 1156
  7.3 25.5 %copy-start.23 = (bf16[768]{0:T(1024)(128)(2,1)S(1)}, bf16[768]{0:T(1024)(128)(2,1)}, u32[]{:S(2)}) copy-start(bf16[768]{0:T(1024)(128)(2,1)} %param.30) | copy-start | bytes 4612
  7.3 25.5 %copy-start.26 = (bf16[192]{0:T(256)(128)(2,1)S(1)}, bf16[192]{0:T(256)(128)(2,1)}, u32[]{:S(2)}) copy-start(bf16[192]{0:T(256)(128)(2,1)} %param.32) | copy-start | bytes 1156
  7.3 25.5 %copy-start.18 = (bf16[1728]{0:T(1024)(128)(2,1)S(1)}, bf16[1728]{0:T(1024)(128)(2,1)}, u32[]{:S(2)}) copy-start(bf16[1728]{0:T(1024)(128)(2,1)} %param.34) | copy-start | bytes 10372
  7.3 106.0 %all-gather.13.cloned.1.call-start = ((), (), s32[]{:S(2)}) async-start(), calls=%async_computation.15 | async-start | bytes 5308416 | tf_op jit(solution)/shard_map/all_gather | solution.py:838
  10.3 34.7 %copy-start.5 = (bf16[192,6912]{1,0:T(8,128)(2,1)S(1)}, bf16[192,6912]{1,0:T(8,128)(2,1)}, u32[]{:S(2)}) copy-start(bf16[192,6912]{1,0:T(8,128)(2,1)} %param.33) | copy-start | bytes 7962628
  35.2 9.0 %all-to-all-start.1 = ((bf16[4,2,3648]{2,1,0:T(2,128)(2,1)}), bf16[4,2,3648]{2,1,0:T(2,128)(2,1)S(1)}, u32[]{:S(2)}, u32[]{:S(2)}) async-start(bf16[4,2,3648]{2,1,0:T(2,128)(2,1)} %reshape.441), calls=%async_computation.1 | async-start | bytes 118784 | tf_op jit(solution)/shard_map/all_to_all | solution.py:666
  47.1 32.1 %copy-start.9 = (bf16[192,768]{1,0:T(8,128)(2,1)S(1)}, bf16[192,768]{1,0:T(8,128)(2,1)}, u32[]{:S(2)}) copy-start(bf16[192,768]{1,0:T(8,128)(2,1)} %get-tuple-element.211) | copy-start | bytes 884740
  47.1 14.6 %all-to-all-start.2 = ((f32[4,4,6912]{2,1,0:T(4,128)}), f32[4,4,6912]{2,1,0:T(4,128)S(1)}, u32[]{:S(2)}, u32[]{:S(2)}) async-start(f32[4,4,6912]{2,1,0:T(4,128)} %reshape.365), calls=%async_computation.2 | async-start | bytes 884736 | tf_op jit(solution)/shard_map/all_to_all | solution.py:842
  50.7 106.6 %all-gather.15.cloned.1.call-start = ((), (), s32[]{:S(2)}) async-start(), calls=%async_computation.16 | async-start | bytes 5308416 | tf_op jit(solution)/shard_map/all_gather | solution.py:846
  79.2 121.2 %all-gather.17.cloned.1.call-start = ((), (), s32[]{:S(2)}) async-start(), calls=%async_computation.17 | async-start | bytes 10616832 | tf_op jit(solution)/shard_map/all_gather | solution.py:849
  83.6 11.8 %collective-permute-start.2 = (bf16[192,768]{1,0:T(8,128)(2,1)S(1)}, bf16[192,768]{1,0:T(8,128)(2,1)S(1)}, u32[]{:S(2)}, u32[]{:S(2)}) collective-permute-start(bf16[192,768]{1,0:T(8,128)(2,1)S(1)} %dynamic-slice_dynamic-update-slice_fusion), channel_id=1, source_target_pairs={{0,1},{1,2},{2,3},{3,0},{4,5},{5,6},{6,7},{7,4},{8,9},{9,10},{10,1... | collective-permute-start | bytes 884744 | tf_op jit(solution)/shard_map/ppermute | solution.py:691
  84.0 21.3 %collective-permute-start.3 = (bf16[192,768]{1,0:T(8,128)(2,1)S(1)}, bf16[192,768]{1,0:T(8,128)(2,1)S(1)}, u32[]{:S(2)}, u32[]{:S(2)}) collective-permute-start(bf16[192,768]{1,0:T(8,128)(2,1)S(1)} %dynamic-slice_dynamic-update-slice_fusion), channel_id=1, source_target_pairs={{0,2},{1,3},{2,0},{3,1},{4,6},{5,7},{6,4},{7,5},{8,10},{9,11},{10,... | collective-permute-start | bytes 884744 | tf_op jit(solution)/shard_map/ppermute | solution.py:691
  85.6 19.7 %collective-permute-start.4 = (bf16[192,768]{1,0:T(8,128)(2,1)S(1)}, bf16[192,768]{1,0:T(8,128)(2,1)S(1)}, u32[]{:S(2)}, u32[]{:S(2)}) collective-permute-start(bf16[192,768]{1,0:T(8,128)(2,1)S(1)} %dynamic-slice_dynamic-update-slice_fusion), channel_id=1, source_target_pairs={{0,3},{1,0},{2,1},{3,2},{4,7},{5,4},{6,5},{7,6},{8,11},{9,8},{10,9... | collective-permute-start | bytes 884744 | tf_op jit(solution)/shard_map/ppermute | solution.py:691
  106.7 271.8 %reduce-scatter.3.cloned.1.call-start = ((), (), s32[]{:S(2)}) async-start(), calls=%async_computation.11 | async-start | bytes 10616832 | tf_op jit(solution)/shard_map/reduce_scatter | solution.py:877
  146.7 24.4 %collective-permute-start = (bf16[2,256,768]{2,1,0:T(8,128)(2,1)S(1)}, bf16[2,256,768]{2,1,0:T(8,128)(2,1)}, u32[]{:S(2)}, u32[]{:S(2)}) collective-permute-start(bf16[2,256,768]{2,1,0:T(8,128)(2,1)S(1)} %get-tuple-element.172), channel_id=1, source_target_pairs={{0,1},{1,2},{2,3},{4,5},{5,6},{6,7},{8,9},{9,10},{10,11},{12,13},{... | collective-permute-start | bytes 2359304 | tf_op jit(solution)/shard_map/ppermute | solution.py:747
  155.9 20.4 %collective-permute-start.1 = (bf16[2,256,768]{2,1,0:T(8,128)(2,1)S(1)}, bf16[2,256,768]{2,1,0:T(8,128)(2,1)}, u32[]{:S(2)}, u32[]{:S(2)}) collective-permute-start(bf16[2,256,768]{2,1,0:T(8,128)(2,1)S(1)} %get-tuple-element.171), channel_id=1, source_target_pairs={{1,0},{2,1},{3,2},{5,4},{6,5},{7,6},{9,8},{10,9},{11,10},{13,12},{... | collective-permute-start | bytes 2359304 | tf_op jit(solution)/shard_map/ppermute | solution.py:747
  301.5 16.5 %slice-start = ((s8[4718592]{0:T(1024)(128)(4,1)}), s8[524288]{0:T(1024)(128)(4,1)S(1)}, s32[]{:S(2)}) async-start(s8[4718592]{0:T(1024)(128)(4,1)} %bitcast.125), calls=%async_computation.18 | async-start | bytes 1048576
  305.0 13.0 %collective-permute-start.5 = (bf16[4,4,96,768]{3,2,1,0:T(8,128)(2,1)}, bf16[4,4,96,768]{3,2,1,0:T(8,128)(2,1)S(1)}, u32[]{:S(2)}, u32[]{:S(2)}) collective-permute-start(bf16[4,4,96,768]{3,2,1,0:T(8,128)(2,1)} %constant_dynamic-slice_fusion.17), channel_id=1, source_target_pairs={{0,4},{4,0},{8,12},{12,8},{16,20},{20,16},{24,28},{28,24},{1,5},{5... | collective-permute-start | bytes 7077896 | tf_op jit(solution)/shard_map/ppermute | solution.py:755
  305.0 19.3 %collective-permute-start.6 = (bf16[2,256,768]{2,1,0:T(8,128)(2,1)}, bf16[2,256,768]{2,1,0:T(8,128)(2,1)}, u32[]{:S(2)}, u32[]{:S(2)}) collective-permute-start(bf16[2,256,768]{2,1,0:T(8,128)(2,1)} %get-tuple-element.103), channel_id=1, source_target_pairs={{0,1},{1,2},{2,3},{4,5},{5,6},{6,7},{8,9},{9,10},{10,11},{12,13},{... | collective-permute-start | bytes 2359304 | tf_op jit(solution)/shard_map/ppermute | solution.py:747
  307.3 22.1 %collective-permute-start.7 = (bf16[2,256,768]{2,1,0:T(8,128)(2,1)}, bf16[2,256,768]{2,1,0:T(8,128)(2,1)}, u32[]{:S(2)}, u32[]{:S(2)}) collective-permute-start(bf16[2,256,768]{2,1,0:T(8,128)(2,1)} %get-tuple-element.104), channel_id=1, source_target_pairs={{1,0},{2,1},{3,2},{5,4},{6,5},{7,6},{9,8},{10,9},{11,10},{13,12},{... | collective-permute-start | bytes 2359304 | tf_op jit(solution)/shard_map/ppermute | solution.py:747
  308.7 9.3 %slice-start.1 = ((s8[4718592]{0:T(1024)(128)(4,1)}), s8[4194304]{0:T(1024)(128)(4,1)S(1)}, s32[]{:S(2)}) async-start(s8[4718592]{0:T(1024)(128)(4,1)} %bitcast.125), calls=%async_computation.19 | async-start | bytes 8388608
  343.2 23.7 %collective-permute-start.8 = (bf16[4,8064]{1,0:T(4,128)(2,1)S(1)}, bf16[4,8064]{1,0:T(4,128)(2,1)S(1)}, u32[]{:S(2)}, u32[]{:S(2)}) collective-permute-start(bf16[4,8064]{1,0:T(4,128)(2,1)S(1)} %pad_maximum_fusion.16), channel_id=1, source_target_pairs={{0,1},{1,2},{2,3},{3,0},{4,5},{5,6},{6,7},{7,4},{8,9},{9,10},{10,1... | collective-permute-start | bytes 193544 | tf_op jit(solution)/shard_map/ppermute | solution.py:691
  343.3 23.6 %collective-permute-start.9 = (bf16[4,8064]{1,0:T(4,128)(2,1)S(1)}, bf16[4,8064]{1,0:T(4,128)(2,1)S(1)}, u32[]{:S(2)}, u32[]{:S(2)}) collective-permute-start(bf16[4,8064]{1,0:T(4,128)(2,1)S(1)} %pad_maximum_fusion.16), channel_id=1, source_target_pairs={{0,2},{1,3},{2,0},{3,1},{4,6},{5,7},{6,4},{7,5},{8,10},{9,11},{10,... | collective-permute-start | bytes 193544 | tf_op jit(solution)/shard_map/ppermute | solution.py:691
  343.4 23.6 %collective-permute-start.10 = (bf16[4,8064]{1,0:T(4,128)(2,1)S(1)}, bf16[4,8064]{1,0:T(4,128)(2,1)S(1)}, u32[]{:S(2)}, u32[]{:S(2)}) collective-permute-start(bf16[4,8064]{1,0:T(4,128)(2,1)S(1)} %pad_maximum_fusion.16), channel_id=1, source_target_pairs={{0,3},{1,0},{2,1},{3,2},{4,7},{5,4},{6,5},{7,6},{8,11},{9,8},{10,9... | collective-permute-start | bytes 193544 | tf_op jit(solution)/shard_map/ppermute | solution.py:691
  347.1 30.7 %all-to-all-start.4 = ((bf16[4,4,96,768]{3,2,1,0:T(8,128)(2,1)}), bf16[4,4,96,768]{3,2,1,0:T(8,128)(2,1)S(1)}, u32[]{:S(2)}, u32[]{:S(2)}) async-start(bf16[4,4,96,768]{3,2,1,0:T(8,128)(2,1)} %add_convert_fusion.1), calls=%async_computation.4 | async-start | bytes 4718592 | tf_op jit(solution)/shard_map/all_to_all | solution.py:783
  350.8 78.4 %reduce-scatter.5.cloned.1.call-start = ((), (), s32[]{:S(2)}) async-start(), calls=%async_computation.12 | async-start | bytes 2211840 | tf_op jit(solution)/shard_map/reduce_scatter | solution.py:917
  388.6 39.3 %all-to-all-start.5 = ((bf16[8,4,120,384]{3,2,1,0:T(8,128)(2,1)}), bf16[8,4,120,384]{3,2,1,0:T(8,128)(2,1)S(1)}, u32[]{:S(2)}, u32[]{:S(2)}) async-start(bf16[8,4,120,384]{3,2,1,0:T(8,128)(2,1)} %outer_pieces.8), calls=%async_computation.7 | async-start | bytes 5898240 | tf_op jit(solution)/shard_map/all_to_all | solution.py:788
  392.3 73.1 %all-gather.9.cloned.1.call-start = ((), (), s32[]{:S(2)}) async-start(), calls=%async_computation.13 | async-start | bytes 1916928 | tf_op jit(solution)/shard_map/all_gather | solution.py:914
  392.9 125.8 %all-gather.11.cloned.1.call-start = ((), (), s32[]{:S(2)}) async-start(), calls=%async_computation.14 | async-start | bytes 3981312 | tf_op jit(solution)/shard_map/all_gather | solution.py:932
  418.8 10.4 %copy-start.16 = (f32[1,1152]{1,0:T(1,128)S(1)}, f32[1,1152]{1,0:T(1,128)}, u32[]{:S(2)}) copy-start(f32[1,1152]{1,0:T(1,128)} %get-tuple-element.136) | copy-start | bytes 13828
  418.8 10.4 %copy-start.17 = (f32[1,1152]{1,0:T(1,128)S(1)}, f32[1,1152]{1,0:T(1,128)}, u32[]{:S(2)}) copy-start(f32[1,1152]{1,0:T(1,128)} %get-tuple-element.137) | copy-start | bytes 13828
  418.8 10.6 %copy-start.12 = (f32[4,2,768]{2,1,0:T(2,128)S(1)}, f32[4,2,768]{2,1,0:T(2,128)}, u32[]{:S(2)}) copy-start(f32[4,2,768]{2,1,0:T(2,128)} %get-tuple-element.135) | copy-start | bytes 73732
  429.5 11.5 %collective-permute-start.12 = (bf16[4,2112]{1,0:T(4,128)(2,1)S(1)}, bf16[4,2112]{1,0:T(4,128)(2,1)S(1)}, u32[]{:S(2)}, u32[]{:S(2)}) collective-permute-start(bf16[4,2112]{1,0:T(4,128)(2,1)S(1)} %constant_dynamic-update-slice_fusion), channel_id=1, source_target_pairs={{0,1},{1,2},{2,3},{3,0},{4,5},{5,6},{6,7},{7,4},{8,9},{9,10},{10,1... | collective-permute-start | bytes 50696 | tf_op jit(solution)/shard_map/ppermute | solution.py:691
  430.1 10.9 %collective-permute-start.13 = (bf16[4,2112]{1,0:T(4,128)(2,1)S(1)}, bf16[4,2112]{1,0:T(4,128)(2,1)S(1)}, u32[]{:S(2)}, u32[]{:S(2)}) collective-permute-start(bf16[4,2112]{1,0:T(4,128)(2,1)S(1)} %constant_dynamic-update-slice_fusion), channel_id=1, source_target_pairs={{0,2},{1,3},{2,0},{3,1},{4,6},{5,7},{6,4},{7,5},{8,10},{9,11},{10,... | collective-permute-start | bytes 50696 | tf_op jit(solution)/shard_map/ppermute | solution.py:691
  431.3 9.7 %collective-permute-start.14 = (bf16[4,2112]{1,0:T(4,128)(2,1)S(1)}, bf16[4,2112]{1,0:T(4,128)(2,1)S(1)}, u32[]{:S(2)}, u32[]{:S(2)}) collective-permute-start(bf16[4,2112]{1,0:T(4,128)(2,1)S(1)} %constant_dynamic-update-slice_fusion), channel_id=1, source_target_pairs={{0,3},{1,0},{2,1},{3,2},{4,7},{5,4},{6,5},{7,6},{8,11},{9,8},{10,9... | collective-permute-start | bytes 50696 | tf_op jit(solution)/shard_map/ppermute | solution.py:691
  440.9 2.6 collective-permute-start.11
  443.8 17.1 %copy-start.8 = (bf16[4,120,384]{2,1,0:T(8,128)(2,1)S(1)}, bf16[4,120,384]{2,1,0:T(8,128)(2,1)}, u32[]{:S(2)}) copy-start(bf16[4,120,384]{2,1,0:T(8,128)(2,1)} %reduce_sum.114) | copy-start | bytes 1105924
  461.8 17.5 %all-to-all-start.7 = ((bf16[4,192,384]{2,1,0:T(8,128)(2,1)}), bf16[4,192,384]{2,1,0:T(8,128)(2,1)S(1)}, u32[]{:S(2)}, u32[]{:S(2)}) async-start(bf16[4,192,384]{2,1,0:T(8,128)(2,1)} %pad_maximum_fusion.7), calls=%async_computation.9 | async-start | bytes 1179648 | tf_op jit(solution)/shard_map/all_to_all | solution.py:792
  480.7 25.0 %all-to-all-start.8 = ((bf16[8,262,384]{2,1,0:T(8,128)(2,1)}), bf16[8,262,384]{2,1,0:T(8,128)(2,1)S(1)}, u32[]{:S(2)}, u32[]{:S(2)}) async-start(bf16[8,262,384]{2,1,0:T(8,128)(2,1)} %broadcast_in_dim.15), calls=%async_computation.10 | async-start | bytes 3244032 | tf_op jit(solution)/shard_map/all_to_all | solution.py:798
  487.9 8.8 %collective-permute-start.15 = (f32[4,192]{1,0:T(4,128)S(1)}, f32[4,192]{1,0:T(4,128)S(1)}, u32[]{:S(2)}, u32[]{:S(2)}) collective-permute-start(f32[4,192]{1,0:T(4,128)S(1)} %get-tuple-element.206), channel_id=1, source_target_pairs={{0,1},{1,2},{2,3},{3,0},{4,5},{5,6},{6,7},{7,4},{8,9},{9,10},{10,1... | collective-permute-start | bytes 9224 | tf_op jit(solution)/shard_map/ppermute | solution.py:676
  488.0 8.7 %collective-permute-start.16 = (f32[4,192]{1,0:T(4,128)S(1)}, f32[4,192]{1,0:T(4,128)S(1)}, u32[]{:S(2)}, u32[]{:S(2)}) collective-permute-start(f32[4,192]{1,0:T(4,128)S(1)} %get-tuple-element.205), channel_id=1, source_target_pairs={{0,2},{1,3},{2,0},{3,1},{4,6},{5,7},{6,4},{7,5},{8,10},{9,11},{10,... | collective-permute-start | bytes 9224 | tf_op jit(solution)/shard_map/ppermute | solution.py:676
  490.0 6.7 %collective-permute-start.17 = (f32[4,192]{1,0:T(4,128)S(1)}, f32[4,192]{1,0:T(4,128)S(1)}, u32[]{:S(2)}, u32[]{:S(2)}) collective-permute-start(f32[4,192]{1,0:T(4,128)S(1)} %get-tuple-element.204), channel_id=1, source_target_pairs={{0,3},{1,0},{2,1},{3,2},{4,7},{5,4},{6,5},{7,6},{8,11},{9,8},{10,9... | collective-permute-start | bytes 9224 | tf_op jit(solution)/shard_map/ppermute | solution.py:676
  (14 other events, 85.0 us)
Sparse Core Ops, SparseCore 0:
  32.8 37.8 all-gather.12
  79.3 37.8 all-gather.14
  119.7 58.6 all-gather.16
  261.8 74.8 reduce-scatter.2
  381.3 36.8 reduce-scatter.4
  420.5 25.0 all-gather.8
  447.5 33.8 all-gather.10

commit v4 on v3

--- a/solution.py
+++ b/solution.py
@@ -11,6 +11,8 @@
 HEADS = 12
 HEAD_DIM = 64
 WINDOW = 2
+DP = "dp"
+FRAME = "frame"
 
 F32 = jnp.float32
 BF16 = jnp.bfloat16
@@ -77,7 +79,32 @@
     return pl.BlockSpec((lead, tile, width), lambda i: (0, i, 0))
 
 
-def spatial_kernel(x_ref, mod_ref, wsi, bsi, n1_ref, qkv1_ref, attn_ref):
+def lay_out(raw, whole, first=0):
+    @pl.when(pl.program_id(0) == 0)
+    def _():
+        groups, parts, _, width = raw.shape
+        rows = whole.shape[0] // (groups * parts)
+        for f in range(parts):
+            for d in range(groups):
+                at = (f * groups + d) * rows
+                for tile in range(whole.shape[1] // width):
+                    source = (first + tile) * rows
+                    whole[at : at + rows, tile * width : (tile + 1) * width] = raw[
+                        d, f, source : source + rows
+                    ]
+
+
+def rows_of(raw, stacks, total, at=0):
+    groups, parts, height, width = raw.shape
+    return pl.BlockSpec(
+        (groups, parts, height * stacks // total, width),
+        lambda *_: (0, 0, at, 0),
+        pipeline_mode=pl.Buffered(1),
+    )
+
+
+def spatial_kernel(x_ref, mod_ref, raw, bsi, n1_ref, qkv1_ref, attn_ref, wsi):
+    lay_out(raw, wsi)
     x = x_ref[0].astype(F32)
     width = x.shape[1]
     xhat, _ = unit(x)
@@ -97,7 +124,7 @@
         attn_ref[0, :, at : at + 2 * HEAD_DIM] = out.astype(BF16)
 
 
-def spatial_forward(x, mod, wsi, bsi):
+def spatial_forward(x, mod, space, bsi):
     frames, patches, width = x.shape
     block = lambda n: per_first((patches, n))
     outs = [width, 3 * width, width]
@@ -105,15 +132,20 @@
     return pl.pallas_call(
         spatial_kernel,
         grid=(frames,),
-        in_specs=[block(width), per_first(mod.shape[1:]), fixed(wsi.shape), fixed(bsi.shape)],
+        in_specs=[
+            block(width), per_first(mod.shape[1:]),
+            rows_of(space, 3, 4), fixed(bsi.shape),
+        ],
         out_specs=[block(n) for n in outs],
         out_shape=[jax.ShapeDtypeStruct((frames, patches, n), BF16) for n in outs],
+        scratch_shapes=[pltpu.VMEM((width, 3 * width), BF16)],
         name="spatial_forward",
         **params(2 * tokens * width * (3 * width + 4 * patches), 12e6, tokens * patches * HEADS),
-    )(x, mod, wsi, bsi)
-
-
-def project_kernel(x_ref, attn_ref, mod_ref, wso, bso, branch_ref, after_ref, n2_ref):
+    )(x, mod, space, bsi)
+
+
+def project_kernel(x_ref, attn_ref, mod_ref, raw, bso, branch_ref, after_ref, n2_ref, wso):
+    lay_out(raw, wso)
     branch = mm(attn_ref[0], wso[...]) + bso[...]
     branch_ref[0] = branch
     after = x_ref[0].astype(F32) + mod_ref[0, 2:3] * branch
@@ -122,19 +154,42 @@
     n2_ref[0] = (xhat * (1.0 + mod_ref[0, 4:5]) + mod_ref[0, 3:4]).astype(BF16)
 
 
-def project_forward(x, attn, mod, wso, bso):
+def project_forward(x, attn, mod, space, bso):
     frames, patches, width = x.shape
     block = per_first((patches, width))
     tokens = frames * patches
     return pl.pallas_call(
         project_kernel,
         grid=(frames,),
-        in_specs=[block, block, per_first(mod.shape[1:]), fixed(wso.shape), fixed(bso.shape)],
+        in_specs=[
+            block, block, per_first(mod.shape[1:]), rows_of(space, 1, 4, 3), fixed(bso.shape)
+        ],
+        scratch_shapes=[pltpu.VMEM((width, width), BF16)],
         out_specs=[block] * 3,
         out_shape=[jax.ShapeDtypeStruct(x.shape, t) for t in (F32, F32, BF16)],
         name="project_forward",
         **params(2 * tokens * width * width, 13e6),
-    )(x, attn, mod, wso, bso)
+    )(x, attn, mod, space, bso)
+
+
+def qkv_kernel(n_ref, raw, bias, out_ref, whole):
+    lay_out(raw, whole)
+    out_ref[0] = (mm(n_ref[0], whole[...]) + bias[...]).astype(BF16)
+
+
+def temporal_qkv(n, time, bias):
+    frames, patches, width = n.shape
+    tokens = frames * patches
+    return pl.pallas_call(
+        qkv_kernel,
+        grid=(frames,),
+        in_specs=[per_first((patches, width)), rows_of(time, 3, 4), fixed(bias.shape)],
+        out_specs=per_first((patches, 3 * width)),
+        out_shape=jax.ShapeDtypeStruct((frames, patches, 3 * width), BF16),
+        scratch_shapes=[pltpu.VMEM((width, 3 * width), BF16)],
+        name="temporal_qkv",
+        **params(6 * tokens * width * width, 10e6),
+    )(n, time, bias)
 
 
 def split_store(hi_ref, lo_ref, row, prod):
@@ -159,12 +214,14 @@
 
 
 def temporal_kernel(
-    allowed, qkv_ref, nl_ref, nr_ref, after_ref, mod_ref, wti, bti, wto, bto, ones, ones_t,
-    probs_ref, attn_ref, branch_ref, out_ref, left_ref, right_ref, hi_ref, lo_ref,
+    allowed, qkv_ref, nl_ref, nr_ref, after_ref, mod_ref, raw_in, bti, raw_out, bto, ones, ones_t,
+    probs_ref, attn_ref, branch_ref, out_ref, left_ref, right_ref, hi_ref, lo_ref, wkv, wto,
 ):
     frames, tile, width = after_ref.shape
+    lay_out(raw_in, wkv, 1)
+    lay_out(raw_out, wto)
     for near, kv_ref in ((nl_ref, left_ref), (nr_ref, right_ref)):
-        kv = mm(near[...].reshape(WINDOW * tile, width), wti[:, width:]) + bti[:, width:]
+        kv = mm(near[...].reshape(WINDOW * tile, width), wkv[...]) + bti[:, width:]
         kv_ref[...] = kv.astype(BF16).reshape(WINDOW, tile, 2 * width)
     for t in range(frames):
         q = qkv_ref[t, :, :width].astype(F32)
@@ -207,7 +264,7 @@
     return (head == jnp.arange(128, dtype=jnp.int32)[None, :]).astype(BF16)
 
 
-def temporal_forward(allowed, qkv, near_left, near_right, after, mod, wti, bti, wto, bto):
+def temporal_forward(allowed, qkv, near_left, near_right, after, mod, time, bti, bto):
     frames, patches, width = after.shape
     tile = 64
     ones = head_ones(width)
@@ -222,7 +279,7 @@
         in_specs=[
             pl.BlockSpec(memory_space=pltpu.SMEM),
             spec(3 * width), near, near, spec(width), fixed(mod.shape),
-            fixed(wti.shape), fixed(bti.shape), fixed(wto.shape), fixed(bto.shape),
+            rows_of(time, 3, 4), fixed(bti.shape), rows_of(time, 1, 4, 3), fixed(bto.shape),
             fixed(ones.shape), fixed(ones.shape[::-1]),
         ],
         out_specs=[
@@ -235,16 +292,19 @@
             jax.ShapeDtypeStruct((WINDOW, patches, 2 * width), BF16),
             jax.ShapeDtypeStruct((WINDOW, patches, 2 * width), BF16),
         ],
-        scratch_shapes=[pltpu.VMEM((frames * SPAN, tile, width), BF16)] * 2,
+        scratch_shapes=[pltpu.VMEM((frames * SPAN, tile, width), BF16)] * 2
+        + [pltpu.VMEM((width, 2 * width), BF16), pltpu.VMEM((width, width), BF16)],
         name="temporal_forward",
         **params(2 * tokens * width * (width + SPAN * 400), 22e6, tokens * SPAN * 128),
-    )(allowed, qkv, near_left, near_right, after, mod, wti, bti, wto, bto, ones, ones.T)
+    )(allowed, qkv, near_left, near_right, after, mod, time, bti, time, bto, ones, ones.T)
 
 
 def feed_kernel(
-    after_ref, cot_ref, mod_ref, w1, b1, w2, b2,
-    out_ref, g_ref, n_ref, act_ref, dpre_ref, db_ref, dmod_ref, sum1_ref, sum2_ref,
+    after_ref, cot_ref, mod_ref, raw1, b1, raw2, b2,
+    out_ref, g_ref, n_ref, act_ref, dpre_ref, db_ref, dmod_ref, sum1_ref, sum2_ref, w1, w2,
 ):
+    lay_out(raw1, w1)
+    lay_out(raw2, w2)
     after = after_ref[0]
     width = after.shape[1]
     hidden = w1.shape[1]
@@ -287,9 +347,9 @@
     g_ref[0] = g3 + unit_back(dn, xhat, inv, scale)
 
 
-def feed_forward(after, cot, mod, w1, b1, w2, b2):
+def feed_forward(after, cot, mod, dense, b1, b2):
     frames, patches, width = after.shape
-    hidden = w1.shape[1]
+    hidden = b1.shape[1]
     shape = lambda n, t: jax.ShapeDtypeStruct((frames, patches, n), t)
     block = lambda n: per_first((patches, n))
     outs = [(width, BF16), (width, F32), (width, BF16), (hidden, BF16), (hidden, BF16), (width, BF16)]
@@ -297,8 +357,11 @@
     return pl.pallas_call(
         feed_kernel,
         grid=(frames,),
-        in_specs=[block(width), block(width), per_first(mod.shape[1:])]
-        + [fixed(w.shape) for w in (w1, b1, w2, b2)],
+        in_specs=[
+            block(width), block(width), per_first(mod.shape[1:]),
+            rows_of(dense, 1, 2), fixed(b1.shape), rows_of(dense, 1, 2, 1), fixed(b2.shape),
+        ],
+        scratch_shapes=[pltpu.VMEM((width, hidden), BF16), pltpu.VMEM((hidden, width), BF16)],
         out_specs=[block(n) for n, _ in outs]
         + [per_first((3, width)), pl.BlockSpec((1, hidden), lambda i: (0, 0)),
            pl.BlockSpec((1, width), lambda i: (0, 0))],
@@ -307,15 +370,17 @@
            jax.ShapeDtypeStruct((1, hidden), F32), jax.ShapeDtypeStruct((1, width), F32)],
         name="feed_forward",
         **params(8 * tokens * width * hidden, 32e6, 2 * tokens * hidden),
-    )(after, cot, mod, w1, b1, w2, b2)
+    )(after, cot, mod, dense, b1, dense, b2)
 
 
 def temporal_back_kernel(
-    g_ref, branch_ref, mod_ref, wto, wti, qkv_ref, left_ref, right_ref, probs_ref, ones, ones_t,
+    g_ref, branch_ref, mod_ref, raw_out, raw_in, qkv_ref, left_ref, right_ref, probs_ref, ones, ones_t,
     db_ref, dqkv_ref, dleft_ref, dright_ref, nleft_ref, nright_ref, dgate_ref, sum_ref, sumq_ref,
-    hi_ref, lo_ref, da_ref, ds_ref, pw_ref,
+    hi_ref, lo_ref, da_ref, ds_ref, pw_ref, wkv, wto,
 ):
     frames, tile, width = g_ref.shape
+    lay_out(raw_in, wkv, 1)
+    lay_out(raw_out, wto)
 
     @pl.when(pl.program_id(0) == 0)
     def _():
@@ -378,11 +443,11 @@
     for dkv_ref, near_ref in ((dleft_ref, nleft_ref), (dright_ref, nright_ref)):
         flat = dkv_ref[...].reshape(WINDOW * tile, 2 * width)
         sumq_ref[:, width:] += down(flat.astype(F32))
-        near_ref[...] = mm_nt(flat, wti[:, width:]).astype(BF16).reshape(WINDOW, tile, width)
+        near_ref[...] = mm_nt(flat, wkv[...]).astype(BF16).reshape(WINDOW, tile, width)
     sumq_ref[...] += down(dqkv_ref[...].reshape(frames * tile, 3 * width).astype(F32))
 
 
-def temporal_backward(g, branch, mod, wto, wti, qkv, left, right, probs):
+def temporal_backward(g, branch, mod, time, qkv, left, right, probs):
     frames, patches, width = g.shape
     tile = 64
     ones = head_ones(width)
@@ -395,7 +460,7 @@
         temporal_back_kernel,
         grid=(patches // tile,),
         in_specs=[
-            spec(width), spec(width), fixed(mod.shape), fixed(wto.shape), fixed(wti.shape),
+            spec(width), spec(width), fixed(mod.shape), rows_of(time, 1, 4, 3), rows_of(time, 3, 4),
             spec(3 * width), halo, halo,
             pl.BlockSpec((frames, SPAN, tile, 128), lambda i: (0, 0, i, 0)),
             fixed(ones.shape), fixed(ones.shape[::-1]),
@@ -415,23 +480,26 @@
         ],
         scratch_shapes=[pltpu.VMEM((frames * SPAN, tile, width), BF16)] * 2
         + [pltpu.VMEM((frames, tile, width), BF16)]
-        + [pltpu.VMEM((frames * SPAN, tile, width), BF16)] * 2,
+        + [pltpu.VMEM((frames * SPAN, tile, width), BF16)] * 2
+        + [pltpu.VMEM((width, 2 * width), BF16), pltpu.VMEM((width, width), BF16)],
         name="temporal_backward",
         **params(2 * tokens * width * (width + SPAN * 500), 36e6),
-    )(g, branch, mod, wto, wti, qkv, left, right, probs, ones, ones.T)
+    )(g, branch, mod, time, time, qkv, left, right, probs, ones, ones.T)
 
 
 def project_back_kernel(
-    dn_ref, fl_ref, fr_ref, after_ref, g2_ref, branch_ref, mod_ref, wso,
-    g_ref, db_ref, da_ref, dmod_ref, sum_ref,
+    dqkv_ref, fl_ref, fr_ref, after_ref, g2_ref, branch_ref, mod_ref, raw_in, raw_out,
+    g_ref, db_ref, da_ref, dmod_ref, sum_ref, wti, wso,
 ):
+    lay_out(raw_in, wti)
+    lay_out(raw_out, wso)
     at = pl.program_id(0)
 
     @pl.when(at == 0)
     def _():
         sum_ref[...] = jnp.zeros_like(sum_ref)
 
-    dn = dn_ref[0] + jnp.where(at < WINDOW, fl_ref[0].astype(F32), fr_ref[0].astype(F32))
+    dn = mm_nt(dqkv_ref[0], wti[...]) + jnp.where(at < WINDOW, fl_ref[0].astype(F32), fr_ref[0].astype(F32))
     xhat, inv = unit(after_ref[0])
     dmod_ref[0, 1:2] = down(dn)
     dmod_ref[0, 2:3] = down(dn * xhat)
@@ -444,7 +512,7 @@
     da_ref[0] = mm_nt(db, wso[...]).astype(BF16)
 
 
-def project_backward(dn2, from_left, from_right, after, g2, branch, mod, wso):
+def project_backward(dqkv2, from_left, from_right, after, g2, branch, mod, time, space):
     frames, patches, width = after.shape
     block = per_first((patches, width))
     tokens = frames * patches
@@ -452,18 +520,19 @@
         project_back_kernel,
         grid=(frames,),
         in_specs=[
-            block,
+            per_first((patches, 3 * width)),
             pl.BlockSpec((1, patches, width), lambda i: (jnp.minimum(i, WINDOW - 1), 0, 0)),
             pl.BlockSpec((1, patches, width), lambda i: (jnp.maximum(i - WINDOW, 0), 0, 0)),
-            block, block, block, per_first(mod.shape[1:]), fixed(wso.shape),
+            block, block, block, per_first(mod.shape[1:]), rows_of(time, 3, 4), rows_of(space, 1, 4, 3),
         ],
+        scratch_shapes=[pltpu.VMEM((width, 3 * width), BF16), pltpu.VMEM((width, width), BF16)],
         out_specs=[block, block, block, per_first((3, width)),
                    pl.BlockSpec((1, width), lambda i: (0, 0))],
         out_shape=[jax.ShapeDtypeStruct(after.shape, t) for t in (F32, BF16, BF16)]
         + [jax.ShapeDtypeStruct((frames, 3, width), F32), jax.ShapeDtypeStruct((1, width), F32)],
         name="project_backward",
-        **params(2 * tokens * width * width, 22e6),
-    )(dn2, from_left, from_right, after, g2, branch, mod, wso)
+        **params(8 * tokens * width * width, 24e6),
+    )(dqkv2, from_left, from_right, after, g2, branch, mod, time, space)
 
 
 def heads_back(q_ref, k_ref, v_ref, da_ref, out_ref, sum_ref):
@@ -498,9 +567,10 @@
 
 
 def last_heads_kernel(
-    q_ref, k_ref, v_ref, da_ref, first_ref, g_ref, x_ref, mod_ref, wsi,
-    out_ref, sum_ref, grad_ref, dmod_ref,
+    q_ref, k_ref, v_ref, da_ref, first_ref, g_ref, x_ref, mod_ref, raw,
+    out_ref, sum_ref, grad_ref, dmod_ref, wsi,
 ):
+    lay_out(raw, wsi)
     heads_back(q_ref, k_ref, v_ref, da_ref, out_ref, sum_ref)
     width = q_ref.shape[2]
     dn = None
@@ -528,11 +598,13 @@
         jax.ShapeDtypeStruct((frames, patches, 3 * part), BF16),
         jax.ShapeDtypeStruct((1, 3 * part), F32),
     ]
+    scratch = []
     if rest is not None:
-        first, g1, x, mod, wsi = rest
+        first, g1, x, mod, space = rest
         in_specs += [block(3 * part), block(width), block(width), per_first(mod.shape[1:]),
-                     fixed(wsi.shape)]
-        operands += [first, g1, x, mod, wsi]
+                     rows_of(space, 3, 4)]
+        operands += [first, g1, x, mod, space]
+        scratch = [pltpu.VMEM((width, 3 * width), BF16)]
         out_specs += [block(width), per_first((2, width))]
         out_shape += [
             jax.ShapeDtypeStruct((frames, patches, width), F32),
@@ -544,6 +616,7 @@
         in_specs=in_specs,
         out_specs=out_specs,
         out_shape=out_shape,
+        scratch_shapes=scratch,
         name="first_heads_backward" if rest is None else "last_heads_backward",
         **params(2 * tokens * width * (5 * patches + (0 if rest is None else 3 * width)),
                  16e6, tokens * patches * HEADS // 2),
@@ -641,9 +714,67 @@
     )(*operands)
 
 
+def last_kernel(own_ref, *refs, sizes):
+    groups = len(refs) - 9
+    pieces, (columns, early) = refs[:groups], refs[groups : groups + 2]
+    in_ref, out_ref, mod_ref, sum_ref, bias_ref, late_ref, turned = refs[groups + 2 :]
+    part = pieces[0].shape[1]
+    rows = in_ref.shape[0] // groups
+    tall = sizes[2] // 4
+    begin = sizes[0] + sizes[1]
+    bias = None
+    for far, piece in enumerate(pieces):
+        d = own_ref[0] ^ far
+        there = pl.ds(pl.multiple_of(d * rows, 8), rows)
+        for at in range(3):
+            for side, top in enumerate((0, sizes[0])):
+                column = (2 * at + side) * part
+                in_ref[there, column : column + part] = piece[
+                    top + at * rows : top + (at + 1) * rows
+                ].astype(F32)
+        for at in range(2):
+            source = (3 + at) * rows
+            out_ref[there, at * part : (at + 1) * part] = piece[source : source + rows].astype(F32)
+        there = pl.ds(pl.multiple_of(d * tall, 16), tall)
+        for at in range(4):
+            source = begin + at * tall
+            late_ref[there, at * part : (at + 1) * part] = piece[source : source + tall]
+        term = piece[begin + sizes[2] : begin + sizes[2] + sizes[3]].astype(F32)
+        bias = term if bias is None else bias + term
+    bias_ref[...] = bias
+    turned[...] = columns[...].T
+    wide = 4 * part
+    mod_ref[:, :wide] = mm(turned[...], late_ref[...])
+    sum_ref[:, :wide] = down(late_ref[...].astype(F32))
+    for at in range(early.shape[1] // wide + 1):
+        cols = slice(at * wide, min((at + 1) * wide, early.shape[1]))
+        mod_ref[:, wide + cols.start : wide + cols.stop] = mm(turned[...], early[:, cols])
+        sum_ref[:, wide + cols.start : wide + cols.stop] = down(early[:, cols].astype(F32))
+
+
+def last_outputs(pieces, columns, early, sizes, rows):
+    part = pieces[0].shape[1]
+    tokens, more = early.shape
+    total = more + 4 * part
+    shapes = [(rows, 6 * part), (rows, 2 * part), (rows, total), (1, total), (sizes[3], part)]
+    own = lax.axis_index(DP).reshape(1)
+    whole = pl.BlockSpec(memory_space=pltpu.VMEM)
+    return pl.pallas_call(
+        functools.partial(last_kernel, sizes=tuple(sizes)),
+        in_specs=[pl.BlockSpec(memory_space=pltpu.SMEM)] + [whole] * (len(pieces) + 2),
+        out_specs=[whole] * 5,
+        out_shape=[jax.ShapeDtypeStruct(s, F32) for s in shapes],
+        scratch_shapes=[
+            pltpu.VMEM((tokens, 4 * part), BF16), pltpu.VMEM((rows, tokens), BF16),
+        ],
+        name="last_outputs",
+        **params(2 * rows * tokens * total, 12e6),
+    )(own, *pieces, columns, early)
+
+
 def own_part(vector):
-    size = vector.shape[0] // lax.axis_size("frame")
-    return lax.dynamic_slice_in_dim(vector, lax.axis_index("frame") * size, size)
+    size = vector.shape[0] // lax.axis_size(FRAME)
+    return lax.dynamic_slice_in_dim(vector, lax.axis_index(FRAME) * size, size)
 
 
 def stacked(block, width):
@@ -661,19 +792,19 @@
 
 
 def line_gathered(mine):
-    parts = lax.axis_size("frame")
+    parts = lax.axis_size(FRAME)
     copies = jnp.broadcast_to(mine[None], (parts,) + mine.shape)
-    return lax.all_to_all(copies, "frame", split_axis=0, concat_axis=0)
+    return lax.all_to_all(copies, FRAME, split_axis=0, concat_axis=0)
 
 
 def line_swapped(pieces):
-    parts = lax.axis_size("frame")
-    place = lax.axis_index("frame")
+    parts = lax.axis_size(FRAME)
+    place = lax.axis_index(FRAME)
     pick = lambda at: lax.dynamic_index_in_dim(pieces, (place + at) % parts, keepdims=False)
     seen = [pick(0)]
     for far in range(1, parts):
         pairs = [(i, (i + far) % parts) for i in range(parts)]
-        seen.append(lax.ppermute(pick(far), "frame", pairs))
+        seen.append(lax.ppermute(pick(far), FRAME, pairs))
     seen = jnp.stack(seen)
     return jnp.stack(
         [
@@ -684,11 +815,11 @@
 
 
 def line_rotated(mine):
-    parts = lax.axis_size("frame")
-    place = lax.axis_index("frame")
+    parts = lax.axis_size(FRAME)
+    place = lax.axis_index(FRAME)
     seen = [mine]
     for far in range(1, parts):
-        seen.append(lax.ppermute(mine, "frame", [(i, (i + far) % parts) for i in range(parts)]))
+        seen.append(lax.ppermute(mine, FRAME, [(i, (i + far) % parts) for i in range(parts)]))
     seen = jnp.stack(seen)
     return jnp.stack(
         [
@@ -699,31 +830,35 @@
 
 
 def packed(shards):
-    groups = lax.axis_size("dp")
+    groups = lax.axis_size(DP)
     width = min(shard.shape[1] for shard in shards)
     pieces = []
     for shard in shards:
         rows = shard.shape[0] // groups
-        piece = lax.dynamic_slice_in_dim(shard, lax.axis_index("dp") * rows, rows)
+        piece = lax.dynamic_slice_in_dim(shard, lax.axis_index(DP) * rows, rows)
         pieces.append(stacked(piece, width))
     return jnp.concatenate(pieces, axis=0)
 
 
-def unpacked(whole, shards):
-    groups, parts = lax.axis_size("dp"), lax.axis_size("frame")
+def plane_pieces(column, shards):
+    groups, parts = lax.axis_size(DP), lax.axis_size(FRAME)
+    whole = lax.all_gather(column, DP, axis=0)
+    if shards[0].shape[0] // groups % 8 == 0:
+        return whole
     width = whole.shape[-1]
     results, at = [], 0
     for shard in shards:
         stacks = shard.shape[1] // width
         height = stacks * shard.shape[0] // groups
         part = unstacked(whole[:, :, at : at + height], stacks)
-        results.append(jnp.swapaxes(part, 0, 1).reshape(parts * shard.shape[0], shard.shape[1]))
+        part = jnp.swapaxes(part, 0, 1).reshape(parts * shard.shape[0], shard.shape[1])
+        results.append(stacked(part, width))
         at += height
-    return results
+    return jnp.concatenate(results, axis=0)[None, None]
 
 
 def gathered_small(biases, condition):
-    parts = lax.axis_size("frame")
+    parts = lax.axis_size(FRAME)
     flat = jnp.concatenate(biases + [condition.reshape(-1)])
     rows = line_gathered(flat)
     results, at = [], 0
@@ -735,9 +870,9 @@
 
 
 def modulated(act_group, matrix, frames):
-    parts = lax.axis_size("frame")
+    parts = lax.axis_size(FRAME)
     rows, width = matrix.shape
-    columns = lax.dynamic_slice_in_dim(act_group, lax.axis_index("frame") * rows, rows, axis=1)
+    columns = lax.dynamic_slice_in_dim(act_group, lax.axis_index(FRAME) * rows, rows, axis=1)
     return mm(columns, matrix).reshape(parts, frames, width)
 
 
@@ -748,15 +883,11 @@
 
 
 def own_bit(bit):
-    return (lax.axis_index("dp") >> bit) & 1
+    return (lax.axis_index(DP) >> bit) & 1
 
 
 def swapped(x, bit):
-    return lax.ppermute(x, "dp", [(i, i ^ (1 << bit)) for i in range(lax.axis_size("dp"))])
-
-
-def added(a, b):
-    return (a.astype(F32) + b.astype(F32)).astype(BF16)
+    return lax.ppermute(x, DP, [(i, i ^ (1 << bit)) for i in range(lax.axis_size(DP))])
 
 
 def halved(blocks, bit):
@@ -764,38 +895,61 @@
     mine = own_bit(bit)
     sent = lax.dynamic_slice_in_dim(blocks, (1 - mine) * half, half)
     kept = lax.dynamic_slice_in_dim(blocks, mine * half, half)
-    return added(kept, swapped(sent, bit))
+    return kept.astype(F32) + swapped(sent, bit).astype(F32)
 
 
 def summed(pieces):
-    return jnp.sum(pieces.astype(F32), axis=0).astype(BF16)
+    return jnp.sum(pieces.astype(F32), axis=0)
 
 
 def core_order():
-    groups = lax.axis_size("dp")
+    groups = lax.axis_size(DP)
     return [(d & 1) * (groups // 2) + (d >> 1) for d in range(groups)]
 
 
 def plane_summed(blocks):
-    groups = lax.axis_size("dp")
-    same = [list(range(core, groups, 2)) for core in range(2)]
-    return summed(
-        lax.all_to_all(blocks, "dp", split_axis=0, concat_axis=0, axis_index_groups=same)
-    )
+    count = blocks.shape[0]
+    own = lax.axis_index(DP) >> 1
+    pick = lambda at: lax.dynamic_index_in_dim(blocks, at, keepdims=False)
+    total = pick(own)
+    for far in range(1, count):
+        pairs = [(i, i ^ (2 * far)) for i in range(2 * count)]
+        total = total + lax.ppermute(pick(own ^ far).astype(BF16), DP, pairs).astype(F32)
+    return total
 
 
 def dp_summed_start(blocks):
-    return lax.all_to_all(blocks, "dp", split_axis=0, concat_axis=0)
-
-
-def line_summed(blocks):
-    return summed(lax.all_to_all(blocks, "frame", split_axis=0, concat_axis=0))
+    return lax.all_to_all(blocks, DP, split_axis=0, concat_axis=0)
+
+
+def line_summed(blocks, sent=BF16):
+    parts = blocks.shape[0]
+    place = lax.axis_index(FRAME)
+    pick = lambda at: lax.dynamic_index_in_dim(blocks, (place + at) % parts, keepdims=False)
+    total = pick(0)
+    for far in range(1, parts):
+        pairs = [(i, (i + far) % parts) for i in range(parts)]
+        total = total + lax.ppermute(pick(far).astype(sent), FRAME, pairs).astype(F32)
+    return total
 
 
 def plane_gathered(piece):
-    groups = lax.axis_size("dp")
-    copies = jnp.broadcast_to(piece[None], (groups,) + piece.shape)
-    return lax.all_to_all(copies, "dp", split_axis=0, concat_axis=0)
+    groups = lax.axis_size(DP)
+    if groups > 8:
+        copies = jnp.broadcast_to(piece[None], (groups,) + piece.shape)
+        return lax.all_to_all(copies, DP, split_axis=0, concat_axis=0)
+    pairs = lambda far: [(i, i ^ far) for i in range(groups)]
+    return [piece] + [lax.ppermute(piece, DP, pairs(far)) for far in range(1, groups)]
+
+
+def in_order(seen):
+    if not isinstance(seen, list):
+        return seen
+    own = lax.axis_index(DP)
+    seen = jnp.stack(seen)
+    return jnp.stack(
+        [lax.dynamic_index_in_dim(seen, own ^ d, keepdims=False) for d in range(len(seen))]
+    )
 
 
 def per_device(
@@ -818,9 +972,9 @@
     modulate_bias,
     cotangent,
 ):
-    groups, parts = lax.axis_size("dp"), lax.axis_size("frame")
-    place = lax.axis_index("frame")
-    frames, patches, width = frames_in.shape
+    groups, parts = lax.axis_size(DP), lax.axis_size(FRAME)
+    place = lax.axis_index(FRAME)
+    frames, _, width = frames_in.shape
     space, time = [spatial_in, spatial_out], [temporal_in, temporal_out]
     dense = [expand_weight, shrink_weight]
     biases = [
@@ -832,38 +986,35 @@
         shrink_bias,
         modulate_bias,
     ]
-    space_column = line_gathered(packed(space))
-    condition_held, space_column = lax.optimization_barrier((condition, space_column))
-    *full_biases, cond_group = gathered_small(biases, condition_held)
-    full_spatial_in, full_spatial_out = unpacked(lax.all_gather(space_column, "dp", axis=0), space)
+    space_column = line_rotated(packed(space))
+    time_piece, space_column = lax.optimization_barrier((packed(time), space_column))
+    time_column = line_rotated(time_piece)
+    *full_biases, cond_group = gathered_small(biases, condition)
+    space_raw = plane_pieces(space_column, space)
     sinb, soutb, tinb, toutb, expb, shrb, modb = [b.astype(F32)[None, :] for b in full_biases]
     act_group = jax.nn.silu(cond_group.astype(F32)).astype(BF16)
     partial = modulated(act_group, modulate_weight, frames)
-    partial = lax.all_to_all(partial, "frame", split_axis=0, concat_axis=0)
-    time_piece, partial = lax.optimization_barrier((packed(time), partial))
-    mod = (jnp.sum(partial, axis=0) + modb).reshape(frames, 9, width)
-    time_column = line_gathered(time_piece)
-    full_temporal_in, full_temporal_out = unpacked(lax.all_gather(time_column, "dp", axis=0), time)
-    dense_piece, time_column, mod = lax.optimization_barrier((packed(dense), time_column, mod))
+    partial = line_summed(partial, F32)
+    mod = (partial + modb).reshape(frames, 9, width)
+    time_raw = plane_pieces(time_column, time)
+    dense_piece, time_column = lax.optimization_barrier((packed(dense), time_column))
     dense_column = line_rotated(dense_piece)
-    full_expand, full_shrink = unpacked(lax.all_gather(dense_column, "dp", axis=0), dense)
-    n1, qkv1, attn1 = spatial_forward(frames_in, mod, full_spatial_in, sinb)
-    branch1, after1, n2 = project_forward(frames_in, attn1, mod, full_spatial_out, soutb)
-    near_left = passed_along(n2[frames - WINDOW :], "frame", 1)
-    near_right = passed_along(n2[:WINDOW], "frame", -1)
-    qkv2 = (mm(n2.reshape(-1, width), full_temporal_in) + tinb).astype(BF16)
-    qkv2 = qkv2.reshape(frames, patches, 3 * width)
+    dense_raw = plane_pieces(dense_column, dense)
+    n1, qkv1, attn1 = spatial_forward(frames_in, mod, space_raw, sinb)
+    branch1, after1, n2 = project_forward(frames_in, attn1, mod, space_raw, soutb)
+    near_left = passed_along(n2[frames - WINDOW :], FRAME, 1)
+    near_right = passed_along(n2[:WINDOW], FRAME, -1)
+    qkv2 = temporal_qkv(n2, time_raw, tinb)
     seg_row = segments[0]
     seg_pad = jnp.pad(seg_row, (WINDOW, WINDOW), constant_values=-1)
     nearby = lax.dynamic_slice_in_dim(seg_pad, place * frames, frames + 2 * WINDOW)
     own_seg = nearby[WINDOW : WINDOW + frames]
     allowed = jnp.stack([nearby[o : o + frames] == own_seg for o in range(SPAN)]).astype(jnp.int32)
     probs, attn2, branch2, after2, left, right = temporal_forward(
-        allowed, qkv2, near_left, near_right, after1, mod, full_temporal_in, tinb,
-        full_temporal_out, toutb,
+        allowed, qkv2, near_left, near_right, after1, mod, time_raw, tinb, toutb
     )
     frames_out, g2, n3, act, dpre, db3, dmod3, sum_exp, sum_shr = feed_forward(
-        after2, cotangent, mod, full_expand, expb, full_shrink, shrb
+        after2, cotangent, mod, dense_raw, expb, shrb
     )
     plain = list(range(groups))
     hidden = dpre.shape[-1]
@@ -874,12 +1025,12 @@
     feed = outer_pieces(
         [[(act, db3, 0, 1)]], width, groups, parts, plain, total_rows=high, into=feed
     )
-    feed = lax.psum_scatter(feed.reshape(-1, width), "dp", scatter_dimension=0, tiled=True)
+    feed = lax.psum_scatter(feed.reshape(-1, width), DP, scatter_dimension=0, tiled=True)
     db2, dqkv2, dleft, dright, nleft, nright, dgate2, sum_tout, sum_tin = temporal_backward(
-        g2, branch2, mod, full_temporal_out, full_temporal_in, qkv2, left, right, probs
-    )
-    from_right = passed_along(nleft, "frame", -1)
-    from_left = passed_along(nright, "frame", 1)
+        g2, branch2, mod, time_raw, qkv2, left, right, probs
+    )
+    from_right = passed_along(nleft, FRAME, -1)
+    from_left = passed_along(nright, FRAME, 1)
     order = core_order()
     halo = lambda t: [(near_left, dleft, t, 1), (near_right, dright, t, 1)]
     temporal = outer_pieces(
@@ -892,11 +1043,10 @@
         width, groups, parts, order,
     )
     temporal = halved(temporal, 0)
-    dn2 = mm_nt(dqkv2.reshape(-1, 3 * width), full_temporal_in).reshape(frames, patches, width)
-    dn2, temporal = lax.optimization_barrier((dn2, temporal))
+    dqkv2, temporal = lax.optimization_barrier((dqkv2, temporal))
     temporal = plane_summed(temporal)
     g1, db1, da1, dmod1, sum_sout = project_backward(
-        dn2, from_left, from_right, after1, g2, branch1, mod, full_spatial_out
+        dqkv2, from_left, from_right, after1, g2, branch1, mod, time_raw, space_raw
     )
     cond_float = condition.astype(F32)
     own_act = jax.nn.silu(cond_float).astype(BF16)
@@ -904,32 +1054,31 @@
     early_mod = early_mod.reshape(frames, 7 * width).astype(BF16)
     early_sums = [s[0] for s in (sum_sout, sum_tin, sum_tout, sum_exp, sum_shr)]
     early_rows = jnp.concatenate(early_sums).astype(BF16).reshape(frames, -1)
-    early = line_rotated(jnp.concatenate([own_act, early_mod, early_rows], axis=1))
+    early = jnp.concatenate([own_act, early_mod, early_rows], axis=1)
     dheads, sum_first = heads_backward(qkv1, da1, 0)
+    dheads, temporal, feed, early = lax.optimization_barrier((dheads, temporal, feed, early))
+    early = line_rotated(early)
+    feed = jnp.concatenate([feed.reshape(parts, high, width), temporal.astype(BF16)], axis=1)
+    total_high = feed.shape[1]
+    feed = lax.psum_scatter(
+        feed.reshape(-1, width), FRAME, scatter_dimension=0, tiled=True
+    )
+    part = width // 2
+    first = outer_pieces([[(n1, dheads, 0, 3)], [(attn1, db1, 0, 2)]], part, groups, parts, plain)
+    dheads, first, early = lax.optimization_barrier((dheads, first, early))
     early_rows = jnp.sum(early[:, :, 8 * width :].astype(F32), axis=0).astype(BF16)
     early = early[:, :, : 8 * width].reshape(parts * frames, 8 * width)
     early_group = early[:, width:]
     early = jnp.concatenate([early, early_rows.reshape(parts * frames, -1)], axis=1)
-    dheads, temporal, feed, early = lax.optimization_barrier((dheads, temporal, feed, early))
-    early = lax.all_gather(early, "dp", axis=0, tiled=True)
-    feed = jnp.concatenate([feed.reshape(parts, high, width), temporal], axis=1)
-    total_high = feed.shape[1]
-    feed = lax.psum_scatter(
-        feed.reshape(-1, width), "frame", scatter_dimension=0, tiled=True
-    )
-    part = width // 2
-    first = outer_pieces(
-        [[(n1, dheads, 0, 3)], [(attn1, db1, 0, 2)]], part, groups, parts, plain
-    )
-    dheads, first = lax.optimization_barrier((dheads, first))
+    early = lax.all_gather(early, DP, axis=0, tiled=True)
     first = dp_summed_start(first)
     dtail, sum_last, grad_frames, dmod0 = heads_backward(
-        qkv1, da1, 1, (dheads, g1, frames_in, mod, full_spatial_in)
+        qkv1, da1, 1, (dheads, g1, frames_in, mod, space_raw)
     )
     dtail, dmod0, sum_first, sum_last, feed = lax.optimization_barrier(
         (dtail, dmod0, sum_first, sum_last, feed)
     )
-    feed = lax.all_gather(feed, "dp", axis=0, tiled=True).reshape(groups, total_high, width)
+    feed = lax.all_gather(feed, DP, axis=0, tiled=True).reshape(groups, total_high, width)
     sums = [s[0].reshape(3, part) for s in (sum_first, sum_last)]
     sum_sin = jnp.stack(sums, axis=1).reshape(1, 3 * width)
     late_mod = dmod0.reshape(frames, 2 * width).astype(BF16)
@@ -944,13 +1093,9 @@
     late_group = late[:, :, : 2 * width].reshape(parts * frames, 2 * width)
     both = line_summed(jnp.concatenate([first, last], axis=1))
     sizes = [first.shape[1], last.shape[1], 4 * parts * frames, 3 * width // part]
-    both = plane_gathered(
-        jnp.concatenate(
-            [both, late_group.reshape(-1, part), late_rows.reshape(-1, part)], axis=0
-        )
-    )
-    cuts = [sum(sizes[: at + 1]) for at in range(3)]
-    first, last, late, late_rows = jnp.split(both, cuts, axis=1)
+    sizes = [first.shape[1], last.shape[1], 4 * parts * frames, 3 * width // part]
+    piece = [both.astype(BF16), stacked(late_group, part), late_rows.reshape(-1, part)]
+    both = plane_gathered(jnp.concatenate(piece, axis=0))
     blocks = lambda whole, count: jnp.split(whole, count, axis=1)
     flat = lambda pieces: jnp.concatenate(
         [p.reshape(-1, p.shape[-1]) for p in pieces], axis=1
@@ -958,18 +1103,38 @@
     feed, temporal = feed[:, :high], feed[:, high:]
     *wide, narrow = blocks(temporal, 4)
     grad_temporal_in_sum, grad_temporal_out_sum = flat(wide), flat([narrow])
-    starts, ends = blocks(first, 5), blocks(last, 3)
-    grad_spatial_in_sum = flat([p for pair in zip(starts[:3], ends) for p in pair])
-    grad_spatial_out_sum = flat(starts[3:])
     wide = unstacked(feed[:, : high // 2], hidden // width)
     grad_expand_sum = wide.reshape(-1, hidden).astype(F32)
     grad_shrink_sum = feed[:, high // 2 :].reshape(-1, width).astype(F32)
+    (
+        both,
+        early,
+        grad_temporal_in_sum,
+        grad_temporal_out_sum,
+        grad_expand_sum,
+        grad_shrink_sum,
+    ) = lax.optimization_barrier(
+        (both, early, grad_temporal_in_sum, grad_temporal_out_sum, grad_expand_sum, grad_shrink_sum)
+    )
     rows = modulate_weight.shape[0]
     own_columns = lax.dynamic_slice_in_dim(early[:, :width], place * rows, rows, axis=1)
-    late_all = late.reshape(groups * parts * frames, 2 * width)
-    dmod_all = jnp.concatenate([late_all, early[:, width : 8 * width]], axis=1)
-    grad_modulate_weight = mm_tn(own_columns, dmod_all)
-    grad_modulate_bias = own_part(jnp.sum(dmod_all.astype(F32), axis=0))
+    early_mod = early[:, width : 8 * width]
+    if rows // groups % 8 == 0 and groups <= 8:
+        outs = last_outputs(both, own_columns, early_mod, sizes, rows)
+        grad_spatial_in_sum, grad_spatial_out_sum, grad_modulate_weight, mod_sum, sin_sum = outs
+        mod_sum, sin_sum = mod_sum[0], sin_sum.reshape(-1)
+    else:
+        cuts = [sum(sizes[: at + 1]) for at in range(3)]
+        first, last, late, late_rows = jnp.split(in_order(both), cuts, axis=1)
+        starts, ends = blocks(first, 5), blocks(last, 3)
+        grad_spatial_in_sum = flat([p for pair in zip(starts[:3], ends) for p in pair])
+        grad_spatial_out_sum = flat(starts[3:])
+        late_all = unstacked(late, 4).reshape(groups * parts * frames, 2 * width)
+        dmod_all = jnp.concatenate([late_all, early_mod], axis=1)
+        grad_modulate_weight = mm_tn(own_columns, dmod_all)
+        mod_sum = jnp.sum(dmod_all.astype(F32), axis=0)
+        sin_sum = jnp.sum(late_rows.astype(F32), axis=0).reshape(-1)
+    grad_modulate_bias = own_part(mod_sum)
     dact_group = mm_nt(late_group, modulate_weight[:, : 2 * width])
     dact_group = dact_group + mm_nt(early_group, modulate_weight[:, 2 * width :])
     pieces_act = line_swapped(dact_group.reshape(parts, frames, rows))
@@ -977,8 +1142,7 @@
     grad_condition = jax.vjp(jax.nn.silu, cond_float)[1](dcond_act)[0]
     early_rows = early[:, 8 * width :].astype(F32).reshape(groups, parts * frames, -1)
     early_rows = jnp.sum(early_rows, axis=0).reshape(-1)
-    late_rows = jnp.sum(late_rows.astype(F32), axis=0).reshape(-1)
-    bias_sums, at = [own_part(late_rows)], 0
+    bias_sums, at = [own_part(sin_sum)], 0
     for grad in early_sums:
         bias_sums.append(own_part(early_rows[at : at + grad.shape[0]]))
         at += grad.shape[0]
@@ -1005,43 +1169,43 @@
 
 def solution(mesh):
     in_specs = (
-        P(("dp", "frame"), None, None),
-        P(("dp", "frame"), None),
-        P("dp", None),
-        P("frame", None),
-        P("frame"),
-        P("frame", None),
-        P("frame"),
-        P("frame", None),
-        P("frame"),
-        P("frame", None),
-        P("frame"),
-        P("frame", None),
-        P("frame"),
-        P("frame", None),
-        P("frame"),
-        P("frame", None),
-        P("frame"),
-        P(("dp", "frame"), None, None),
+        P((DP, FRAME), None, None),
+        P((DP, FRAME), None),
+        P(DP, None),
+        P(FRAME, None),
+        P(FRAME),
+        P(FRAME, None),
+        P(FRAME),
+        P(FRAME, None),
+        P(FRAME),
+        P(FRAME, None),
+        P(FRAME),
+        P(FRAME, None),
+        P(FRAME),
+        P(FRAME, None),
+        P(FRAME),
+        P(FRAME, None),
+        P(FRAME),
+        P((DP, FRAME), None, None),
     )
     out_specs = (
-        P(("dp", "frame"), None, None),
-        P(("dp", "frame"), None, None),
-        P(("dp", "frame"), None),
-        P("frame", None),
-        P("frame"),
-        P("frame", None),
-        P("frame"),
-        P("frame", None),
-        P("frame"),
-        P("frame", None),
-        P("frame"),
-        P("frame", None),
-        P("frame"),
-        P("frame", None),
-        P("frame"),
-        P("frame", None),
-        P("frame"),
+        P((DP, FRAME), None, None),
+        P((DP, FRAME), None, None),
+        P((DP, FRAME), None),
+        P(FRAME, None),
+        P(FRAME),
+        P(FRAME, None),
+        P(FRAME),
+        P(FRAME, None),
+        P(FRAME),
+        P(FRAME, None),
+        P(FRAME),
+        P(FRAME, None),
+        P(FRAME),
+        P(FRAME, None),
+        P(FRAME),
+        P(FRAME, None),
+        P(FRAME),
     )
 
     return jax.shard_map(

time: 543 us -> 546 us (level)
  blocking collectives: 56.5 us -> 0 us
  waiting for transfers between devices: 92.9 us -> 147 us
  starting transfers between devices: 52.2 us -> 80.6 us
  local copies, waits for them, and re-layouts: 59.8 us -> 35.5 us
  Pallas kernels: 205 us -> 225 us
  matrix products: 22.8 us -> 4.17 us
    all_to_all x3 -> x0, blocking collectives: 56.5 us -> none  [the longest x2 39.6 us: line_gathered(): return lax.all_to_all(copies, 'frame', split_axis=0, concat_axis=0)]
    ppermute x14 -> x39, waiting for transfers between devices: 20.3 us -> 76 us  [the longest x15 35.1 us: line_rotated(): lax.ppermute(mine, FRAME, [(i, (i + far) % parts) for i in range(parts)])]
    ppermute x14 -> x39, starting transfers between devices: 16.5 us -> 55.9 us  [the longest x15 27.8 us: line_rotated(): lax.ppermute(mine, FRAME, [(i, (i + far) % parts) for i in range(parts)])]
    pallas_call x1 -> x3, Pallas kernels: 11 us -> 28.9 us  [the longest x1 14.8 us: project_backward(): pl.pallas_call(project_back_kernel, grid=(frames,), in_specs=[per_first((...]
    transpose x6 -> x0, local copies, waits for them, and re-layouts: 10 us -> none  [unpacked(): jnp.swapaxes(part, 0, 1).reshape(parts * shard.shape[0], shard.shape[1])]
    dot_general x3 -> x2, matrix products: 12.6 us -> 3.63 us  [mm_nt(): lax.dot_general(a, b, (((1,), (1,)), ((), ())), preferred_element_type=F32)]
    all_to_all x6 -> x2, starting transfers between devices: 21.2 us -> 12.5 us  [the longest x1 8.86 us: line_gathered(): return lax.all_to_all(copies, FRAME, split_axis=0, concat_axis=0)]
    add x1 -> x5, other arithmetic: 0.69 us -> 8.1 us  [the longest x2 5.27 us: halved(): return kept.astype(F32) + swapped(sent, bit).astype(F32)]
  transfers between devices with their start and end apart: 31 -> 52, of which waited for: 13 -> 22; matrix products, arithmetic and copies ran while one was open for 16% -> 10% of each run, Pallas kernels for 29% -> 31%
where the time goes in v4:
time: 546 us; the launch traced here: 537 us
  Pallas kernels  225 us (41%)
  waiting for transfers between devices  147 us (27%)
  starting transfers between devices  80.6 us (15%)
  local copies, waits for them, and re-layouts  35.5 us (7%)
  other arithmetic  29.3 us (5%)
  between operations  15.5 us (3%)
    all_to_all x1, waiting for transfers between devices, dp_summed_start(): return lax.all_to_all(blocks, DP, split_axis=0, concat_axis=0)  47.1 us
    pallas_call x5, Pallas kernels, outer_pieces(): pl.pallas_call(functools.partial(outer_kernel, jobs=tuple(terms), order=t...  46.8 us
    pallas_call x2, Pallas kernels, heads_backward(): pl.pallas_call(first_heads_kernel if rest is None else last_heads_kernel,...  41.7 us
    ppermute x15, waiting for transfers between devices, line_rotated(): lax.ppermute(mine, FRAME, [(i, (i + far) % parts) for i in range(parts)])  35.1 us
    pallas_call x1, Pallas kernels, feed_forward(): pl.pallas_call(feed_kernel, grid=(frames,), in_specs=[block(width), block...  31.4 us
    ppermute x15, starting transfers between devices, line_rotated(): lax.ppermute(mine, FRAME, [(i, (i + far) % parts) for i in range(parts)])  27.8 us
    pallas_call x1, Pallas kernels, temporal_backward(): pl.pallas_call(temporal_back_kernel, grid=(patches // tile,), in_specs=[s...  25.5 us
    pallas_call x1, Pallas kernels, temporal_forward(): pl.pallas_call(temporal_kernel, grid=(patches // tile,), in_specs=[pl.Blo...  24.3 us
  transfers between devices with their start and end apart: 52, of which 22 were waited for; matrix products, arithmetic and copies ran while one was open for 10% of the time, Pallas kernels for 31%

profile of v4, /device:TPU:0, one launch (start us, length us, event | category | flops | bytes accessed | tf_op | source)
XLA Modules:
  0.0 536.8 jit_solution(14974388207399522122)
XLA Ops:
  9.0 3.1 collective-permute-start.3
  12.1 2.6 collective-permute-start.4
  16.1 2.9 collective-permute-done.3
  18.9 5.5 %collective-permute-done.4 = bf16[96,768]{1,0:T(8,128)(2,1)S(1)} collective-permute-done((bf16[96,768]{1,0:T(8,128)(2,1)S(1)}, bf16[96,768]{1,0:T(8,128)(2,1)S(1)}, u32[]{:S(2)}, u32[]{:S(2)}) %collective-permute-start.4) | collective-permute-done | bytes 147488 | tf_op jit(solution)/shard_map/ppermute | solution.py:822
  25.5 3.7 collective-permute-start.6
  31.6 3.0 collective-permute-done.6
  34.6 5.2 collective-permute-done.7
  44.2 3.7 collective-permute-start.11
  50.3 7.2 %collective-permute-done.11 = bf16[192,768]{1,0:T(8,128)(2,1)S(1)} collective-permute-done((bf16[192,768]{1,0:T(8,128)(2,1)S(1)}, bf16[192,768]{1,0:T(8,128)(2,1)S(1)}, u32[]{:S(2)}, u32[]{:S(2)}) %collective-permute-start.11) | collective-permute-done | bytes 294944 | tf_op jit(solution)/shard_map/ppermute | solution.py:822
  57.5 11.4 %collective-permute-done.12 = bf16[192,768]{1,0:T(8,128)(2,1)S(1)} collective-permute-done((bf16[192,768]{1,0:T(8,128)(2,1)S(1)}, bf16[192,768]{1,0:T(8,128)(2,1)S(1)}, u32[]{:S(2)}, u32[]{:S(2)}) %collective-permute-start.12) | collective-permute-done | bytes 294944 | tf_op jit(solution)/shard_map/ppermute | solution.py:822
  72.9 8.9 %all-to-all-start = ((bf16[4,2,3648]{2,1,0:T(2,128)(2,1)}), bf16[4,2,3648]{2,1,0:T(2,128)(2,1)S(1)}, u32[]{:S(2)}, u32[]{:S(2)}) async-start(bf16[4,2,3648]{2,1,0:T(2,128)(2,1)} %reshape.376), calls=%async_computation | async-start | bytes 118784 | tf_op jit(solution)/shard_map/all_to_all | solution.py:797
  83.4 4.1 all-to-all-done
  89.8 2.5 collective-permute-start.2
  96.0 2.6 collective-permute-done.1
  99.4 19.2 %spatial_forward.1 = (bf16[4,256,768]{2,1,0:T(8,128)(2,1)}, bf16[4,256,2304]{2,1,0:T(8,128)(2,1)}, bf16[4,256,768]{2,1,0:T(8,128)(2,1)}) custom-call(bf16[4,256,768]{2,1,0:T(8,128)(2,1)} %x_ref.5, f32[4,9,768]{2,1,0:T(8,128)} %reshape.316.mod_ref, bf16[8,4,96,768]{3,2,1,0:T(8,128)(2,1)} %bitcast.162, f32[1,2304]{1,0:T(1,128)} %reshape.354.bsi), custom_call_target="tpu_custom_call" | custom-call | flops 5234491392 | bytes 12000000 | tf_op jit(solution)/shard_map/spatial_forward/pallas_call | solution.py:132
  118.6 6.8 %project_forward.1 = (f32[4,256,768]{2,1,0:T(8,128)}, f32[4,256,768]{2,1,0:T(8,128)}, bf16[4,256,768]{2,1,0:T(8,128)(2,1)}) custom-call(bf16[4,256,768]{2,1,0:T(8,128)(2,1)} %x_ref.5, bf16[4,256,768]{2,1,0:T(8,128)(2,1)} %get-tuple-element.97.attn_ref, f32[4,9,768]{2,1,0:T(8,128)} %reshape.316.mod_ref, bf16[8,4,96,768]{3,2,1,0:T(8,128)(2,1)} %bitcast.163, ...), custom_call_target="tpu_custom_call" | custom-call | flops 1207959552 | bytes 13000000 | tf_op jit(solution)/shard_map/project_forward/pallas_call | solution.py:161
  128.2 5.2 collective-permute-start.9
  136.8 8.1 %temporal_qkv.1.qkv_ref = bf16[4,256,2304]{2,1,0:T(8,128)(2,1)} custom-call(bf16[4,256,768]{2,1,0:T(8,128)(2,1)} %get-tuple-element.98.n_ref, bf16[8,4,96,768]{3,2,1,0:T(8,128)(2,1)} %bitcast.153, f32[1,2304]{1,0:T(1,128)} %reshape.356.bias.bti), custom_call_target="tpu_custom_call" | custom-call | flops 3623878656 | bytes 10000000 | tf_op jit(solution)/shard_map/temporal_qkv/pallas_call | solution.py:183
  144.9 3.5 collective-permute-done.10.nr_ref
  150.4 24.3 %temporal_forward.1 = (f32[4,5,256,128]{3,2,1,0:T(8,128)}, bf16[4,256,768]{2,1,0:T(8,128)(2,1)}, f32[4,256,768]{2,1,0:T(8,128)}, f32[4,256,768]{2,1,0:T(8,128)},...) custom-call(s32[5,4]{1,0:T(8,128)} %convert_element_type.266.allowed, ...), custom_call_target="tpu_custom_call" | custom-call | flops 4353687552 | bytes 22000000 | tf_op jit(solution)/shard_map/temporal_forward/pallas_call | solution.py:276
  174.7 31.4 %feed_forward.1 = (bf16[4,256,768]{2,1,0:T(8,128)(2,1)}, f32[4,256,768]{2,1,0:T(8,128)}, bf16[4,256,768]{2,1,0:T(8,128)(2,1)}, bf16[4,256,3072]{2,1,0:T(8,128)(2...) custom-call(f32[4,256,768]{2,1,0:T(8,128)} %get-tuple-element.101.af, ...), custom_call_target="tpu_custom_call" | custom-call | flops 19327352832 | bytes 32000000 | tf_op jit(solution)/shard_map/feed_forward/pallas_call | solution.py:357
  206.2 10.1 %outer_pieces.6.refs_2_ = bf16[8,4,192,768]{3,2,1,0:T(8,128)(2,1)} custom-call(bf16[1024,768]{1,0:T(8,128)(2,1)} %bitcast.226, bf16[1024,3072]{1,0:T(8,128)(2,1)} %bitcast.223), custom_call_target="tpu_custom_call" | custom-call | flops 4831838208 | bytes 12000000 | tf_op jit(solution)/shard_map/outer_pieces/pallas_call | solution.py:705
  216.2 9.2 %outer_pieces.7 = bf16[8,4,192,768]{3,2,1,0:T(8,128)(2,1)} custom-call(bf16[1024,3072]{1,0:T(8,128)(2,1)} %bitcast.168, bf16[1024,768]{1,0:T(8,128)(2,1)} %bitcast.180, bf16[8,4,192,768]{3,2,1,0:T(8,128)(2,1)} %outer_pieces.6.refs_2_), custom_call_target="tpu_custom_call", output_to_operand_aliasing={{}: (2, {})} | custom-call | flops 4831838208 | bytes 12000000 | tf_op jit(solution)/shard_map/outer_pieces/pallas_call | solution.py:705
  225.5 25.5 %temporal_backward.1 = (bf16[4,256,768]{2,1,0:T(8,128)(2,1)}, bf16[4,256,2304]{2,1,0:T(8,128)(2,1)}, bf16[2,256,1536]{2,1,0:T(8,128)(2,1)}, bf16[2,256,1536]{2,1...) custom-call(f32[4,256,768]{2,1,0:T(8,128)} %get-tuple-element.105.g_, ...), custom_call_target="tpu_custom_call" | custom-call | flops 5140119552 | bytes 36000000 | tf_op jit(solution)/shard_map/temporal_backward/pallas_call | solution.py:459
  251.1 14.6 %outer_pieces.5 = bf16[8,4,96,768]{3,2,1,0:T(8,128)(2,1)} custom-call(bf16[1024,768]{1,0:T(8,128)(2,1)} %bitcast.169, bf16[1024,2304]{1,0:T(8,128)(2,1)} %bitcast.159, bf16[1024,2304]{1,0:T(8,128)(2,1)} %bitcast.160, bf16[512,768]{1,0:T(8,128)(2,1)} %bitcast.177, bf16[512,1536]{1,0:T(8,128)(2,1)} %bitcast.170, bf16[512,768]{1,0:T(8,128)(2,1)} %bitcast.176, ...), custom_call_target="tpu_custom_call" | custom-call | flops 7247757312 | bytes 12000000 | tf_op jit(solution)/shard_map/outer_pieces/pallas_call | solution.py:705
  268.0 4.1 collective-permute-start.15
  273.7 5.1 convert_add_fusion
  278.8 11.0 %collective-permute-done.15.fl_ref = bf16[2,256,768]{2,1,0:T(8,128)(2,1)S(1)} collective-permute-done((bf16[2,256,768]{2,1,0:T(8,128)(2,1)}, bf16[2,256,768]{2,1,0:T(8,128)(2,1)S(1)}, u32[]{:S(2)}, u32[]{:S(2)}) %collective-permute-start.15) | collective-permute-done | bytes 786464 | tf_op jit(solution)/shard_map/ppermute | solution.py:882
  289.8 4.2 collective-permute-done.16.fr_ref
  294.0 14.8 %project_backward.1 = (f32[4,256,768]{2,1,0:T(8,128)}, bf16[4,256,768]{2,1,0:T(8,128)(2,1)}, bf16[4,256,768]{2,1,0:T(8,128)(2,1)}, f32[4,3,768]{2,1,0:T(4,128)}, f32[1,768]{1,0:T(1,128)}) custom-call(bf16[4,256,2304]{2,1,0:T(8,128)(2,1)} %get-tuple-element.115.dqkv_ref, bf16[2,256,768]{2,1,0:T(8,128)(2,1)} %copy-done.7, ...), custom_call_target="tpu_custom_call" | custom-call | flops 4831838208 | bytes 24000000 | tf_op jit(solution)/shard_map/project_backward/pallas_call | solution.py:519
  317.4 16.1 %first_heads_backward.1 = (bf16[4,256,1152]{2,1,0:T(8,128)(2,1)}, f32[1,1152]{1,0:T(1,128)}) custom-call(bf16[4,256,2304]{2,1,0:T(8,128)(2,1)} %get-tuple-element.104.q_ref.k_ref.v_ref, bf16[4,256,2304]{2,1,0:T(8,128)(2,1)} %get-tuple-element.104.q_ref.k_ref.v_ref, bf16[4,256,2304]{2,1,0:T(8,128)(2,1)} %get-tuple-element.104.q_ref.k_ref.v_ref, ...), custom_call_target="tpu_custom_call" | custom-call | flops 2013265920 | bytes 16000000 | tf_op jit(solution)/shard_map/first_heads_backward/pallas_call | solution.py:613
  333.5 8.8 %collective-permute-done.18 = bf16[4,96,768]{2,1,0:T(8,128)(2,1)S(1)} collective-permute-done((bf16[4,96,768]{2,1,0:T(8,128)(2,1)S(1)}, bf16[4,96,768]{2,1,0:T(8,128)(2,1)S(1)}, u32[]{:S(2)}, u32[]{:S(2)}) %collective-permute-start.18) | collective-permute-done | bytes 589856 | tf_op jit(solution)/shard_map/ppermute | solution.py:917
  343.9 2.6 pad_maximum_fusion
  348.4 2.8 collective-permute-start.22
  351.2 7.6 %outer_pieces.8 = bf16[8,4,120,384]{3,2,1,0:T(8,128)(2,1)} custom-call(bf16[1024,768]{1,0:T(8,128)(2,1)} %bitcast.224, bf16[1024,1152]{1,0:T(8,128)(2,1)} %bitcast.178, bf16[1024,768]{1,0:T(8,128)(2,1)} %bitcast.181, bf16[1024,768]{1,0:T(8,128)(2,1)} %bitcast.221), custom_call_target="tpu_custom_call" | custom-call | flops 3019898880 | bytes 12000000 | tf_op jit(solution)/shard_map/outer_pieces/pallas_call | solution.py:705
  359.4 25.6 %last_heads_backward.1 = (bf16[4,256,1152]{2,1,0:T(8,128)(2,1)}, f32[1,1152]{1,0:T(1,128)}, f32[4,256,768]{2,1,0:T(8,128)}, f32[4,2,768]{2,1,0:T(2,128)}) custom-call(bf16[4,256,2304]{2,1,0:T(8,128)(2,1)} %get-tuple-element.104.q_ref.k_ref.v_ref, bf16[4,256,2304]{2,1,0:T(8,128)(2,1)} %get-tuple-element.104.q_ref.k_ref.v_ref, ...), custom_call_target="tpu_custom_call" | custom-call | flops 5637144576 | bytes 16000000 | tf_op jit(solution)/shard_map/last_heads_backward/pallas_call | solution.py:613
  385.1 3.7 all-to-all-start.1
  391.4 47.1 %all-to-all-done.1 = bf16[8,4,120,384]{3,2,1,0:T(8,128)(2,1)S(1)} async-done(((bf16[8,4,120,384]{3,2,1,0:T(8,128)(2,1)}), bf16[8,4,120,384]{3,2,1,0:T(8,128)(2,1)S(1)}, u32[]{:S(2)}, u32[]{:S(2)}) %all-to-all-start.1) | async-done | bytes 2949152 | tf_op jit(solution)/shard_map/all_to_all | solution.py:922
  440.9 3.0 collective-permute-start.26
  443.9 5.3 outer_pieces.9
  459.3 2.8 collective-permute-start.29
  466.0 4.6 collective-permute-done.30
  470.6 4.8 collective-permute-done.32
  485.4 4.9 collective-permute-done.34
  505.8 5.1 collective-permute-done.41.refs_6_
  511.0 3.3 collective-permute-done.42.refs_7_
  514.2 2.6 slice.203.refs_9_
  517.8 6.0 %last_outputs.1 = (f32[192,2304]{1,0:T(8,128)}, f32[192,768]{1,0:T(8,128)}, f32[192,6912]{1,0:T(8,128)}, f32[1,6912]{1,0:T(1,128)}, f32[6,384]{1,0:T(8,128)}) custom-call(s32[1]{0:T(128)} %bitcast.64.own_ref, bf16[262,384]{1,0:T(8,128)(2,1)} %copy-done.9, bf16[262,384]{1,0:T(8,128)(2,1)} %copy-done.10, bf16[262,384]{1,0:T(8,128)(2,1)} %copy-done.11, ...), custom_call_target="tpu_custom_call" | custom-call | flops 339738624 | bytes 12000000 | tf_op jit(solution)/shard_map/last_outputs/pallas_call | solution.py:762
  (300 shorter events, 101.3 us)
Async XLA Ops:
  7.2 92.2 %all-gather.13.cloned.1.call-start = ((), (), s32[]{:S(2)}) async-start(), calls=%async_computation.8 | async-start | bytes 5308416 | tf_op jit(solution)/shard_map/all_gather | solution.py:845
  9.0 9.9 %collective-permute-start.3 = (bf16[96,768]{1,0:T(8,128)(2,1)S(1)}, bf16[96,768]{1,0:T(8,128)(2,1)S(1)}, u32[]{:S(2)}, u32[]{:S(2)}) collective-permute-start(bf16[96,768]{1,0:T(8,128)(2,1)S(1)} %get-tuple-element.220), channel_id=1, source_target_pairs={{0,1},{1,2},{2,3},{3,0},{4,5},{5,6},{6,7},{7,4},{8,9},{9,10},{10,1... | collective-permute-start | bytes 442376 | tf_op jit(solution)/shard_map/ppermute | solution.py:822
  12.1 12.3 %collective-permute-start.4 = (bf16[96,768]{1,0:T(8,128)(2,1)S(1)}, bf16[96,768]{1,0:T(8,128)(2,1)S(1)}, u32[]{:S(2)}, u32[]{:S(2)}) collective-permute-start(bf16[96,768]{1,0:T(8,128)(2,1)S(1)} %get-tuple-element.220), channel_id=1, source_target_pairs={{0,2},{1,3},{2,0},{3,1},{4,6},{5,7},{6,4},{7,5},{8,10},{9,11},{10,... | collective-permute-start | bytes 442376 | tf_op jit(solution)/shard_map/ppermute | solution.py:822
  14.7 9.7 %collective-permute-start.5 = (bf16[96,768]{1,0:T(8,128)(2,1)S(1)}, bf16[96,768]{1,0:T(8,128)(2,1)S(1)}, u32[]{:S(2)}, u32[]{:S(2)}) collective-permute-start(bf16[96,768]{1,0:T(8,128)(2,1)S(1)} %get-tuple-element.220), channel_id=1, source_target_pairs={{0,3},{1,0},{2,1},{3,2},{4,7},{5,4},{6,5},{7,6},{8,11},{9,8},{10,9... | collective-permute-start | bytes 442376 | tf_op jit(solution)/shard_map/ppermute | solution.py:822
  25.5 111.3 %all-gather.15.cloned.1.call-start = ((), (), s32[]{:S(2)}) async-start(), calls=%async_computation.9 | async-start | bytes 5308416 | tf_op jit(solution)/shard_map/all_gather | solution.py:845
  25.5 9.1 %collective-permute-start.6 = (bf16[96,768]{1,0:T(8,128)(2,1)S(1)}, bf16[96,768]{1,0:T(8,128)(2,1)S(1)}, u32[]{:S(2)}, u32[]{:S(2)}) collective-permute-start(bf16[96,768]{1,0:T(8,128)(2,1)S(1)} %pad_maximum_fusion.11), channel_id=1, source_target_pairs={{0,1},{1,2},{2,3},{3,0},{4,5},{5,6},{6,7},{7,4},{8,9},{9,10},{10,1... | collective-permute-start | bytes 442376 | tf_op jit(solution)/shard_map/ppermute | solution.py:822
  29.2 10.6 %collective-permute-start.7 = (bf16[96,768]{1,0:T(8,128)(2,1)S(1)}, bf16[96,768]{1,0:T(8,128)(2,1)S(1)}, u32[]{:S(2)}, u32[]{:S(2)}) collective-permute-start(bf16[96,768]{1,0:T(8,128)(2,1)S(1)} %pad_maximum_fusion.11), channel_id=1, source_target_pairs={{0,2},{1,3},{2,0},{3,1},{4,6},{5,7},{6,4},{7,5},{8,10},{9,11},{10,... | collective-permute-start | bytes 442376 | tf_op jit(solution)/shard_map/ppermute | solution.py:822
  30.8 9.0 %collective-permute-start.8 = (bf16[96,768]{1,0:T(8,128)(2,1)S(1)}, bf16[96,768]{1,0:T(8,128)(2,1)S(1)}, u32[]{:S(2)}, u32[]{:S(2)}) collective-permute-start(bf16[96,768]{1,0:T(8,128)(2,1)S(1)} %pad_maximum_fusion.11), channel_id=1, source_target_pairs={{0,3},{1,0},{2,1},{3,2},{4,7},{5,4},{6,5},{7,6},{8,11},{9,8},{10,9... | collective-permute-start | bytes 442376 | tf_op jit(solution)/shard_map/ppermute | solution.py:822
  40.9 133.9 %all-gather.17.cloned.1.call-start = ((), (), s32[]{:S(2)}) async-start(), calls=%async_computation.10 | async-start | bytes 10616832 | tf_op jit(solution)/shard_map/all_gather | solution.py:845
  44.2 13.3 %collective-permute-start.11 = (bf16[192,768]{1,0:T(8,128)(2,1)S(1)}, bf16[192,768]{1,0:T(8,128)(2,1)S(1)}, u32[]{:S(2)}, u32[]{:S(2)}) collective-permute-start(bf16[192,768]{1,0:T(8,128)(2,1)S(1)} %dynamic-slice_dynamic-update-slice_fusion), channel_id=1, source_target_pairs={{0,1},{1,2},{2,3},{3,0},{4,5},{5,6},{6,7},{7,4},{8,9},{9,10},{10,1... | collective-permute-start | bytes 884744 | tf_op jit(solution)/shard_map/ppermute | solution.py:822
  47.8 21.0 %collective-permute-start.12 = (bf16[192,768]{1,0:T(8,128)(2,1)S(1)}, bf16[192,768]{1,0:T(8,128)(2,1)S(1)}, u32[]{:S(2)}, u32[]{:S(2)}) collective-permute-start(bf16[192,768]{1,0:T(8,128)(2,1)S(1)} %dynamic-slice_dynamic-update-slice_fusion), channel_id=1, source_target_pairs={{0,2},{1,3},{2,0},{3,1},{4,6},{5,7},{6,4},{7,5},{8,10},{9,11},{10,... | collective-permute-start | bytes 884744 | tf_op jit(solution)/shard_map/ppermute | solution.py:822
  50.0 18.8 %collective-permute-start.13 = (bf16[192,768]{1,0:T(8,128)(2,1)S(1)}, bf16[192,768]{1,0:T(8,128)(2,1)S(1)}, u32[]{:S(2)}, u32[]{:S(2)}) collective-permute-start(bf16[192,768]{1,0:T(8,128)(2,1)S(1)} %dynamic-slice_dynamic-update-slice_fusion), channel_id=1, source_target_pairs={{0,3},{1,0},{2,1},{3,2},{4,7},{5,4},{6,5},{7,6},{8,11},{9,8},{10,9... | collective-permute-start | bytes 884744 | tf_op jit(solution)/shard_map/ppermute | solution.py:822
  72.9 14.6 %all-to-all-start = ((bf16[4,2,3648]{2,1,0:T(2,128)(2,1)}), bf16[4,2,3648]{2,1,0:T(2,128)(2,1)S(1)}, u32[]{:S(2)}, u32[]{:S(2)}) async-start(bf16[4,2,3648]{2,1,0:T(2,128)(2,1)} %reshape.376), calls=%async_computation | async-start | bytes 118784 | tf_op jit(solution)/shard_map/all_to_all | solution.py:797
  81.8 262.1 %reduce-scatter.3.cloned.1.call-start = ((), (), s32[]{:S(2)}) async-start(), calls=%async_computation.4 | async-start | bytes 10616832 | tf_op jit(solution)/shard_map/reduce_scatter | solution.py:1028
  88.5 7.5 %collective-permute-start = (f32[4,6912]{1,0:T(4,128)S(1)}, f32[4,6912]{1,0:T(4,128)S(1)}, u32[]{:S(2)}, u32[]{:S(2)}) collective-permute-start(f32[4,6912]{1,0:T(4,128)S(1)} %get-tuple-element.212), channel_id=1, source_target_pairs={{0,1},{1,2},{2,3},{3,0},{4,5},{5,6},{6,7},{7,4},{8,9},{9,10},{10,1... | collective-permute-start | bytes 331784 | tf_op jit(solution)/shard_map/ppermute | solution.py:932
  89.4 9.2 %collective-permute-start.1 = (f32[4,6912]{1,0:T(4,128)S(1)}, f32[4,6912]{1,0:T(4,128)S(1)}, u32[]{:S(2)}, u32[]{:S(2)}) collective-permute-start(f32[4,6912]{1,0:T(4,128)S(1)} %get-tuple-element.214), channel_id=1, source_target_pairs={{0,2},{1,3},{2,0},{3,1},{4,6},{5,7},{6,4},{7,5},{8,10},{9,11},{10,... | collective-permute-start | bytes 331784 | tf_op jit(solution)/shard_map/ppermute | solution.py:932
  89.8 8.8 %collective-permute-start.2 = (f32[4,6912]{1,0:T(4,128)S(1)}, f32[4,6912]{1,0:T(4,128)S(1)}, u32[]{:S(2)}, u32[]{:S(2)}) collective-permute-start(f32[4,6912]{1,0:T(4,128)S(1)} %get-tuple-element.213), channel_id=1, source_target_pairs={{0,3},{1,0},{2,1},{3,2},{4,7},{5,4},{6,5},{7,6},{8,11},{9,8},{10,9... | collective-permute-start | bytes 331784 | tf_op jit(solution)/shard_map/ppermute | solution.py:932
  126.9 21.4 %collective-permute-start.10 = (bf16[2,256,768]{2,1,0:T(8,128)(2,1)S(1)}, bf16[2,256,768]{2,1,0:T(8,128)(2,1)S(1)}, u32[]{:S(2)}, u32[]{:S(2)}) collective-permute-start(bf16[2,256,768]{2,1,0:T(8,128)(2,1)S(1)} %get-tuple-element.189), channel_id=1, source_target_pairs={{1,0},{2,1},{3,2},{5,4},{6,5},{7,6},{9,8},{10,9},{11,10},{13,12},{... | collective-permute-start | bytes 2359304 | tf_op jit(solution)/shard_map/ppermute | solution.py:882
  128.2 21.3 %collective-permute-start.9 = (bf16[2,256,768]{2,1,0:T(8,128)(2,1)S(1)}, bf16[2,256,768]{2,1,0:T(8,128)(2,1)S(1)}, u32[]{:S(2)}, u32[]{:S(2)}) collective-permute-start(bf16[2,256,768]{2,1,0:T(8,128)(2,1)S(1)} %get-tuple-element.190), channel_id=1, source_target_pairs={{0,1},{1,2},{2,3},{4,5},{5,6},{6,7},{8,9},{9,10},{10,11},{12,13},{... | collective-permute-start | bytes 2359304 | tf_op jit(solution)/shard_map/ppermute | solution.py:882
  225.5 159.6 %reduce-scatter.5.cloned.1.call-start = ((), (), s32[]{:S(2)}) async-start(), calls=%async_computation.5 | async-start | bytes 2211840 | tf_op jit(solution)/shard_map/reduce_scatter | solution.py:1063
  268.0 21.8 %collective-permute-start.15 = (bf16[2,256,768]{2,1,0:T(8,128)(2,1)}, bf16[2,256,768]{2,1,0:T(8,128)(2,1)S(1)}, u32[]{:S(2)}, u32[]{:S(2)}) collective-permute-start(bf16[2,256,768]{2,1,0:T(8,128)(2,1)} %get-tuple-element.116), channel_id=1, source_target_pairs={{0,1},{1,2},{2,3},{4,5},{5,6},{6,7},{8,9},{9,10},{10,11},{12,13},{... | collective-permute-start | bytes 2359304 | tf_op jit(solution)/shard_map/ppermute | solution.py:882
  272.2 21.8 %collective-permute-start.16 = (bf16[2,256,768]{2,1,0:T(8,128)(2,1)}, bf16[2,256,768]{2,1,0:T(8,128)(2,1)}, u32[]{:S(2)}, u32[]{:S(2)}) collective-permute-start(bf16[2,256,768]{2,1,0:T(8,128)(2,1)} %get-tuple-element.117), channel_id=1, source_target_pairs={{1,0},{2,1},{3,2},{5,4},{6,5},{7,6},{9,8},{10,9},{11,10},{13,12},{... | collective-permute-start | bytes 2359304 | tf_op jit(solution)/shard_map/ppermute | solution.py:882
  313.9 19.7 %collective-permute-start.17 = (bf16[4,96,768]{2,1,0:T(8,128)(2,1)S(1)}, bf16[4,96,768]{2,1,0:T(8,128)(2,1)S(1)}, u32[]{:S(2)}, u32[]{:S(2)}) collective-permute-start(bf16[4,96,768]{2,1,0:T(8,128)(2,1)S(1)} %get-tuple-element.175), channel_id=1, source_target_pairs={{0,8},{4,12},{8,0},{12,4},{16,24},{20,28},{24,16},{28,20},{1,9},{5... | collective-permute-start | bytes 1769480 | tf_op jit(solution)/shard_map/ppermute | solution.py:917
  315.4 26.9 %collective-permute-start.18 = (bf16[4,96,768]{2,1,0:T(8,128)(2,1)S(1)}, bf16[4,96,768]{2,1,0:T(8,128)(2,1)S(1)}, u32[]{:S(2)}, u32[]{:S(2)}) collective-permute-start(bf16[4,96,768]{2,1,0:T(8,128)(2,1)S(1)} %get-tuple-element.177), channel_id=1, source_target_pairs={{0,16},{4,20},{8,24},{12,28},{16,0},{20,4},{24,8},{28,12},{1,17},{... | collective-permute-start | bytes 1769480 | tf_op jit(solution)/shard_map/ppermute | solution.py:917
  316.9 25.5 %collective-permute-start.19 = (bf16[4,96,768]{2,1,0:T(8,128)(2,1)S(1)}, bf16[4,96,768]{2,1,0:T(8,128)(2,1)S(1)}, u32[]{:S(2)}, u32[]{:S(2)}) collective-permute-start(bf16[4,96,768]{2,1,0:T(8,128)(2,1)S(1)} %get-tuple-element.176), channel_id=1, source_target_pairs={{0,24},{4,28},{8,16},{12,20},{16,8},{20,12},{24,0},{28,4},{1,25},{... | collective-permute-start | bytes 1769480 | tf_op jit(solution)/shard_map/ppermute | solution.py:917
  346.5 147.7 %all-gather.11.cloned.1.call-start = ((), (), s32[]{:S(2)}) async-start(), calls=%async_computation.7 | async-start | bytes 3981312 | tf_op jit(solution)/shard_map/all_gather | solution.py:1081
  346.6 12.2 %collective-permute-start.20 = (bf16[4,8064]{1,0:T(4,128)(2,1)S(1)}, bf16[4,8064]{1,0:T(4,128)(2,1)S(1)}, u32[]{:S(2)}, u32[]{:S(2)}) collective-permute-start(bf16[4,8064]{1,0:T(4,128)(2,1)S(1)} %pad_maximum_fusion.15), channel_id=1, source_target_pairs={{0,1},{1,2},{2,3},{3,0},{4,5},{5,6},{6,7},{7,4},{8,9},{9,10},{10,1... | collective-permute-start | bytes 193544 | tf_op jit(solution)/shard_map/ppermute | solution.py:822
  348.3 10.5 %collective-permute-start.21 = (bf16[4,8064]{1,0:T(4,128)(2,1)S(1)}, bf16[4,8064]{1,0:T(4,128)(2,1)S(1)}, u32[]{:S(2)}, u32[]{:S(2)}) collective-permute-start(bf16[4,8064]{1,0:T(4,128)(2,1)S(1)} %pad_maximum_fusion.15), channel_id=1, source_target_pairs={{0,2},{1,3},{2,0},{3,1},{4,6},{5,7},{6,4},{7,5},{8,10},{9,11},{10,... | collective-permute-start | bytes 193544 | tf_op jit(solution)/shard_map/ppermute | solution.py:822
  348.4 10.4 %collective-permute-start.22 = (bf16[4,8064]{1,0:T(4,128)(2,1)S(1)}, bf16[4,8064]{1,0:T(4,128)(2,1)S(1)}, u32[]{:S(2)}, u32[]{:S(2)}) collective-permute-start(bf16[4,8064]{1,0:T(4,128)(2,1)S(1)} %pad_maximum_fusion.15), channel_id=1, source_target_pairs={{0,3},{1,0},{2,1},{3,2},{4,7},{5,4},{6,5},{7,6},{8,11},{9,8},{10,9... | collective-permute-start | bytes 193544 | tf_op jit(solution)/shard_map/ppermute | solution.py:822
  385.1 53.4 %all-to-all-start.1 = ((bf16[8,4,120,384]{3,2,1,0:T(8,128)(2,1)}), bf16[8,4,120,384]{3,2,1,0:T(8,128)(2,1)S(1)}, u32[]{:S(2)}, u32[]{:S(2)}) async-start(bf16[8,4,120,384]{3,2,1,0:T(8,128)(2,1)} %outer_pieces.8), calls=%async_computation.3 | async-start | bytes 5898240 | tf_op jit(solution)/shard_map/all_to_all | solution.py:922
  388.8 117.0 %all-gather.9.cloned.1.call-start = ((), (), s32[]{:S(2)}) async-start(), calls=%async_computation.6 | async-start | bytes 1916928 | tf_op jit(solution)/shard_map/all_gather | solution.py:1073
  440.0 10.6 %collective-permute-start.24 = (bf16[4,2112]{1,0:T(4,128)(2,1)S(1)}, bf16[4,2112]{1,0:T(4,128)(2,1)S(1)}, u32[]{:S(2)}, u32[]{:S(2)}) collective-permute-start(bf16[4,2112]{1,0:T(4,128)(2,1)S(1)} %constant_dynamic-update-slice_fusion), channel_id=1, source_target_pairs={{0,1},{1,2},{2,3},{3,0},{4,5},{5,6},{6,7},{7,4},{8,9},{9,10},{10,1... | collective-permute-start | bytes 50696 | tf_op jit(solution)/shard_map/ppermute | solution.py:822
  440.1 10.6 %collective-permute-start.25 = (bf16[4,2112]{1,0:T(4,128)(2,1)S(1)}, bf16[4,2112]{1,0:T(4,128)(2,1)S(1)}, u32[]{:S(2)}, u32[]{:S(2)}) collective-permute-start(bf16[4,2112]{1,0:T(4,128)(2,1)S(1)} %constant_dynamic-update-slice_fusion), channel_id=1, source_target_pairs={{0,2},{1,3},{2,0},{3,1},{4,6},{5,7},{6,4},{7,5},{8,10},{9,11},{10,... | collective-permute-start | bytes 50696 | tf_op jit(solution)/shard_map/ppermute | solution.py:822
  440.9 9.8 %collective-permute-start.26 = (bf16[4,2112]{1,0:T(4,128)(2,1)S(1)}, bf16[4,2112]{1,0:T(4,128)(2,1)S(1)}, u32[]{:S(2)}, u32[]{:S(2)}) collective-permute-start(bf16[4,2112]{1,0:T(4,128)(2,1)S(1)} %constant_dynamic-update-slice_fusion), channel_id=1, source_target_pairs={{0,3},{1,0},{2,1},{3,2},{4,7},{5,4},{6,5},{7,6},{8,11},{9,8},{10,9... | collective-permute-start | bytes 50696 | tf_op jit(solution)/shard_map/ppermute | solution.py:822
  457.8 8.1 %collective-permute-start.28 = (f32[4,192]{1,0:T(4,128)S(1)}, f32[4,192]{1,0:T(4,128)S(1)}, u32[]{:S(2)}, u32[]{:S(2)}) collective-permute-start(f32[4,192]{1,0:T(4,128)S(1)} %get-tuple-element.239), channel_id=1, source_target_pairs={{0,2},{1,3},{2,0},{3,1},{4,6},{5,7},{6,4},{7,5},{8,10},{9,11},{10,... | collective-permute-start | bytes 9224 | tf_op jit(solution)/shard_map/ppermute | solution.py:807
  462.2 8.5 %collective-permute-start.30 = (bf16[4,72,384]{2,1,0:T(8,128)(2,1)S(1)}, bf16[4,72,384]{2,1,0:T(8,128)(2,1)}, u32[]{:S(2)}, u32[]{:S(2)}) collective-permute-start(bf16[4,72,384]{2,1,0:T(8,128)(2,1)S(1)} %get-tuple-element.186), channel_id=1, source_target_pairs={{0,8},{4,12},{8,0},{12,4},{16,24},{20,28},{24,16},{28,20},{1,9},{5... | collective-permute-start | bytes 663560 | tf_op jit(solution)/shard_map/ppermute | solution.py:917
  462.2 8.4 %collective-permute-start.31 = (bf16[4,72,384]{2,1,0:T(8,128)(2,1)S(1)}, bf16[4,72,384]{2,1,0:T(8,128)(2,1)}, u32[]{:S(2)}, u32[]{:S(2)}) collective-permute-start(bf16[4,72,384]{2,1,0:T(8,128)(2,1)S(1)} %get-tuple-element.188), channel_id=1, source_target_pairs={{0,16},{4,20},{8,24},{12,28},{16,0},{20,4},{24,8},{28,12},{1,17},{... | collective-permute-start | bytes 663560 | tf_op jit(solution)/shard_map/ppermute | solution.py:917
  463.5 11.9 %collective-permute-start.32 = (bf16[4,72,384]{2,1,0:T(8,128)(2,1)S(1)}, bf16[4,72,384]{2,1,0:T(8,128)(2,1)}, u32[]{:S(2)}, u32[]{:S(2)}) collective-permute-start(bf16[4,72,384]{2,1,0:T(8,128)(2,1)S(1)} %get-tuple-element.187), channel_id=1, source_target_pairs={{0,24},{4,28},{8,16},{12,20},{16,8},{20,12},{24,0},{28,4},{1,25},{... | collective-permute-start | bytes 663560 | tf_op jit(solution)/shard_map/ppermute | solution.py:917
  476.7 8.7 %collective-permute-start.33 = (bf16[192,384]{1,0:T(8,128)(2,1)S(1)}, bf16[192,384]{1,0:T(8,128)(2,1)S(1)}, u32[]{:S(2)}, u32[]{:S(2)}) collective-permute-start(bf16[192,384]{1,0:T(8,128)(2,1)S(1)} %get-tuple-element.191), channel_id=1, source_target_pairs={{0,1},{1,2},{2,3},{3,0},{4,5},{5,6},{6,7},{7,4},{8,9},{9,10},{10,1... | collective-permute-start | bytes 442376 | tf_op jit(solution)/shard_map/ppermute | solution.py:932
  478.3 12.1 %collective-permute-start.34 = (bf16[192,384]{1,0:T(8,128)(2,1)S(1)}, bf16[192,384]{1,0:T(8,128)(2,1)S(1)}, u32[]{:S(2)}, u32[]{:S(2)}) collective-permute-start(bf16[192,384]{1,0:T(8,128)(2,1)S(1)} %get-tuple-element.192), channel_id=1, source_target_pairs={{0,2},{1,3},{2,0},{3,1},{4,6},{5,7},{6,4},{7,5},{8,10},{9,11},{10,... | collective-permute-start | bytes 442376 | tf_op jit(solution)/shard_map/ppermute | solution.py:932
  480.5 9.9 %collective-permute-start.35 = (bf16[192,384]{1,0:T(8,128)(2,1)S(1)}, bf16[192,384]{1,0:T(8,128)(2,1)S(1)}, u32[]{:S(2)}, u32[]{:S(2)}) collective-permute-start(bf16[192,384]{1,0:T(8,128)(2,1)S(1)} %get-tuple-element.193), channel_id=1, source_target_pairs={{0,3},{1,0},{2,1},{3,2},{4,7},{5,4},{6,5},{7,6},{8,11},{9,8},{10,9... | collective-permute-start | bytes 442376 | tf_op jit(solution)/shard_map/ppermute | solution.py:932
  490.5 11.6 %collective-permute-start.36 = (bf16[262,384]{1,0:T(8,128)(2,1)S(1)}, bf16[262,384]{1,0:T(8,128)(2,1)S(1)}, u32[]{:S(2)}, u32[]{:S(2)}) collective-permute-start(bf16[262,384]{1,0:T(8,128)(2,1)S(1)} %constant_dynamic-update-slice_fusion.2.refs_0_), channel_id=1, source_target_pairs={{0,4},{4,0},{8,12},{12,8},{16,20},{20,16},{24,28},{28,24},{1,5},{5... | collective-permute-start | bytes 603656 | tf_op jit(solution)/shard_map/ppermute | solution.py:942
  490.6 12.0 %collective-permute-start.37 = (bf16[262,384]{1,0:T(8,128)(2,1)S(1)}, bf16[262,384]{1,0:T(8,128)(2,1)S(1)}, u32[]{:S(2)}, u32[]{:S(2)}) collective-permute-start(bf16[262,384]{1,0:T(8,128)(2,1)S(1)} %constant_dynamic-update-slice_fusion.2.refs_0_), channel_id=1, source_target_pairs={{0,8},{4,12},{8,0},{12,4},{16,24},{20,28},{24,16},{28,20},{1,9},{5... | collective-permute-start | bytes 603656 | tf_op jit(solution)/shard_map/ppermute | solution.py:942
  491.2 14.5 %collective-permute-start.38 = (bf16[262,384]{1,0:T(8,128)(2,1)S(1)}, bf16[262,384]{1,0:T(8,128)(2,1)S(1)}, u32[]{:S(2)}, u32[]{:S(2)}) collective-permute-start(bf16[262,384]{1,0:T(8,128)(2,1)S(1)} %constant_dynamic-update-slice_fusion.2.refs_0_), channel_id=1, source_target_pairs={{0,12},{4,8},{8,4},{12,0},{16,28},{20,24},{24,20},{28,16},{1,13},{... | collective-permute-start | bytes 603656 | tf_op jit(solution)/shard_map/ppermute | solution.py:942
  492.5 13.3 %collective-permute-start.39 = (bf16[262,384]{1,0:T(8,128)(2,1)S(1)}, bf16[262,384]{1,0:T(8,128)(2,1)S(1)}, u32[]{:S(2)}, u32[]{:S(2)}) collective-permute-start(bf16[262,384]{1,0:T(8,128)(2,1)S(1)} %constant_dynamic-update-slice_fusion.2.refs_0_), channel_id=1, source_target_pairs={{0,16},{4,20},{8,24},{12,28},{16,0},{20,4},{24,8},{28,12},{1,17},{... | collective-permute-start | bytes 603656 | tf_op jit(solution)/shard_map/ppermute | solution.py:942
  492.8 13.0 %collective-permute-start.40 = (bf16[262,384]{1,0:T(8,128)(2,1)S(1)}, bf16[262,384]{1,0:T(8,128)(2,1)S(1)}, u32[]{:S(2)}, u32[]{:S(2)}) collective-permute-start(bf16[262,384]{1,0:T(8,128)(2,1)S(1)} %constant_dynamic-update-slice_fusion.2.refs_0_), channel_id=1, source_target_pairs={{0,20},{4,16},{8,28},{12,24},{16,4},{20,0},{24,12},{28,8},{1,21},{... | collective-permute-start | bytes 603656 | tf_op jit(solution)/shard_map/ppermute | solution.py:942
  502.1 8.8 %collective-permute-start.41 = (bf16[262,384]{1,0:T(8,128)(2,1)S(1)}, bf16[262,384]{1,0:T(8,128)(2,1)S(1)}, u32[]{:S(2)}, u32[]{:S(2)}) collective-permute-start(bf16[262,384]{1,0:T(8,128)(2,1)S(1)} %constant_dynamic-update-slice_fusion.2.refs_0_), channel_id=1, source_target_pairs={{0,24},{4,28},{8,16},{12,20},{16,8},{20,12},{24,0},{28,4},{1,25},{... | collective-permute-start | bytes 603656 | tf_op jit(solution)/shard_map/ppermute | solution.py:942
  502.6 11.6 %collective-permute-start.42 = (bf16[262,384]{1,0:T(8,128)(2,1)S(1)}, bf16[262,384]{1,0:T(8,128)(2,1)S(1)}, u32[]{:S(2)}, u32[]{:S(2)}) collective-permute-start(bf16[262,384]{1,0:T(8,128)(2,1)S(1)} %constant_dynamic-update-slice_fusion.2.refs_0_), channel_id=1, source_target_pairs={{0,28},{4,24},{8,20},{12,16},{16,12},{20,8},{24,4},{28,0},{1,29},{... | collective-permute-start | bytes 603656 | tf_op jit(solution)/shard_map/ppermute | solution.py:942
  (41 other events, 415.8 us)
Sparse Core Ops, SparseCore 0:
  25.6 41.1 all-gather.12
  69.2 38.7 all-gather.14
  110.5 58.6 all-gather.16
  225.6 78.0 reduce-scatter.2
  346.6 36.9 reduce-scatter.4
  385.3 53.8 all-gather.10
  441.7 25.1 all-gather.8

commit v5 on v4

--- a/solution.py
+++ b/solution.py
@@ -134,7 +134,7 @@
         grid=(frames,),
         in_specs=[
             block(width), per_first(mod.shape[1:]),
-            rows_of(space, 3, 4), fixed(bsi.shape),
+            rows_of(space, 1, 1), fixed(bsi.shape),
         ],
         out_specs=[block(n) for n in outs],
         out_shape=[jax.ShapeDtypeStruct((frames, patches, n), BF16) for n in outs],
@@ -154,7 +154,7 @@
     n2_ref[0] = (xhat * (1.0 + mod_ref[0, 4:5]) + mod_ref[0, 3:4]).astype(BF16)
 
 
-def project_forward(x, attn, mod, space, bso):
+def project_forward(x, attn, mod, time, bso):
     frames, patches, width = x.shape
     block = per_first((patches, width))
     tokens = frames * patches
@@ -162,14 +162,14 @@
         project_kernel,
         grid=(frames,),
         in_specs=[
-            block, block, per_first(mod.shape[1:]), rows_of(space, 1, 4, 3), fixed(bso.shape)
+            block, block, per_first(mod.shape[1:]), rows_of(time, 1, 5, 4), fixed(bso.shape)
         ],
         scratch_shapes=[pltpu.VMEM((width, width), BF16)],
         out_specs=[block] * 3,
         out_shape=[jax.ShapeDtypeStruct(x.shape, t) for t in (F32, F32, BF16)],
         name="project_forward",
         **params(2 * tokens * width * width, 13e6),
-    )(x, attn, mod, space, bso)
+    )(x, attn, mod, time, bso)
 
 
 def qkv_kernel(n_ref, raw, bias, out_ref, whole):
@@ -183,7 +183,7 @@
     return pl.pallas_call(
         qkv_kernel,
         grid=(frames,),
-        in_specs=[per_first((patches, width)), rows_of(time, 3, 4), fixed(bias.shape)],
+        in_specs=[per_first((patches, width)), rows_of(time, 3, 5), fixed(bias.shape)],
         out_specs=per_first((patches, 3 * width)),
         out_shape=jax.ShapeDtypeStruct((frames, patches, 3 * width), BF16),
         scratch_shapes=[pltpu.VMEM((width, 3 * width), BF16)],
@@ -192,12 +192,6 @@
     )(n, time, bias)
 
 
-def split_store(hi_ref, lo_ref, row, prod):
-    hi = prod.astype(BF16)
-    hi_ref[row] = hi
-    lo_ref[row] = (prod - hi.astype(F32)).astype(BF16)
-
-
 def ext_rows(e, frames, left, own, right, base, width):
     if e < WINDOW:
         return left[e, :, base - width : base]
@@ -206,16 +200,14 @@
     return right[e - WINDOW - frames, :, base - width : base]
 
 
-def head_sums(hi_ref, lo_ref, first, count, ones):
-    tile, width = hi_ref.shape[1:]
-    hi = hi_ref[first : first + count].reshape(count * tile, width)
-    lo = lo_ref[first : first + count].reshape(count * tile, width)
-    return mm(hi, ones) + mm(lo, ones)
+def head_sums(prod_ref, first, count, ones):
+    tile, width = prod_ref.shape[1:]
+    return mm(prod_ref[first : first + count].reshape(count * tile, width), ones)
 
 
 def temporal_kernel(
     allowed, qkv_ref, nl_ref, nr_ref, after_ref, mod_ref, raw_in, bti, raw_out, bto, ones, ones_t,
-    probs_ref, attn_ref, branch_ref, out_ref, left_ref, right_ref, hi_ref, lo_ref, wkv, wto,
+    probs_ref, attn_ref, branch_ref, out_ref, left_ref, right_ref, prod_ref, wkv, wto,
 ):
     frames, tile, width = after_ref.shape
     lay_out(raw_in, wkv, 1)
@@ -227,9 +219,9 @@
         q = qkv_ref[t, :, :width].astype(F32)
         for o in range(SPAN):
             k = ext_rows(t + o, frames, left_ref, qkv_ref, right_ref, width, width)
-            split_store(hi_ref, lo_ref, t * SPAN + o, q * k.astype(F32))
+            prod_ref[t * SPAN + o] = (q * k.astype(F32)).astype(BF16)
     for t in range(frames):
-        raw = head_sums(hi_ref, lo_ref, t * SPAN, SPAN, ones[...]) * SCALE
+        raw = head_sums(prod_ref, t * SPAN, SPAN, ones[...]) * SCALE
         raw = [
             jnp.where(allowed[o, t] > 0, raw[o * tile : (o + 1) * tile], -1e30)
             for o in range(SPAN)
@@ -279,7 +271,7 @@
         in_specs=[
             pl.BlockSpec(memory_space=pltpu.SMEM),
             spec(3 * width), near, near, spec(width), fixed(mod.shape),
-            rows_of(time, 3, 4), fixed(bti.shape), rows_of(time, 1, 4, 3), fixed(bto.shape),
+            rows_of(time, 3, 5), fixed(bti.shape), rows_of(time, 1, 5, 3), fixed(bto.shape),
             fixed(ones.shape), fixed(ones.shape[::-1]),
         ],
         out_specs=[
@@ -292,7 +284,7 @@
             jax.ShapeDtypeStruct((WINDOW, patches, 2 * width), BF16),
             jax.ShapeDtypeStruct((WINDOW, patches, 2 * width), BF16),
         ],
-        scratch_shapes=[pltpu.VMEM((frames * SPAN, tile, width), BF16)] * 2
+        scratch_shapes=[pltpu.VMEM((frames * SPAN, tile, width), BF16)]
         + [pltpu.VMEM((width, 2 * width), BF16), pltpu.VMEM((width, width), BF16)],
         name="temporal_forward",
         **params(2 * tokens * width * (width + SPAN * 400), 22e6, tokens * SPAN * 128),
@@ -376,7 +368,7 @@
 def temporal_back_kernel(
     g_ref, branch_ref, mod_ref, raw_out, raw_in, qkv_ref, left_ref, right_ref, probs_ref, ones, ones_t,
     db_ref, dqkv_ref, dleft_ref, dright_ref, nleft_ref, nright_ref, dgate_ref, sum_ref, sumq_ref,
-    hi_ref, lo_ref, da_ref, ds_ref, pw_ref, wkv, wto,
+    prod_ref, da_ref, ds_ref, pw_ref, wkv, wto,
 ):
     frames, tile, width = g_ref.shape
     lay_out(raw_in, wkv, 1)
@@ -400,9 +392,9 @@
         da = da_ref[t].astype(F32)
         for o in range(SPAN):
             v = ext_rows(t + o, frames, left_ref, qkv_ref, right_ref, 2 * width, width)
-            split_store(hi_ref, lo_ref, t * SPAN + o, da * v.astype(F32))
+            prod_ref[t * SPAN + o] = (da * v.astype(F32)).astype(BF16)
     for t in range(frames):
-        dp = head_sums(hi_ref, lo_ref, t * SPAN, SPAN, ones[...])
+        dp = head_sums(prod_ref, t * SPAN, SPAN, ones[...])
         probs = probs_ref[t].reshape(SPAN * tile, 128)
         both = probs * dp
         dot = both[:tile]
@@ -460,7 +452,7 @@
         temporal_back_kernel,
         grid=(patches // tile,),
         in_specs=[
-            spec(width), spec(width), fixed(mod.shape), rows_of(time, 1, 4, 3), rows_of(time, 3, 4),
+            spec(width), spec(width), fixed(mod.shape), rows_of(time, 1, 5, 3), rows_of(time, 3, 5),
             spec(3 * width), halo, halo,
             pl.BlockSpec((frames, SPAN, tile, 128), lambda i: (0, 0, i, 0)),
             fixed(ones.shape), fixed(ones.shape[::-1]),
@@ -478,7 +470,7 @@
             jax.ShapeDtypeStruct((frames, width), F32), jax.ShapeDtypeStruct((1, width), F32),
             jax.ShapeDtypeStruct((1, 3 * width), F32),
         ],
-        scratch_shapes=[pltpu.VMEM((frames * SPAN, tile, width), BF16)] * 2
+        scratch_shapes=[pltpu.VMEM((frames * SPAN, tile, width), BF16)]
         + [pltpu.VMEM((frames, tile, width), BF16)]
         + [pltpu.VMEM((frames * SPAN, tile, width), BF16)] * 2
         + [pltpu.VMEM((width, 2 * width), BF16), pltpu.VMEM((width, width), BF16)],
@@ -512,7 +504,7 @@
     da_ref[0] = mm_nt(db, wso[...]).astype(BF16)
 
 
-def project_backward(dqkv2, from_left, from_right, after, g2, branch, mod, time, space):
+def project_backward(dqkv2, from_left, from_right, after, g2, branch, mod, time):
     frames, patches, width = after.shape
     block = per_first((patches, width))
     tokens = frames * patches
@@ -523,7 +515,7 @@
             per_first((patches, 3 * width)),
             pl.BlockSpec((1, patches, width), lambda i: (jnp.minimum(i, WINDOW - 1), 0, 0)),
             pl.BlockSpec((1, patches, width), lambda i: (jnp.maximum(i - WINDOW, 0), 0, 0)),
-            block, block, block, per_first(mod.shape[1:]), rows_of(time, 3, 4), rows_of(space, 1, 4, 3),
+            block, block, block, per_first(mod.shape[1:]), rows_of(time, 3, 5), rows_of(time, 1, 5, 4),
         ],
         scratch_shapes=[pltpu.VMEM((width, 3 * width), BF16), pltpu.VMEM((width, width), BF16)],
         out_specs=[block, block, block, per_first((3, width)),
@@ -532,7 +524,7 @@
         + [jax.ShapeDtypeStruct((frames, 3, width), F32), jax.ShapeDtypeStruct((1, width), F32)],
         name="project_backward",
         **params(8 * tokens * width * width, 24e6),
-    )(dqkv2, from_left, from_right, after, g2, branch, mod, time, space)
+    )(dqkv2, from_left, from_right, after, g2, branch, mod, time, time)
 
 
 def heads_back(q_ref, k_ref, v_ref, da_ref, out_ref, sum_ref):
@@ -602,7 +594,7 @@
     if rest is not None:
         first, g1, x, mod, space = rest
         in_specs += [block(3 * part), block(width), block(width), per_first(mod.shape[1:]),
-                     rows_of(space, 3, 4)]
+                     rows_of(space, 1, 1)]
         operands += [first, g1, x, mod, space]
         scratch = [pltpu.VMEM((width, 3 * width), BF16)]
         out_specs += [block(width), per_first((2, width))]
@@ -623,9 +615,9 @@
     )(*operands)
 
 
-def outer_kernel(*refs, jobs, order):
-    out_ref = refs[-1]
-    parts = out_ref.shape[1]
+def outer_kernel(*refs, jobs, order, split):
+    refs, out_refs = (refs[:-2], refs[-2:]) if split else (refs[:-1], refs[-1:])
+    parts, width = out_refs[0].shape[1], out_refs[0].shape[3]
     groups = len(order)
     top = 0
     turned = {}
@@ -637,18 +629,31 @@
             term = mm(turned[left], refs[right][...])
             total = term if total is None else total + term
         rows = total.shape[0] // (groups * parts)
-        width = out_ref.shape[3]
-        for tile in range(total.shape[1] // width):
-            for f in range(parts):
-                for d in range(groups):
-                    row = (f * groups + d) * rows
-                    out_ref[order[d], f, top : top + rows] = total[
-                        row : row + rows, tile * width : (tile + 1) * width
-                    ].astype(BF16)
-            top += rows
-
-
-def outer_pieces(jobs, width, groups, parts, order, total_rows=None, into=None):
+
+        def write(first, total=total, top=top):
+            for tile in range(total.shape[1] // width):
+                for f in range(parts):
+                    for d in range(groups):
+                        row = (f * groups + d) * rows
+                        at = order[d]
+                        ref = out_refs[0]
+                        if split:
+                            ref = out_refs[at // (groups // 2) ^ first]
+                            at = at % (groups // 2)
+                        ref[at, f, top + tile * rows : top + (tile + 1) * rows] = total[
+                            row : row + rows, tile * width : (tile + 1) * width
+                        ].astype(BF16)
+
+        if split:
+            core = refs[-1][0]
+            pl.when(core == 0)(functools.partial(write, 0))
+            pl.when(core == 1)(functools.partial(write, 1))
+        else:
+            write(0)
+        top += rows * (total.shape[1] // width)
+
+
+def outer_pieces(jobs, width, groups, parts, order, total_rows=None, into=None, core=None):
     shaped = {}
 
     def flat(a):
@@ -668,7 +673,12 @@
                 total = total.astype(BF16).reshape(parts, groups, rows, width).swapaxes(0, 1)
                 pieces.append(jnp.stack([total[order.index(d)] for d in range(groups)]))
         whole = jnp.concatenate(pieces, axis=2)
-        return jnp.pad(whole, ((0, 0), (0, 0), (0, total_rows - whole.shape[2]), (0, 0)))
+        whole = jnp.pad(whole, ((0, 0), (0, 0), (0, total_rows - whole.shape[2]), (0, 0)))
+        if core is None:
+            return whole
+        half = groups // 2
+        part = lambda number: lax.dynamic_slice_in_dim(whole, number * half, half)
+        return part(core), part(1 - core)
     step = 1
     while (step * depth // parts) % 128:
         step *= 2
@@ -702,12 +712,19 @@
         aliases = {len(operands): 0}
         specs.append(pl.BlockSpec(memory_space=pl.ANY))
         operands.append(into)
+    split = core is not None
+    if split:
+        specs.append(pl.BlockSpec(memory_space=pltpu.SMEM))
+        operands.append(core.reshape(1))
+    lead = groups // 2 if split else groups
+    spec = pl.BlockSpec((lead, step, height, width), lambda i: (0, i, place, 0))
+    shape = jax.ShapeDtypeStruct((lead, parts, total_rows, width), BF16)
     return pl.pallas_call(
-        functools.partial(outer_kernel, jobs=tuple(terms), order=tuple(order)),
+        functools.partial(outer_kernel, jobs=tuple(terms), order=tuple(order), split=split),
         grid=(parts // step,),
         in_specs=specs,
-        out_specs=pl.BlockSpec((groups, step, height, width), lambda i: (0, i, place, 0)),
-        out_shape=jax.ShapeDtypeStruct((groups, parts, total_rows, width), BF16),
+        out_specs=[spec] * 2 if split else spec,
+        out_shape=[shape] * 2 if split else shape,
         input_output_aliases=aliases,
         name="outer_pieces",
         **params(flops, 12e6),
@@ -772,6 +789,46 @@
     )(own, *pieces, columns, early)
 
 
+def feed_outputs_kernel(
+    piece, expand_ref, shrink_ref, in_ref, out_ref, act_ref, mod_ref, sum_ref
+):
+    width = piece.shape[2]
+    at = 0
+    for ref in (expand_ref, shrink_ref, in_ref, out_ref, act_ref, mod_ref):
+        height = ref.shape[0]
+        for tile in range(ref.shape[1] // width):
+            block = piece[0, at : at + height]
+            ref[:, tile * width : (tile + 1) * width] = block.astype(ref.dtype)
+            at += height
+
+    @pl.when(pl.program_id(0) == 0)
+    def _():
+        sum_ref[...] = jnp.zeros_like(sum_ref)
+
+    sum_ref[...] += piece[0, at:].astype(F32)
+
+
+def feed_outputs(feed, hidden, rows, tall):
+    groups, height, width = feed.shape
+    more = hidden // width
+    shapes = [
+        (rows, hidden, F32), (more * rows, width, F32), (rows, 3 * width, F32), (rows, width, F32),
+        (tall, width, BF16), (tall, 7 * width, BF16),
+    ]
+    left = height - 2 * more * rows - 4 * rows - 8 * tall
+    return pl.pallas_call(
+        feed_outputs_kernel,
+        grid=(groups,),
+        in_specs=[pl.BlockSpec((1, height, width), lambda d: (d, 0, 0))],
+        out_specs=[pl.BlockSpec((h, w), lambda d: (d, 0)) for h, w, _ in shapes]
+        + [pl.BlockSpec((left, width), lambda d: (0, 0))],
+        out_shape=[jax.ShapeDtypeStruct((groups * h, w), t) for h, w, t in shapes]
+        + [jax.ShapeDtypeStruct((left, width), F32)],
+        name="feed_outputs",
+        **params(0, 15e6),
+    )(feed)
+
+
 def own_part(vector):
     size = vector.shape[0] // lax.axis_size(FRAME)
     return lax.dynamic_slice_in_dim(vector, lax.axis_index(FRAME) * size, size)
@@ -829,9 +886,8 @@
     )
 
 
-def packed(shards):
+def packed(shards, width):
     groups = lax.axis_size(DP)
-    width = min(shard.shape[1] for shard in shards)
     pieces = []
     for shard in shards:
         rows = shard.shape[0] // groups
@@ -890,12 +946,8 @@
     return lax.ppermute(x, DP, [(i, i ^ (1 << bit)) for i in range(lax.axis_size(DP))])
 
 
-def halved(blocks, bit):
-    half = blocks.shape[0] // 2
-    mine = own_bit(bit)
-    sent = lax.dynamic_slice_in_dim(blocks, (1 - mine) * half, half)
-    kept = lax.dynamic_slice_in_dim(blocks, mine * half, half)
-    return kept.astype(F32) + swapped(sent, bit).astype(F32)
+def paired(kept, sent):
+    return kept.astype(F32) + swapped(sent, 0).astype(F32)
 
 
 def summed(pieces):
@@ -975,7 +1027,7 @@
     groups, parts = lax.axis_size(DP), lax.axis_size(FRAME)
     place = lax.axis_index(FRAME)
     frames, _, width = frames_in.shape
-    space, time = [spatial_in, spatial_out], [temporal_in, temporal_out]
+    space, time = [spatial_in], [temporal_in, temporal_out, spatial_out]
     dense = [expand_weight, shrink_weight]
     biases = [
         spatial_in_bias,
@@ -986,8 +1038,8 @@
         shrink_bias,
         modulate_bias,
     ]
-    space_column = line_rotated(packed(space))
-    time_piece, space_column = lax.optimization_barrier((packed(time), space_column))
+    space_column = line_rotated(packed(space, width))
+    time_piece, space_column = lax.optimization_barrier((packed(time, width), space_column))
     time_column = line_rotated(time_piece)
     *full_biases, cond_group = gathered_small(biases, condition)
     space_raw = plane_pieces(space_column, space)
@@ -997,11 +1049,11 @@
     partial = line_summed(partial, F32)
     mod = (partial + modb).reshape(frames, 9, width)
     time_raw = plane_pieces(time_column, time)
-    dense_piece, time_column = lax.optimization_barrier((packed(dense), time_column))
+    dense_piece, time_column = lax.optimization_barrier((packed(dense, width), time_column))
     dense_column = line_rotated(dense_piece)
     dense_raw = plane_pieces(dense_column, dense)
     n1, qkv1, attn1 = spatial_forward(frames_in, mod, space_raw, sinb)
-    branch1, after1, n2 = project_forward(frames_in, attn1, mod, space_raw, soutb)
+    branch1, after1, n2 = project_forward(frames_in, attn1, mod, time_raw, soutb)
     near_left = passed_along(n2[frames - WINDOW :], FRAME, 1)
     near_right = passed_along(n2[:WINDOW], FRAME, -1)
     qkv2 = temporal_qkv(n2, time_raw, tinb)
@@ -1040,13 +1092,13 @@
             [(n2, dqkv2, 2, 1)] + halo(1),
             [(attn2, db2, 0, 1)],
         ],
-        width, groups, parts, order,
-    )
-    temporal = halved(temporal, 0)
+        width, groups, parts, order, core=own_bit(0),
+    )
+    temporal = paired(*temporal)
     dqkv2, temporal = lax.optimization_barrier((dqkv2, temporal))
     temporal = plane_summed(temporal)
     g1, db1, da1, dmod1, sum_sout = project_backward(
-        dqkv2, from_left, from_right, after1, g2, branch1, mod, time_raw, space_raw
+        dqkv2, from_left, from_right, after1, g2, branch1, mod, time_raw
     )
     cond_float = condition.astype(F32)
     own_act = jax.nn.silu(cond_float).astype(BF16)
@@ -1069,29 +1121,31 @@
     early_rows = jnp.sum(early[:, :, 8 * width :].astype(F32), axis=0).astype(BF16)
     early = early[:, :, : 8 * width].reshape(parts * frames, 8 * width)
     early_group = early[:, width:]
-    early = jnp.concatenate([early, early_rows.reshape(parts * frames, -1)], axis=1)
-    early = lax.all_gather(early, DP, axis=0, tiled=True)
+    early = jnp.concatenate([stacked(early, width), early_rows.reshape(-1, width)], axis=0)
     first = dp_summed_start(first)
     dtail, sum_last, grad_frames, dmod0 = heads_backward(
         qkv1, da1, 1, (dheads, g1, frames_in, mod, space_raw)
     )
-    dtail, dmod0, sum_first, sum_last, feed = lax.optimization_barrier(
-        (dtail, dmod0, sum_first, sum_last, feed)
-    )
-    feed = lax.all_gather(feed, DP, axis=0, tiled=True).reshape(groups, total_high, width)
+    dtail, dmod0, sum_first, sum_last, feed, early = lax.optimization_barrier(
+        (dtail, dmod0, sum_first, sum_last, feed, early)
+    )
+    whole_high = total_high + early.shape[0]
+    feed = jnp.concatenate([feed, early], axis=0)
+    feed = lax.all_gather(feed, DP, axis=0, tiled=True).reshape(groups, whole_high, width)
     sums = [s[0].reshape(3, part) for s in (sum_first, sum_last)]
     sum_sin = jnp.stack(sums, axis=1).reshape(1, 3 * width)
     late_mod = dmod0.reshape(frames, 2 * width).astype(BF16)
     late_rows = sum_sin.astype(BF16).reshape(frames, -1)
     late = line_rotated(jnp.concatenate([late_mod, late_rows], axis=1))
-    last = outer_pieces([[(n1, dtail, 0, 3)]], part, groups, parts, order)
-    last = halved(last, 0)
+    last = outer_pieces([[(n1, dtail, 0, 3)]], part, groups, parts, order, core=own_bit(0))
+    last = paired(*last)
     first = summed(first)
     last, first, late = lax.optimization_barrier((last, first, late))
     last = plane_summed(last)
     late_rows = jnp.sum(late[:, :, 2 * width :].astype(F32), axis=0).astype(BF16)
     late_group = late[:, :, : 2 * width].reshape(parts * frames, 2 * width)
     both = line_summed(jnp.concatenate([first, last], axis=1))
+    late_held, both = lax.optimization_barrier((late_group, both))
     sizes = [first.shape[1], last.shape[1], 4 * parts * frames, 3 * width // part]
     sizes = [first.shape[1], last.shape[1], 4 * parts * frames, 3 * width // part]
     piece = [both.astype(BF16), stacked(late_group, part), late_rows.reshape(-1, part)]
@@ -1100,25 +1154,49 @@
     flat = lambda pieces: jnp.concatenate(
         [p.reshape(-1, p.shape[-1]) for p in pieces], axis=1
     ).astype(F32)
-    feed, temporal = feed[:, :high], feed[:, high:]
-    *wide, narrow = blocks(temporal, 4)
-    grad_temporal_in_sum, grad_temporal_out_sum = flat(wide), flat([narrow])
-    wide = unstacked(feed[:, : high // 2], hidden // width)
-    grad_expand_sum = wide.reshape(-1, hidden).astype(F32)
-    grad_shrink_sum = feed[:, high // 2 :].reshape(-1, width).astype(F32)
+    tall = parts * frames
+    share = modulate_weight.shape[0] // groups
+    if share % 8 == 0:
+        (
+            grad_expand_sum,
+            grad_shrink_sum,
+            grad_temporal_in_sum,
+            grad_temporal_out_sum,
+            acts,
+            early_mod,
+            early_rows,
+        ) = feed_outputs(feed, hidden, share, tall)
+        early_rows = early_rows.reshape(-1)
+    else:
+        early = feed[:, total_high:]
+        acts = early[:, :tall].reshape(-1, width)
+        pick = lambda k: early[:, k * tall : (k + 1) * tall].reshape(-1, width)
+        early_mod = jnp.concatenate([pick(k) for k in range(1, 8)], axis=1)
+        early_rows = jnp.sum(early[:, 8 * tall :].astype(F32), axis=0).reshape(-1)
+        feed, temporal = feed[:, :high], feed[:, high:total_high]
+        *wide, narrow = blocks(temporal, 4)
+        grad_temporal_in_sum, grad_temporal_out_sum = flat(wide), flat([narrow])
+        wide = unstacked(feed[:, : high // 2], hidden // width)
+        grad_expand_sum = wide.reshape(-1, hidden).astype(F32)
+        grad_shrink_sum = feed[:, high // 2 :].reshape(-1, width).astype(F32)
+    early_biases, at = [], 0
+    for grad in early_sums:
+        early_biases.append(own_part(early_rows[at : at + grad.shape[0]]))
+        at += grad.shape[0]
     (
         both,
-        early,
+        acts,
+        early_mod,
+        early_biases,
         grad_temporal_in_sum,
         grad_temporal_out_sum,
         grad_expand_sum,
         grad_shrink_sum,
     ) = lax.optimization_barrier(
-        (both, early, grad_temporal_in_sum, grad_temporal_out_sum, grad_expand_sum, grad_shrink_sum)
+        (both, acts, early_mod, early_biases, grad_temporal_in_sum, grad_temporal_out_sum, grad_expand_sum, grad_shrink_sum)
     )
     rows = modulate_weight.shape[0]
-    own_columns = lax.dynamic_slice_in_dim(early[:, :width], place * rows, rows, axis=1)
-    early_mod = early[:, width : 8 * width]
+    own_columns = lax.dynamic_slice_in_dim(acts, place * rows, rows, axis=1)
     if rows // groups % 8 == 0 and groups <= 8:
         outs = last_outputs(both, own_columns, early_mod, sizes, rows)
         grad_spatial_in_sum, grad_spatial_out_sum, grad_modulate_weight, mod_sum, sin_sum = outs
@@ -1135,17 +1213,12 @@
         mod_sum = jnp.sum(dmod_all.astype(F32), axis=0)
         sin_sum = jnp.sum(late_rows.astype(F32), axis=0).reshape(-1)
     grad_modulate_bias = own_part(mod_sum)
-    dact_group = mm_nt(late_group, modulate_weight[:, : 2 * width])
+    dact_group = mm_nt(late_held, modulate_weight[:, : 2 * width])
     dact_group = dact_group + mm_nt(early_group, modulate_weight[:, 2 * width :])
     pieces_act = line_swapped(dact_group.reshape(parts, frames, rows))
     dcond_act = jnp.swapaxes(pieces_act, 0, 1).reshape(frames, parts * rows)
     grad_condition = jax.vjp(jax.nn.silu, cond_float)[1](dcond_act)[0]
-    early_rows = early[:, 8 * width :].astype(F32).reshape(groups, parts * frames, -1)
-    early_rows = jnp.sum(early_rows, axis=0).reshape(-1)
-    bias_sums, at = [own_part(sin_sum)], 0
-    for grad in early_sums:
-        bias_sums.append(own_part(early_rows[at : at + grad.shape[0]]))
-        at += grad.shape[0]
+    bias_sums = [own_part(sin_sum)] + early_biases
     return (
         frames_out,
         grad_frames,

time: 546 us -> 543 us (level)
  blocking collectives: 0 us -> 52.8 us
  waiting for transfers between devices: 147 us -> 99.1 us
  other arithmetic: 29.3 us -> 22.3 us
    all_to_all x0 -> x1, blocking collectives: none -> 52.8 us  [dp_summed_start(): return lax.all_to_all(blocks, DP, split_axis=0, concat_axis=0)]
    all_to_all x1 -> x0, waiting for transfers between devices: 47.1 us -> none  [dp_summed_start(): return lax.all_to_all(blocks, DP, split_axis=0, concat_axis=0)]
    pallas_call x1, Pallas kernels: 24.3 us -> 15.8 us  [temporal_forward(): pl.pallas_call(temporal_kernel, grid=(patches // tile,), in_specs=[pl.Blo...]
    pallas_call x0 -> x1, Pallas kernels: none -> 7.85 us  [feed_outputs(): pl.pallas_call(feed_outputs_kernel, grid=(groups,), in_specs=[pl.BlockSpe...]
    pallas_call x5, Pallas kernels: 46.8 us -> 53.1 us  [outer_pieces(): pl.pallas_call(functools.partial(outer_kernel, jobs=tuple(terms), order=t...]
    convert_element_type x4 -> x0, other arithmetic: 5.59 us -> none  [the longest x2 2.2 us: per_device(): flat = lambda pieces: jnp.concatenate([p.reshape(-1, p.shape[-1]) for p i...]
  transfers between devices with their start and end apart: 52 -> 50, of which waited for: 22 -> 22; matrix products, arithmetic and copies ran while one was open for 10% -> 9% of each run, Pallas kernels for 31% -> 33%
where the time goes in v5:
time: 543 us; the launch traced here: 533 us
  Pallas kernels  230 us (42%)
  waiting for transfers between devices  99.1 us (18%)
  starting transfers between devices  77.6 us (14%)
  blocking collectives  52.8 us (10%)
  local copies, waits for them, and re-layouts  32.2 us (6%)
  other arithmetic  22.3 us (4%)
  between operations  15.4 us (3%)
    pallas_call x5, Pallas kernels, outer_pieces(): pl.pallas_call(functools.partial(outer_kernel, jobs=tuple(terms), order=t...  53.1 us
    all_to_all x1, blocking collectives, dp_summed_start(): return lax.all_to_all(blocks, DP, split_axis=0, concat_axis=0)  52.8 us
    pallas_call x2, Pallas kernels, heads_backward(): pl.pallas_call(first_heads_kernel if rest is None else last_heads_kernel,...  42.1 us
    pallas_call x1, Pallas kernels, feed_forward(): pl.pallas_call(feed_kernel, grid=(frames,), in_specs=[block(width), block...  31.4 us
    ppermute x15, waiting for transfers between devices, line_rotated(): lax.ppermute(mine, FRAME, [(i, (i + far) % parts) for i in range(parts)])  31.3 us
    ppermute x15, starting transfers between devices, line_rotated(): lax.ppermute(mine, FRAME, [(i, (i + far) % parts) for i in range(parts)])  27.6 us
    pallas_call x1, Pallas kernels, temporal_backward(): pl.pallas_call(temporal_back_kernel, grid=(patches // tile,), in_specs=[s...  25.2 us
    ppermute x4, waiting for transfers between devices, passed_along(): return lax.ppermute(x, axis, pairs)  20.1 us
  transfers between devices with their start and end apart: 50, of which 22 were waited for; matrix products, arithmetic and copies ran while one was open for 9% of the time, Pallas kernels for 33%

profile of v5, /device:TPU:0, one launch (start us, length us, event | category | flops | bytes accessed | tf_op | source)
XLA Modules:
  0.0 533.5 jit_solution(14117166069401167616)
XLA Ops:
  8.1 3.1 collective-permute-start.3
  11.2 2.6 collective-permute-start.4
  22.1 2.9 collective-permute-start.6
  27.5 4.2 collective-permute-done.6
  31.7 6.8 %collective-permute-done.7 = bf16[120,768]{1,0:T(8,128)(2,1)S(1)} collective-permute-done((bf16[120,768]{1,0:T(8,128)(2,1)S(1)}, bf16[120,768]{1,0:T(8,128)(2,1)S(1)}, u32[]{:S(2)}, u32[]{:S(2)}) %collective-permute-start.7) | collective-permute-done | bytes 184352 | tf_op jit(solution)/shard_map/ppermute | solution.py:879
  43.7 4.5 collective-permute-start.11
  50.6 6.7 %collective-permute-done.11 = bf16[192,768]{1,0:T(8,128)(2,1)S(1)} collective-permute-done((bf16[192,768]{1,0:T(8,128)(2,1)S(1)}, bf16[192,768]{1,0:T(8,128)(2,1)S(1)}, u32[]{:S(2)}, u32[]{:S(2)}) %collective-permute-start.11) | collective-permute-done | bytes 294944 | tf_op jit(solution)/shard_map/ppermute | solution.py:879
  57.3 11.4 %collective-permute-done.12 = bf16[192,768]{1,0:T(8,128)(2,1)S(1)} collective-permute-done((bf16[192,768]{1,0:T(8,128)(2,1)S(1)}, bf16[192,768]{1,0:T(8,128)(2,1)S(1)}, u32[]{:S(2)}, u32[]{:S(2)}) %collective-permute-start.12) | collective-permute-done | bytes 294944 | tf_op jit(solution)/shard_map/ppermute | solution.py:879
  72.9 9.2 %all-to-all-start = ((bf16[4,2,3648]{2,1,0:T(2,128)(2,1)}), bf16[4,2,3648]{2,1,0:T(2,128)(2,1)S(1)}, u32[]{:S(2)}, u32[]{:S(2)}) async-start(bf16[4,2,3648]{2,1,0:T(2,128)(2,1)} %reshape.355), calls=%async_computation | async-start | bytes 118784 | tf_op jit(solution)/shard_map/all_to_all | solution.py:854
  83.7 4.1 all-to-all-done
  90.0 2.5 collective-permute-start.2
  96.1 2.8 collective-permute-done.1
  99.7 19.3 %spatial_forward.1 = (bf16[4,256,768]{2,1,0:T(8,128)(2,1)}, bf16[4,256,2304]{2,1,0:T(8,128)(2,1)}, bf16[4,256,768]{2,1,0:T(8,128)(2,1)}) custom-call(bf16[4,256,768]{2,1,0:T(8,128)(2,1)} %x_ref.5, f32[4,9,768]{2,1,0:T(8,128)} %reshape.302.mod_ref, bf16[8,4,72,768]{3,2,1,0:T(8,128)(2,1)} %bitcast.154, f32[1,2304]{1,0:T(1,128)} %reshape.335.bsi), custom_call_target="tpu_custom_call" | custom-call | flops 5234491392 | bytes 12000000 | tf_op jit(solution)/shard_map/spatial_forward/pallas_call | solution.py:132
  118.9 6.7 %project_forward.1 = (f32[4,256,768]{2,1,0:T(8,128)}, f32[4,256,768]{2,1,0:T(8,128)}, bf16[4,256,768]{2,1,0:T(8,128)(2,1)}) custom-call(bf16[4,256,768]{2,1,0:T(8,128)(2,1)} %x_ref.5, bf16[4,256,768]{2,1,0:T(8,128)(2,1)} %get-tuple-element.117.attn_ref, f32[4,9,768]{2,1,0:T(8,128)} %reshape.302.mod_ref, bf16[8,4,120,768]{3,2,1,0:T(8,128)(2,1)} %bitcast.140, ...), custom_call_target="tpu_custom_call" | custom-call | flops 1207959552 | bytes 13000000 | tf_op jit(solution)/shard_map/project_forward/pallas_call | solution.py:161
  128.4 4.8 collective-permute-start.9
  136.6 8.1 %temporal_qkv.1.qkv_ref = bf16[4,256,2304]{2,1,0:T(8,128)(2,1)} custom-call(bf16[4,256,768]{2,1,0:T(8,128)(2,1)} %get-tuple-element.119.n_ref, bf16[8,4,120,768]{3,2,1,0:T(8,128)(2,1)} %bitcast.141, f32[1,2304]{1,0:T(1,128)} %reshape.337.bias.bti), custom_call_target="tpu_custom_call" | custom-call | flops 3623878656 | bytes 10000000 | tf_op jit(solution)/shard_map/temporal_qkv/pallas_call | solution.py:183
  144.7 3.5 collective-permute-done.10.nr_ref
  150.2 15.8 %temporal_forward.1 = (f32[4,5,256,128]{3,2,1,0:T(8,128)}, bf16[4,256,768]{2,1,0:T(8,128)(2,1)}, f32[4,256,768]{2,1,0:T(8,128)}, f32[4,256,768]{2,1,0:T(8,128)},...) custom-call(s32[5,4]{1,0:T(8,128)} %convert_element_type.244.allowed, ...), custom_call_target="tpu_custom_call" | custom-call | flops 4353687552 | bytes 22000000 | tf_op jit(solution)/shard_map/temporal_forward/pallas_call | solution.py:268
  166.1 31.4 %feed_forward.1 = (bf16[4,256,768]{2,1,0:T(8,128)(2,1)}, f32[4,256,768]{2,1,0:T(8,128)}, bf16[4,256,768]{2,1,0:T(8,128)(2,1)}, bf16[4,256,3072]{2,1,0:T(8,128)(2...) custom-call(f32[4,256,768]{2,1,0:T(8,128)} %get-tuple-element.121.af, ...), custom_call_target="tpu_custom_call" | custom-call | flops 19327352832 | bytes 32000000 | tf_op jit(solution)/shard_map/feed_forward/pallas_call | solution.py:349
  197.5 10.0 %outer_pieces.6.refs_2_ = bf16[8,4,192,768]{3,2,1,0:T(8,128)(2,1)} custom-call(bf16[1024,768]{1,0:T(8,128)(2,1)} %bitcast.210, bf16[1024,3072]{1,0:T(8,128)(2,1)} %bitcast.207), custom_call_target="tpu_custom_call" | custom-call | flops 4831838208 | bytes 12000000 | tf_op jit(solution)/shard_map/outer_pieces/pallas_call | solution.py:722
  207.5 9.2 %outer_pieces.7 = bf16[8,4,192,768]{3,2,1,0:T(8,128)(2,1)} custom-call(bf16[1024,3072]{1,0:T(8,128)(2,1)} %bitcast.150, bf16[1024,768]{1,0:T(8,128)(2,1)} %bitcast.157, bf16[8,4,192,768]{3,2,1,0:T(8,128)(2,1)} %outer_pieces.6.refs_2_), custom_call_target="tpu_custom_call", output_to_operand_aliasing={{}: (2, {})} | custom-call | flops 4831838208 | bytes 12000000 | tf_op jit(solution)/shard_map/outer_pieces/pallas_call | solution.py:722
  216.8 25.2 %temporal_backward.1 = (bf16[4,256,768]{2,1,0:T(8,128)(2,1)}, bf16[4,256,2304]{2,1,0:T(8,128)(2,1)}, bf16[2,256,1536]{2,1,0:T(8,128)(2,1)}, bf16[2,256,1536]{2,1...) custom-call(f32[4,256,768]{2,1,0:T(8,128)} %get-tuple-element.125.g_, ...), custom_call_target="tpu_custom_call" | custom-call | flops 5140119552 | bytes 36000000 | tf_op jit(solution)/shard_map/temporal_backward/pallas_call | solution.py:451
  242.1 20.8 %outer_pieces.5 = (bf16[4,4,96,768]{3,2,1,0:T(8,128)(2,1)}, bf16[4,4,96,768]{3,2,1,0:T(8,128)(2,1)}) custom-call(bf16[1024,768]{1,0:T(8,128)(2,1)} %bitcast.158, bf16[1024,2304]{1,0:T(8,128)(2,1)} %bitcast.151, bf16[1024,2304]{1,0:T(8,128)(2,1)} %bitcast.152, bf16[512,768]{1,0:T(8,128)(2,1)} %bitcast.162, bf16[512,1536]{1,0:T(8,128)(2,1)} %bitcast.202, ...), custom_call_target="tpu_custom_call" | custom-call | flops 7247757312 | bytes 12000000 | tf_op jit(solution)/shard_map/outer_pieces/pallas_call | solution.py:722
  263.0 4.3 collective-permute-start.15
  269.2 4.4 convert_add_fusion
  273.7 11.3 %collective-permute-done.15.fl_ref = bf16[2,256,768]{2,1,0:T(8,128)(2,1)S(1)} collective-permute-done((bf16[2,256,768]{2,1,0:T(8,128)(2,1)}, bf16[2,256,768]{2,1,0:T(8,128)(2,1)S(1)}, u32[]{:S(2)}, u32[]{:S(2)}) %collective-permute-start.15) | collective-permute-done | bytes 786464 | tf_op jit(solution)/shard_map/ppermute | solution.py:938
  285.0 4.2 collective-permute-done.16.fr_ref
  289.1 14.4 %project_backward.1 = (f32[4,256,768]{2,1,0:T(8,128)}, bf16[4,256,768]{2,1,0:T(8,128)(2,1)}, bf16[4,256,768]{2,1,0:T(8,128)(2,1)}, f32[4,3,768]{2,1,0:T(4,128)}, f32[1,768]{1,0:T(1,128)}) custom-call(bf16[4,256,2304]{2,1,0:T(8,128)(2,1)} %get-tuple-element.137.dqkv_ref, bf16[2,256,768]{2,1,0:T(8,128)(2,1)} %copy-done.4, ...), custom_call_target="tpu_custom_call" | custom-call | flops 4831838208 | bytes 24000000 | tf_op jit(solution)/shard_map/project_backward/pallas_call | solution.py:511
  312.1 16.1 %first_heads_backward.1 = (bf16[4,256,1152]{2,1,0:T(8,128)(2,1)}, f32[1,1152]{1,0:T(1,128)}) custom-call(bf16[4,256,2304]{2,1,0:T(8,128)(2,1)} %get-tuple-element.124.q_ref.k_ref.v_ref, bf16[4,256,2304]{2,1,0:T(8,128)(2,1)} %get-tuple-element.124.q_ref.k_ref.v_ref, bf16[4,256,2304]{2,1,0:T(8,128)(2,1)} %get-tuple-element.124.q_ref.k_ref.v_ref, ...), custom_call_target="tpu_custom_call" | custom-call | flops 2013265920 | bytes 16000000 | tf_op jit(solution)/shard_map/first_heads_backward/pallas_call | solution.py:605
  328.3 8.8 %collective-permute-done.18 = bf16[4,96,768]{2,1,0:T(8,128)(2,1)S(1)} collective-permute-done((bf16[4,96,768]{2,1,0:T(8,128)(2,1)S(1)}, bf16[4,96,768]{2,1,0:T(8,128)(2,1)S(1)}, u32[]{:S(2)}, u32[]{:S(2)}) %collective-permute-start.18) | collective-permute-done | bytes 589856 | tf_op jit(solution)/shard_map/ppermute | solution.py:969
  340.4 2.7 collective-permute-start.22
  343.1 2.6 pad_maximum_fusion
  345.9 7.5 %outer_pieces.8 = bf16[8,4,120,384]{3,2,1,0:T(8,128)(2,1)} custom-call(bf16[1024,768]{1,0:T(8,128)(2,1)} %bitcast.208, bf16[1024,1152]{1,0:T(8,128)(2,1)} %bitcast.156, bf16[1024,768]{1,0:T(8,128)(2,1)} %bitcast.159, bf16[1024,768]{1,0:T(8,128)(2,1)} %bitcast.199), custom_call_target="tpu_custom_call" | custom-call | flops 3019898880 | bytes 12000000 | tf_op jit(solution)/shard_map/outer_pieces/pallas_call | solution.py:722
  354.4 26.1 %last_heads_backward.1 = (bf16[4,256,1152]{2,1,0:T(8,128)(2,1)}, f32[1,1152]{1,0:T(1,128)}, f32[4,256,768]{2,1,0:T(8,128)}, f32[4,2,768]{2,1,0:T(2,128)}) custom-call(bf16[4,256,2304]{2,1,0:T(8,128)(2,1)} %get-tuple-element.124.q_ref.k_ref.v_ref, bf16[4,256,2304]{2,1,0:T(8,128)(2,1)} %get-tuple-element.124.q_ref.k_ref.v_ref, ...), custom_call_target="tpu_custom_call" | custom-call | flops 5637144576 | bytes 16000000 | tf_op jit(solution)/shard_map/last_heads_backward/pallas_call | solution.py:605
  384.7 52.8 %all_to_all.14 = bf16[8,4,120,384]{3,2,1,0:T(8,128)(2,1)S(1)} all-to-all(bf16[8,4,120,384]{3,2,1,0:T(8,128)(2,1)S(1)} %copy-done.1), channel_id=1, replica_groups=mesh['dp'=8,'frame'=4] {'dp'}, dimensions={0} | all-to-all | bytes 5898240 | tf_op jit(solution)/shard_map/all_to_all | solution.py:974
  439.0 3.3 collective-permute-start.26
  442.3 5.5 %outer_pieces.9 = (bf16[4,4,72,384]{3,2,1,0:T(8,128)(2,1)}, bf16[4,4,72,384]{3,2,1,0:T(8,128)(2,1)}) custom-call(bf16[1024,768]{1,0:T(8,128)(2,1)} %bitcast.209, bf16[1024,1152]{1,0:T(8,128)(2,1)} %bitcast.198, s32[1]{0:T(128)} %bitcast.32.refs_12_.refs_2_), custom_call_target="tpu_custom_call" | custom-call | flops 1811939328 | bytes 12000000 | tf_op jit(solution)/shard_map/outer_pieces/pallas_call | solution.py:722
  448.1 2.4 collective-permute-done.23
  455.5 4.8 collective-permute-done.27
  460.4 3.9 collective-permute-done.29
  466.6 2.8 collective-permute-start.32
  469.6 3.4 collective-permute-done.30
  473.1 4.7 collective-permute-done.31
  481.4 3.1 collective-permute-start.33
  491.6 7.9 %feed_outputs.1 = (f32[192,3072]{1,0:T(8,128)}, f32[768,768]{1,0:T(8,128)}, f32[192,2304]{1,0:T(8,128)}, f32[192,768]{1,0:T(8,128)}, bf16[128,768]{1,0:T(8,128)(...) custom-call(bf16[8,426,768]{2,1,0:T(8,128)(2,1)} %all-gather.15.cloned.1.call-done.piece), custom_call_target="tpu_custom_call" | custom-call | bytes 15000000 | tf_op jit(solution)/shard_map/feed_outputs/pallas_call | solution.py:819
  507.6 4.5 collective-permute-done.41.refs_6_
  512.1 3.8 collective-permute-done.42.refs_7_
  517.6 6.0 %last_outputs.1 = (f32[192,2304]{1,0:T(8,128)}, f32[192,768]{1,0:T(8,128)}, f32[192,6912]{1,0:T(8,128)}, f32[1,6912]{1,0:T(1,128)}, f32[6,384]{1,0:T(8,128)}) custom-call(s32[1]{0:T(128)} %bitcast.73.own_ref, bf16[262,384]{1,0:T(8,128)(2,1)} %copy-done.5, bf16[262,384]{1,0:T(8,128)(2,1)} %copy-done.6, bf16[262,384]{1,0:T(8,128)(2,1)} %copy-done.7, ...), custom_call_target="tpu_custom_call" | custom-call | flops 339738624 | bytes 12000000 | tf_op jit(solution)/shard_map/last_outputs/pallas_call | solution.py:779
  (286 shorter events, 91.0 us)
Async XLA Ops:
  7.2 92.5 %all-gather.9.cloned.1.call-start = ((), (), s32[]{:S(2)}) async-start(), calls=%async_computation.6 | async-start | bytes 3981312 | tf_op jit(solution)/shard_map/all_gather | solution.py:901
  8.1 10.9 %collective-permute-start.3 = (bf16[72,768]{1,0:T(8,128)(2,1)S(1)}, bf16[72,768]{1,0:T(8,128)(2,1)S(1)}, u32[]{:S(2)}, u32[]{:S(2)}) collective-permute-start(bf16[72,768]{1,0:T(8,128)(2,1)S(1)} %get-tuple-element.249), channel_id=1, source_target_pairs={{0,1},{1,2},{2,3},{3,0},{4,5},{5,6},{6,7},{7,4},{8,9},{9,10},{10,1... | collective-permute-start | bytes 331784 | tf_op jit(solution)/shard_map/ppermute | solution.py:879
  11.2 9.9 %collective-permute-start.4 = (bf16[72,768]{1,0:T(8,128)(2,1)S(1)}, bf16[72,768]{1,0:T(8,128)(2,1)S(1)}, u32[]{:S(2)}, u32[]{:S(2)}) collective-permute-start(bf16[72,768]{1,0:T(8,128)(2,1)S(1)} %get-tuple-element.249), channel_id=1, source_target_pairs={{0,2},{1,3},{2,0},{3,1},{4,6},{5,7},{6,4},{7,5},{8,10},{9,11},{10,... | collective-permute-start | bytes 331784 | tf_op jit(solution)/shard_map/ppermute | solution.py:879
  13.8 7.3 %collective-permute-start.5 = (bf16[72,768]{1,0:T(8,128)(2,1)S(1)}, bf16[72,768]{1,0:T(8,128)(2,1)S(1)}, u32[]{:S(2)}, u32[]{:S(2)}) collective-permute-start(bf16[72,768]{1,0:T(8,128)(2,1)S(1)} %get-tuple-element.249), channel_id=1, source_target_pairs={{0,3},{1,0},{2,1},{3,2},{4,7},{5,4},{6,5},{7,6},{8,11},{9,8},{10,9... | collective-permute-start | bytes 331784 | tf_op jit(solution)/shard_map/ppermute | solution.py:879
  22.1 96.8 %all-gather.11.cloned.1.call-start = ((), (), s32[]{:S(2)}) async-start(), calls=%async_computation.7 | async-start | bytes 6635520 | tf_op jit(solution)/shard_map/all_gather | solution.py:901
  22.1 9.6 %collective-permute-start.6 = (bf16[120,768]{1,0:T(8,128)(2,1)S(1)}, bf16[120,768]{1,0:T(8,128)(2,1)S(1)}, u32[]{:S(2)}, u32[]{:S(2)}) collective-permute-start(bf16[120,768]{1,0:T(8,128)(2,1)S(1)} %constant_dynamic-update-slice_fusion), channel_id=1, source_target_pairs={{0,1},{1,2},{2,3},{3,0},{4,5},{5,6},{6,7},{7,4},{8,9},{9,10},{10,1... | collective-permute-start | bytes 552968 | tf_op jit(solution)/shard_map/ppermute | solution.py:879
  25.0 13.5 %collective-permute-start.7 = (bf16[120,768]{1,0:T(8,128)(2,1)S(1)}, bf16[120,768]{1,0:T(8,128)(2,1)S(1)}, u32[]{:S(2)}, u32[]{:S(2)}) collective-permute-start(bf16[120,768]{1,0:T(8,128)(2,1)S(1)} %constant_dynamic-update-slice_fusion), channel_id=1, source_target_pairs={{0,2},{1,3},{2,0},{3,1},{4,6},{5,7},{6,4},{7,5},{8,10},{9,11},{10,... | collective-permute-start | bytes 552968 | tf_op jit(solution)/shard_map/ppermute | solution.py:879
  26.6 11.8 %collective-permute-start.8 = (bf16[120,768]{1,0:T(8,128)(2,1)S(1)}, bf16[120,768]{1,0:T(8,128)(2,1)S(1)}, u32[]{:S(2)}, u32[]{:S(2)}) collective-permute-start(bf16[120,768]{1,0:T(8,128)(2,1)S(1)} %constant_dynamic-update-slice_fusion), channel_id=1, source_target_pairs={{0,3},{1,0},{2,1},{3,2},{4,7},{5,4},{6,5},{7,6},{8,11},{9,8},{10,9... | collective-permute-start | bytes 552968 | tf_op jit(solution)/shard_map/ppermute | solution.py:879
  39.6 126.5 %all-gather.13.cloned.1.call-start = ((), (), s32[]{:S(2)}) async-start(), calls=%async_computation.8 | async-start | bytes 10616832 | tf_op jit(solution)/shard_map/all_gather | solution.py:901
  43.7 13.7 %collective-permute-start.11 = (bf16[192,768]{1,0:T(8,128)(2,1)S(1)}, bf16[192,768]{1,0:T(8,128)(2,1)S(1)}, u32[]{:S(2)}, u32[]{:S(2)}) collective-permute-start(bf16[192,768]{1,0:T(8,128)(2,1)S(1)} %dynamic-slice_dynamic-update-slice_fusion), channel_id=1, source_target_pairs={{0,1},{1,2},{2,3},{3,0},{4,5},{5,6},{6,7},{7,4},{8,9},{9,10},{10,1... | collective-permute-start | bytes 884744 | tf_op jit(solution)/shard_map/ppermute | solution.py:879
  48.2 20.6 %collective-permute-start.12 = (bf16[192,768]{1,0:T(8,128)(2,1)S(1)}, bf16[192,768]{1,0:T(8,128)(2,1)S(1)}, u32[]{:S(2)}, u32[]{:S(2)}) collective-permute-start(bf16[192,768]{1,0:T(8,128)(2,1)S(1)} %dynamic-slice_dynamic-update-slice_fusion), channel_id=1, source_target_pairs={{0,2},{1,3},{2,0},{3,1},{4,6},{5,7},{6,4},{7,5},{8,10},{9,11},{10,... | collective-permute-start | bytes 884744 | tf_op jit(solution)/shard_map/ppermute | solution.py:879
  49.9 18.9 %collective-permute-start.13 = (bf16[192,768]{1,0:T(8,128)(2,1)S(1)}, bf16[192,768]{1,0:T(8,128)(2,1)S(1)}, u32[]{:S(2)}, u32[]{:S(2)}) collective-permute-start(bf16[192,768]{1,0:T(8,128)(2,1)S(1)} %dynamic-slice_dynamic-update-slice_fusion), channel_id=1, source_target_pairs={{0,3},{1,0},{2,1},{3,2},{4,7},{5,4},{6,5},{7,6},{8,11},{9,8},{10,9... | collective-permute-start | bytes 884744 | tf_op jit(solution)/shard_map/ppermute | solution.py:879
  72.9 14.9 %all-to-all-start = ((bf16[4,2,3648]{2,1,0:T(2,128)(2,1)}), bf16[4,2,3648]{2,1,0:T(2,128)(2,1)S(1)}, u32[]{:S(2)}, u32[]{:S(2)}) async-start(bf16[4,2,3648]{2,1,0:T(2,128)(2,1)} %reshape.355), calls=%async_computation | async-start | bytes 118784 | tf_op jit(solution)/shard_map/all_to_all | solution.py:854
  82.0 256.6 %reduce-scatter.3.cloned.1.call-start = ((), (), s32[]{:S(2)}) async-start(), calls=%async_computation.4 | async-start | bytes 10616832 | tf_op jit(solution)/shard_map/reduce_scatter | solution.py:1080
  88.7 7.4 %collective-permute-start = (f32[4,6912]{1,0:T(4,128)S(1)}, f32[4,6912]{1,0:T(4,128)S(1)}, u32[]{:S(2)}, u32[]{:S(2)}) collective-permute-start(f32[4,6912]{1,0:T(4,128)S(1)} %get-tuple-element.241), channel_id=1, source_target_pairs={{0,1},{1,2},{2,3},{3,0},{4,5},{5,6},{6,7},{7,4},{8,9},{9,10},{10,1... | collective-permute-start | bytes 331784 | tf_op jit(solution)/shard_map/ppermute | solution.py:984
  89.6 9.2 %collective-permute-start.1 = (f32[4,6912]{1,0:T(4,128)S(1)}, f32[4,6912]{1,0:T(4,128)S(1)}, u32[]{:S(2)}, u32[]{:S(2)}) collective-permute-start(f32[4,6912]{1,0:T(4,128)S(1)} %get-tuple-element.243), channel_id=1, source_target_pairs={{0,2},{1,3},{2,0},{3,1},{4,6},{5,7},{6,4},{7,5},{8,10},{9,11},{10,... | collective-permute-start | bytes 331784 | tf_op jit(solution)/shard_map/ppermute | solution.py:984
  90.0 8.8 %collective-permute-start.2 = (f32[4,6912]{1,0:T(4,128)S(1)}, f32[4,6912]{1,0:T(4,128)S(1)}, u32[]{:S(2)}, u32[]{:S(2)}) collective-permute-start(f32[4,6912]{1,0:T(4,128)S(1)} %get-tuple-element.242), channel_id=1, source_target_pairs={{0,3},{1,0},{2,1},{3,2},{4,7},{5,4},{6,5},{7,6},{8,11},{9,8},{10,9... | collective-permute-start | bytes 331784 | tf_op jit(solution)/shard_map/ppermute | solution.py:984
  127.1 21.0 %collective-permute-start.10 = (bf16[2,256,768]{2,1,0:T(8,128)(2,1)S(1)}, bf16[2,256,768]{2,1,0:T(8,128)(2,1)S(1)}, u32[]{:S(2)}, u32[]{:S(2)}) collective-permute-start(bf16[2,256,768]{2,1,0:T(8,128)(2,1)S(1)} %get-tuple-element.221), channel_id=1, source_target_pairs={{1,0},{2,1},{3,2},{5,4},{6,5},{7,6},{9,8},{10,9},{11,10},{13,12},{... | collective-permute-start | bytes 2359304 | tf_op jit(solution)/shard_map/ppermute | solution.py:938
  128.4 20.9 %collective-permute-start.9 = (bf16[2,256,768]{2,1,0:T(8,128)(2,1)S(1)}, bf16[2,256,768]{2,1,0:T(8,128)(2,1)S(1)}, u32[]{:S(2)}, u32[]{:S(2)}) collective-permute-start(bf16[2,256,768]{2,1,0:T(8,128)(2,1)S(1)} %get-tuple-element.222), channel_id=1, source_target_pairs={{0,1},{1,2},{2,3},{4,5},{5,6},{6,7},{8,9},{9,10},{10,11},{12,13},{... | collective-permute-start | bytes 2359304 | tf_op jit(solution)/shard_map/ppermute | solution.py:938
  216.7 166.0 %reduce-scatter.5.cloned.1.call-start = ((), (), s32[]{:S(2)}) async-start(), calls=%async_computation.5 | async-start | bytes 2211840 | tf_op jit(solution)/shard_map/reduce_scatter | solution.py:1115
  262.9 6.3 %collective-permute-start.14 = (bf16[4,4,96,768]{3,2,1,0:T(8,128)(2,1)}, bf16[4,4,96,768]{3,2,1,0:T(8,128)(2,1)S(1)}, u32[]{:S(2)}, u32[]{:S(2)}) collective-permute-start(bf16[4,4,96,768]{3,2,1,0:T(8,128)(2,1)} %get-tuple-element.136), channel_id=1, source_target_pairs={{0,4},{4,0},{8,12},{12,8},{16,20},{20,16},{24,28},{28,24},{1,5},{5... | collective-permute-start | bytes 7077896 | tf_op jit(solution)/shard_map/ppermute | solution.py:946
  263.0 22.0 %collective-permute-start.15 = (bf16[2,256,768]{2,1,0:T(8,128)(2,1)}, bf16[2,256,768]{2,1,0:T(8,128)(2,1)S(1)}, u32[]{:S(2)}, u32[]{:S(2)}) collective-permute-start(bf16[2,256,768]{2,1,0:T(8,128)(2,1)} %get-tuple-element.138), channel_id=1, source_target_pairs={{0,1},{1,2},{2,3},{4,5},{5,6},{6,7},{8,9},{9,10},{10,11},{12,13},{... | collective-permute-start | bytes 2359304 | tf_op jit(solution)/shard_map/ppermute | solution.py:938
  267.3 21.8 %collective-permute-start.16 = (bf16[2,256,768]{2,1,0:T(8,128)(2,1)}, bf16[2,256,768]{2,1,0:T(8,128)(2,1)}, u32[]{:S(2)}, u32[]{:S(2)}) collective-permute-start(bf16[2,256,768]{2,1,0:T(8,128)(2,1)} %get-tuple-element.139), channel_id=1, source_target_pairs={{1,0},{2,1},{3,2},{5,4},{6,5},{7,6},{9,8},{10,9},{11,10},{13,12},{... | collective-permute-start | bytes 2359304 | tf_op jit(solution)/shard_map/ppermute | solution.py:938
  308.6 19.7 %collective-permute-start.17 = (bf16[4,96,768]{2,1,0:T(8,128)(2,1)S(1)}, bf16[4,96,768]{2,1,0:T(8,128)(2,1)S(1)}, u32[]{:S(2)}, u32[]{:S(2)}) collective-permute-start(bf16[4,96,768]{2,1,0:T(8,128)(2,1)S(1)} %get-tuple-element.215), channel_id=1, source_target_pairs={{0,8},{4,12},{8,0},{12,4},{16,24},{20,28},{24,16},{28,20},{1,9},{5... | collective-permute-start | bytes 1769480 | tf_op jit(solution)/shard_map/ppermute | solution.py:969
  310.2 26.9 %collective-permute-start.18 = (bf16[4,96,768]{2,1,0:T(8,128)(2,1)S(1)}, bf16[4,96,768]{2,1,0:T(8,128)(2,1)S(1)}, u32[]{:S(2)}, u32[]{:S(2)}) collective-permute-start(bf16[4,96,768]{2,1,0:T(8,128)(2,1)S(1)} %get-tuple-element.217), channel_id=1, source_target_pairs={{0,16},{4,20},{8,24},{12,28},{16,0},{20,4},{24,8},{28,12},{1,17},{... | collective-permute-start | bytes 1769480 | tf_op jit(solution)/shard_map/ppermute | solution.py:969
  311.7 25.4 %collective-permute-start.19 = (bf16[4,96,768]{2,1,0:T(8,128)(2,1)S(1)}, bf16[4,96,768]{2,1,0:T(8,128)(2,1)S(1)}, u32[]{:S(2)}, u32[]{:S(2)}) collective-permute-start(bf16[4,96,768]{2,1,0:T(8,128)(2,1)S(1)} %get-tuple-element.216), channel_id=1, source_target_pairs={{0,24},{4,28},{8,16},{12,20},{16,8},{20,12},{24,0},{28,4},{1,25},{... | collective-permute-start | bytes 1769480 | tf_op jit(solution)/shard_map/ppermute | solution.py:969
  338.7 14.8 %collective-permute-start.20 = (bf16[4,8064]{1,0:T(4,128)(2,1)S(1)}, bf16[4,8064]{1,0:T(4,128)(2,1)S(1)}, u32[]{:S(2)}, u32[]{:S(2)}) collective-permute-start(bf16[4,8064]{1,0:T(4,128)(2,1)S(1)} %pad_maximum_fusion.12), channel_id=1, source_target_pairs={{0,1},{1,2},{2,3},{3,0},{4,5},{5,6},{6,7},{7,4},{8,9},{9,10},{10,1... | collective-permute-start | bytes 193544 | tf_op jit(solution)/shard_map/ppermute | solution.py:879
  340.4 13.1 %collective-permute-start.21 = (bf16[4,8064]{1,0:T(4,128)(2,1)S(1)}, bf16[4,8064]{1,0:T(4,128)(2,1)S(1)}, u32[]{:S(2)}, u32[]{:S(2)}) collective-permute-start(bf16[4,8064]{1,0:T(4,128)(2,1)S(1)} %pad_maximum_fusion.12), channel_id=1, source_target_pairs={{0,2},{1,3},{2,0},{3,1},{4,6},{5,7},{6,4},{7,5},{8,10},{9,11},{10,... | collective-permute-start | bytes 193544 | tf_op jit(solution)/shard_map/ppermute | solution.py:879
  340.4 13.1 %collective-permute-start.22 = (bf16[4,8064]{1,0:T(4,128)(2,1)S(1)}, bf16[4,8064]{1,0:T(4,128)(2,1)S(1)}, u32[]{:S(2)}, u32[]{:S(2)}) collective-permute-start(bf16[4,8064]{1,0:T(4,128)(2,1)S(1)} %pad_maximum_fusion.12), channel_id=1, source_target_pairs={{0,3},{1,0},{2,1},{3,2},{4,7},{5,4},{6,5},{7,6},{8,11},{9,8},{10,9... | collective-permute-start | bytes 193544 | tf_op jit(solution)/shard_map/ppermute | solution.py:879
  345.7 145.9 %all-gather.15.cloned.1.call-start = ((), (), s32[]{:S(2)}) async-start(), calls=%async_computation.9 | async-start | bytes 5971968 | tf_op jit(solution)/shard_map/all_gather | solution.py:1134
  438.4 9.4 %collective-permute-start.24 = (bf16[4,2112]{1,0:T(4,128)(2,1)S(1)}, bf16[4,2112]{1,0:T(4,128)(2,1)S(1)}, u32[]{:S(2)}, u32[]{:S(2)}) collective-permute-start(bf16[4,2112]{1,0:T(4,128)(2,1)S(1)} %constant_dynamic-update-slice_fusion.18), channel_id=1, source_target_pairs={{0,1},{1,2},{2,3},{3,0},{4,5},{5,6},{6,7},{7,4},{8,9},{9,10},{10,1... | collective-permute-start | bytes 50696 | tf_op jit(solution)/shard_map/ppermute | solution.py:879
  438.5 9.4 %collective-permute-start.25 = (bf16[4,2112]{1,0:T(4,128)(2,1)S(1)}, bf16[4,2112]{1,0:T(4,128)(2,1)S(1)}, u32[]{:S(2)}, u32[]{:S(2)}) collective-permute-start(bf16[4,2112]{1,0:T(4,128)(2,1)S(1)} %constant_dynamic-update-slice_fusion.18), channel_id=1, source_target_pairs={{0,2},{1,3},{2,0},{3,1},{4,6},{5,7},{6,4},{7,5},{8,10},{9,11},{10,... | collective-permute-start | bytes 50696 | tf_op jit(solution)/shard_map/ppermute | solution.py:879
  439.0 8.9 %collective-permute-start.26 = (bf16[4,2112]{1,0:T(4,128)(2,1)S(1)}, bf16[4,2112]{1,0:T(4,128)(2,1)S(1)}, u32[]{:S(2)}, u32[]{:S(2)}) collective-permute-start(bf16[4,2112]{1,0:T(4,128)(2,1)S(1)} %constant_dynamic-update-slice_fusion.18), channel_id=1, source_target_pairs={{0,3},{1,0},{2,1},{3,2},{4,7},{5,4},{6,5},{7,6},{8,11},{9,8},{10,9... | collective-permute-start | bytes 50696 | tf_op jit(solution)/shard_map/ppermute | solution.py:879
  451.9 8.4 %collective-permute-start.27 = (bf16[4,72,384]{2,1,0:T(8,128)(2,1)S(1)}, bf16[4,72,384]{2,1,0:T(8,128)(2,1)S(1)}, u32[]{:S(2)}, u32[]{:S(2)}) collective-permute-start(bf16[4,72,384]{2,1,0:T(8,128)(2,1)S(1)} %get-tuple-element.218), channel_id=1, source_target_pairs={{0,8},{4,12},{8,0},{12,4},{16,24},{20,28},{24,16},{28,20},{1,9},{5... | collective-permute-start | bytes 663560 | tf_op jit(solution)/shard_map/ppermute | solution.py:969
  452.3 8.1 %collective-permute-start.28 = (bf16[4,72,384]{2,1,0:T(8,128)(2,1)S(1)}, bf16[4,72,384]{2,1,0:T(8,128)(2,1)S(1)}, u32[]{:S(2)}, u32[]{:S(2)}) collective-permute-start(bf16[4,72,384]{2,1,0:T(8,128)(2,1)S(1)} %get-tuple-element.220), channel_id=1, source_target_pairs={{0,16},{4,20},{8,24},{12,28},{16,0},{20,4},{24,8},{28,12},{1,17},{... | collective-permute-start | bytes 663560 | tf_op jit(solution)/shard_map/ppermute | solution.py:969
  453.1 11.2 %collective-permute-start.29 = (bf16[4,72,384]{2,1,0:T(8,128)(2,1)S(1)}, bf16[4,72,384]{2,1,0:T(8,128)(2,1)S(1)}, u32[]{:S(2)}, u32[]{:S(2)}) collective-permute-start(bf16[4,72,384]{2,1,0:T(8,128)(2,1)S(1)} %get-tuple-element.219), channel_id=1, source_target_pairs={{0,24},{4,28},{8,16},{12,20},{16,8},{20,12},{24,0},{28,4},{1,25},{... | collective-permute-start | bytes 663560 | tf_op jit(solution)/shard_map/ppermute | solution.py:969
  464.5 8.6 %collective-permute-start.30 = (bf16[192,384]{1,0:T(8,128)(2,1)S(1)}, bf16[192,384]{1,0:T(8,128)(2,1)S(1)}, u32[]{:S(2)}, u32[]{:S(2)}) collective-permute-start(bf16[192,384]{1,0:T(8,128)(2,1)S(1)} %get-tuple-element.223), channel_id=1, source_target_pairs={{0,1},{1,2},{2,3},{3,0},{4,5},{5,6},{6,7},{7,4},{8,9},{9,10},{10,1... | collective-permute-start | bytes 442376 | tf_op jit(solution)/shard_map/ppermute | solution.py:984
  465.1 12.6 %collective-permute-start.31 = (bf16[192,384]{1,0:T(8,128)(2,1)S(1)}, bf16[192,384]{1,0:T(8,128)(2,1)S(1)}, u32[]{:S(2)}, u32[]{:S(2)}) collective-permute-start(bf16[192,384]{1,0:T(8,128)(2,1)S(1)} %get-tuple-element.224), channel_id=1, source_target_pairs={{0,2},{1,3},{2,0},{3,1},{4,6},{5,7},{6,4},{7,5},{8,10},{9,11},{10,... | collective-permute-start | bytes 442376 | tf_op jit(solution)/shard_map/ppermute | solution.py:984
  466.6 11.1 %collective-permute-start.32 = (bf16[192,384]{1,0:T(8,128)(2,1)S(1)}, bf16[192,384]{1,0:T(8,128)(2,1)S(1)}, u32[]{:S(2)}, u32[]{:S(2)}) collective-permute-start(bf16[192,384]{1,0:T(8,128)(2,1)S(1)} %get-tuple-element.225), channel_id=1, source_target_pairs={{0,3},{1,0},{2,1},{3,2},{4,7},{5,4},{6,5},{7,6},{8,11},{9,8},{10,9... | collective-permute-start | bytes 442376 | tf_op jit(solution)/shard_map/ppermute | solution.py:984
  481.4 6.5 %collective-permute-start.33 = (f32[4,192]{1,0:T(4,128)S(1)}, f32[4,192]{1,0:T(4,128)S(1)}, u32[]{:S(2)}, u32[]{:S(2)}) collective-permute-start(f32[4,192]{1,0:T(4,128)S(1)} %get-tuple-element.269), channel_id=1, source_target_pairs={{0,1},{1,2},{2,3},{3,0},{4,5},{5,6},{6,7},{7,4},{8,9},{9,10},{10,1... | collective-permute-start | bytes 9224 | tf_op jit(solution)/shard_map/ppermute | solution.py:864
  484.5 4.7 collective-permute-start.34
  487.2 16.0 %collective-permute-start.36 = (bf16[262,384]{1,0:T(8,128)(2,1)S(1)}, bf16[262,384]{1,0:T(8,128)(2,1)S(1)}, u32[]{:S(2)}, u32[]{:S(2)}) collective-permute-start(bf16[262,384]{1,0:T(8,128)(2,1)S(1)} %constant_dynamic-update-slice_fusion.20.refs_0_), channel_id=1, source_target_pairs={{0,4},{4,0},{8,12},{12,8},{16,20},{20,16},{24,28},{28,24},{1,5},{5... | collective-permute-start | bytes 603656 | tf_op jit(solution)/shard_map/ppermute | solution.py:994
  487.3 17.3 %collective-permute-start.37 = (bf16[262,384]{1,0:T(8,128)(2,1)S(1)}, bf16[262,384]{1,0:T(8,128)(2,1)S(1)}, u32[]{:S(2)}, u32[]{:S(2)}) collective-permute-start(bf16[262,384]{1,0:T(8,128)(2,1)S(1)} %constant_dynamic-update-slice_fusion.20.refs_0_), channel_id=1, source_target_pairs={{0,8},{4,12},{8,0},{12,4},{16,24},{20,28},{24,16},{28,20},{1,9},{5... | collective-permute-start | bytes 603656 | tf_op jit(solution)/shard_map/ppermute | solution.py:994
  488.0 19.6 %collective-permute-start.38 = (bf16[262,384]{1,0:T(8,128)(2,1)S(1)}, bf16[262,384]{1,0:T(8,128)(2,1)S(1)}, u32[]{:S(2)}, u32[]{:S(2)}) collective-permute-start(bf16[262,384]{1,0:T(8,128)(2,1)S(1)} %constant_dynamic-update-slice_fusion.20.refs_0_), channel_id=1, source_target_pairs={{0,12},{4,8},{8,4},{12,0},{16,28},{20,24},{24,20},{28,16},{1,13},{... | collective-permute-start | bytes 603656 | tf_op jit(solution)/shard_map/ppermute | solution.py:994
  489.1 18.5 %collective-permute-start.39 = (bf16[262,384]{1,0:T(8,128)(2,1)S(1)}, bf16[262,384]{1,0:T(8,128)(2,1)S(1)}, u32[]{:S(2)}, u32[]{:S(2)}) collective-permute-start(bf16[262,384]{1,0:T(8,128)(2,1)S(1)} %constant_dynamic-update-slice_fusion.20.refs_0_), channel_id=1, source_target_pairs={{0,16},{4,20},{8,24},{12,28},{16,0},{20,4},{24,8},{28,12},{1,17},{... | collective-permute-start | bytes 603656 | tf_op jit(solution)/shard_map/ppermute | solution.py:994
  490.6 17.0 %collective-permute-start.40 = (bf16[262,384]{1,0:T(8,128)(2,1)S(1)}, bf16[262,384]{1,0:T(8,128)(2,1)S(1)}, u32[]{:S(2)}, u32[]{:S(2)}) collective-permute-start(bf16[262,384]{1,0:T(8,128)(2,1)S(1)} %constant_dynamic-update-slice_fusion.20.refs_0_), channel_id=1, source_target_pairs={{0,20},{4,16},{8,28},{12,24},{16,4},{20,0},{24,12},{28,8},{1,21},{... | collective-permute-start | bytes 603656 | tf_op jit(solution)/shard_map/ppermute | solution.py:994
  503.2 8.9 %collective-permute-start.41 = (bf16[262,384]{1,0:T(8,128)(2,1)S(1)}, bf16[262,384]{1,0:T(8,128)(2,1)S(1)}, u32[]{:S(2)}, u32[]{:S(2)}) collective-permute-start(bf16[262,384]{1,0:T(8,128)(2,1)S(1)} %constant_dynamic-update-slice_fusion.20.refs_0_), channel_id=1, source_target_pairs={{0,24},{4,28},{8,16},{12,20},{16,8},{20,12},{24,0},{28,4},{1,25},{... | collective-permute-start | bytes 603656 | tf_op jit(solution)/shard_map/ppermute | solution.py:994
  504.6 11.3 %collective-permute-start.42 = (bf16[262,384]{1,0:T(8,128)(2,1)S(1)}, bf16[262,384]{1,0:T(8,128)(2,1)S(1)}, u32[]{:S(2)}, u32[]{:S(2)}) collective-permute-start(bf16[262,384]{1,0:T(8,128)(2,1)S(1)} %constant_dynamic-update-slice_fusion.20.refs_0_), channel_id=1, source_target_pairs={{0,28},{4,24},{8,20},{12,16},{16,12},{20,8},{24,4},{28,0},{1,29},{... | collective-permute-start | bytes 603656 | tf_op jit(solution)/shard_map/ppermute | solution.py:994
  (33 other events, 332.3 us)
Sparse Core Ops, SparseCore 0:
  22.2 35.3 all-gather.8
  60.1 43.7 all-gather.10
  106.4 58.6 all-gather.12
  216.9 77.9 reduce-scatter.2
  345.8 36.8 reduce-scatter.4
  385.1 60.9 all-gather.14
